TPU v7x, 128 devices: a whole 4x4x4 slice. The times are simulated.
128 devices in a mesh: scene: 8 (over z, core), rows: 16 (over y, x).
Axes of the slice: x: 4, y: 4, z: 4, core: 2. Of those that a mesh axis runs over, the one named last changes fastest.
Arguments:
- observations: float32 [2048, 256, 512], P(('scene', 'rows')), may hold values from -100 to 100
- inverse_factor: float32 [512, 512], replicated, may hold values from -2 to 2, as said below
- tile_count: int32 [128], P(('scene', 'rows')), may hold values from 0 to 16
- tile_owner: int32 [2048], P(('scene', 'rows')), may hold values from 0 to 7, as said below
- tile_slot: int32 [2048], P(('scene', 'rows')), may hold values from 0 to 7
Outputs:
- orthonormal: float32 [1024, 256, 512], P(('scene', 'rows'))
- factor: float32 [512, 512], replicated
Inputs may be any that keep to these rules, and one draw needn't show every extreme that they name: `tile_owner`: within each group (fixed rows index), every row-block owner's 8 slots are each named by exactly one live tile of that group; at most 2 live tiles of one device name the same owner, and in every group one device names every owner 2 times. `inverse_factor`: upper triangular with a positive diagonal.
All inputs are finite; a program needn't handle non-finite values.
Results may differ from a plain program's by a relative error of at most 0.0001.
Values sent between devices are 32-bit elements; how exact they have to be, the bound alone decides.
No kernel may reach another device: no remote copies, remote signals or barrier semaphores. Data moves between devices by JAX's collectives and lax.ppermute only.
A program may use at most 128 MiB of HBM per device.

v0:
```python
import jax
import jax.numpy as jnp
from jax import lax
from jax.sharding import PartitionSpec as P

OWN_TILES = 8


def from_partner(shard, axis, bit):
    return lax.ppermute(shard, axis, [(i, i ^ 1 << bit) for i in range(lax.axis_size(axis))])


def gram_term(projected):
    return lax.dot_general(
        projected,
        projected,
        (((0,), (0,)), ((), ())),
        precision=lax.Precision.HIGHEST,
        preferred_element_type=jnp.float32,
    )


def shards(observations, inverse_factor, tile_count, tile_owner, tile_slot):
    scenes = lax.axis_size("scene")
    devices = scenes * lax.axis_size("rows")
    capacity = tile_owner.shape[0]
    pair_most = capacity // scenes
    tile_rows = observations.shape[1]
    column_count = observations.shape[2]
    position = jnp.arange(capacity, dtype=jnp.int32)
    is_live = position < tile_count[0]
    earlier = (
        (tile_owner[:, None] == tile_owner[None, :])
        & is_live[None, :]
        & (position[None, :] < position[:, None])
    )
    seat_rank = earlier.sum(1)
    target = jnp.where(is_live, tile_owner * pair_most + seat_rank, -1)
    selector = (target[None, :] == position[:, None]).astype(jnp.int32)
    filled = selector.sum(1) > 0
    chosen = (selector * position[None, :]).sum(1)
    slot_sent = (
        jnp.where(filled, (selector * tile_slot[None, :]).sum(1), -1)
        .astype(jnp.float32)
        .reshape(scenes, pair_most)
    )
    keep_mask = filled.astype(jnp.float32)[:, None, None]
    outgoing = jnp.take(observations, chosen, axis=0) * keep_mask
    received, slot_ids = (
        lax.all_to_all(
            outgoing.reshape(scenes, pair_most, tile_rows, column_count),
            "scene",
            split_axis=0,
            concat_axis=0,
            tiled=True,
        ),
        lax.all_to_all(slot_sent, "scene", split_axis=0, concat_axis=0, tiled=True),
    )
    flat_tiles = received.reshape(capacity, tile_rows, column_count)
    slot_flat = slot_ids.reshape(capacity).astype(jnp.int32)
    matches = (slot_flat[None, :] == jnp.arange(OWN_TILES, dtype=jnp.int32)[:, None]).astype(
        jnp.int32
    )
    order_idx = (matches * position[None, :]).sum(1)
    row_block = jnp.take(flat_tiles, order_idx, axis=0).reshape(-1, column_count)
    projected = jnp.dot(
        row_block,
        inverse_factor,
        precision=lax.Precision.HIGHEST,
        preferred_element_type=jnp.float32,
    )
    partial_value = gram_term(projected)
    gram_sum = partial_value
    for bit_index in range(devices.bit_length() - 1):
        gram_sum = gram_sum + from_partner(gram_sum, ("scene", "rows"), bit_index)
    weight = gram_sum / (devices * OWN_TILES * tile_rows)
    lower_factor = jnp.linalg.cholesky(weight)
    identity = jnp.eye(column_count, dtype=jnp.float32)
    inv_upper = jax.scipy.linalg.solve_triangular(lower_factor, identity, lower=True).T
    orthonormal = jnp.dot(
        projected, inv_upper, precision=lax.Precision.HIGHEST, preferred_element_type=jnp.float32
    )
    return (orthonormal.reshape(OWN_TILES, tile_rows, column_count), lower_factor.T)


def solution(mesh):
    in_specs = (
        P(("scene", "rows"), None, None),
        P(),
        P(("scene", "rows")),
        P(("scene", "rows")),
        P(("scene", "rows")),
    )
    out_specs = (P(("scene", "rows"), None, None), P())
    return jax.shard_map(shards, mesh=mesh, in_specs=in_specs, out_specs=out_specs, check_vma=False)
```

profile of v0, /device:TPU:1, one launch (start us, length us, event | category | flops | bytes accessed | tf_op | source)
XLA Modules:
  0.0 462.8 jit_solution(8798924410623399791)
XLA Ops:
  4.5 6.8 %all-to-all-start = ((f32[8,1,2]{2,1,0:T(1,128)}), f32[8,1,2]{2,1,0:T(1,128)S(1)}, u32[]{:S(2)}, u32[]{:S(2)}) async-start(f32[8,1,2]{2,1,0:T(1,128)} %bitcast.1), calls=%async_computation | async-start | bytes 8192 | tf_op jit(solution)/shard_map/all_to_all | solution.py:57
  11.5 7.7 %gather_fusion = f32[16,256,512]{2,1,0:T(8,128)} fusion(f32[16,256,512]{2,1,0:T(8,128)} %param.5, s32[1024]{0:T(1024)S(1)} %pad_clamp_fusion.1), kind=kCustom, calls=%fused_computation | custom fusion | bytes 16777280 | tf_op jit(solution)/shard_map/jit(_take)/gather | solution.py:48
  19.1 7.8 %select_multiply_fusion = f32[8,2,256,512]{3,2,1,0:T(8,128)} fusion(f32[8,2,256,512]{3,2,1,0:T(8,128)} %bitcast.72, f32[8,2]{1,0:T(8,128)S(1)} %reshape.173, pred[8,2]{1,0:T(8,128)(4,1)S(1)} %compare_and_fusion), kind=kLoop, calls=%fused_computation.4 | loop fusion | flops 4194304 | bytes 16777296 | tf_op jit(solution)/shard_map/mul | solution.py:48
  27.0 4.9 %all-to-all-start.1 = ((f32[8,2,256,512]{3,2,1,0:T(8,128)}), f32[8,2,256,512]{3,2,1,0:T(8,128)}, u32[]{:S(2)}, u32[]{:S(2)}) async-start(f32[8,2,256,512]{3,2,1,0:T(8,128)} %select_multiply_fusion), calls=%async_computation.1 | async-start | bytes 16777216 | tf_op jit(solution)/shard_map/all_to_all | solution.py:50
  32.3 93.5 %all-to-all-done.1 = f32[8,2,256,512]{3,2,1,0:T(8,128)} async-done(((f32[8,2,256,512]{3,2,1,0:T(8,128)}), f32[8,2,256,512]{3,2,1,0:T(8,128)}, u32[]{:S(2)}, u32[]{:S(2)}) %all-to-all-start.1) | async-done | bytes 8388640 | tf_op jit(solution)/shard_map/all_to_all | solution.py:50
  125.8 6.2 %gather_fusion.1 = f32[8,256,512]{2,1,0:T(8,128)} fusion(f32[16,256,512]{2,1,0:T(8,128)} %bitcast.5, s32[1024]{0:T(1024)S(1)} %pad_clamp_fusion), kind=kCustom, calls=%fused_computation.1 | custom fusion | bytes 8388640 | tf_op jit(solution)/shard_map/jit(_take)/gather | solution.py:65
  134.7 7.5 %fusion.47 = f32[2048,512]{1,0:T(8,128)S(1)} fusion(f32[2048,512]{1,0:T(8,128)S(1)} %bitcast_select_fusion, f32[512,512]{1,0:T(8,128)S(1)} %copy-done), kind=kOutput, calls=%fused_computation.109 | convolution fusion | flops 6442450944 | bytes 9437184 | tf_op jit(solution)/shard_map/dot_general | solution.py:66
  142.2 7.5 %fusion.48 = f32[512,512]{0,1:T(8,128)S(1)} fusion(f32[2048,512]{1,0:T(8,128)S(1)} %fusion.47), kind=kOutput, calls=%fused_computation.110 | convolution fusion | flops 6442450944 | bytes 5242880 | tf_op jit(solution)/shard_map/dot_general | solution.py:14
  151.0 22.6 %collective-permute-done = f32[512,512]{0,1:T(8,128)S(1)} collective-permute-done((f32[512,512]{0,1:T(8,128)S(1)}, f32[512,512]{0,1:T(8,128)S(1)}, u32[]{:S(2)}, u32[]{:S(2)}) %collective-permute-start) | collective-permute-done | bytes 1048608 | tf_op jit(solution)/shard_map/ppermute | solution.py:10
  176.6 21.6 %collective-permute-done.1 = f32[512,512]{0,1:T(8,128)S(1)} collective-permute-done((f32[512,512]{0,1:T(8,128)S(1)}, f32[512,512]{0,1:T(8,128)S(1)}, u32[]{:S(2)}, u32[]{:S(2)}) %collective-permute-start.1) | collective-permute-done | bytes 1048608 | tf_op jit(solution)/shard_map/ppermute | solution.py:10
  199.8 20.6 %collective-permute-done.2 = f32[512,512]{0,1:T(8,128)S(1)} collective-permute-done((f32[512,512]{0,1:T(8,128)S(1)}, f32[512,512]{0,1:T(8,128)S(1)}, u32[]{:S(2)}, u32[]{:S(2)}) %collective-permute-start.2) | collective-permute-done | bytes 1048608 | tf_op jit(solution)/shard_map/ppermute | solution.py:10
  223.7 22.0 %collective-permute-done.3 = f32[512,512]{0,1:T(8,128)S(1)} collective-permute-done((f32[512,512]{0,1:T(8,128)S(1)}, f32[512,512]{0,1:T(8,128)S(1)}, u32[]{:S(2)}, u32[]{:S(2)}) %collective-permute-start.3) | collective-permute-done | bytes 1048608 | tf_op jit(solution)/shard_map/ppermute | solution.py:10
  252.2 24.1 %collective-permute-done.5 = f32[512,512]{0,1:T(8,128)S(1)} collective-permute-done((f32[512,512]{0,1:T(8,128)S(1)}, f32[512,512]{0,1:T(8,128)S(1)}, u32[]{:S(2)}, u32[]{:S(2)}) %collective-permute-start.5) | collective-permute-done | bytes 1048608 | tf_op jit(solution)/shard_map/ppermute | solution.py:10
  277.6 24.0 %collective-permute-done.6 = f32[512,512]{0,1:T(8,128)} collective-permute-done((f32[512,512]{0,1:T(8,128)S(1)}, f32[512,512]{0,1:T(8,128)}, u32[]{:S(2)}, u32[]{:S(2)}) %collective-permute-start.6) | collective-permute-done | bytes 1048608 | tf_op jit(solution)/shard_map/ppermute | solution.py:10
  304.6 11.7 %cholesky.104 = f32[128,128]{1,0:T(8,128)S(1)} custom-call(f32[128,128]{1,0:T(8,128)S(1)} %cholesky.266), custom_call_target="Cholesky" | custom-call | tf_op jit(solution)/shard_map/jit(cholesky)/cholesky | solution.py:77
  316.5 9.8 %custom-call.31 = f32[1,128,128]{1,2,0:T(8,128)S(1)} custom-call(f32[1,128,128]{2,1,0:T(8,128)S(1)} %get-tuple-element.42), custom_call_target="InvertDiagBlocksLowerTriangular" | custom-call | tf_op jit(solution)/shard_map/jit(cholesky)/cholesky | solution.py:77
  328.8 11.7 %cholesky.217 = f32[128,128]{1,0:T(8,128)S(1)} custom-call(f32[128,128]{1,0:T(8,128)S(1)} %cholesky.270), custom_call_target="Cholesky" | custom-call | tf_op jit(solution)/shard_map/jit(cholesky)/cholesky | solution.py:77
  340.6 10.0 %custom-call.32 = f32[1,128,128]{1,2,0:T(8,128)S(1)} custom-call(f32[1,128,128]{2,1,0:T(8,128)S(1)} %get-tuple-element.39), custom_call_target="InvertDiagBlocksLowerTriangular" | custom-call | tf_op jit(solution)/shard_map/jit(cholesky)/cholesky | solution.py:77
  352.1 11.7 %cholesky.238 = f32[128,128]{1,0:T(8,128)S(1)} custom-call(f32[128,128]{1,0:T(8,128)S(1)} %cholesky.275), custom_call_target="Cholesky" | custom-call | tf_op jit(solution)/shard_map/jit(cholesky)/cholesky | solution.py:77
  364.6 9.8 %custom-call.33 = f32[1,128,128]{1,2,0:T(8,128)S(1)} custom-call(f32[1,128,128]{2,1,0:T(8,128)S(1)} %get-tuple-element.36), custom_call_target="InvertDiagBlocksLowerTriangular" | custom-call | tf_op jit(solution)/shard_map/jit(cholesky)/cholesky | solution.py:77
  375.8 11.9 %cholesky.255 = f32[128,128]{1,0:T(8,128)S(1)} custom-call(f32[128,128]{1,0:T(8,128)S(1)} %convolution_subtract_fusion.5), custom_call_target="Cholesky" | custom-call | tf_op jit(solution)/shard_map/jit(cholesky)/cholesky | solution.py:77
  392.8 14.1 %while.1 = (s32[]{:T(128)}, f32[512,512]{1,0:T(8,128)}, s32[4,2]{0,1:T(2,128)S(1)}, f32[4,128,128]{2,1,0:T(8,128)}, s32[]{:T(128)}) while((s32[]{:T(128)}, f32[512,512]{1,0:T(8,128)}, s32[4,2]{0,1:T(2,128)S(1)}, f32[4,128,128]{2,1,0:T(8,128)}, s32[]{:T(128)}) %tuple.38), condition=%wide.while_cond, body=%wide.while_body.sunk | while | flops 2 | bytes 132705 | solution.py:79
  406.9 40.1 %custom-call.34 = f32[4,128,128]{1,2,0:T(8,128)S(1)} custom-call(f32[4,128,128]{2,1,0:T(8,128)} %get-tuple-element.9), custom_call_target="InvertDiagBlocksLowerTriangular" | custom-call | tf_op jit(solution)/shard_map/jit(_solve_triangular)/triangular_solve | solution.py:79
  453.0 8.3 %fusion = f32[2048,512]{1,0:T(8,128)} fusion(f32[2048,512]{1,0:T(8,128)S(1)} %copy-done.3, f32[128,512]{1,0:T(8,128)S(1)} %fusion.30, f32[128,512]{1,0:T(8,128)S(1)} %fusion.31, f32[128,512]{1,0:T(8,128)S(1)} %fusion.33, f32[128,512]{1,0:T(8,128)S(1)} %fusion.21), kind=kOutput, calls=%fused_computation.14 | convolution fusion | flops 6443237376 | bytes 9437184 | tf_op jit(solution)/shard_map/dot_general | solution.py:80
  (92 shorter events, 56.4 us)
Async XLA Ops:
  0.6 134.0 %copy-start = (f32[512,512]{1,0:T(8,128)S(1)}, f32[512,512]{1,0:T(8,128)}, u32[]{:S(2)}) copy-start(f32[512,512]{1,0:T(8,128)} %param.6) | copy-start | bytes 3145732
  4.5 22.5 %all-to-all-start = ((f32[8,1,2]{2,1,0:T(1,128)}), f32[8,1,2]{2,1,0:T(1,128)S(1)}, u32[]{:S(2)}, u32[]{:S(2)}) async-start(f32[8,1,2]{2,1,0:T(1,128)} %bitcast.1), calls=%async_computation | async-start | bytes 8192 | tf_op jit(solution)/shard_map/all_to_all | solution.py:57
  27.0 98.8 %all-to-all-start.1 = ((f32[8,2,256,512]{3,2,1,0:T(8,128)}), f32[8,2,256,512]{3,2,1,0:T(8,128)}, u32[]{:S(2)}, u32[]{:S(2)}) async-start(f32[8,2,256,512]{3,2,1,0:T(8,128)} %select_multiply_fusion), calls=%async_computation.1 | async-start | bytes 16777216 | tf_op jit(solution)/shard_map/all_to_all | solution.py:50
  142.2 7.5 %copy-start.2 = (f32[2048,512]{1,0:T(8,128)}, f32[2048,512]{1,0:T(8,128)S(1)}, u32[]{:S(2)}) copy-start(f32[2048,512]{1,0:T(8,128)S(1)} %fusion.47) | copy-start | bytes 12582916
  149.7 23.9 %collective-permute-start = (f32[512,512]{0,1:T(8,128)S(1)}, f32[512,512]{0,1:T(8,128)S(1)}, u32[]{:S(2)}, u32[]{:S(2)}) collective-permute-start(f32[512,512]{0,1:T(8,128)S(1)} %fusion.48), channel_id=1, source_target_pairs={{0,1},{1,0},{2,3},{3,2},{4,5},{5,4},{6,7},{7,6},{8,9},{9,8},{10,11... | collective-permute-start | bytes 3145736 | tf_op jit(solution)/shard_map/ppermute | solution.py:10
  173.8 24.5 %collective-permute-start.1 = (f32[512,512]{0,1:T(8,128)S(1)}, f32[512,512]{0,1:T(8,128)S(1)}, u32[]{:S(2)}, u32[]{:S(2)}) collective-permute-start(f32[512,512]{0,1:T(8,128)S(1)} %add.101), channel_id=1, source_target_pairs={{0,2},{1,3},{2,0},{3,1},{4,6},{5,7},{6,4},{7,5},{8,10},{9,11},{10,... | collective-permute-start | bytes 3145736 | tf_op jit(solution)/shard_map/ppermute | solution.py:10
  198.4 22.0 %collective-permute-start.2 = (f32[512,512]{0,1:T(8,128)S(1)}, f32[512,512]{0,1:T(8,128)S(1)}, u32[]{:S(2)}, u32[]{:S(2)}) collective-permute-start(f32[512,512]{0,1:T(8,128)S(1)} %add.102), channel_id=1, source_target_pairs={{0,4},{1,5},{2,6},{3,7},{4,0},{5,1},{6,2},{7,3},{8,12},{9,13},{10,... | collective-permute-start | bytes 3145736 | tf_op jit(solution)/shard_map/ppermute | solution.py:10
  220.7 25.0 %collective-permute-start.3 = (f32[512,512]{0,1:T(8,128)S(1)}, f32[512,512]{0,1:T(8,128)S(1)}, u32[]{:S(2)}, u32[]{:S(2)}) collective-permute-start(f32[512,512]{0,1:T(8,128)S(1)} %add.103), channel_id=1, source_target_pairs={{0,8},{1,9},{2,10},{3,11},{4,12},{5,13},{6,14},{7,15},{8,0},{9,1},... | collective-permute-start | bytes 3145736 | tf_op jit(solution)/shard_map/ppermute | solution.py:10
  245.8 5.7 %collective-permute-start.4 = (f32[512,512]{0,1:T(8,128)S(1)}, f32[512,512]{0,1:T(8,128)S(1)}, u32[]{:S(2)}, u32[]{:S(2)}) collective-permute-start(f32[512,512]{0,1:T(8,128)S(1)} %add.104), channel_id=1, source_target_pairs={{0,16},{1,17},{2,18},{3,19},{4,20},{5,21},{6,22},{7,23},{8,24},{9,... | collective-permute-start | bytes 3145736 | tf_op jit(solution)/shard_map/ppermute | solution.py:10
  251.8 24.5 %collective-permute-start.5 = (f32[512,512]{0,1:T(8,128)S(1)}, f32[512,512]{0,1:T(8,128)S(1)}, u32[]{:S(2)}, u32[]{:S(2)}) collective-permute-start(f32[512,512]{0,1:T(8,128)S(1)} %add.105), channel_id=1, source_target_pairs={{0,32},{1,33},{2,34},{3,35},{4,36},{5,37},{6,38},{7,39},{8,40},{9,... | collective-permute-start | bytes 3145736 | tf_op jit(solution)/shard_map/ppermute | solution.py:10
  276.5 25.1 %collective-permute-start.6 = (f32[512,512]{0,1:T(8,128)S(1)}, f32[512,512]{0,1:T(8,128)}, u32[]{:S(2)}, u32[]{:S(2)}) collective-permute-start(f32[512,512]{0,1:T(8,128)S(1)} %add.106), channel_id=1, source_target_pairs={{0,64},{1,65},{2,66},{3,67},{4,68},{5,69},{6,70},{7,71},{8,72},{9,... | collective-permute-start | bytes 3145736 | tf_op jit(solution)/shard_map/ppermute | solution.py:10
  303.6 1.0 copy-start.4
  447.1 5.9 %copy-start.3 = (f32[2048,512]{1,0:T(8,128)S(1)}, f32[2048,512]{1,0:T(8,128)}, u32[]{:S(2)}) copy-start(f32[2048,512]{1,0:T(8,128)} %copy-done.2) | copy-start | bytes 12582916
  453.0 9.6 %copy-start.1 = (f32[512,512]{1,0:T(8,128)S(1)}, f32[512,512]{1,0:T(8,128)}, u32[]{:S(2)}) copy-start(f32[512,512]{1,0:T(8,128)} %param.6) | copy-start | bytes 3145732
where the time goes:
time: 467 us; the launch traced here: 463 us
  waiting for transfers between devices  231 us (49%)
  other arithmetic  136 us (29%)
  matrix products  34.6 us (7%)
  local copies, waits for them, and re-layouts  31.8 us (7%)
  starting transfers between devices  25 us (5%)
    ppermute x7, waiting for transfers between devices, from_partner(): lax.ppermute(shard, axis, [(i, i ^ 1 << bit) for i in range(lax.axis_size...  137 us
    all_to_all x1, waiting for transfers between devices, shards(): lax.all_to_all(outgoing.reshape(scenes, pair_most, tile_rows, column_coun...  93.5 us
    another operation x14, other arithmetic, shards(): lower_factor = jnp.linalg.cholesky(weight)  78.8 us
    another operation x2, other arithmetic, shards(): jax.scipy.linalg.solve_triangular(lower_factor, identity, lower=True)  40.1 us
    another operation x12, local copies, waits for them, and re-layouts  14.1 us
    ppermute x7, starting transfers between devices, from_partner(): lax.ppermute(shard, axis, [(i, i ^ 1 << bit) for i in range(lax.axis_size...  13.3 us
  transfers between devices with their start and end apart: 9, of which 8 were waited for; matrix products, arithmetic and copies ran while one was open for 4% of the time, Pallas kernels for 0%

commit v1 on v0

v1 whole, which is shorter than its diff:
```python
import functools

import jax
import jax.numpy as jnp
from jax import lax
from jax.experimental import pallas as pl
from jax.experimental.pallas import tpu as pltpu
from jax.sharding import PartitionSpec as P

OWN_TILES = 8
BLOCK = 128
PIVOT = 8
HALF = 256


def split(value):
    head = value.astype(jnp.bfloat16)
    return head, (value - head.astype(jnp.float32)).astype(jnp.bfloat16)


def dot16(left, right, left_dim=1, right_dim=0):
    return lax.dot_general(
        left,
        right,
        (((left_dim,), (right_dim,)), ((), ())),
        preferred_element_type=jnp.float32,
    )


def dot32(left, right, left_dim=1, right_dim=0):
    return lax.dot_general(
        left,
        right,
        (((left_dim,), (right_dim,)), ((), ())),
        precision=lax.Precision.HIGHEST,
        preferred_element_type=jnp.float32,
    )


def dot_split(left, right):
    return dot16(left[0], right[0]) + (dot16(left[0], right[1]) + dot16(left[1], right[0]))


def pack_kernel(count_ref, owner_ref, slot_ref, tiles_ref, packed_ref, seat_slot_ref, used, sems):
    capacity, scenes = owner_ref.shape[0], used.shape[0]
    for seat in range(capacity):
        seat_slot_ref[seat] = -1
    for owner in range(scenes):
        used[owner] = 0
    for i in range(capacity):

        @pl.when(i < count_ref[0])
        def _():
            owner = owner_ref[i]
            rank = used[owner]
            used[owner] = rank + 1
            seat = owner * (capacity // scenes) + rank
            seat_slot_ref[seat] = slot_ref[i]
            pltpu.make_async_copy(tiles_ref.at[i], packed_ref.at[seat], sems.at[i]).start()

    for i in range(capacity):

        @pl.when(i < count_ref[0])
        def _():
            pltpu.make_async_copy(tiles_ref.at[i], packed_ref.at[0], sems.at[i]).wait()


def pack(tiles, tile_count, tile_owner, tile_slot, scenes):
    smem = pl.BlockSpec(memory_space=pltpu.SMEM)
    hbm = pl.BlockSpec(memory_space=pl.ANY)
    capacity = tile_owner.shape[0]
    return pl.pallas_call(
        pack_kernel,
        out_shape=(
            jax.ShapeDtypeStruct(tiles.shape, tiles.dtype),
            jax.ShapeDtypeStruct((capacity,), jnp.int32),
        ),
        in_specs=[smem, smem, smem, hbm],
        out_specs=(hbm, smem),
        scratch_shapes=[pltpu.SMEM((scenes,), jnp.int32), pltpu.SemaphoreType.DMA((capacity,))],
        cost_estimate=pl.CostEstimate(flops=0, bytes_accessed=2 * tiles.size * 4, transcendentals=0),
        name="pack",
    )(tile_count, tile_owner, tile_slot, tiles)


def gram_kernel(count_ref, tile_ref, inverse_ref, gram_ref, inv_head, inv_tail, cross):
    step = pl.program_id(0)

    @pl.when(step == 0)
    def _():
        head, tail = split(inverse_ref[...])
        inv_head[...] = head
        inv_tail[...] = tail
        gram_ref[...] = jnp.zeros_like(gram_ref)
        cross[...] = jnp.zeros_like(cross)

    @pl.when(step < count_ref[0])
    def _():
        head, tail = split(tile_ref[0])
        left = dot_split(
            (head[:, :HALF], tail[:, :HALF]), (inv_head[:HALF, :HALF], inv_tail[:HALF, :HALF])
        )
        right = dot_split((head, tail), (inv_head[:, HALF:], inv_tail[:, HALF:]))
        left_head, left_tail = split(left)
        right_head, right_tail = split(right)
        gram_ref[:HALF, :] += dot16(left_head, left_head, 0, 0)
        cross[:HALF, :] += dot16(left_head, left_tail, 0, 0)
        gram_ref[HALF : 2 * HALF, :] += (
            dot16(left_head, right_head, 0, 0)
            + dot16(left_head, right_tail, 0, 0)
            + dot16(left_tail, right_head, 0, 0)
        )
        gram_ref[2 * HALF :, :] += dot16(right_head, right_head, 0, 0)
        cross[HALF:, :] += dot16(right_head, right_tail, 0, 0)

    @pl.when(step == pl.num_programs(0) - 1)
    def _():
        gram_ref[:HALF, :] += cross[:HALF, :] + cross[:HALF, :].T
        gram_ref[2 * HALF :, :] += cross[HALF:, :] + cross[HALF:, :].T


def gram(tiles, inverse_factor, tile_count):
    capacity, rows, columns = tiles.shape
    return pl.pallas_call(
        gram_kernel,
        out_shape=jax.ShapeDtypeStruct((3 * HALF, HALF), jnp.float32),
        grid_spec=pltpu.PrefetchScalarGridSpec(
            num_scalar_prefetch=1,
            grid=(capacity,),
            in_specs=[
                pl.BlockSpec(
                    (1, rows, columns),
                    lambda i, count: (jnp.minimum(i, jnp.maximum(count[0] - 1, 0)), 0, 0),
                ),
                pl.BlockSpec((columns, columns), lambda i, count: (0, 0)),
            ],
            out_specs=pl.BlockSpec((3 * HALF, HALF), lambda i, count: (0, 0)),
            scratch_shapes=[
                pltpu.VMEM((columns, columns), jnp.bfloat16),
                pltpu.VMEM((columns, columns), jnp.bfloat16),
                pltpu.VMEM((2 * HALF, HALF), jnp.float32),
            ],
        ),
        compiler_params=pltpu.CompilerParams(
            dimension_semantics=("arbitrary",), vmem_limit_bytes=56 << 20
        ),
        cost_estimate=pl.CostEstimate(
            flops=1_000_000, bytes_accessed=1 << 16, transcendentals=0
        ),
        name="gram",
    )(tile_count, tiles, inverse_factor)


def ring_pairs(size, span, stride, shift):
    ring = [i // stride % span for i in range(size)]
    return [(i, i + ((r + shift) % span - r) * stride) for i, r in enumerate(ring)]


def scatter_sum(value, axis, span, stride):
    size = lax.axis_size(axis)
    me = lax.axis_index(axis) // stride % span
    parts = value.reshape((span, -1) + value.shape[1:])
    total = lax.dynamic_index_in_dim(parts, me, 0, keepdims=False)
    for shift in range(1, span):
        sent = lax.dynamic_index_in_dim(parts, (me + shift) % span, 0, keepdims=False)
        total = total + lax.ppermute(sent, axis, ring_pairs(size, span, stride, shift))
    return total


def select_one(tests, values):
    chosen = values[0]
    for test, value in zip(tests[1:], values[1:]):
        chosen = jnp.where(test, value, chosen)
    return chosen


def gather(value, axis, span, stride):
    size = lax.axis_size(axis)
    me = lax.axis_index(axis) // stride % span
    onward = [value] + [
        lax.ppermute(value, axis, ring_pairs(size, span, stride, span - ahead))
        for ahead in range(1, span)
    ]
    ordered = [
        select_one([(me + ahead) % span == place for ahead in range(span)], onward)
        for place in range(span)
    ]
    return jnp.concatenate(ordered, 0)


def sum_everywhere(value, scenes, rows):
    side = 4
    stages = [("scene", 2, 1), ("rows", side, 1), ("rows", rows // side, side), ("scene", scenes // 2, 2)]
    for axis, span, stride in stages:
        value = scatter_sum(value, axis, span, stride)
    for axis, span, stride in reversed(stages):
        value = gather(value, axis, span, stride)
    return value


def sweep(block):
    shape = (PIVOT, BLOCK)
    lane = lax.broadcasted_iota(jnp.int32, shape, 1)
    sub = lax.broadcasted_iota(jnp.int32, shape, 0)
    strips = [block[PIVOT * v : PIVOT * (v + 1), :] for v in range(BLOCK // PIVOT)]
    upper = []
    for s in range(len(strips)):
        base = PIVOT * s
        inside = (lane >= base) & (lane < base + PIVOT)
        own = [jnp.broadcast_to(strips[s][q : q + 1, :], shape) for q in range(PIVOT)]
        pivot = {
            (r, c): jnp.broadcast_to(own[r][:, base + c : base + c + 1], shape)
            for r in range(PIVOT)
            for c in range(r, PIVOT)
        }
        u = {}
        scale = []
        for q in range(PIVOT):
            scale.append(lax.rsqrt(pivot[q, q]))
            for c in range(q + 1, PIVOT):
                u[q, c] = pivot[q, c] * scale[q]
            for r in range(q + 1, PIVOT):
                for c in range(r, PIVOT):
                    pivot[r, c] = pivot[r, c] - u[q, r] * u[q, c]
        swept = [
            jnp.where(inside, jnp.where(lane == base + q, 1.0, 0.0), own[q]) for q in range(PIVOT)
        ]
        for q in range(PIVOT):
            for r in range(q):
                own[q] = own[q] - u[r, q] * own[r]
                swept[q] = swept[q] - u[r, q] * swept[r]
            own[q] = own[q] * scale[q]
            swept[q] = swept[q] * scale[q]
        for v in range(s + 1, len(strips)):
            column = []
            for q in range(PIVOT):
                entry = jnp.broadcast_to(strips[v][:, base + q : base + q + 1], shape)
                for r in range(q):
                    entry = entry - u[r, q] * column[r]
                column.append(entry * scale[q])
            rest = jnp.where(inside, 0.0, strips[v])
            for q in range(PIVOT):
                rest = rest - column[q] * swept[q]
            strips[v] = rest
        factor_rows, inverse_rows = own[0], swept[0]
        for q in range(1, PIVOT):
            factor_rows = jnp.where(sub == q, own[q], factor_rows)
            inverse_rows = jnp.where(sub == q, swept[q], inverse_rows)
        upper.append(jnp.where(lane >= base + sub, factor_rows, 0.0))
        strips[s] = jnp.where(lane <= base + sub, inverse_rows, 0.0)
    return jnp.concatenate(upper, 0), jnp.concatenate(strips, 0)


def factor_kernel(row_count, gram_ref, inverse_ref, factor_ref, head_ref, tail_ref, work):
    size = work.shape[0]
    work[:HALF, :HALF] = gram_ref[:HALF, :] / row_count
    work[:HALF, HALF:] = gram_ref[HALF : 2 * HALF, :] / row_count
    work[HALF:, HALF:] = gram_ref[2 * HALF :, :] / row_count
    work[HALF:, :HALF] = jnp.zeros((HALF, HALF), jnp.float32)

    @pl.loop(0, size // BLOCK)
    def _(k):
        offset = pl.multiple_of(k * BLOCK, BLOCK)
        here = pl.ds(offset, BLOCK)
        upper, inverse = sweep(work[here, here])
        right = dot32(inverse, work[here, :])
        lane = lax.broadcasted_iota(jnp.int32, (BLOCK, size), 1)
        beyond = jnp.where(lane >= offset + BLOCK, right, 0.0)
        factor_ref[here, :] = beyond
        factor_ref[here, here] = upper
        work[here, :] = right
        work[here, here] = inverse

        @pl.when(k < size // BLOCK - 1)
        def _():
            row = lax.broadcasted_iota(jnp.int32, (size, BLOCK), 0)
            work[:, here] = jnp.where(row >= offset + BLOCK, 0.0, work[:, here])
            work[...] = work[...] - dot32(beyond, work[here, :], 0, 0)

    row = lax.broadcasted_iota(jnp.int32, work.shape, 0)
    lane = lax.broadcasted_iota(jnp.int32, work.shape, 1)
    inverse = jnp.where(lane <= row, work[...], 0.0)
    head_ref[...], tail_ref[...] = split(dot32(inverse_ref[...], inverse, 1, 1))


def factor(gram_sum, inverse_factor, row_count):
    vmem = pl.BlockSpec(memory_space=pltpu.VMEM)
    size = inverse_factor.shape[0]
    return pl.pallas_call(
        functools.partial(factor_kernel, row_count),
        out_shape=(
            jax.ShapeDtypeStruct((size, size), jnp.float32),
            jax.ShapeDtypeStruct((size, size), jnp.bfloat16),
            jax.ShapeDtypeStruct((size, size), jnp.bfloat16),
        ),
        in_specs=[vmem, vmem],
        out_specs=(vmem, vmem, vmem),
        scratch_shapes=[pltpu.VMEM((size, size), jnp.float32)],
        compiler_params=pltpu.CompilerParams(vmem_limit_bytes=24 << 20),
        cost_estimate=pl.CostEstimate(
            flops=1_000_000, bytes_accessed=1 << 16, transcendentals=0
        ),
        name="factor",
    )(gram_sum, inverse_factor)


def finish_kernel(
    slot_ref, head_ref, tail_ref, received, out_ref, tiles, results, in_sems, out_sems
):
    for seat in range(slot_ref.shape[0]):
        slot = slot_ref[seat]

        @pl.when(slot >= 0)
        def _():
            pltpu.make_async_copy(received.at[seat], tiles.at[slot], in_sems.at[slot]).start()

    def result_copy(j):
        return pltpu.make_async_copy(results.at[j], out_ref.at[j], out_sems.at[j])

    @pl.loop(0, OWN_TILES)
    def _(j):
        pltpu.make_async_copy(received.at[0], tiles.at[j], in_sems.at[j]).wait()
        head, tail = split(tiles[j])
        results[j, :, :HALF] = dot_split(
            (head[:, :HALF], tail[:, :HALF]), (head_ref[:HALF, :HALF], tail_ref[:HALF, :HALF])
        )
        results[j, :, HALF:] = dot_split((head, tail), (head_ref[:, HALF:], tail_ref[:, HALF:]))
        result_copy(j).start()

    @pl.loop(0, OWN_TILES)
    def _(j):
        result_copy(j).wait()


def finish(slots, received, head, tail):
    _, rows, columns = received.shape
    hbm = pl.BlockSpec(memory_space=pl.ANY)
    vmem = pl.BlockSpec(memory_space=pltpu.VMEM)
    return pl.pallas_call(
        finish_kernel,
        out_shape=jax.ShapeDtypeStruct((OWN_TILES, rows, columns), jnp.float32),
        in_specs=[pl.BlockSpec(memory_space=pltpu.SMEM), vmem, vmem, hbm],
        out_specs=hbm,
        scratch_shapes=[
            pltpu.VMEM((OWN_TILES, rows, columns), jnp.float32),
            pltpu.VMEM((OWN_TILES, rows, columns), jnp.float32),
            pltpu.SemaphoreType.DMA((OWN_TILES,)),
            pltpu.SemaphoreType.DMA((OWN_TILES,)),
        ],
        compiler_params=pltpu.CompilerParams(vmem_limit_bytes=48 << 20),
        cost_estimate=pl.CostEstimate(
            flops=5_000_000_000, bytes_accessed=8 << 20, transcendentals=0
        ),
        name="finish",
    )(slots, head, tail, received)


def shards(observations, inverse_factor, tile_count, tile_owner, tile_slot):
    scenes, rows = lax.axis_size("scene"), lax.axis_size("rows")
    capacity, tile_rows, _ = observations.shape
    packed, seat_slot = pack(observations, tile_count, tile_owner, tile_slot, scenes)
    me = lax.axis_index("scene")
    group_slots = lax.all_gather(seat_slot.reshape(scenes, capacity // scenes), "scene")
    slots = lax.dynamic_index_in_dim(group_slots, me, 1, keepdims=False).reshape(capacity)
    received = lax.all_to_all(
        packed.reshape((scenes, capacity // scenes) + packed.shape[1:]), "scene", 0, 0, tiled=True
    ).reshape(packed.shape)
    tiles, _ = lax.optimization_barrier((observations, seat_slot))
    gram_sum = sum_everywhere(gram(tiles, inverse_factor, tile_count), scenes, rows)
    upper, head, tail = factor(gram_sum, inverse_factor, scenes * rows * OWN_TILES * tile_rows)
    return finish(slots, received, head, tail), upper


def solution(mesh):
    in_specs = (
        P(("scene", "rows"), None, None),
        P(),
        P(("scene", "rows")),
        P(("scene", "rows")),
        P(("scene", "rows")),
    )
    out_specs = (P(("scene", "rows"), None, None), P())
    return jax.shard_map(shards, mesh=mesh, in_specs=in_specs, out_specs=out_specs, check_vma=False)
```

time: 467 us -> 426 us (0.912)
  starting transfers between devices: 25 us -> 239 us
  waiting for transfers between devices: 231 us -> 70 us
  other arithmetic: 136 us -> 1.35 us
  Pallas kernels: 0 us -> 103 us
  matrix products: 34.6 us -> 0 us
  local copies, waits for them, and re-layouts: 31.8 us -> 1.61 us
  blocking collectives: 0 us -> 8.66 us
    all_to_all x2 -> x1, starting transfers between devices: 11.7 us -> 197 us  [shards(): lax.all_to_all(packed.reshape((scenes, capacity // scenes) + packed.shape...]
    another operation x16 -> x0, other arithmetic: 119 us -> none  [the longest x14 78.8 us: shards(): lower_factor = jnp.linalg.cholesky(weight)]
    pallas_call x0 -> x4, Pallas kernels: none -> 103 us  [the longest x1 66 us: pack(): pl.pallas_call(pack_kernel, out_shape=(jax.ShapeDtypeStruct(tiles.shape,...]
    all_to_all x2 -> x1, waiting for transfers between devices: 93.5 us -> 0.01 us  [shards(): lax.all_to_all(packed.reshape((scenes, capacity // scenes) + packed.shape...]
    ppermute x7 -> x20, waiting for transfers between devices: 137 us -> 70 us  [the longest x10 58.1 us: scatter_sum(): lax.ppermute(sent, axis, ring_pairs(size, span, stride, shift))]
    ppermute x7 -> x20, starting transfers between devices: 13.3 us -> 42 us  [the longest x10 26.7 us: scatter_sum(): lax.ppermute(sent, axis, ring_pairs(size, span, stride, shift))]
    dot_general x3 -> x0, matrix products: 23.3 us -> none  [the longest x1 8.28 us: shards(): jnp.dot(projected, inv_upper, precision=lax.Precision.HIGHEST, preferred_...]
    another operation x17 -> x2, local copies, waits for them, and re-layouts: 14.2 us -> 0.16 us  [shards(): lax.all_gather(seat_slot.reshape(scenes, capacity // scenes), 'scene')]
  transfers between devices with their start and end apart: 9 -> 21, of which waited for: 8 -> 16; matrix products, arithmetic and copies ran while one was open for 4% -> 1% of each run, Pallas kernels for 0% -> 7%
where the time goes in v1:
time: 426 us
  starting transfers between devices  239 us (56%)
  Pallas kernels  103 us (24%)
  waiting for transfers between devices  70 us (16%)
  blocking collectives  8.66 us (2%)
    all_to_all x1, starting transfers between devices, shards(): lax.all_to_all(packed.reshape((scenes, capacity // scenes) + packed.shape...  197 us
    pallas_call x1, Pallas kernels, pack(): pl.pallas_call(pack_kernel, out_shape=(jax.ShapeDtypeStruct(tiles.shape,...  66 us
    ppermute x10, waiting for transfers between devices, scatter_sum(): lax.ppermute(sent, axis, ring_pairs(size, span, stride, shift))  58.1 us
    ppermute x10, starting transfers between devices, scatter_sum(): lax.ppermute(sent, axis, ring_pairs(size, span, stride, shift))  26.7 us
    pallas_call x1, Pallas kernels, factor(): pl.pallas_call(functools.partial(factor_kernel, row_count), out_shape=(ja...  23.5 us
    ppermute x10, starting transfers between devices, gather(): lax.ppermute(value, axis, ring_pairs(size, span, stride, span - ahead))  15.3 us
    ppermute x10, waiting for transfers between devices, gather(): lax.ppermute(value, axis, ring_pairs(size, span, stride, span - ahead))  11.9 us
    all_gather x1, blocking collectives, shards(): lax.all_gather(seat_slot.reshape(scenes, capacity // scenes), 'scene')  8.66 us
  transfers between devices with their start and end apart: 21, of which 16 were waited for; matrix products, arithmetic and copies ran while one was open for 1% of the time, Pallas kernels for 7%

profile of v1, /device:TPU:1, one launch (start us, length us, event | category | flops | bytes accessed | tf_op | source)
XLA Modules:
  0.0 425.6 jit_solution(12940788357580817212)
XLA Ops:
  1.3 66.0 %pack.1 = (f32[16,256,512]{2,1,0:T(8,128)}, s32[16]{0:T(128)}) custom-call(s32[1]{0:T(128)S(6)} %copy.8.count_ref, s32[16]{0:T(128)} %owner_ref.1, s32[16]{0:T(128)} %slot_ref.1, f32[16,256,512]{2,1,0:T(8,128)} %tile_ref), custom_call_target="tpu_custom_call" | custom-call | bytes 16777216 | tf_op jit(solution)/shard_map/pack/pallas_call | solution.py:72
  67.3 197.2 %all-to-all-start = ((f32[8,2,256,512]{3,2,1,0:T(8,128)}), f32[8,2,256,512]{3,2,1,0:T(8,128)}, u32[]{:S(2)}, u32[]{:S(2)}) async-start(f32[8,2,256,512]{3,2,1,0:T(8,128)} %bitcast.45), calls=%async_computation | async-start | bytes 16777216 | tf_op jit(solution)/shard_map/all_to_all | solution.py:365
  264.5 7.1 %gram.1 = f32[768,256]{1,0:T(8,128)} custom-call(s32[1]{0:T(128)S(6)} %copy.8.count_ref, f32[16,256,512]{2,1,0:T(8,128)} %tile_ref, f32[512,512]{1,0:T(8,128)} %inverse_ref.3), custom_call_target="tpu_custom_call" | custom-call | flops 1000000 | bytes 65536 | tf_op jit(solution)/shard_map/gram/pallas_call | solution.py:124
  272.7 3.0 collective-permute-start
  278.2 7.7 %collective-permute-start.3 = (f32[96,256]{1,0:T(8,128)S(1)}, f32[96,256]{1,0:T(8,128)S(1)}, u32[]{:S(2)}, u32[]{:S(2)}) collective-permute-start(f32[96,256]{1,0:T(8,128)S(1)} %get-tuple-element.21), channel_id=1, source_target_pairs={{0,3},{1,0},{2,1},{3,2},{4,7},{5,4},{6,5},{7,6},{8,11},{9,8},{10,9... | collective-permute-start | bytes 294920 | tf_op jit(solution)/shard_map/ppermute | solution.py:166
  285.9 2.7 collective-permute-start.2
  289.8 2.2 collective-permute-done.2
  292.0 2.2 collective-permute-start.4
  294.2 3.1 collective-permute-start.6
  297.3 2.0 collective-permute-start.5
  299.3 2.2 collective-permute-done.5
  301.5 1.8 collective-permute-start.7
  303.3 2.7 collective-permute-start.9
  307.3 47.8 %collective-permute-done.7 = f32[6,256]{1,0:T(8,128)S(1)} collective-permute-done((f32[6,256]{1,0:T(8,128)S(1)}, f32[6,256]{1,0:T(8,128)S(1)}, u32[]{:S(2)}, u32[]{:S(2)}) %collective-permute-start.7) | collective-permute-done | bytes 6176 | tf_op jit(solution)/shard_map/ppermute | solution.py:166
  355.1 1.9 collective-permute-done.9
  361.1 2.5 collective-permute-done.11
  364.5 2.5 collective-permute-start.15
  368.0 3.2 collective-permute-done.14
  371.5 2.6 collective-permute-start.18
  375.8 3.4 collective-permute-done.17
  380.3 5.8 %collective-permute-start.19 = (f32[384,256]{1,0:T(8,128)S(1)}, f32[384,256]{1,0:T(8,128)S(1)}, u32[]{:S(2)}, u32[]{:S(2)}) collective-permute-start(f32[384,256]{1,0:T(8,128)S(1)} %pad_maximum_fusion.1), channel_id=1, source_target_pairs={{0,16},{16,0},{32,48},{48,32},{64,80},{80,64},{96,112},{112,96},{1... | collective-permute-start | bytes 1179656 | tf_op jit(solution)/shard_map/ppermute | solution.py:181
  386.3 8.7 %all_gather.3 = s32[8,8,2]{1,2,0:T(2,128)S(1)} all-gather(s32[1,8,2]{1,2,0:T(2,128)S(1)} %copy.7), channel_id=1, replica_groups=mesh['scene'=8,'rows'=16] {'scene'}, dimensions={0}, use_global_device_ids=true | all-gather | bytes 576 | tf_op jit(solution)/shard_map/all_gather | solution.py:363
  395.4 23.5 %factor.1 = (f32[512,512]{1,0:T(8,128)}, bf16[512,512]{1,0:T(8,128)(2,1)S(1)}, bf16[512,512]{1,0:T(8,128)(2,1)S(1)}) custom-call(f32[768,256]{1,0:T(8,128)S(1)} %pad_maximum_fusion.gram_ref, f32[512,512]{1,0:T(8,128)S(1)} %copy-done), custom_call_target="tpu_custom_call" | custom-call | flops 1000000 | bytes 65536 | tf_op jit(solution)/shard_map/factor/pallas_call | solution.py:289
  418.9 6.5 %finish.1 = f32[8,256,512]{2,1,0:T(8,128)} custom-call(s32[16]{0:T(128)S(1)} %reshape.26.slot_ref, bf16[512,512]{1,0:T(8,128)(2,1)S(1)} %get-tuple-element.10.head_ref, bf16[512,512]{1,0:T(8,128)(2,1)S(1)} %get-tuple-element.11.tail_ref, f32[16,256,512]{2,1,0:T(8,128)} %bitcast.18.received), custom_call_target="tpu_custom_call" | custom-call | flops 5000000000 | bytes 8388608 | tf_op jit(solution)/shard_map/finish/pallas_call | solution.py:339
  (49 shorter events, 15.6 us)
Async XLA Ops:
  67.3 351.7 %all-to-all-start = ((f32[8,2,256,512]{3,2,1,0:T(8,128)}), f32[8,2,256,512]{3,2,1,0:T(8,128)}, u32[]{:S(2)}, u32[]{:S(2)}) async-start(f32[8,2,256,512]{3,2,1,0:T(8,128)} %bitcast.45), calls=%async_computation | async-start | bytes 16777216 | tf_op jit(solution)/shard_map/all_to_all | solution.py:365
  264.5 121.6 %copy-start.1 = (s32[16]{0:T(128)S(1)}, s32[16]{0:T(128)}, u32[]{:S(2)}) copy-start(s32[16]{0:T(128)} %get-tuple-element.8) | copy-start | bytes 196
  264.5 130.9 %copy-start = (f32[512,512]{1,0:T(8,128)S(1)}, f32[512,512]{1,0:T(8,128)}, u32[]{:S(2)}) copy-start(f32[512,512]{1,0:T(8,128)} %inverse_ref.3) | copy-start | bytes 3145732
  272.7 4.4 %collective-permute-start = (f32[384,256]{1,0:T(8,128)S(1)}, f32[384,256]{1,0:T(8,128)S(1)}, u32[]{:S(2)}, u32[]{:S(2)}) collective-permute-start(f32[384,256]{1,0:T(8,128)S(1)} %dynamic-slice_bitcast_fusion), channel_id=1, source_target_pairs={{0,16},{16,0},{32,48},{48,32},{64,80},{80,64},{96,112},{112,96},{1... | collective-permute-start | bytes 1179656 | tf_op jit(solution)/shard_map/ppermute | solution.py:166
  278.1 10.7 %collective-permute-start.1 = (f32[96,256]{1,0:T(8,128)S(1)}, f32[96,256]{1,0:T(8,128)S(1)}, u32[]{:S(2)}, u32[]{:S(2)}) collective-permute-start(f32[96,256]{1,0:T(8,128)S(1)} %get-tuple-element.20), channel_id=1, source_target_pairs={{0,1},{1,2},{2,3},{3,0},{4,5},{5,6},{6,7},{7,4},{8,9},{9,10},{10,1... | collective-permute-start | bytes 294920 | tf_op jit(solution)/shard_map/ppermute | solution.py:166
  278.2 11.6 %collective-permute-start.3 = (f32[96,256]{1,0:T(8,128)S(1)}, f32[96,256]{1,0:T(8,128)S(1)}, u32[]{:S(2)}, u32[]{:S(2)}) collective-permute-start(f32[96,256]{1,0:T(8,128)S(1)} %get-tuple-element.21), channel_id=1, source_target_pairs={{0,3},{1,0},{2,1},{3,2},{4,7},{5,4},{6,5},{7,6},{8,11},{9,8},{10,9... | collective-permute-start | bytes 294920 | tf_op jit(solution)/shard_map/ppermute | solution.py:166
  285.9 6.0 %collective-permute-start.2 = (f32[96,256]{1,0:T(8,128)S(1)}, f32[96,256]{1,0:T(8,128)S(1)}, u32[]{:S(2)}, u32[]{:S(2)}) collective-permute-start(f32[96,256]{1,0:T(8,128)S(1)} %get-tuple-element.22), channel_id=1, source_target_pairs={{0,2},{1,3},{2,0},{3,1},{4,6},{5,7},{6,4},{7,5},{8,10},{9,11},{10,... | collective-permute-start | bytes 294920 | tf_op jit(solution)/shard_map/ppermute | solution.py:166
  292.0 7.3 %collective-permute-start.4 = (f32[24,256]{1,0:T(8,128)S(1)}, f32[24,256]{1,0:T(8,128)S(1)}, u32[]{:S(2)}, u32[]{:S(2)}) collective-permute-start(f32[24,256]{1,0:T(8,128)S(1)} %get-tuple-element.27), channel_id=1, source_target_pairs={{0,4},{1,5},{2,6},{3,7},{4,8},{5,9},{6,10},{7,11},{8,12},{9,13},{1... | collective-permute-start | bytes 73736 | tf_op jit(solution)/shard_map/ppermute | solution.py:166
  294.2 5.1 %collective-permute-start.6 = (f32[24,256]{1,0:T(8,128)S(1)}, f32[24,256]{1,0:T(8,128)S(1)}, u32[]{:S(2)}, u32[]{:S(2)}) collective-permute-start(f32[24,256]{1,0:T(8,128)S(1)} %get-tuple-element.28), channel_id=1, source_target_pairs={{0,12},{1,13},{2,14},{3,15},{4,0},{5,1},{6,2},{7,3},{8,4},{9,5},{1... | collective-permute-start | bytes 73736 | tf_op jit(solution)/shard_map/ppermute | solution.py:166
  297.3 4.2 collective-permute-start.5
  301.5 53.7 %collective-permute-start.7 = (f32[6,256]{1,0:T(8,128)S(1)}, f32[6,256]{1,0:T(8,128)S(1)}, u32[]{:S(2)}, u32[]{:S(2)}) collective-permute-start(f32[6,256]{1,0:T(8,128)S(1)} %get-tuple-element.34), channel_id=1, source_target_pairs={{0,32},{16,48},{32,64},{48,80},{64,96},{80,112},{96,0},{112,16},{1... | collective-permute-start | bytes 18440 | tf_op jit(solution)/shard_map/ppermute | solution.py:166
  303.3 53.7 %collective-permute-start.9 = (f32[6,256]{1,0:T(8,128)S(1)}, f32[6,256]{1,0:T(8,128)S(1)}, u32[]{:S(2)}, u32[]{:S(2)}) collective-permute-start(f32[6,256]{1,0:T(8,128)S(1)} %get-tuple-element.35), channel_id=1, source_target_pairs={{0,96},{16,112},{32,0},{48,16},{64,32},{80,48},{96,64},{112,80},{1... | collective-permute-start | bytes 18440 | tf_op jit(solution)/shard_map/ppermute | solution.py:166
  306.0 52.6 %collective-permute-start.8 = (f32[6,256]{1,0:T(8,128)S(1)}, f32[6,256]{1,0:T(8,128)S(1)}, u32[]{:S(2)}, u32[]{:S(2)}) collective-permute-start(f32[6,256]{1,0:T(8,128)S(1)} %get-tuple-element.36), channel_id=1, source_target_pairs={{0,64},{16,80},{32,96},{48,112},{64,0},{80,16},{96,32},{112,48},{1... | collective-permute-start | bytes 18440 | tf_op jit(solution)/shard_map/ppermute | solution.py:166
  358.6 2.5 collective-permute-start.12
  359.6 4.0 collective-permute-start.11
  360.8 3.7 collective-permute-start.10
  364.5 3.5 collective-permute-start.15
  367.1 4.2 collective-permute-start.14
  367.5 4.0 collective-permute-start.13
  371.5 4.3 %collective-permute-start.18 = (f32[96,256]{1,0:T(8,128)S(1)}, f32[96,256]{1,0:T(8,128)S(1)}, u32[]{:S(2)}, u32[]{:S(2)}) collective-permute-start(f32[96,256]{1,0:T(8,128)S(1)} %pad_maximum_fusion.2), channel_id=1, source_target_pairs={{0,3},{1,0},{2,1},{3,2},{4,7},{5,4},{6,5},{7,6},{8,11},{9,8},{10,9... | collective-permute-start | bytes 294920 | tf_op jit(solution)/shard_map/ppermute | solution.py:181
  374.2 5.0 %collective-permute-start.17 = (f32[96,256]{1,0:T(8,128)S(1)}, f32[96,256]{1,0:T(8,128)S(1)}, u32[]{:S(2)}, u32[]{:S(2)}) collective-permute-start(f32[96,256]{1,0:T(8,128)S(1)} %pad_maximum_fusion.2), channel_id=1, source_target_pairs={{0,2},{1,3},{2,0},{3,1},{4,6},{5,7},{6,4},{7,5},{8,10},{9,11},{10,... | collective-permute-start | bytes 294920 | tf_op jit(solution)/shard_map/ppermute | solution.py:181
  375.0 5.2 %collective-permute-start.16 = (f32[96,256]{1,0:T(8,128)S(1)}, f32[96,256]{1,0:T(8,128)S(1)}, u32[]{:S(2)}, u32[]{:S(2)}) collective-permute-start(f32[96,256]{1,0:T(8,128)S(1)} %pad_maximum_fusion.2), channel_id=1, source_target_pairs={{0,1},{1,2},{2,3},{3,0},{4,5},{5,6},{6,7},{7,4},{8,9},{9,10},{10,1... | collective-permute-start | bytes 294920 | tf_op jit(solution)/shard_map/ppermute | solution.py:181
  380.3 15.0 %collective-permute-start.19 = (f32[384,256]{1,0:T(8,128)S(1)}, f32[384,256]{1,0:T(8,128)S(1)}, u32[]{:S(2)}, u32[]{:S(2)}) collective-permute-start(f32[384,256]{1,0:T(8,128)S(1)} %pad_maximum_fusion.1), channel_id=1, source_target_pairs={{0,16},{16,0},{32,48},{48,32},{64,80},{80,64},{96,112},{112,96},{1... | collective-permute-start | bytes 1179656 | tf_op jit(solution)/shard_map/ppermute | solution.py:181

commit v2 on v1

--- a/solution.py
+++ b/solution.py
@@ -11,6 +11,8 @@
 BLOCK = 128
 PIVOT = 8
 HALF = 256
+EARLY = 120
+HEADER = 8
 
 
 def split(value):
@@ -41,49 +43,88 @@
     return dot16(left[0], right[0]) + (dot16(left[0], right[1]) + dot16(left[1], right[0]))
 
 
-def pack_kernel(count_ref, owner_ref, slot_ref, tiles_ref, packed_ref, seat_slot_ref, used, sems):
-    capacity, scenes = owner_ref.shape[0], used.shape[0]
+def seat_of(i, owner_ref, used):
+    owner = owner_ref[i]
+    rank = used[owner]
+    used[owner] = rank + 1
+    return owner, rank
+
+
+def pack_kernel(
+    count_ref, owner_ref, slot_ref, tiles_ref, early_ref, staged, header, used, slots, sems, out_sems
+):
+    scenes, capacity = used.shape[0], owner_ref.shape[0]
+    for i in range(capacity):
+
+        @pl.when(i < count_ref[0])
+        def _():
+            source = tiles_ref.at[i, pl.ds(0, EARLY)]
+            pltpu.make_async_copy(source, staged.at[i], sems.at[i]).start()
+
     for seat in range(capacity):
-        seat_slot_ref[seat] = -1
+        slots[seat] = -1
     for owner in range(scenes):
         used[owner] = 0
+
+    def store(i, owner, rank):
+        target = early_ref.at[owner, pl.ds(pl.multiple_of(rank * EARLY, 8), EARLY)]
+        return pltpu.make_async_copy(staged.at[i], target, sems.at[i])
+
     for i in range(capacity):
 
         @pl.when(i < count_ref[0])
         def _():
-            owner = owner_ref[i]
-            rank = used[owner]
-            used[owner] = rank + 1
-            seat = owner * (capacity // scenes) + rank
-            seat_slot_ref[seat] = slot_ref[i]
-            pltpu.make_async_copy(tiles_ref.at[i], packed_ref.at[seat], sems.at[i]).start()
-
+            owner, rank = seat_of(i, owner_ref, used)
+            slots[2 * owner + rank] = slot_ref[i]
+            source = tiles_ref.at[i, pl.ds(0, EARLY)]
+            pltpu.make_async_copy(source, staged.at[i], sems.at[i]).wait()
+            store(i, owner, rank).start()
+
+    lane = lax.broadcasted_iota(jnp.int32, header.shape[1:], 1)
+    half = header.shape[2] // 2
+    headers = []
+    for owner in range(scenes):
+        pair = jnp.where(lane < half, slots[2 * owner], slots[2 * owner + 1])
+        header[owner] = pair.astype(jnp.float32)
+        target = early_ref.at[owner, pl.ds(2 * EARLY, HEADER)]
+        headers.append(pltpu.make_async_copy(header.at[owner], target, out_sems.at[owner]))
+        headers[-1].start()
     for i in range(capacity):
 
         @pl.when(i < count_ref[0])
         def _():
-            pltpu.make_async_copy(tiles_ref.at[i], packed_ref.at[0], sems.at[i]).wait()
+            store(i, 0, 0).wait()
+
+    for copy in headers:
+        copy.wait()
 
 
 def pack(tiles, tile_count, tile_owner, tile_slot, scenes):
     smem = pl.BlockSpec(memory_space=pltpu.SMEM)
     hbm = pl.BlockSpec(memory_space=pl.ANY)
-    capacity = tile_owner.shape[0]
+    capacity, columns = tile_owner.shape[0], tiles.shape[2]
     return pl.pallas_call(
         pack_kernel,
-        out_shape=(
-            jax.ShapeDtypeStruct(tiles.shape, tiles.dtype),
-            jax.ShapeDtypeStruct((capacity,), jnp.int32),
-        ),
+        out_shape=jax.ShapeDtypeStruct((scenes, 2 * EARLY + HEADER, columns), tiles.dtype),
         in_specs=[smem, smem, smem, hbm],
-        out_specs=(hbm, smem),
-        scratch_shapes=[pltpu.SMEM((scenes,), jnp.int32), pltpu.SemaphoreType.DMA((capacity,))],
-        cost_estimate=pl.CostEstimate(flops=0, bytes_accessed=2 * tiles.size * 4, transcendentals=0),
+        out_specs=hbm,
+        scratch_shapes=[
+            pltpu.VMEM((capacity, EARLY, columns), jnp.float32),
+            pltpu.VMEM((scenes, HEADER, columns), jnp.float32),
+            pltpu.SMEM((scenes,), jnp.int32),
+            pltpu.SMEM((capacity,), jnp.int32),
+            pltpu.SemaphoreType.DMA((capacity,)),
+            pltpu.SemaphoreType.DMA((scenes,)),
+        ],
+        compiler_params=pltpu.CompilerParams(vmem_limit_bytes=56 << 20),
+        cost_estimate=pl.CostEstimate(flops=0, bytes_accessed=8 << 20, transcendentals=0),
         name="pack",
     )(tile_count, tile_owner, tile_slot, tiles)
 
 
-def gram_kernel(count_ref, tile_ref, inverse_ref, gram_ref, inv_head, inv_tail, cross):
+def gram_kernel(
+    count_ref, owner_ref, tile_ref, inverse_ref, gram_ref, late_ref, inv_head, inv_tail, cross, used, sem
+):
     step = pl.program_id(0)
 
     @pl.when(step == 0)
@@ -93,9 +134,16 @@
         inv_tail[...] = tail
         gram_ref[...] = jnp.zeros_like(gram_ref)
         cross[...] = jnp.zeros_like(cross)
+        for owner in range(used.shape[0]):
+            used[owner] = 0
 
     @pl.when(step < count_ref[0])
     def _():
+        owner, rank = seat_of(step, owner_ref, used)
+        late = late_ref.shape[1] // 2
+        target = late_ref.at[owner, pl.ds(pl.multiple_of(rank * late, 8), late)]
+        copy = pltpu.make_async_copy(tile_ref.at[0, pl.ds(EARLY, late)], target, sem)
+        copy.start()
         head, tail = split(tile_ref[0])
         left = dot_split(
             (head[:, :HALF], tail[:, :HALF]), (inv_head[:HALF, :HALF], inv_tail[:HALF, :HALF])
@@ -112,6 +160,7 @@
         )
         gram_ref[2 * HALF :, :] += dot16(right_head, right_head, 0, 0)
         cross[HALF:, :] += dot16(right_head, right_tail, 0, 0)
+        copy.wait()
 
     @pl.when(step == pl.num_programs(0) - 1)
     def _():
@@ -119,26 +168,34 @@
         gram_ref[2 * HALF :, :] += cross[HALF:, :] + cross[HALF:, :].T
 
 
-def gram(tiles, inverse_factor, tile_count):
+def gram(tiles, inverse_factor, tile_count, tile_owner, scenes):
     capacity, rows, columns = tiles.shape
     return pl.pallas_call(
         gram_kernel,
-        out_shape=jax.ShapeDtypeStruct((3 * HALF, HALF), jnp.float32),
+        out_shape=(
+            jax.ShapeDtypeStruct((3 * HALF, HALF), jnp.float32),
+            jax.ShapeDtypeStruct((scenes, 2 * (rows - EARLY), columns), jnp.float32),
+        ),
         grid_spec=pltpu.PrefetchScalarGridSpec(
-            num_scalar_prefetch=1,
+            num_scalar_prefetch=2,
             grid=(capacity,),
             in_specs=[
                 pl.BlockSpec(
                     (1, rows, columns),
-                    lambda i, count: (jnp.minimum(i, jnp.maximum(count[0] - 1, 0)), 0, 0),
+                    lambda i, count, _: (jnp.minimum(i, jnp.maximum(count[0] - 1, 0)), 0, 0),
                 ),
-                pl.BlockSpec((columns, columns), lambda i, count: (0, 0)),
+                pl.BlockSpec((columns, columns), lambda i, *_: (0, 0)),
             ],
-            out_specs=pl.BlockSpec((3 * HALF, HALF), lambda i, count: (0, 0)),
+            out_specs=(
+                pl.BlockSpec((3 * HALF, HALF), lambda i, *_: (0, 0)),
+                pl.BlockSpec(memory_space=pl.ANY),
+            ),
             scratch_shapes=[
                 pltpu.VMEM((columns, columns), jnp.bfloat16),
                 pltpu.VMEM((columns, columns), jnp.bfloat16),
                 pltpu.VMEM((2 * HALF, HALF), jnp.float32),
+                pltpu.SMEM((scenes,), jnp.int32),
+                pltpu.SemaphoreType.DMA,
             ],
         ),
         compiler_params=pltpu.CompilerParams(
@@ -148,7 +205,7 @@
             flops=1_000_000, bytes_accessed=1 << 16, transcendentals=0
         ),
         name="gram",
-    )(tile_count, tiles, inverse_factor)
+    )(tile_count, tile_owner, tiles, inverse_factor)
 
 
 def ring_pairs(size, span, stride, shift):
@@ -188,14 +245,17 @@
     return jnp.concatenate(ordered, 0)
 
 
-def sum_everywhere(value, scenes, rows):
+def reduction_stages(scenes, rows):
     side = 4
-    stages = [("scene", 2, 1), ("rows", side, 1), ("rows", rows // side, side), ("scene", scenes // 2, 2)]
-    for axis, span, stride in stages:
-        value = scatter_sum(value, axis, span, stride)
-    for axis, span, stride in reversed(stages):
-        value = gather(value, axis, span, stride)
-    return value
+    return [("scene", 2, 1), ("rows", side, 1), ("rows", rows // side, side)]
+
+
+def sum_along_z(value, scenes):
+    parts = gather(value, "scene", scenes // 2, 2).reshape((scenes // 2,) + value.shape)
+    total = parts[0]
+    for place in range(1, scenes // 2):
+        total = total + parts[place]
+    return total
 
 
 def sweep(block):
@@ -305,21 +365,39 @@
 
 
 def finish_kernel(
-    slot_ref, head_ref, tail_ref, received, out_ref, tiles, results, in_sems, out_sems
+    slot_ref, head_ref, tail_ref, early_ref, late_ref, out_ref, tiles, results, in_sems, out_sems
 ):
+    late = late_ref.shape[1] // 2
+
+    def fetch(owner, rank, slot):
+        return (
+            pltpu.make_async_copy(
+                early_ref.at[owner, pl.ds(rank * EARLY, EARLY)],
+                tiles.at[slot, pl.ds(0, EARLY)],
+                in_sems.at[slot, 0],
+            ),
+            pltpu.make_async_copy(
+                late_ref.at[owner, pl.ds(rank * late, late)],
+                tiles.at[slot, pl.ds(EARLY, late)],
+                in_sems.at[slot, 1],
+            ),
+        )
+
     for seat in range(slot_ref.shape[0]):
         slot = slot_ref[seat]
 
         @pl.when(slot >= 0)
         def _():
-            pltpu.make_async_copy(received.at[seat], tiles.at[slot], in_sems.at[slot]).start()
+            for copy in fetch(seat // 2, seat % 2, slot):
+                copy.start()
 
     def result_copy(j):
         return pltpu.make_async_copy(results.at[j], out_ref.at[j], out_sems.at[j])
 
     @pl.loop(0, OWN_TILES)
     def _(j):
-        pltpu.make_async_copy(received.at[0], tiles.at[j], in_sems.at[j]).wait()
+        for copy in fetch(0, 0, j):
+            copy.wait()
         head, tail = split(tiles[j])
         results[j, :, :HALF] = dot_split(
             (head[:, :HALF], tail[:, :HALF]), (head_ref[:HALF, :HALF], tail_ref[:HALF, :HALF])
@@ -332,43 +410,52 @@
         result_copy(j).wait()
 
 
-def finish(slots, received, head, tail):
-    _, rows, columns = received.shape
+def finish(slots, early, late, head, tail):
+    columns = early.shape[2]
+    rows = EARLY + late.shape[1] // 2
     hbm = pl.BlockSpec(memory_space=pl.ANY)
     vmem = pl.BlockSpec(memory_space=pltpu.VMEM)
     return pl.pallas_call(
         finish_kernel,
         out_shape=jax.ShapeDtypeStruct((OWN_TILES, rows, columns), jnp.float32),
-        in_specs=[pl.BlockSpec(memory_space=pltpu.SMEM), vmem, vmem, hbm],
+        in_specs=[pl.BlockSpec(memory_space=pltpu.SMEM), vmem, vmem, hbm, hbm],
         out_specs=hbm,
         scratch_shapes=[
             pltpu.VMEM((OWN_TILES, rows, columns), jnp.float32),
             pltpu.VMEM((OWN_TILES, rows, columns), jnp.float32),
-            pltpu.SemaphoreType.DMA((OWN_TILES,)),
+            pltpu.SemaphoreType.DMA((OWN_TILES, 2)),
             pltpu.SemaphoreType.DMA((OWN_TILES,)),
         ],
-        compiler_params=pltpu.CompilerParams(vmem_limit_bytes=48 << 20),
+        compiler_params=pltpu.CompilerParams(vmem_limit_bytes=32 << 20),
         cost_estimate=pl.CostEstimate(
             flops=5_000_000_000, bytes_accessed=8 << 20, transcendentals=0
         ),
         name="finish",
-    )(slots, head, tail, received)
+    )(slots, head, tail, early, late)
 
 
 def shards(observations, inverse_factor, tile_count, tile_owner, tile_slot):
     scenes, rows = lax.axis_size("scene"), lax.axis_size("rows")
-    capacity, tile_rows, _ = observations.shape
-    packed, seat_slot = pack(observations, tile_count, tile_owner, tile_slot, scenes)
-    me = lax.axis_index("scene")
-    group_slots = lax.all_gather(seat_slot.reshape(scenes, capacity // scenes), "scene")
-    slots = lax.dynamic_index_in_dim(group_slots, me, 1, keepdims=False).reshape(capacity)
-    received = lax.all_to_all(
-        packed.reshape((scenes, capacity // scenes) + packed.shape[1:]), "scene", 0, 0, tiled=True
-    ).reshape(packed.shape)
-    tiles, _ = lax.optimization_barrier((observations, seat_slot))
-    gram_sum = sum_everywhere(gram(tiles, inverse_factor, tile_count), scenes, rows)
-    upper, head, tail = factor(gram_sum, inverse_factor, scenes * rows * OWN_TILES * tile_rows)
-    return finish(slots, received, head, tail), upper
+    tile_rows, columns = observations.shape[1:]
+
+    def exchange(packed):
+        return lax.all_to_all(packed, "scene", 0, 0, tiled=True)
+
+    packed = pack(observations, tile_count, tile_owner, tile_slot, scenes)
+    early = exchange(packed)
+    tiles, _ = lax.optimization_barrier((observations, packed))
+    value, rest = gram(tiles, inverse_factor, tile_count, tile_owner, scenes)
+    stages = reduction_stages(scenes, rows)
+    for axis, span, stride in stages:
+        value = scatter_sum(value, axis, span, stride)
+    value = sum_along_z(value, scenes)
+    rest, value = lax.optimization_barrier((rest, value))
+    late = exchange(rest)
+    for axis, span, stride in reversed(stages):
+        value = gather(value, axis, span, stride)
+    upper, head, tail = factor(value, inverse_factor, scenes * rows * OWN_TILES * tile_rows)
+    slots = early[:, 2 * EARLY, :: columns // 2].astype(jnp.int32).reshape(-1)
+    return finish(slots, early, late, head, tail), upper
 
 
 def solution(mesh):

time: 426 us -> 128 us (0.30)
  starting transfers between devices: 239 us -> 40.1 us
  Pallas kernels: 103 us -> 49.1 us
  waiting for transfers between devices: 70 us -> 32.7 us
  blocking collectives: 8.66 us -> 0 us
    all_to_all x1 -> x2, starting transfers between devices: 197 us -> 14.7 us  [exchange(): return lax.all_to_all(packed, 'scene', 0, 0, tiled=True)]
    pallas_call x2, Pallas kernels: 73.1 us -> 18.4 us  [the longest x1 14.9 us: gram(): pl.pallas_call(gram_kernel, out_shape=(jax.ShapeDtypeStruct((3 * HALF, HA...]
    ppermute x10 -> x7, waiting for transfers between devices: 58.1 us -> 8.62 us  [scatter_sum(): lax.ppermute(sent, axis, ring_pairs(size, span, stride, shift))]
    ppermute x10 -> x7, starting transfers between devices: 26.7 us -> 12 us  [scatter_sum(): lax.ppermute(sent, axis, ring_pairs(size, span, stride, shift))]
    all_gather x1 -> x0, blocking collectives: 8.66 us -> none  [shards(): lax.all_gather(seat_slot.reshape(scenes, capacity // scenes), 'scene')]
    all_to_all x1 -> x2, waiting for transfers between devices: 0.01 us -> 7.88 us  [exchange(): return lax.all_to_all(packed, 'scene', 0, 0, tiled=True)]
    ppermute x10, waiting for transfers between devices: 11.9 us -> 16.2 us  [gather(): lax.ppermute(value, axis, ring_pairs(size, span, stride, span - ahead))]
  transfers between devices with their start and end apart: 21 -> 19, of which waited for: 16 -> 17; matrix products, arithmetic and copies ran while one was open for 1% -> 3% of each run, Pallas kernels for 7% -> 30%
where the time goes in v2:
time: 128 us; the launch traced here: 127 us
  Pallas kernels  49.1 us (38%)
  starting transfers between devices  40.1 us (31%)
  waiting for transfers between devices  32.7 us (26%)
  local copies, waits for them, and re-layouts  2.15 us (2%)
  between operations  1.65 us (1%)
  other arithmetic  1.35 us (1%)
    pallas_call x1, Pallas kernels, factor(): pl.pallas_call(functools.partial(factor_kernel, row_count), out_shape=(ja...  23.5 us
    ppermute x10, waiting for transfers between devices, gather(): lax.ppermute(value, axis, ring_pairs(size, span, stride, span - ahead))  16.2 us
    pallas_call x1, Pallas kernels, gram(): pl.pallas_call(gram_kernel, out_shape=(jax.ShapeDtypeStruct((3 * HALF, HA...  14.9 us
    all_to_all x2, starting transfers between devices, exchange(): return lax.all_to_all(packed, 'scene', 0, 0, tiled=True)  14.7 us
    ppermute x10, starting transfers between devices, gather(): lax.ppermute(value, axis, ring_pairs(size, span, stride, span - ahead))  13.3 us
    ppermute x7, starting transfers between devices, scatter_sum(): lax.ppermute(sent, axis, ring_pairs(size, span, stride, shift))  12 us
    ppermute x7, waiting for transfers between devices, scatter_sum(): lax.ppermute(sent, axis, ring_pairs(size, span, stride, shift))  8.62 us
    all_to_all x2, waiting for transfers between devices, exchange(): return lax.all_to_all(packed, 'scene', 0, 0, tiled=True)  7.88 us
  transfers between devices with their start and end apart: 19, of which 17 were waited for; matrix products, arithmetic and copies ran while one was open for 3% of the time, Pallas kernels for 30%

profile of v2, /device:TPU:1, one launch (start us, length us, event | category | flops | bytes accessed | tf_op | source)
XLA Modules:
  0.0 127.1 jit_solution(4731604240580438985)
XLA Ops:
  1.3 3.5 %pack.1 = f32[8,248,512]{2,1,0:T(8,128)} custom-call(s32[1]{0:T(128)S(6)} %copy.7.count_ref, s32[16]{0:T(128)} %owner_ref.3, s32[16]{0:T(128)} %slot_ref.1, f32[16,256,512]{2,1,0:T(8,128)} %tile_ref), custom_call_target="tpu_custom_call" | custom-call | bytes 8388608 | tf_op jit(solution)/shard_map/pack/pallas_call | solution.py:106
  4.8 8.1 %all-to-all-start = ((f32[8,248,512]{2,1,0:T(8,128)}), f32[8,248,512]{2,1,0:T(8,128)}, u32[]{:S(2)}, u32[]{:S(2)}) async-start(f32[8,248,512]{2,1,0:T(8,128)} %pack.1), calls=%async_computation | async-start | bytes 8126464 | tf_op jit(solution)/shard_map/all_to_all | solution.py:442
  12.8 14.9 %gram.1 = (f32[768,256]{1,0:T(8,128)}, f32[8,272,512]{2,1,0:T(8,128)}) custom-call(s32[1]{0:T(128)S(6)} %copy.7.count_ref, s32[16]{0:T(128)} %owner_ref.3, f32[16,256,512]{2,1,0:T(8,128)} %tile_ref, f32[512,512]{1,0:T(8,128)} %inverse_ref.3), custom_call_target="tpu_custom_call" | custom-call | flops 1000000 | bytes 65536 | tf_op jit(solution)/shard_map/gram/pallas_call | solution.py:173
  28.9 1.6 %collective-permute-done = f32[384,256]{1,0:T(8,128)S(1)} collective-permute-done((f32[384,256]{1,0:T(8,128)S(1)}, f32[384,256]{1,0:T(8,128)S(1)}, u32[]{:S(2)}, u32[]{:S(2)}) %collective-permute-start) | collective-permute-done | bytes 393248 | tf_op jit(solution)/shard_map/ppermute | solution.py:223
  31.6 3.6 %collective-permute-start.1 = (f32[96,256]{1,0:T(8,128)S(1)}, f32[96,256]{1,0:T(8,128)S(1)}, u32[]{:S(2)}, u32[]{:S(2)}) collective-permute-start(f32[96,256]{1,0:T(8,128)S(1)} %get-tuple-element.24), channel_id=1, source_target_pairs={{0,1},{1,2},{2,3},{3,0},{4,5},{5,6},{6,7},{7,4},{8,9},{9,10},{10,1... | collective-permute-start | bytes 294920 | tf_op jit(solution)/shard_map/ppermute | solution.py:223
  35.2 4.6 %collective-permute-start.2 = (f32[96,256]{1,0:T(8,128)S(1)}, f32[96,256]{1,0:T(8,128)S(1)}, u32[]{:S(2)}, u32[]{:S(2)}) collective-permute-start(f32[96,256]{1,0:T(8,128)S(1)} %get-tuple-element.26), channel_id=1, source_target_pairs={{0,2},{1,3},{2,0},{3,1},{4,6},{5,7},{6,4},{7,5},{8,10},{9,11},{10,... | collective-permute-start | bytes 294920 | tf_op jit(solution)/shard_map/ppermute | solution.py:223
  40.6 2.6 %collective-permute-done.2 = f32[96,256]{1,0:T(8,128)S(1)} collective-permute-done((f32[96,256]{1,0:T(8,128)S(1)}, f32[96,256]{1,0:T(8,128)S(1)}, u32[]{:S(2)}, u32[]{:S(2)}) %collective-permute-start.2) | collective-permute-done | bytes 98336 | tf_op jit(solution)/shard_map/ppermute | solution.py:223
  43.3 1.9 %collective-permute-start.4 = (f32[24,256]{1,0:T(8,128)S(1)}, f32[24,256]{1,0:T(8,128)S(1)}, u32[]{:S(2)}, u32[]{:S(2)}) collective-permute-start(f32[24,256]{1,0:T(8,128)S(1)} %get-tuple-element.31), channel_id=1, source_target_pairs={{0,4},{1,5},{2,6},{3,7},{4,8},{5,9},{6,10},{7,11},{8,12},{9,13},{1... | collective-permute-start | bytes 73736 | tf_op jit(solution)/shard_map/ppermute | solution.py:223
  46.1 1.1 collective-permute-start.5
  48.3 2.3 %collective-permute-done.5 = f32[24,256]{1,0:T(8,128)S(1)} collective-permute-done((f32[24,256]{1,0:T(8,128)S(1)}, f32[24,256]{1,0:T(8,128)S(1)}, u32[]{:S(2)}, u32[]{:S(2)}) %collective-permute-start.5) | collective-permute-done | bytes 24608 | tf_op jit(solution)/shard_map/ppermute | solution.py:223
  50.7 4.6 %collective-permute-start.9 = (f32[24,256]{1,0:T(8,128)S(1)}, f32[24,256]{1,0:T(8,128)S(1)}, u32[]{:S(2)}, u32[]{:S(2)}) collective-permute-start(f32[24,256]{1,0:T(8,128)S(1)} %fusion.3), channel_id=1, source_target_pairs={{0,96},{16,112},{32,0},{48,16},{64,32},{80,48},{96,64},{112,80},{1... | collective-permute-start | bytes 73736 | tf_op jit(solution)/shard_map/ppermute | solution.py:238
  55.9 3.5 %collective-permute-done.9 = f32[24,256]{1,0:T(8,128)S(1)} collective-permute-done((f32[24,256]{1,0:T(8,128)S(1)}, f32[24,256]{1,0:T(8,128)S(1)}, u32[]{:S(2)}, u32[]{:S(2)}) %collective-permute-start.9) | collective-permute-done | bytes 24608 | tf_op jit(solution)/shard_map/ppermute | solution.py:238
  59.4 1.5 %collective-permute-done.8 = f32[24,256]{1,0:T(8,128)S(1)} collective-permute-done((f32[24,256]{1,0:T(8,128)S(1)}, f32[24,256]{1,0:T(8,128)S(1)}, u32[]{:S(2)}, u32[]{:S(2)}) %collective-permute-start.8) | collective-permute-done | bytes 24608 | tf_op jit(solution)/shard_map/ppermute | solution.py:238
  61.3 6.7 %all-to-all-start.1 = ((f32[8,272,512]{2,1,0:T(8,128)}), f32[8,272,512]{2,1,0:T(8,128)}, u32[]{:S(2)}, u32[]{:S(2)}) async-start(f32[8,272,512]{2,1,0:T(8,128)} %get-tuple-element.16), calls=%async_computation.1 | async-start | bytes 8912896 | tf_op jit(solution)/shard_map/all_to_all | solution.py:442
  68.0 1.4 %collective-permute-start.12 = (f32[24,256]{1,0:T(8,128)S(1)}, f32[24,256]{1,0:T(8,128)S(1)}, u32[]{:S(2)}, u32[]{:S(2)}) collective-permute-start(f32[24,256]{1,0:T(8,128)S(1)} %select_add_fusion), channel_id=1, source_target_pairs={{0,12},{1,13},{2,14},{3,15},{4,0},{5,1},{6,2},{7,3},{8,4},{9,5},{1... | collective-permute-start | bytes 73736 | tf_op jit(solution)/shard_map/ppermute | solution.py:238
  70.7 3.3 %collective-permute-done.11 = f32[24,256]{1,0:T(8,128)S(1)} collective-permute-done((f32[24,256]{1,0:T(8,128)S(1)}, f32[24,256]{1,0:T(8,128)S(1)}, u32[]{:S(2)}, u32[]{:S(2)}) %collective-permute-start.11) | collective-permute-done | bytes 24608 | tf_op jit(solution)/shard_map/ppermute | solution.py:238
  74.3 2.3 %collective-permute-start.15 = (f32[96,256]{1,0:T(8,128)S(1)}, f32[96,256]{1,0:T(8,128)S(1)}, u32[]{:S(2)}, u32[]{:S(2)}) collective-permute-start(f32[96,256]{1,0:T(8,128)S(1)} %pad_maximum_fusion.2), channel_id=1, source_target_pairs={{0,3},{1,0},{2,1},{3,2},{4,7},{5,4},{6,5},{7,6},{8,11},{9,8},{10,9... | collective-permute-start | bytes 294920 | tf_op jit(solution)/shard_map/ppermute | solution.py:238
  77.2 1.7 %collective-permute-done.15 = f32[96,256]{1,0:T(8,128)S(1)} collective-permute-done((f32[96,256]{1,0:T(8,128)S(1)}, f32[96,256]{1,0:T(8,128)S(1)}, u32[]{:S(2)}, u32[]{:S(2)}) %collective-permute-start.15) | collective-permute-done | bytes 98336 | tf_op jit(solution)/shard_map/ppermute | solution.py:238
  79.0 3.0 %collective-permute-done.14 = f32[96,256]{1,0:T(8,128)S(1)} collective-permute-done((f32[96,256]{1,0:T(8,128)S(1)}, f32[96,256]{1,0:T(8,128)S(1)}, u32[]{:S(2)}, u32[]{:S(2)}) %collective-permute-start.14) | collective-permute-done | bytes 98336 | tf_op jit(solution)/shard_map/ppermute | solution.py:238
  83.1 2.7 %collective-permute-start.16 = (f32[384,256]{1,0:T(8,128)S(1)}, f32[384,256]{1,0:T(8,128)S(1)}, u32[]{:S(2)}, u32[]{:S(2)}) collective-permute-start(f32[384,256]{1,0:T(8,128)S(1)} %pad_maximum_fusion.1), channel_id=1, source_target_pairs={{0,16},{16,0},{32,48},{48,32},{64,80},{80,64},{96,112},{112,96},{1... | collective-permute-start | bytes 1179656 | tf_op jit(solution)/shard_map/ppermute | solution.py:238
  85.8 1.3 %collective-permute-done.16 = f32[384,256]{1,0:T(8,128)S(1)} collective-permute-done((f32[384,256]{1,0:T(8,128)S(1)}, f32[384,256]{1,0:T(8,128)S(1)}, u32[]{:S(2)}, u32[]{:S(2)}) %collective-permute-start.16) | collective-permute-done | bytes 393248 | tf_op jit(solution)/shard_map/ppermute | solution.py:238
  87.2 23.5 %factor.1 = (f32[512,512]{1,0:T(8,128)}, bf16[512,512]{1,0:T(8,128)(2,1)S(1)}, bf16[512,512]{1,0:T(8,128)(2,1)S(1)}) custom-call(f32[768,256]{1,0:T(8,128)S(1)} %pad_maximum_fusion.gram_ref, f32[512,512]{1,0:T(8,128)S(1)} %copy-done), custom_call_target="tpu_custom_call" | custom-call | flops 1000000 | bytes 65536 | tf_op jit(solution)/shard_map/factor/pallas_call | solution.py:349
  111.9 7.9 %all-to-all-done.1.late_ref = f32[8,272,512]{2,1,0:T(8,128)} async-done(((f32[8,272,512]{2,1,0:T(8,128)}), f32[8,272,512]{2,1,0:T(8,128)}, u32[]{:S(2)}, u32[]{:S(2)}) %all-to-all-start.1) | async-done | bytes 4456480 | tf_op jit(solution)/shard_map/all_to_all | solution.py:442
  119.7 7.2 %finish.1 = f32[8,256,512]{2,1,0:T(8,128)} custom-call(s32[16]{0:T(128)S(1)} %convert_element_type.8.slot_ref, bf16[512,512]{1,0:T(8,128)(2,1)S(1)} %get-tuple-element.14.head_ref, bf16[512,512]{1,0:T(8,128)(2,1)S(1)} %get-tuple-element.15.tail_ref, f32[8,248,512]{2,1,0:T(8,128)} %all-to-all-done.early_ref, f32[8,272,512]{2,1,0:T(8,128)} %all-to-all-done.1.late_ref), custom_call_target="tpu_custom_call" | custom-call | flops 5000000000 | bytes 8388608 | tf_op jit(solution)/shard_map/finish/pallas_call | solution.py:418
  (37 shorter events, 10.7 us)
Async XLA Ops:
  4.8 56.5 %all-to-all-start = ((f32[8,248,512]{2,1,0:T(8,128)}), f32[8,248,512]{2,1,0:T(8,128)}, u32[]{:S(2)}, u32[]{:S(2)}) async-start(f32[8,248,512]{2,1,0:T(8,128)} %pack.1), calls=%async_computation | async-start | bytes 8126464 | tf_op jit(solution)/shard_map/all_to_all | solution.py:442
  28.8 1.8 %collective-permute-start = (f32[384,256]{1,0:T(8,128)S(1)}, f32[384,256]{1,0:T(8,128)S(1)}, u32[]{:S(2)}, u32[]{:S(2)}) collective-permute-start(f32[384,256]{1,0:T(8,128)S(1)} %dynamic-slice_bitcast_fusion), channel_id=1, source_target_pairs={{0,16},{16,0},{32,48},{48,32},{64,80},{80,64},{96,112},{112,96},{1... | collective-permute-start | bytes 1179656 | tf_op jit(solution)/shard_map/ppermute | solution.py:223
  31.6 8.1 %collective-permute-start.1 = (f32[96,256]{1,0:T(8,128)S(1)}, f32[96,256]{1,0:T(8,128)S(1)}, u32[]{:S(2)}, u32[]{:S(2)}) collective-permute-start(f32[96,256]{1,0:T(8,128)S(1)} %get-tuple-element.24), channel_id=1, source_target_pairs={{0,1},{1,2},{2,3},{3,0},{4,5},{5,6},{6,7},{7,4},{8,9},{9,10},{10,1... | collective-permute-start | bytes 294920 | tf_op jit(solution)/shard_map/ppermute | solution.py:223
  35.2 5.4 %collective-permute-start.3 = (f32[96,256]{1,0:T(8,128)S(1)}, f32[96,256]{1,0:T(8,128)S(1)}, u32[]{:S(2)}, u32[]{:S(2)}) collective-permute-start(f32[96,256]{1,0:T(8,128)S(1)} %get-tuple-element.25), channel_id=1, source_target_pairs={{0,3},{1,0},{2,1},{3,2},{4,7},{5,4},{6,5},{7,6},{8,11},{9,8},{10,9... | collective-permute-start | bytes 294920 | tf_op jit(solution)/shard_map/ppermute | solution.py:223
  35.2 8.1 %collective-permute-start.2 = (f32[96,256]{1,0:T(8,128)S(1)}, f32[96,256]{1,0:T(8,128)S(1)}, u32[]{:S(2)}, u32[]{:S(2)}) collective-permute-start(f32[96,256]{1,0:T(8,128)S(1)} %get-tuple-element.26), channel_id=1, source_target_pairs={{0,2},{1,3},{2,0},{3,1},{4,6},{5,7},{6,4},{7,5},{8,10},{9,11},{10,... | collective-permute-start | bytes 294920 | tf_op jit(solution)/shard_map/ppermute | solution.py:223
  43.3 4.4 %collective-permute-start.4 = (f32[24,256]{1,0:T(8,128)S(1)}, f32[24,256]{1,0:T(8,128)S(1)}, u32[]{:S(2)}, u32[]{:S(2)}) collective-permute-start(f32[24,256]{1,0:T(8,128)S(1)} %get-tuple-element.31), channel_id=1, source_target_pairs={{0,4},{1,5},{2,6},{3,7},{4,8},{5,9},{6,10},{7,11},{8,12},{9,13},{1... | collective-permute-start | bytes 73736 | tf_op jit(solution)/shard_map/ppermute | solution.py:223
  45.3 3.1 %collective-permute-start.6 = (f32[24,256]{1,0:T(8,128)S(1)}, f32[24,256]{1,0:T(8,128)S(1)}, u32[]{:S(2)}, u32[]{:S(2)}) collective-permute-start(f32[24,256]{1,0:T(8,128)S(1)} %get-tuple-element.32), channel_id=1, source_target_pairs={{0,12},{1,13},{2,14},{3,15},{4,0},{5,1},{6,2},{7,3},{8,4},{9,5},{1... | collective-permute-start | bytes 73736 | tf_op jit(solution)/shard_map/ppermute | solution.py:223
  46.1 4.6 %collective-permute-start.5 = (f32[24,256]{1,0:T(8,128)S(1)}, f32[24,256]{1,0:T(8,128)S(1)}, u32[]{:S(2)}, u32[]{:S(2)}) collective-permute-start(f32[24,256]{1,0:T(8,128)S(1)} %get-tuple-element.33), channel_id=1, source_target_pairs={{0,8},{1,9},{2,10},{3,11},{4,12},{5,13},{6,14},{7,15},{8,0},{9,1},... | collective-permute-start | bytes 73736 | tf_op jit(solution)/shard_map/ppermute | solution.py:223
  50.7 8.7 %collective-permute-start.9 = (f32[24,256]{1,0:T(8,128)S(1)}, f32[24,256]{1,0:T(8,128)S(1)}, u32[]{:S(2)}, u32[]{:S(2)}) collective-permute-start(f32[24,256]{1,0:T(8,128)S(1)} %fusion.3), channel_id=1, source_target_pairs={{0,96},{16,112},{32,0},{48,16},{64,32},{80,48},{96,64},{112,80},{1... | collective-permute-start | bytes 73736 | tf_op jit(solution)/shard_map/ppermute | solution.py:238
  55.3 5.6 %collective-permute-start.8 = (f32[24,256]{1,0:T(8,128)S(1)}, f32[24,256]{1,0:T(8,128)S(1)}, u32[]{:S(2)}, u32[]{:S(2)}) collective-permute-start(f32[24,256]{1,0:T(8,128)S(1)} %fusion.3), channel_id=1, source_target_pairs={{0,64},{16,80},{32,96},{48,112},{64,0},{80,16},{96,32},{112,48},{1... | collective-permute-start | bytes 73736 | tf_op jit(solution)/shard_map/ppermute | solution.py:238
  55.3 6.0 %collective-permute-start.7 = (f32[24,256]{1,0:T(8,128)S(1)}, f32[24,256]{1,0:T(8,128)S(1)}, u32[]{:S(2)}, u32[]{:S(2)}) collective-permute-start(f32[24,256]{1,0:T(8,128)S(1)} %fusion.3), channel_id=1, source_target_pairs={{0,32},{16,48},{32,64},{48,80},{64,96},{80,112},{96,0},{112,16},{1... | collective-permute-start | bytes 73736 | tf_op jit(solution)/shard_map/ppermute | solution.py:238
  61.3 58.4 %all-to-all-start.1 = ((f32[8,272,512]{2,1,0:T(8,128)}), f32[8,272,512]{2,1,0:T(8,128)}, u32[]{:S(2)}, u32[]{:S(2)}) async-start(f32[8,272,512]{2,1,0:T(8,128)} %get-tuple-element.16), calls=%async_computation.1 | async-start | bytes 8912896 | tf_op jit(solution)/shard_map/all_to_all | solution.py:442
  68.0 19.2 %copy-start = (f32[512,512]{1,0:T(8,128)S(1)}, f32[512,512]{1,0:T(8,128)}, u32[]{:S(2)}) copy-start(f32[512,512]{1,0:T(8,128)} %inverse_ref.3) | copy-start | bytes 3145732
  68.0 2.7 %collective-permute-start.12 = (f32[24,256]{1,0:T(8,128)S(1)}, f32[24,256]{1,0:T(8,128)S(1)}, u32[]{:S(2)}, u32[]{:S(2)}) collective-permute-start(f32[24,256]{1,0:T(8,128)S(1)} %select_add_fusion), channel_id=1, source_target_pairs={{0,12},{1,13},{2,14},{3,15},{4,0},{5,1},{6,2},{7,3},{8,4},{9,5},{1... | collective-permute-start | bytes 73736 | tf_op jit(solution)/shard_map/ppermute | solution.py:238
  69.5 4.6 %collective-permute-start.11 = (f32[24,256]{1,0:T(8,128)S(1)}, f32[24,256]{1,0:T(8,128)S(1)}, u32[]{:S(2)}, u32[]{:S(2)}) collective-permute-start(f32[24,256]{1,0:T(8,128)S(1)} %select_add_fusion), channel_id=1, source_target_pairs={{0,8},{1,9},{2,10},{3,11},{4,12},{5,13},{6,14},{7,15},{8,0},{9,1},... | collective-permute-start | bytes 73736 | tf_op jit(solution)/shard_map/ppermute | solution.py:238
  69.7 4.6 %collective-permute-start.10 = (f32[24,256]{1,0:T(8,128)S(1)}, f32[24,256]{1,0:T(8,128)S(1)}, u32[]{:S(2)}, u32[]{:S(2)}) collective-permute-start(f32[24,256]{1,0:T(8,128)S(1)} %select_add_fusion), channel_id=1, source_target_pairs={{0,4},{1,5},{2,6},{3,7},{4,8},{5,9},{6,10},{7,11},{8,12},{9,13},{1... | collective-permute-start | bytes 73736 | tf_op jit(solution)/shard_map/ppermute | solution.py:238
  74.3 4.7 %collective-permute-start.15 = (f32[96,256]{1,0:T(8,128)S(1)}, f32[96,256]{1,0:T(8,128)S(1)}, u32[]{:S(2)}, u32[]{:S(2)}) collective-permute-start(f32[96,256]{1,0:T(8,128)S(1)} %pad_maximum_fusion.2), channel_id=1, source_target_pairs={{0,3},{1,0},{2,1},{3,2},{4,7},{5,4},{6,5},{7,6},{8,11},{9,8},{10,9... | collective-permute-start | bytes 294920 | tf_op jit(solution)/shard_map/ppermute | solution.py:238
  76.6 5.4 %collective-permute-start.14 = (f32[96,256]{1,0:T(8,128)S(1)}, f32[96,256]{1,0:T(8,128)S(1)}, u32[]{:S(2)}, u32[]{:S(2)}) collective-permute-start(f32[96,256]{1,0:T(8,128)S(1)} %pad_maximum_fusion.2), channel_id=1, source_target_pairs={{0,2},{1,3},{2,0},{3,1},{4,6},{5,7},{6,4},{7,5},{8,10},{9,11},{10,... | collective-permute-start | bytes 294920 | tf_op jit(solution)/shard_map/ppermute | solution.py:238
  77.2 5.8 %collective-permute-start.13 = (f32[96,256]{1,0:T(8,128)S(1)}, f32[96,256]{1,0:T(8,128)S(1)}, u32[]{:S(2)}, u32[]{:S(2)}) collective-permute-start(f32[96,256]{1,0:T(8,128)S(1)} %pad_maximum_fusion.2), channel_id=1, source_target_pairs={{0,1},{1,2},{2,3},{3,0},{4,5},{5,6},{6,7},{7,4},{8,9},{9,10},{10,1... | collective-permute-start | bytes 294920 | tf_op jit(solution)/shard_map/ppermute | solution.py:238
  83.1 4.0 %collective-permute-start.16 = (f32[384,256]{1,0:T(8,128)S(1)}, f32[384,256]{1,0:T(8,128)S(1)}, u32[]{:S(2)}, u32[]{:S(2)}) collective-permute-start(f32[384,256]{1,0:T(8,128)S(1)} %pad_maximum_fusion.1), channel_id=1, source_target_pairs={{0,16},{16,0},{32,48},{48,32},{64,80},{80,64},{96,112},{112,96},{1... | collective-permute-start | bytes 1179656 | tf_op jit(solution)/shard_map/ppermute | solution.py:238

commit v3 on v2

--- a/solution.py
+++ b/solution.py
@@ -11,8 +11,9 @@
 BLOCK = 128
 PIVOT = 8
 HALF = 256
-EARLY = 120
+EARLY = 128
 HEADER = 8
+GROUP = 4
 
 
 def split(value):
@@ -123,9 +124,14 @@
 
 
 def gram_kernel(
-    count_ref, owner_ref, tile_ref, inverse_ref, gram_ref, late_ref, inv_head, inv_tail, cross, used, sem
+    count_ref, owner_ref, tile_ref, inverse_ref, gram_ref, late_ref, inv_head, inv_tail, cross, used, sems
 ):
     step = pl.program_id(0)
+    late = late_ref.shape[1] // 2
+
+    def late_copy(i, owner, rank):
+        target = late_ref.at[owner, pl.ds(pl.multiple_of(rank * late, 8), late)]
+        return pltpu.make_async_copy(tile_ref.at[i, pl.ds(EARLY, late)], target, sems.at[i])
 
     @pl.when(step == 0)
     def _():
@@ -137,14 +143,20 @@
         for owner in range(used.shape[0]):
             used[owner] = 0
 
-    @pl.when(step < count_ref[0])
+    tiles = tile_ref.shape[0]
+    for i in range(tiles):
+
+        @pl.when(tiles * step + i < count_ref[0])
+        def _():
+            owner, rank = seat_of(tiles * step + i, owner_ref, used)
+            late_copy(i, owner, rank).start()
+
+    @pl.when(tiles * step < count_ref[0])
     def _():
-        owner, rank = seat_of(step, owner_ref, used)
-        late = late_ref.shape[1] // 2
-        target = late_ref.at[owner, pl.ds(pl.multiple_of(rank * late, 8), late)]
-        copy = pltpu.make_async_copy(tile_ref.at[0, pl.ds(EARLY, late)], target, sem)
-        copy.start()
-        head, tail = split(tile_ref[0])
+        live = [tile_ref[0]]
+        for i in range(1, tiles):
+            live.append(jnp.where(tiles * step + i < count_ref[0], tile_ref[i], 0.0))
+        head, tail = split(jnp.concatenate(live, 0))
         left = dot_split(
             (head[:, :HALF], tail[:, :HALF]), (inv_head[:HALF, :HALF], inv_tail[:HALF, :HALF])
         )
@@ -160,7 +172,12 @@
         )
         gram_ref[2 * HALF :, :] += dot16(right_head, right_head, 0, 0)
         cross[HALF:, :] += dot16(right_head, right_tail, 0, 0)
-        copy.wait()
+
+    for i in range(tiles):
+
+        @pl.when(tiles * step + i < count_ref[0])
+        def _():
+            late_copy(i, 0, 0).wait()
 
     @pl.when(step == pl.num_programs(0) - 1)
     def _():
@@ -178,11 +195,13 @@
         ),
         grid_spec=pltpu.PrefetchScalarGridSpec(
             num_scalar_prefetch=2,
-            grid=(capacity,),
+            grid=(capacity // GROUP,),
             in_specs=[
                 pl.BlockSpec(
-                    (1, rows, columns),
-                    lambda i, count, _: (jnp.minimum(i, jnp.maximum(count[0] - 1, 0)), 0, 0),
+                    (GROUP, rows, columns),
+                    lambda i, count, _: (
+                        jnp.minimum(i, jnp.maximum(count[0] - 1, 0) // GROUP), 0, 0
+                    ),
                 ),
                 pl.BlockSpec((columns, columns), lambda i, *_: (0, 0)),
             ],
@@ -195,7 +214,7 @@
                 pltpu.VMEM((columns, columns), jnp.bfloat16),
                 pltpu.VMEM((2 * HALF, HALF), jnp.float32),
                 pltpu.SMEM((scenes,), jnp.int32),
-                pltpu.SemaphoreType.DMA,
+                pltpu.SemaphoreType.DMA((GROUP,)),
             ],
         ),
         compiler_params=pltpu.CompilerParams(
@@ -231,18 +250,25 @@
     return chosen
 
 
-def gather(value, axis, span, stride):
+def from_ahead(value, axis, span, stride):
     size = lax.axis_size(axis)
-    me = lax.axis_index(axis) // stride % span
-    onward = [value] + [
+    return [value] + [
         lax.ppermute(value, axis, ring_pairs(size, span, stride, span - ahead))
         for ahead in range(1, span)
     ]
-    ordered = [
-        select_one([(me + ahead) % span == place for ahead in range(span)], onward)
+
+
+def in_order(ahead_values, axis, stride):
+    span = len(ahead_values)
+    me = lax.axis_index(axis) // stride % span
+    return [
+        select_one([(me + ahead) % span == place for ahead in range(span)], ahead_values)
         for place in range(span)
     ]
-    return jnp.concatenate(ordered, 0)
+
+
+def gather(value, axis, span, stride):
+    return jnp.concatenate(in_order(from_ahead(value, axis, span, stride), axis, stride), 0)
 
 
 def reduction_stages(scenes, rows):
@@ -250,12 +276,13 @@
     return [("scene", 2, 1), ("rows", side, 1), ("rows", rows // side, side)]
 
 
-def sum_along_z(value, scenes):
-    parts = gather(value, "scene", scenes // 2, 2).reshape((scenes // 2,) + value.shape)
-    total = parts[0]
-    for place in range(1, scenes // 2):
-        total = total + parts[place]
-    return total
+def sum_along_z(value, scenes, rest):
+    parts = from_ahead(value, "scene", scenes // 2, 2)
+    rest, *parts = lax.optimization_barrier((rest, *parts))
+    total, *more = in_order(parts, "scene", 2)
+    for part in more:
+        total = total + part
+    return total, rest
 
 
 def sweep(block):
@@ -448,8 +475,7 @@
     stages = reduction_stages(scenes, rows)
     for axis, span, stride in stages:
         value = scatter_sum(value, axis, span, stride)
-    value = sum_along_z(value, scenes)
-    rest, value = lax.optimization_barrier((rest, value))
+    value, rest = sum_along_z(value, scenes, rest)
     late = exchange(rest)
     for axis, span, stride in reversed(stages):
         value = gather(value, axis, span, stride)

time: 128 us -> 126 us (0.984)
  Pallas kernels: 49.1 us -> 45.9 us
    ppermute x10, waiting for transfers between devices: 16.2 us -> 22.1 us  [from_ahead(): lax.ppermute(value, axis, ring_pairs(size, span, stride, span - ahead))]
    all_to_all x2, waiting for transfers between devices: 7.88 us -> 2.84 us  [exchange(): return lax.all_to_all(packed, 'scene', 0, 0, tiled=True)]
    ppermute x10, starting transfers between devices: 13.3 us -> 17.8 us  [from_ahead(): lax.ppermute(value, axis, ring_pairs(size, span, stride, span - ahead))]
    pallas_call x1, Pallas kernels: 14.9 us -> 11.8 us  [gram(): pl.pallas_call(gram_kernel, out_shape=(jax.ShapeDtypeStruct((3 * HALF, HA...]
    all_to_all x2, starting transfers between devices: 14.7 us -> 12.6 us  [exchange(): return lax.all_to_all(packed, 'scene', 0, 0, tiled=True)]
  transfers between devices with their start and end apart: 19 -> 19, of which waited for: 17 -> 14; matrix products, arithmetic and copies ran while one was open for 3% -> 3% of each run, Pallas kernels for 30% -> 28%
where the time goes in v3:
time: 126 us; the launch traced here: 125 us
  Pallas kernels  45.9 us (36%)
  starting transfers between devices  41.3 us (33%)
  waiting for transfers between devices  32.6 us (26%)
  local copies, waits for them, and re-layouts  2.15 us (2%)
  between operations  1.62 us (1%)
  other arithmetic  1.35 us (1%)
    pallas_call x1, Pallas kernels, factor(): pl.pallas_call(functools.partial(factor_kernel, row_count), out_shape=(ja...  23.5 us
    ppermute x10, waiting for transfers between devices, from_ahead(): lax.ppermute(value, axis, ring_pairs(size, span, stride, span - ahead))  22.1 us
    ppermute x10, starting transfers between devices, from_ahead(): lax.ppermute(value, axis, ring_pairs(size, span, stride, span - ahead))  17.8 us
    all_to_all x2, starting transfers between devices, exchange(): return lax.all_to_all(packed, 'scene', 0, 0, tiled=True)  12.6 us
    pallas_call x1, Pallas kernels, gram(): pl.pallas_call(gram_kernel, out_shape=(jax.ShapeDtypeStruct((3 * HALF, HA...  11.8 us
    ppermute x7, starting transfers between devices, scatter_sum(): lax.ppermute(sent, axis, ring_pairs(size, span, stride, shift))  10.9 us
    ppermute x7, waiting for transfers between devices, scatter_sum(): lax.ppermute(sent, axis, ring_pairs(size, span, stride, shift))  7.61 us
    pallas_call x1, Pallas kernels, finish(): pl.pallas_call(finish_kernel, out_shape=jax.ShapeDtypeStruct((OWN_TILES,...  7.11 us
  transfers between devices with their start and end apart: 19, of which 14 were waited for; matrix products, arithmetic and copies ran while one was open for 3% of the time, Pallas kernels for 28%

profile of v3, /device:TPU:1, one launch (start us, length us, event | category | flops | bytes accessed | tf_op | source)
XLA Modules:
  0.0 124.9 jit_solution(15623830213166696992)
XLA Ops:
  1.3 3.5 %pack.1 = f32[8,264,512]{2,1,0:T(8,128)} custom-call(s32[1]{0:T(128)S(6)} %copy.7.count_ref, s32[16]{0:T(128)} %owner_ref.3, s32[16]{0:T(128)} %slot_ref.1, f32[16,256,512]{2,1,0:T(8,128)} %tile_ref), custom_call_target="tpu_custom_call" | custom-call | bytes 8388608 | tf_op jit(solution)/shard_map/pack/pallas_call | solution.py:107
  4.8 7.3 %all-to-all-start = ((f32[8,264,512]{2,1,0:T(8,128)}), f32[8,264,512]{2,1,0:T(8,128)}, u32[]{:S(2)}, u32[]{:S(2)}) async-start(f32[8,264,512]{2,1,0:T(8,128)} %pack.1), calls=%async_computation | async-start | bytes 8650752 | tf_op jit(solution)/shard_map/all_to_all | solution.py:469
  12.1 11.8 %gram.1 = (f32[768,256]{1,0:T(8,128)}, f32[8,256,512]{2,1,0:T(8,128)}) custom-call(s32[1]{0:T(128)S(6)} %copy.7.count_ref, s32[16]{0:T(128)} %owner_ref.3, f32[16,256,512]{2,1,0:T(8,128)} %tile_ref, f32[512,512]{1,0:T(8,128)} %inverse_ref.3), custom_call_target="tpu_custom_call" | custom-call | flops 1000000 | bytes 65536 | tf_op jit(solution)/shard_map/gram/pallas_call | solution.py:190
  25.1 1.6 %collective-permute-done = f32[384,256]{1,0:T(8,128)S(1)} collective-permute-done((f32[384,256]{1,0:T(8,128)S(1)}, f32[384,256]{1,0:T(8,128)S(1)}, u32[]{:S(2)}, u32[]{:S(2)}) %collective-permute-start) | collective-permute-done | bytes 393248 | tf_op jit(solution)/shard_map/ppermute | solution.py:242
  28.7 1.8 %collective-permute-start.3 = (f32[96,256]{1,0:T(8,128)S(1)}, f32[96,256]{1,0:T(8,128)S(1)}, u32[]{:S(2)}, u32[]{:S(2)}) collective-permute-start(f32[96,256]{1,0:T(8,128)S(1)} %get-tuple-element.31), channel_id=1, source_target_pairs={{0,3},{1,0},{2,1},{3,2},{4,7},{5,4},{6,5},{7,6},{8,11},{9,8},{10,9... | collective-permute-start | bytes 294920 | tf_op jit(solution)/shard_map/ppermute | solution.py:242
  30.5 3.6 %collective-permute-start.2 = (f32[96,256]{1,0:T(8,128)S(1)}, f32[96,256]{1,0:T(8,128)S(1)}, u32[]{:S(2)}, u32[]{:S(2)}) collective-permute-start(f32[96,256]{1,0:T(8,128)S(1)} %get-tuple-element.32), channel_id=1, source_target_pairs={{0,2},{1,3},{2,0},{3,1},{4,6},{5,7},{6,4},{7,5},{8,10},{9,11},{10,... | collective-permute-start | bytes 294920 | tf_op jit(solution)/shard_map/ppermute | solution.py:242
  35.0 2.6 %collective-permute-done.2 = f32[96,256]{1,0:T(8,128)S(1)} collective-permute-done((f32[96,256]{1,0:T(8,128)S(1)}, f32[96,256]{1,0:T(8,128)S(1)}, u32[]{:S(2)}, u32[]{:S(2)}) %collective-permute-start.2) | collective-permute-done | bytes 98336 | tf_op jit(solution)/shard_map/ppermute | solution.py:242
  37.7 2.6 %collective-permute-start.4 = (f32[24,256]{1,0:T(8,128)S(1)}, f32[24,256]{1,0:T(8,128)S(1)}, u32[]{:S(2)}, u32[]{:S(2)}) collective-permute-start(f32[24,256]{1,0:T(8,128)S(1)} %get-tuple-element.37), channel_id=1, source_target_pairs={{0,4},{1,5},{2,6},{3,7},{4,8},{5,9},{6,10},{7,11},{8,12},{9,13},{1... | collective-permute-start | bytes 73736 | tf_op jit(solution)/shard_map/ppermute | solution.py:242
  40.4 1.7 %collective-permute-start.5 = (f32[24,256]{1,0:T(8,128)S(1)}, f32[24,256]{1,0:T(8,128)S(1)}, u32[]{:S(2)}, u32[]{:S(2)}) collective-permute-start(f32[24,256]{1,0:T(8,128)S(1)} %get-tuple-element.39), channel_id=1, source_target_pairs={{0,8},{1,9},{2,10},{3,11},{4,12},{5,13},{6,14},{7,15},{8,0},{9,1},... | collective-permute-start | bytes 73736 | tf_op jit(solution)/shard_map/ppermute | solution.py:242
  43.3 1.3 %collective-permute-done.5 = f32[24,256]{1,0:T(8,128)S(1)} collective-permute-done((f32[24,256]{1,0:T(8,128)S(1)}, f32[24,256]{1,0:T(8,128)S(1)}, u32[]{:S(2)}, u32[]{:S(2)}) %collective-permute-start.5) | collective-permute-done | bytes 24608 | tf_op jit(solution)/shard_map/ppermute | solution.py:242
  44.6 2.2 %collective-permute-start.9 = (f32[24,256]{1,0:T(8,128)S(1)}, f32[24,256]{1,0:T(8,128)S(1)}, u32[]{:S(2)}, u32[]{:S(2)}) collective-permute-start(f32[24,256]{1,0:T(8,128)S(1)} %fusion.3), channel_id=1, source_target_pairs={{0,32},{16,48},{32,64},{48,80},{64,96},{80,112},{96,0},{112,16},{1... | collective-permute-start | bytes 73736 | tf_op jit(solution)/shard_map/ppermute | solution.py:256
  46.8 3.5 %collective-permute-start.8 = (f32[24,256]{1,0:T(8,128)S(1)}, f32[24,256]{1,0:T(8,128)S(1)}, u32[]{:S(2)}, u32[]{:S(2)}) collective-permute-start(f32[24,256]{1,0:T(8,128)S(1)} %fusion.3), channel_id=1, source_target_pairs={{0,64},{16,80},{32,96},{48,112},{64,0},{80,16},{96,32},{112,48},{1... | collective-permute-start | bytes 73736 | tf_op jit(solution)/shard_map/ppermute | solution.py:256
  51.6 11.3 %collective-permute-done.9 = f32[24,256]{1,0:T(8,128)S(1)} collective-permute-done((f32[24,256]{1,0:T(8,128)S(1)}, f32[24,256]{1,0:T(8,128)S(1)}, u32[]{:S(2)}, u32[]{:S(2)}) %collective-permute-start.9) | collective-permute-done | bytes 24608 | tf_op jit(solution)/shard_map/ppermute | solution.py:256
  63.4 5.3 %all-to-all-start.1 = ((f32[8,256,512]{2,1,0:T(8,128)}), f32[8,256,512]{2,1,0:T(8,128)}, u32[]{:S(2)}, u32[]{:S(2)}) async-start(f32[8,256,512]{2,1,0:T(8,128)} %get-tuple-element.22), calls=%async_computation.1 | async-start | bytes 8388608 | tf_op jit(solution)/shard_map/all_to_all | solution.py:469
  68.7 2.6 %collective-permute-start.12 = (f32[24,256]{1,0:T(8,128)S(1)}, f32[24,256]{1,0:T(8,128)S(1)}, u32[]{:S(2)}, u32[]{:S(2)}) collective-permute-start(f32[24,256]{1,0:T(8,128)S(1)} %select_add_fusion), channel_id=1, source_target_pairs={{0,12},{1,13},{2,14},{3,15},{4,0},{5,1},{6,2},{7,3},{8,4},{9,5},{1... | collective-permute-start | bytes 73736 | tf_op jit(solution)/shard_map/ppermute | solution.py:256
  73.0 3.0 %collective-permute-done.11 = f32[24,256]{1,0:T(8,128)S(1)} collective-permute-done((f32[24,256]{1,0:T(8,128)S(1)}, f32[24,256]{1,0:T(8,128)S(1)}, u32[]{:S(2)}, u32[]{:S(2)}) %collective-permute-start.11) | collective-permute-done | bytes 24608 | tf_op jit(solution)/shard_map/ppermute | solution.py:256
  76.5 3.0 %collective-permute-start.15 = (f32[96,256]{1,0:T(8,128)S(1)}, f32[96,256]{1,0:T(8,128)S(1)}, u32[]{:S(2)}, u32[]{:S(2)}) collective-permute-start(f32[96,256]{1,0:T(8,128)S(1)} %pad_maximum_fusion.2), channel_id=1, source_target_pairs={{0,3},{1,0},{2,1},{3,2},{4,7},{5,4},{6,5},{7,6},{8,11},{9,8},{10,9... | collective-permute-start | bytes 294920 | tf_op jit(solution)/shard_map/ppermute | solution.py:256
  81.4 3.2 %collective-permute-done.14 = f32[96,256]{1,0:T(8,128)S(1)} collective-permute-done((f32[96,256]{1,0:T(8,128)S(1)}, f32[96,256]{1,0:T(8,128)S(1)}, u32[]{:S(2)}, u32[]{:S(2)}) %collective-permute-start.14) | collective-permute-done | bytes 98336 | tf_op jit(solution)/shard_map/ppermute | solution.py:256
  84.6 1.3 %collective-permute-done.13 = f32[96,256]{1,0:T(8,128)S(1)} collective-permute-done((f32[96,256]{1,0:T(8,128)S(1)}, f32[96,256]{1,0:T(8,128)S(1)}, u32[]{:S(2)}, u32[]{:S(2)}) %collective-permute-start.13) | collective-permute-done | bytes 98336 | tf_op jit(solution)/shard_map/ppermute | solution.py:256
  86.0 2.7 %collective-permute-start.16 = (f32[384,256]{1,0:T(8,128)S(1)}, f32[384,256]{1,0:T(8,128)S(1)}, u32[]{:S(2)}, u32[]{:S(2)}) collective-permute-start(f32[384,256]{1,0:T(8,128)S(1)} %pad_maximum_fusion.1), channel_id=1, source_target_pairs={{0,16},{16,0},{32,48},{48,32},{64,80},{80,64},{96,112},{112,96},{1... | collective-permute-start | bytes 1179656 | tf_op jit(solution)/shard_map/ppermute | solution.py:256
  88.7 1.3 %collective-permute-done.16 = f32[384,256]{1,0:T(8,128)S(1)} collective-permute-done((f32[384,256]{1,0:T(8,128)S(1)}, f32[384,256]{1,0:T(8,128)S(1)}, u32[]{:S(2)}, u32[]{:S(2)}) %collective-permute-start.16) | collective-permute-done | bytes 393248 | tf_op jit(solution)/shard_map/ppermute | solution.py:256
  90.2 23.5 %factor.1 = (f32[512,512]{1,0:T(8,128)}, bf16[512,512]{1,0:T(8,128)(2,1)S(1)}, bf16[512,512]{1,0:T(8,128)(2,1)S(1)}) custom-call(f32[768,256]{1,0:T(8,128)S(1)} %pad_maximum_fusion.gram_ref, f32[512,512]{1,0:T(8,128)S(1)} %copy-done), custom_call_target="tpu_custom_call" | custom-call | flops 1000000 | bytes 65536 | tf_op jit(solution)/shard_map/factor/pallas_call | solution.py:376
  114.8 2.8 %all-to-all-done.1.late_ref = f32[8,256,512]{2,1,0:T(8,128)} async-done(((f32[8,256,512]{2,1,0:T(8,128)}), f32[8,256,512]{2,1,0:T(8,128)}, u32[]{:S(2)}, u32[]{:S(2)}) %all-to-all-start.1) | async-done | bytes 4194336 | tf_op jit(solution)/shard_map/all_to_all | solution.py:469
  117.6 7.1 %finish.1 = f32[8,256,512]{2,1,0:T(8,128)} custom-call(s32[16]{0:T(128)S(1)} %convert_element_type.8.slot_ref, bf16[512,512]{1,0:T(8,128)(2,1)S(1)} %get-tuple-element.20.head_ref, bf16[512,512]{1,0:T(8,128)(2,1)S(1)} %get-tuple-element.21.tail_ref, f32[8,264,512]{2,1,0:T(8,128)} %all-to-all-done.early_ref, f32[8,256,512]{2,1,0:T(8,128)} %all-to-all-done.1.late_ref), custom_call_target="tpu_custom_call" | custom-call | flops 5000000000 | bytes 8388608 | tf_op jit(solution)/shard_map/finish/pallas_call | solution.py:445
  (37 shorter events, 12.5 us)
Async XLA Ops:
  4.8 58.6 %all-to-all-start = ((f32[8,264,512]{2,1,0:T(8,128)}), f32[8,264,512]{2,1,0:T(8,128)}, u32[]{:S(2)}, u32[]{:S(2)}) async-start(f32[8,264,512]{2,1,0:T(8,128)} %pack.1), calls=%async_computation | async-start | bytes 8650752 | tf_op jit(solution)/shard_map/all_to_all | solution.py:469
  24.9 1.8 %collective-permute-start = (f32[384,256]{1,0:T(8,128)S(1)}, f32[384,256]{1,0:T(8,128)S(1)}, u32[]{:S(2)}, u32[]{:S(2)}) collective-permute-start(f32[384,256]{1,0:T(8,128)S(1)} %dynamic-slice_bitcast_fusion), channel_id=1, source_target_pairs={{0,16},{16,0},{32,48},{48,32},{64,80},{80,64},{96,112},{112,96},{1... | collective-permute-start | bytes 1179656 | tf_op jit(solution)/shard_map/ppermute | solution.py:242
  27.8 6.3 %collective-permute-start.1 = (f32[96,256]{1,0:T(8,128)S(1)}, f32[96,256]{1,0:T(8,128)S(1)}, u32[]{:S(2)}, u32[]{:S(2)}) collective-permute-start(f32[96,256]{1,0:T(8,128)S(1)} %get-tuple-element.30), channel_id=1, source_target_pairs={{0,1},{1,2},{2,3},{3,0},{4,5},{5,6},{6,7},{7,4},{8,9},{9,10},{10,1... | collective-permute-start | bytes 294920 | tf_op jit(solution)/shard_map/ppermute | solution.py:242
  28.7 6.3 %collective-permute-start.3 = (f32[96,256]{1,0:T(8,128)S(1)}, f32[96,256]{1,0:T(8,128)S(1)}, u32[]{:S(2)}, u32[]{:S(2)}) collective-permute-start(f32[96,256]{1,0:T(8,128)S(1)} %get-tuple-element.31), channel_id=1, source_target_pairs={{0,3},{1,0},{2,1},{3,2},{4,7},{5,4},{6,5},{7,6},{8,11},{9,8},{10,9... | collective-permute-start | bytes 294920 | tf_op jit(solution)/shard_map/ppermute | solution.py:242
  30.5 7.1 %collective-permute-start.2 = (f32[96,256]{1,0:T(8,128)S(1)}, f32[96,256]{1,0:T(8,128)S(1)}, u32[]{:S(2)}, u32[]{:S(2)}) collective-permute-start(f32[96,256]{1,0:T(8,128)S(1)} %get-tuple-element.32), channel_id=1, source_target_pairs={{0,2},{1,3},{2,0},{3,1},{4,6},{5,7},{6,4},{7,5},{8,10},{9,11},{10,... | collective-permute-start | bytes 294920 | tf_op jit(solution)/shard_map/ppermute | solution.py:242
  37.7 4.5 %collective-permute-start.4 = (f32[24,256]{1,0:T(8,128)S(1)}, f32[24,256]{1,0:T(8,128)S(1)}, u32[]{:S(2)}, u32[]{:S(2)}) collective-permute-start(f32[24,256]{1,0:T(8,128)S(1)} %get-tuple-element.37), channel_id=1, source_target_pairs={{0,4},{1,5},{2,6},{3,7},{4,8},{5,9},{6,10},{7,11},{8,12},{9,13},{1... | collective-permute-start | bytes 73736 | tf_op jit(solution)/shard_map/ppermute | solution.py:242
  40.3 3.1 %collective-permute-start.6 = (f32[24,256]{1,0:T(8,128)S(1)}, f32[24,256]{1,0:T(8,128)S(1)}, u32[]{:S(2)}, u32[]{:S(2)}) collective-permute-start(f32[24,256]{1,0:T(8,128)S(1)} %get-tuple-element.38), channel_id=1, source_target_pairs={{0,12},{1,13},{2,14},{3,15},{4,0},{5,1},{6,2},{7,3},{8,4},{9,5},{1... | collective-permute-start | bytes 73736 | tf_op jit(solution)/shard_map/ppermute | solution.py:242
  40.4 4.2 %collective-permute-start.5 = (f32[24,256]{1,0:T(8,128)S(1)}, f32[24,256]{1,0:T(8,128)S(1)}, u32[]{:S(2)}, u32[]{:S(2)}) collective-permute-start(f32[24,256]{1,0:T(8,128)S(1)} %get-tuple-element.39), channel_id=1, source_target_pairs={{0,8},{1,9},{2,10},{3,11},{4,12},{5,13},{6,14},{7,15},{8,0},{9,1},... | collective-permute-start | bytes 73736 | tf_op jit(solution)/shard_map/ppermute | solution.py:242
  44.6 18.3 %collective-permute-start.9 = (f32[24,256]{1,0:T(8,128)S(1)}, f32[24,256]{1,0:T(8,128)S(1)}, u32[]{:S(2)}, u32[]{:S(2)}) collective-permute-start(f32[24,256]{1,0:T(8,128)S(1)} %fusion.3), channel_id=1, source_target_pairs={{0,32},{16,48},{32,64},{48,80},{64,96},{80,112},{96,0},{112,16},{1... | collective-permute-start | bytes 73736 | tf_op jit(solution)/shard_map/ppermute | solution.py:256
  46.8 16.5 %collective-permute-start.8 = (f32[24,256]{1,0:T(8,128)S(1)}, f32[24,256]{1,0:T(8,128)S(1)}, u32[]{:S(2)}, u32[]{:S(2)}) collective-permute-start(f32[24,256]{1,0:T(8,128)S(1)} %fusion.3), channel_id=1, source_target_pairs={{0,64},{16,80},{32,96},{48,112},{64,0},{80,16},{96,32},{112,48},{1... | collective-permute-start | bytes 73736 | tf_op jit(solution)/shard_map/ppermute | solution.py:256
  50.3 13.1 %collective-permute-start.7 = (f32[24,256]{1,0:T(8,128)S(1)}, f32[24,256]{1,0:T(8,128)S(1)}, u32[]{:S(2)}, u32[]{:S(2)}) collective-permute-start(f32[24,256]{1,0:T(8,128)S(1)} %fusion.3), channel_id=1, source_target_pairs={{0,96},{16,112},{32,0},{48,16},{64,32},{80,48},{96,64},{112,80},{1... | collective-permute-start | bytes 73736 | tf_op jit(solution)/shard_map/ppermute | solution.py:256
  63.4 54.3 %all-to-all-start.1 = ((f32[8,256,512]{2,1,0:T(8,128)}), f32[8,256,512]{2,1,0:T(8,128)}, u32[]{:S(2)}, u32[]{:S(2)}) async-start(f32[8,256,512]{2,1,0:T(8,128)} %get-tuple-element.22), calls=%async_computation.1 | async-start | bytes 8388608 | tf_op jit(solution)/shard_map/all_to_all | solution.py:469
  68.7 21.5 %copy-start = (f32[512,512]{1,0:T(8,128)S(1)}, f32[512,512]{1,0:T(8,128)}, u32[]{:S(2)}) copy-start(f32[512,512]{1,0:T(8,128)} %inverse_ref.3) | copy-start | bytes 3145732
  68.7 4.2 %collective-permute-start.12 = (f32[24,256]{1,0:T(8,128)S(1)}, f32[24,256]{1,0:T(8,128)S(1)}, u32[]{:S(2)}, u32[]{:S(2)}) collective-permute-start(f32[24,256]{1,0:T(8,128)S(1)} %select_add_fusion), channel_id=1, source_target_pairs={{0,12},{1,13},{2,14},{3,15},{4,0},{5,1},{6,2},{7,3},{8,4},{9,5},{1... | collective-permute-start | bytes 73736 | tf_op jit(solution)/shard_map/ppermute | solution.py:256
  71.4 4.6 %collective-permute-start.11 = (f32[24,256]{1,0:T(8,128)S(1)}, f32[24,256]{1,0:T(8,128)S(1)}, u32[]{:S(2)}, u32[]{:S(2)}) collective-permute-start(f32[24,256]{1,0:T(8,128)S(1)} %select_add_fusion), channel_id=1, source_target_pairs={{0,8},{1,9},{2,10},{3,11},{4,12},{5,13},{6,14},{7,15},{8,0},{9,1},... | collective-permute-start | bytes 73736 | tf_op jit(solution)/shard_map/ppermute | solution.py:256
  72.2 4.3 %collective-permute-start.10 = (f32[24,256]{1,0:T(8,128)S(1)}, f32[24,256]{1,0:T(8,128)S(1)}, u32[]{:S(2)}, u32[]{:S(2)}) collective-permute-start(f32[24,256]{1,0:T(8,128)S(1)} %select_add_fusion), channel_id=1, source_target_pairs={{0,4},{1,5},{2,6},{3,7},{4,8},{5,9},{6,10},{7,11},{8,12},{9,13},{1... | collective-permute-start | bytes 73736 | tf_op jit(solution)/shard_map/ppermute | solution.py:256
  76.5 4.9 %collective-permute-start.15 = (f32[96,256]{1,0:T(8,128)S(1)}, f32[96,256]{1,0:T(8,128)S(1)}, u32[]{:S(2)}, u32[]{:S(2)}) collective-permute-start(f32[96,256]{1,0:T(8,128)S(1)} %pad_maximum_fusion.2), channel_id=1, source_target_pairs={{0,3},{1,0},{2,1},{3,2},{4,7},{5,4},{6,5},{7,6},{8,11},{9,8},{10,9... | collective-permute-start | bytes 294920 | tf_op jit(solution)/shard_map/ppermute | solution.py:256
  79.5 5.1 %collective-permute-start.14 = (f32[96,256]{1,0:T(8,128)S(1)}, f32[96,256]{1,0:T(8,128)S(1)}, u32[]{:S(2)}, u32[]{:S(2)}) collective-permute-start(f32[96,256]{1,0:T(8,128)S(1)} %pad_maximum_fusion.2), channel_id=1, source_target_pairs={{0,2},{1,3},{2,0},{3,1},{4,6},{5,7},{6,4},{7,5},{8,10},{9,11},{10,... | collective-permute-start | bytes 294920 | tf_op jit(solution)/shard_map/ppermute | solution.py:256
  79.8 6.0 %collective-permute-start.13 = (f32[96,256]{1,0:T(8,128)S(1)}, f32[96,256]{1,0:T(8,128)S(1)}, u32[]{:S(2)}, u32[]{:S(2)}) collective-permute-start(f32[96,256]{1,0:T(8,128)S(1)} %pad_maximum_fusion.2), channel_id=1, source_target_pairs={{0,1},{1,2},{2,3},{3,0},{4,5},{5,6},{6,7},{7,4},{8,9},{9,10},{10,1... | collective-permute-start | bytes 294920 | tf_op jit(solution)/shard_map/ppermute | solution.py:256
  86.0 4.1 %collective-permute-start.16 = (f32[384,256]{1,0:T(8,128)S(1)}, f32[384,256]{1,0:T(8,128)S(1)}, u32[]{:S(2)}, u32[]{:S(2)}) collective-permute-start(f32[384,256]{1,0:T(8,128)S(1)} %pad_maximum_fusion.1), channel_id=1, source_target_pairs={{0,16},{16,0},{32,48},{48,32},{64,80},{80,64},{96,112},{112,96},{1... | collective-permute-start | bytes 1179656 | tf_op jit(solution)/shard_map/ppermute | solution.py:256

commit v4 on v3

--- a/solution.py
+++ b/solution.py
@@ -11,8 +11,7 @@
 BLOCK = 128
 PIVOT = 8
 HALF = 256
-EARLY = 128
-HEADER = 8
+PAIR = 2
 GROUP = 4
 
 
@@ -44,78 +43,92 @@
     return dot16(left[0], right[0]) + (dot16(left[0], right[1]) + dot16(left[1], right[0]))
 
 
-def seat_of(i, owner_ref, used):
-    owner = owner_ref[i]
-    rank = used[owner]
-    used[owner] = rank + 1
-    return owner, rank
-
-
-def pack_kernel(
-    count_ref, owner_ref, slot_ref, tiles_ref, early_ref, staged, header, used, slots, sems, out_sems
-):
-    scenes, capacity = used.shape[0], owner_ref.shape[0]
-    for i in range(capacity):
+def seats_of_tiles(count_ref, owner_ref, used, note):
+    me = lax.axis_index("scene")
+    chips = used.shape[0] // 2
+    for pair in range(used.shape[0]):
+        used[pair] = 0
+    for i in range(owner_ref.shape[0]):
 
         @pl.when(i < count_ref[0])
         def _():
-            source = tiles_ref.at[i, pl.ds(0, EARLY)]
-            pltpu.make_async_copy(source, staged.at[i], sems.at[i]).start()
-
+            owner = owner_ref[i]
+            up = lax.rem(owner // 2 - me // 2 + chips, chips)
+            other = lax.rem(owner + me, 2)
+            pair = 2 * up + other
+            rank = used[pair]
+            used[pair] = rank + 1
+            note(i, pair, rank)
+
+
+def pack_kernel(
+    count_ref, owner_ref, slot_ref, tiles_ref, up_ref, down_ref, cross_ref, seat_ref, table_ref,
+    staged, used, sems,
+):
+    capacity = owner_ref.shape[0]
+    targets = {
+        2: up_ref.at[0], 3: up_ref.at[1], 6: down_ref.at[0], 7: down_ref.at[1],
+        1: cross_ref.at[0], 5: cross_ref.at[1],
+    }
     for seat in range(capacity):
-        slots[seat] = -1
-    for owner in range(scenes):
-        used[owner] = 0
-
-    def store(i, owner, rank):
-        target = early_ref.at[owner, pl.ds(pl.multiple_of(rank * EARLY, 8), EARLY)]
-        return pltpu.make_async_copy(staged.at[i], target, sems.at[i])
+        table_ref[seat] = -1
+        seat_ref[seat] = 0
+
+    def note(i, pair, rank):
+        seat_ref[i] = PAIR * pair + rank
+        table_ref[PAIR * pair + rank] = slot_ref[i]
+
+    seats_of_tiles(count_ref, owner_ref, used, note)
+
+    def load(i):
+        return pltpu.make_async_copy(tiles_ref.at[i], staged.at[i], sems.at[i])
+
+    def store(i, target, rank):
+        return pltpu.make_async_copy(staged.at[i], target.at[rank], sems.at[i])
+
+    def sent(i):
+        pair = seat_ref[i] // PAIR
+        return (i < count_ref[0]) & (pair != 0) & (pair != 4)
 
     for i in range(capacity):
 
-        @pl.when(i < count_ref[0])
+        @pl.when(sent(i))
         def _():
-            owner, rank = seat_of(i, owner_ref, used)
-            slots[2 * owner + rank] = slot_ref[i]
-            source = tiles_ref.at[i, pl.ds(0, EARLY)]
-            pltpu.make_async_copy(source, staged.at[i], sems.at[i]).wait()
-            store(i, owner, rank).start()
-
-    lane = lax.broadcasted_iota(jnp.int32, header.shape[1:], 1)
-    half = header.shape[2] // 2
-    headers = []
-    for owner in range(scenes):
-        pair = jnp.where(lane < half, slots[2 * owner], slots[2 * owner + 1])
-        header[owner] = pair.astype(jnp.float32)
-        target = early_ref.at[owner, pl.ds(2 * EARLY, HEADER)]
-        headers.append(pltpu.make_async_copy(header.at[owner], target, out_sems.at[owner]))
-        headers[-1].start()
+            load(i).start()
+
     for i in range(capacity):
 
-        @pl.when(i < count_ref[0])
+        @pl.when(sent(i))
         def _():
-            store(i, 0, 0).wait()
-
-    for copy in headers:
-        copy.wait()
+            load(i).wait()
+            for pair, target in targets.items():
+
+                @pl.when(seat_ref[i] // PAIR == pair)
+                def _():
+                    store(i, target, lax.rem(seat_ref[i], PAIR)).start()
+
+    for i in range(capacity):
+
+        @pl.when(sent(i))
+        def _():
+            store(i, up_ref.at[0], 0).wait()
 
 
 def pack(tiles, tile_count, tile_owner, tile_slot, scenes):
     smem = pl.BlockSpec(memory_space=pltpu.SMEM)
     hbm = pl.BlockSpec(memory_space=pl.ANY)
-    capacity, columns = tile_owner.shape[0], tiles.shape[2]
+    capacity = tile_owner.shape[0]
+    two_pairs = jax.ShapeDtypeStruct((2, PAIR) + tiles.shape[1:], tiles.dtype)
+    table = jax.ShapeDtypeStruct((capacity,), jnp.int32)
     return pl.pallas_call(
         pack_kernel,
-        out_shape=jax.ShapeDtypeStruct((scenes, 2 * EARLY + HEADER, columns), tiles.dtype),
+        out_shape=(two_pairs, two_pairs, two_pairs, table, table),
         in_specs=[smem, smem, smem, hbm],
-        out_specs=hbm,
+        out_specs=(hbm, hbm, hbm, smem, smem),
         scratch_shapes=[
-            pltpu.VMEM((capacity, EARLY, columns), jnp.float32),
-            pltpu.VMEM((scenes, HEADER, columns), jnp.float32),
+            pltpu.VMEM(tiles.shape, jnp.float32),
             pltpu.SMEM((scenes,), jnp.int32),
-            pltpu.SMEM((capacity,), jnp.int32),
             pltpu.SemaphoreType.DMA((capacity,)),
-            pltpu.SemaphoreType.DMA((scenes,)),
         ],
         compiler_params=pltpu.CompilerParams(vmem_limit_bytes=56 << 20),
         cost_estimate=pl.CostEstimate(flops=0, bytes_accessed=8 << 20, transcendentals=0),
@@ -124,14 +137,13 @@
 
 
 def gram_kernel(
-    count_ref, owner_ref, tile_ref, inverse_ref, gram_ref, late_ref, inv_head, inv_tail, cross, used, sems
+    count_ref, seat_ref, tile_ref, inverse_ref, gram_ref, own_ref, far_ref, inv_head, inv_tail, cross, sems
 ):
     step = pl.program_id(0)
-    late = late_ref.shape[1] // 2
-
-    def late_copy(i, owner, rank):
-        target = late_ref.at[owner, pl.ds(pl.multiple_of(rank * late, 8), late)]
-        return pltpu.make_async_copy(tile_ref.at[i, pl.ds(EARLY, late)], target, sems.at[i])
+    tiles = tile_ref.shape[0]
+
+    def kept(i, target, rank):
+        return pltpu.make_async_copy(tile_ref.at[i], target.at[rank], sems.at[i])
 
     @pl.when(step == 0)
     def _():
@@ -140,16 +152,14 @@
         inv_tail[...] = tail
         gram_ref[...] = jnp.zeros_like(gram_ref)
         cross[...] = jnp.zeros_like(cross)
-        for owner in range(used.shape[0]):
-            used[owner] = 0
-
-    tiles = tile_ref.shape[0]
+
     for i in range(tiles):
-
-        @pl.when(tiles * step + i < count_ref[0])
-        def _():
-            owner, rank = seat_of(tiles * step + i, owner_ref, used)
-            late_copy(i, owner, rank).start()
+        for pair, target in ((0, own_ref), (4, far_ref.at[0])):
+            seat = seat_ref[tiles * step + i]
+
+            @pl.when((tiles * step + i < count_ref[0]) & (seat // PAIR == pair))
+            def _():
+                kept(i, target, lax.rem(seat, PAIR)).start()
 
     @pl.when(tiles * step < count_ref[0])
     def _():
@@ -174,10 +184,11 @@
         cross[HALF:, :] += dot16(right_head, right_tail, 0, 0)
 
     for i in range(tiles):
-
-        @pl.when(tiles * step + i < count_ref[0])
+        pair = seat_ref[tiles * step + i] // PAIR
+
+        @pl.when((tiles * step + i < count_ref[0]) & ((pair == 0) | (pair == 4)))
         def _():
-            late_copy(i, 0, 0).wait()
+            kept(i, own_ref, 0).wait()
 
     @pl.when(step == pl.num_programs(0) - 1)
     def _():
@@ -185,13 +196,16 @@
         gram_ref[2 * HALF :, :] += cross[HALF:, :] + cross[HALF:, :].T
 
 
-def gram(tiles, inverse_factor, tile_count, tile_owner, scenes):
+def gram(tiles, inverse_factor, tile_count, seats):
     capacity, rows, columns = tiles.shape
+    pair = jax.ShapeDtypeStruct((PAIR, rows, columns), jnp.float32)
+    hbm = pl.BlockSpec(memory_space=pl.ANY)
     return pl.pallas_call(
         gram_kernel,
         out_shape=(
             jax.ShapeDtypeStruct((3 * HALF, HALF), jnp.float32),
-            jax.ShapeDtypeStruct((scenes, 2 * (rows - EARLY), columns), jnp.float32),
+            pair,
+            jax.ShapeDtypeStruct((2, PAIR, rows, columns), jnp.float32),
         ),
         grid_spec=pltpu.PrefetchScalarGridSpec(
             num_scalar_prefetch=2,
@@ -207,13 +221,13 @@
             ],
             out_specs=(
                 pl.BlockSpec((3 * HALF, HALF), lambda i, *_: (0, 0)),
-                pl.BlockSpec(memory_space=pl.ANY),
+                hbm,
+                hbm,
             ),
             scratch_shapes=[
                 pltpu.VMEM((columns, columns), jnp.bfloat16),
                 pltpu.VMEM((columns, columns), jnp.bfloat16),
                 pltpu.VMEM((2 * HALF, HALF), jnp.float32),
-                pltpu.SMEM((scenes,), jnp.int32),
                 pltpu.SemaphoreType.DMA((GROUP,)),
             ],
         ),
@@ -224,7 +238,7 @@
             flops=1_000_000, bytes_accessed=1 << 16, transcendentals=0
         ),
         name="gram",
-    )(tile_count, tile_owner, tiles, inverse_factor)
+    )(tile_count, seats, tiles, inverse_factor)
 
 
 def ring_pairs(size, span, stride, shift):
@@ -276,13 +290,11 @@
     return [("scene", 2, 1), ("rows", side, 1), ("rows", rows // side, side)]
 
 
-def sum_along_z(value, scenes, rest):
-    parts = from_ahead(value, "scene", scenes // 2, 2)
-    rest, *parts = lax.optimization_barrier((rest, *parts))
-    total, *more = in_order(parts, "scene", 2)
-    for part in more:
-        total = total + part
-    return total, rest
+def sum_in_order(ahead_values, axis, stride):
+    total, *more = in_order(ahead_values, axis, stride)
+    for value in more:
+        total = total + value
+    return total
 
 
 def sweep(block):
@@ -391,97 +403,118 @@
     )(gram_sum, inverse_factor)
 
 
-def finish_kernel(
-    slot_ref, head_ref, tail_ref, early_ref, late_ref, out_ref, tiles, results, in_sems, out_sems
-):
-    late = late_ref.shape[1] // 2
-
-    def fetch(owner, rank, slot):
-        return (
-            pltpu.make_async_copy(
-                early_ref.at[owner, pl.ds(rank * EARLY, EARLY)],
-                tiles.at[slot, pl.ds(0, EARLY)],
-                in_sems.at[slot, 0],
-            ),
-            pltpu.make_async_copy(
-                late_ref.at[owner, pl.ds(rank * late, late)],
-                tiles.at[slot, pl.ds(EARLY, late)],
-                in_sems.at[slot, 1],
-            ),
-        )
-
-    for seat in range(slot_ref.shape[0]):
-        slot = slot_ref[seat]
-
-        @pl.when(slot >= 0)
-        def _():
-            for copy in fetch(seat // 2, seat % 2, slot):
-                copy.start()
-
-    def result_copy(j):
-        return pltpu.make_async_copy(results.at[j], out_ref.at[j], out_sems.at[j])
-
-    @pl.loop(0, OWN_TILES)
+def finish_kernel(pairs, slot_ref, head_ref, tail_ref, *refs):
+    out_ref, tiles, results, slots, in_sems, out_sems = refs[-6:]
+    count = jnp.int32(0)
+    for p, place in enumerate(pairs):
+        source = refs[p].at[place] if place is not None else refs[p]
+        for rank in range(PAIR):
+            slot = slot_ref[PAIR * p + rank]
+
+            @pl.when(slot >= 0)
+            def _(source=source, rank=rank, slot=slot, count=count):
+                slots[count] = slot
+                pltpu.make_async_copy(source.at[rank], tiles.at[count], in_sems.at[count]).start()
+
+            count = count + jnp.where(slot >= 0, 1, 0)
+
+    def result_copy(j, slot):
+        return pltpu.make_async_copy(results.at[j], out_ref.at[slot], out_sems.at[j])
+
+    @pl.loop(0, count)
     def _(j):
-        for copy in fetch(0, 0, j):
-            copy.wait()
+        pltpu.make_async_copy(out_ref.at[0], tiles.at[j], in_sems.at[j]).wait()
         head, tail = split(tiles[j])
         results[j, :, :HALF] = dot_split(
             (head[:, :HALF], tail[:, :HALF]), (head_ref[:HALF, :HALF], tail_ref[:HALF, :HALF])
         )
         results[j, :, HALF:] = dot_split((head, tail), (head_ref[:, HALF:], tail_ref[:, HALF:]))
-        result_copy(j).start()
-
-    @pl.loop(0, OWN_TILES)
+        result_copy(j, slots[j]).start()
+
+    @pl.loop(0, count)
     def _(j):
-        result_copy(j).wait()
-
-
-def finish(slots, early, late, head, tail):
-    columns = early.shape[2]
-    rows = EARLY + late.shape[1] // 2
+        result_copy(j, 0).wait()
+
+
+def finish(slots, head, tail, received, pairs, before, name):
+    rows, columns = received[0].shape[-2:]
+    most = min(PAIR * len(pairs), OWN_TILES)
     hbm = pl.BlockSpec(memory_space=pl.ANY)
     vmem = pl.BlockSpec(memory_space=pltpu.VMEM)
+    operands = [slots, head, tail, *received] + ([] if before is None else [before])
     return pl.pallas_call(
-        finish_kernel,
+        functools.partial(finish_kernel, pairs),
         out_shape=jax.ShapeDtypeStruct((OWN_TILES, rows, columns), jnp.float32),
-        in_specs=[pl.BlockSpec(memory_space=pltpu.SMEM), vmem, vmem, hbm, hbm],
+        in_specs=[pl.BlockSpec(memory_space=pltpu.SMEM), vmem, vmem] + [hbm] * (len(operands) - 3),
         out_specs=hbm,
+        input_output_aliases={} if before is None else {len(operands) - 1: 0},
         scratch_shapes=[
-            pltpu.VMEM((OWN_TILES, rows, columns), jnp.float32),
-            pltpu.VMEM((OWN_TILES, rows, columns), jnp.float32),
-            pltpu.SemaphoreType.DMA((OWN_TILES, 2)),
-            pltpu.SemaphoreType.DMA((OWN_TILES,)),
+            pltpu.VMEM((most, rows, columns), jnp.float32),
+            pltpu.VMEM((most, rows, columns), jnp.float32),
+            pltpu.SMEM((most,), jnp.int32),
+            pltpu.SemaphoreType.DMA((most,)),
+            pltpu.SemaphoreType.DMA((most,)),
         ],
         compiler_params=pltpu.CompilerParams(vmem_limit_bytes=32 << 20),
         cost_estimate=pl.CostEstimate(
-            flops=5_000_000_000, bytes_accessed=8 << 20, transcendentals=0
-        ),
-        name="finish",
-    )(slots, head, tail, early, late)
+            flops=1_000_000, bytes_accessed=1 << 16, transcendentals=0
+        ),
+        name=name,
+    )(*operands)
 
 
 def shards(observations, inverse_factor, tile_count, tile_owner, tile_slot):
     scenes, rows = lax.axis_size("scene"), lax.axis_size("rows")
     tile_rows, columns = observations.shape[1:]
-
-    def exchange(packed):
-        return lax.all_to_all(packed, "scene", 0, 0, tiled=True)
-
-    packed = pack(observations, tile_count, tile_owner, tile_slot, scenes)
-    early = exchange(packed)
-    tiles, _ = lax.optimization_barrier((observations, packed))
-    value, rest = gram(tiles, inverse_factor, tile_count, tile_owner, scenes)
+    chips = scenes // 2
+
+    def along_z(value, up):
+        return lax.ppermute(value, "scene", ring_pairs(scenes, chips, 2, up))
+
+    def other_core(value):
+        return lax.ppermute(value, "scene", ring_pairs(scenes, 2, 1, 1))
+
+    up, down, cross, seats, table = pack(observations, tile_count, tile_owner, tile_slot, scenes)
+    from_below, from_above = along_z(up, 1), along_z(down, chips - 1)
+    crossed = other_core(cross)
+    tiles, _ = lax.optimization_barrier((observations, seats))
+    value, own, far = gram(tiles, inverse_factor, tile_count, seats)
+    value, crossed = lax.optimization_barrier((value, crossed))
+    mine = jnp.zeros((8, 128), jnp.float32).at[0, : table.shape[0]].set(table.astype(jnp.float32))
+    tables = jnp.concatenate([mine, other_core(mine)], 1)
     stages = reduction_stages(scenes, rows)
     for axis, span, stride in stages:
         value = scatter_sum(value, axis, span, stride)
-    value, rest = sum_along_z(value, scenes, rest)
-    late = exchange(rest)
+    height = value.shape[0]
+    parts = from_ahead(jnp.concatenate([value, tables], 0), "scene", chips, 2)
+    far = lax.dynamic_update_slice_in_dim(far, crossed[1:], 1, 0)
+    *parts, far, from_below, from_above = lax.optimization_barrier(
+        (*parts, far, from_below, from_above)
+    )
+    far_in = along_z(far, 2)
+    value = sum_in_order([part[:height] for part in parts], "scene", 2)
     for axis, span, stride in reversed(stages):
         value = gather(value, axis, span, stride)
+    passed_on = other_core(jnp.concatenate([from_below[1:], from_above[1:]], 0))
     upper, head, tail = factor(value, inverse_factor, scenes * rows * OWN_TILES * tile_rows)
-    slots = early[:, 2 * EARLY, :: columns // 2].astype(jnp.int32).reshape(-1)
-    return finish(slots, early, late, head, tail), upper
+
+    def slots_of(ahead, other):
+        start = 128 * other + 2 * PAIR * ((chips - ahead) % chips) + PAIR * other
+        return parts[ahead][height, start : start + PAIR]
+
+    near = [(0, 0), (0, 1), (3, 0), (1, 0), (3, 1), (1, 1)]
+    near_slots = jnp.concatenate([slots_of(*source) for source in near]).astype(jnp.int32)
+    far_slots = jnp.concatenate([slots_of(2, 0), slots_of(2, 1)]).astype(jnp.int32)
+    out = finish(
+        near_slots,
+        head,
+        tail,
+        [own, crossed, from_below, from_above, passed_on, passed_on],
+        (None, 0, 0, 0, 0, 1),
+        None,
+        "finish_near",
+    )
+    return finish(far_slots, head, tail, [far_in, far_in], (0, 1), out, "finish_far"), upper
 
 
 def solution(mesh):

time: 126 us -> 126 us (level)
  waiting for transfers between devices: 32.6 us -> 25.3 us
  local copies, waits for them, and re-layouts: 2.15 us -> 9 us
  Pallas kernels: 45.9 us -> 40.3 us
  other arithmetic: 1.35 us -> 5.87 us
    all_to_all x2 -> x0, starting transfers between devices: 12.6 us -> none  [exchange(): return lax.all_to_all(packed, 'scene', 0, 0, tiled=True)]
    ppermute x0 -> x6, starting transfers between devices: none -> 12.3 us  [the longest x3 6.27 us: other_core(): return lax.ppermute(value, 'scene', ring_pairs(scenes, 2, 1, 1))]
    ppermute x10, waiting for transfers between devices: 22.1 us -> 11.5 us  [from_ahead(): lax.ppermute(value, axis, ring_pairs(size, span, stride, span - ahead))]
    ppermute x0 -> x6, waiting for transfers between devices: none -> 6.36 us  [the longest x3 6.35 us: along_z(): return lax.ppermute(value, 'scene', ring_pairs(scenes, chips, 2, up))]
    pallas_call x1, Pallas kernels: 11.8 us -> 6.87 us  [gram(): pl.pallas_call(gram_kernel, out_shape=(jax.ShapeDtypeStruct((3 * HALF, HA...]
    ppermute x7, starting transfers between devices: 10.9 us -> 15.8 us  [scatter_sum(): lax.ppermute(sent, axis, ring_pairs(size, span, stride, shift))]
    ppermute x10, starting transfers between devices: 17.8 us -> 13.9 us  [from_ahead(): lax.ppermute(value, axis, ring_pairs(size, span, stride, span - ahead))]
    all_to_all x2 -> x0, waiting for transfers between devices: 2.84 us -> none  [exchange(): return lax.all_to_all(packed, 'scene', 0, 0, tiled=True)]
  transfers between devices with their start and end apart: 19 -> 23, of which waited for: 14 -> 13; matrix products, arithmetic and copies ran while one was open for 3% -> 9% of each run, Pallas kernels for 28% -> 29%
where the time goes in v4:
time: 126 us; the launch traced here: 124 us
  starting transfers between devices  42.1 us (33%)
  Pallas kernels  40.3 us (32%)
  waiting for transfers between devices  25.3 us (20%)
  local copies, waits for them, and re-layouts  9 us (7%)
  other arithmetic  5.87 us (5%)
  between operations  1.66 us (1%)
    pallas_call x1, Pallas kernels, factor(): pl.pallas_call(functools.partial(factor_kernel, row_count), out_shape=(ja...  23.5 us
    ppermute x7, starting transfers between devices, scatter_sum(): lax.ppermute(sent, axis, ring_pairs(size, span, stride, shift))  15.8 us
    ppermute x10, starting transfers between devices, from_ahead(): lax.ppermute(value, axis, ring_pairs(size, span, stride, span - ahead))  13.9 us
    ppermute x10, waiting for transfers between devices, from_ahead(): lax.ppermute(value, axis, ring_pairs(size, span, stride, span - ahead))  11.5 us
    ppermute x7, waiting for transfers between devices, scatter_sum(): lax.ppermute(sent, axis, ring_pairs(size, span, stride, shift))  7.47 us
    pallas_call x1, Pallas kernels, gram(): pl.pallas_call(gram_kernel, out_shape=(jax.ShapeDtypeStruct((3 * HALF, HA...  6.87 us
    ppermute x3, waiting for transfers between devices, along_z(): return lax.ppermute(value, 'scene', ring_pairs(scenes, chips, 2, up))  6.35 us
    ppermute x3, starting transfers between devices, other_core(): return lax.ppermute(value, 'scene', ring_pairs(scenes, 2, 1, 1))  6.27 us
  transfers between devices with their start and end apart: 23, of which 13 were waited for; matrix products, arithmetic and copies ran while one was open for 9% of the time, Pallas kernels for 29%

profile of v4, /device:TPU:1, one launch (start us, length us, event | category | flops | bytes accessed | tf_op | source)
XLA Modules:
  0.0 124.3 jit_solution(14948486960654274381)
XLA Ops:
  1.3 3.7 %pack.1 = (f32[2,2,256,512]{3,2,1,0:T(8,128)}, f32[2,2,256,512]{3,2,1,0:T(8,128)}, f32[2,2,256,512]{3,2,1,0:T(8,128)}, s32[16]{0:T(128)}, s32[16]{0:T(128)}) custom-call(s32[1]{0:T(128)S(6)} %copy.10.count_ref, s32[16]{0:T(128)} %owner_ref.1, s32[16]{0:T(128)} %slot_ref.1, f32[16,256,512]{2,1,0:T(8,128)} %tile_ref), custom_call_target="tpu_custom_call" | custom-call | bytes 8388608 | tf_op jit(solution)/shard_map/pack/pallas_call | solution.py:123
  5.0 3.2 %collective-permute-start = (f32[2,2,256,512]{3,2,1,0:T(8,128)}, f32[2,2,256,512]{3,2,1,0:T(8,128)S(1)}, u32[]{:S(2)}, u32[]{:S(2)}) collective-permute-start(f32[2,2,256,512]{3,2,1,0:T(8,128)} %get-tuple-element.38), channel_id=1, source_target_pairs={{0,16},{16,0},{32,48},{48,32},{64,80},{80,64},{96,112},{112,96},{1... | collective-permute-start | bytes 6291464 | tf_op jit(solution)/shard_map/ppermute | solution.py:475
  8.2 2.1 %collective-permute-start.12 = (f32[2,2,256,512]{3,2,1,0:T(8,128)}, f32[2,2,256,512]{3,2,1,0:T(8,128)}, u32[]{:S(2)}, u32[]{:S(2)}) collective-permute-start(f32[2,2,256,512]{3,2,1,0:T(8,128)} %get-tuple-element.43), channel_id=1, source_target_pairs={{0,32},{16,48},{32,64},{48,80},{64,96},{80,112},{96,0},{112,16},{1... | collective-permute-start | bytes 6291464 | tf_op jit(solution)/shard_map/ppermute | solution.py:472
  10.3 2.5 %collective-permute-start.13 = (f32[2,2,256,512]{3,2,1,0:T(8,128)}, f32[2,2,256,512]{3,2,1,0:T(8,128)}, u32[]{:S(2)}, u32[]{:S(2)}) collective-permute-start(f32[2,2,256,512]{3,2,1,0:T(8,128)} %get-tuple-element.44), channel_id=1, source_target_pairs={{0,96},{16,112},{32,0},{48,16},{64,32},{80,48},{96,64},{112,80},{1... | collective-permute-start | bytes 6291464 | tf_op jit(solution)/shard_map/ppermute | solution.py:472
  12.8 6.9 %gram.1 = (f32[768,256]{1,0:T(8,128)}, f32[2,256,512]{2,1,0:T(8,128)}, f32[2,2,256,512]{3,2,1,0:T(8,128)}) custom-call(s32[1]{0:T(128)S(6)} %copy.10.count_ref, s32[16]{0:T(128)} %get-tuple-element.35.seat_ref, f32[16,256,512]{2,1,0:T(8,128)} %tile_ref, f32[512,512]{1,0:T(8,128)} %inverse_ref.3), custom_call_target="tpu_custom_call" | custom-call | flops 1000000 | bytes 65536 | tf_op jit(solution)/shard_map/gram/pallas_call | solution.py:203
  21.1 5.8 %collective-permute-start.1 = (f32[384,256]{1,0:T(8,128)S(1)}, f32[384,256]{1,0:T(8,128)S(1)}, u32[]{:S(2)}, u32[]{:S(2)}) collective-permute-start(f32[384,256]{1,0:T(8,128)S(1)} %dynamic-slice_bitcast_fusion), channel_id=1, source_target_pairs={{0,16},{16,0},{32,48},{48,32},{64,80},{80,64},{96,112},{112,96},{1... | collective-permute-start | bytes 1179656 | tf_op jit(solution)/shard_map/ppermute | solution.py:256
  29.3 1.6 %collective-permute-start.2 = (f32[96,256]{1,0:T(8,128)S(1)}, f32[96,256]{1,0:T(8,128)S(1)}, u32[]{:S(2)}, u32[]{:S(2)}) collective-permute-start(f32[96,256]{1,0:T(8,128)S(1)} %get-tuple-element.62), channel_id=1, source_target_pairs={{0,1},{1,2},{2,3},{3,0},{4,5},{5,6},{6,7},{7,4},{8,9},{9,10},{10,1... | collective-permute-start | bytes 294920 | tf_op jit(solution)/shard_map/ppermute | solution.py:256
  30.8 2.8 %collective-permute-start.4 = (f32[96,256]{1,0:T(8,128)S(1)}, f32[96,256]{1,0:T(8,128)S(1)}, u32[]{:S(2)}, u32[]{:S(2)}) collective-permute-start(f32[96,256]{1,0:T(8,128)S(1)} %get-tuple-element.63), channel_id=1, source_target_pairs={{0,3},{1,0},{2,1},{3,2},{4,7},{5,4},{6,5},{7,6},{8,11},{9,8},{10,9... | collective-permute-start | bytes 294920 | tf_op jit(solution)/shard_map/ppermute | solution.py:256
  34.7 1.8 %collective-permute-done.2 = f32[96,256]{1,0:T(8,128)S(1)} collective-permute-done((f32[96,256]{1,0:T(8,128)S(1)}, f32[96,256]{1,0:T(8,128)S(1)}, u32[]{:S(2)}, u32[]{:S(2)}) %collective-permute-start.2) | collective-permute-done | bytes 98336 | tf_op jit(solution)/shard_map/ppermute | solution.py:256
  36.5 2.8 %collective-permute-done.3 = f32[96,256]{1,0:T(8,128)S(1)} collective-permute-done((f32[96,256]{1,0:T(8,128)S(1)}, f32[96,256]{1,0:T(8,128)S(1)}, u32[]{:S(2)}, u32[]{:S(2)}) %collective-permute-start.3) | collective-permute-done | bytes 98336 | tf_op jit(solution)/shard_map/ppermute | solution.py:256
  39.4 3.4 %collective-permute-start.7 = (f32[24,256]{1,0:T(8,128)S(1)}, f32[24,256]{1,0:T(8,128)S(1)}, u32[]{:S(2)}, u32[]{:S(2)}) collective-permute-start(f32[24,256]{1,0:T(8,128)S(1)} %get-tuple-element.70), channel_id=1, source_target_pairs={{0,12},{1,13},{2,14},{3,15},{4,0},{5,1},{6,2},{7,3},{8,4},{9,5},{1... | collective-permute-start | bytes 73736 | tf_op jit(solution)/shard_map/ppermute | solution.py:256
  44.3 1.5 %collective-permute-start.8 = (f32[8,128]{1,0:T(8,128)S(1)}, f32[8,128]{1,0:T(8,128)S(1)}, u32[]{:S(2)}, u32[]{:S(2)}) collective-permute-start(f32[8,128]{1,0:T(8,128)S(1)} %scatter.4), channel_id=1, source_target_pairs={{0,16},{16,0},{32,48},{48,32},{64,80},{80,64},{96,112},{112,96},{1... | collective-permute-start | bytes 12296 | tf_op jit(solution)/shard_map/ppermute | solution.py:475
  47.2 3.6 %collective-permute-start.10 = (f32[32,256]{1,0:T(8,128)S(1)}, f32[32,256]{1,0:T(8,128)S(1)}, u32[]{:S(2)}, u32[]{:S(2)}) collective-permute-start(f32[32,256]{1,0:T(8,128)S(1)} %maximum_maximum_fusion), channel_id=1, source_target_pairs={{0,64},{16,80},{32,96},{48,112},{64,0},{80,16},{96,32},{112,48},{1... | collective-permute-start | bytes 98312 | tf_op jit(solution)/shard_map/ppermute | solution.py:270
  52.4 6.3 %collective-permute-done.12.refs_2_ = f32[2,2,256,512]{3,2,1,0:T(8,128)} collective-permute-done((f32[2,2,256,512]{3,2,1,0:T(8,128)}, f32[2,2,256,512]{3,2,1,0:T(8,128)}, u32[]{:S(2)}, u32[]{:S(2)}) %collective-permute-start.12) | collective-permute-done | bytes 2097184 | tf_op jit(solution)/shard_map/ppermute | solution.py:472
  63.2 1.5 %pad_maximum_fusion = f32[2,2,256,512]{3,2,1,0:T(8,128)} fusion(f32[1,2,256,512]{3,2,1,0:T(8,128)S(1)} %slice.75, f32[1,2,256,512]{3,2,1,0:T(8,128)S(1)} %slice.74), kind=kLoop, calls=%fused_computation | loop fusion | flops 524288 | bytes 4194304 | tf_op jit(solution)/shard_map/concatenate | solution.py:498
  64.7 1.6 %collective-permute-start.22 = (f32[2,2,256,512]{3,2,1,0:T(8,128)}, f32[2,2,256,512]{3,2,1,0:T(8,128)S(1)}, u32[]{:S(2)}, u32[]{:S(2)}) collective-permute-start(f32[2,2,256,512]{3,2,1,0:T(8,128)} %pad_maximum_fusion), channel_id=1, source_target_pairs={{0,16},{16,0},{32,48},{48,32},{64,80},{80,64},{96,112},{112,96},{1... | collective-permute-start | bytes 6291464 | tf_op jit(solution)/shard_map/ppermute | solution.py:475
  67.7 2.1 %collective-permute-start.16 = (f32[24,256]{1,0:T(8,128)S(1)}, f32[24,256]{1,0:T(8,128)S(1)}, u32[]{:S(2)}, u32[]{:S(2)}) collective-permute-start(f32[24,256]{1,0:T(8,128)S(1)} %select_add_fusion), channel_id=1, source_target_pairs={{0,12},{1,13},{2,14},{3,15},{4,0},{5,1},{6,2},{7,3},{8,4},{9,5},{1... | collective-permute-start | bytes 73736 | tf_op jit(solution)/shard_map/ppermute | solution.py:270
  70.8 3.6 %collective-permute-done.15 = f32[24,256]{1,0:T(8,128)S(1)} collective-permute-done((f32[24,256]{1,0:T(8,128)S(1)}, f32[24,256]{1,0:T(8,128)S(1)}, u32[]{:S(2)}, u32[]{:S(2)}) %collective-permute-start.15) | collective-permute-done | bytes 24608 | tf_op jit(solution)/shard_map/ppermute | solution.py:270
  74.5 3.8 %collective-permute-start.19 = (f32[96,256]{1,0:T(8,128)S(1)}, f32[96,256]{1,0:T(8,128)S(1)}, u32[]{:S(2)}, u32[]{:S(2)}) collective-permute-start(f32[96,256]{1,0:T(8,128)S(1)} %pad_maximum_fusion.3), channel_id=1, source_target_pairs={{0,3},{1,0},{2,1},{3,2},{4,7},{5,4},{6,5},{7,6},{8,11},{9,8},{10,9... | collective-permute-start | bytes 294920 | tf_op jit(solution)/shard_map/ppermute | solution.py:270
  79.0 1.5 %collective-permute-done.19 = f32[96,256]{1,0:T(8,128)S(1)} collective-permute-done((f32[96,256]{1,0:T(8,128)S(1)}, f32[96,256]{1,0:T(8,128)S(1)}, u32[]{:S(2)}, u32[]{:S(2)}) %collective-permute-start.19) | collective-permute-done | bytes 98336 | tf_op jit(solution)/shard_map/ppermute | solution.py:270
  80.5 3.2 %collective-permute-done.18 = f32[96,256]{1,0:T(8,128)S(1)} collective-permute-done((f32[96,256]{1,0:T(8,128)S(1)}, f32[96,256]{1,0:T(8,128)S(1)}, u32[]{:S(2)}, u32[]{:S(2)}) %collective-permute-start.18) | collective-permute-done | bytes 98336 | tf_op jit(solution)/shard_map/ppermute | solution.py:270
  85.6 2.4 %collective-permute-start.20 = (f32[384,256]{1,0:T(8,128)}, f32[384,256]{1,0:T(8,128)}, u32[]{:S(2)}, u32[]{:S(2)}) collective-permute-start(f32[384,256]{1,0:T(8,128)} %pad_maximum_fusion.2), channel_id=1, source_target_pairs={{0,16},{16,0},{32,48},{48,32},{64,80},{80,64},{96,112},{112,96},{1... | collective-permute-start | bytes 1179656 | tf_op jit(solution)/shard_map/ppermute | solution.py:270
  94.4 23.5 %factor.1 = (f32[512,512]{1,0:T(8,128)}, bf16[512,512]{1,0:T(8,128)(2,1)S(1)}, bf16[512,512]{1,0:T(8,128)(2,1)S(1)}) custom-call(f32[768,256]{1,0:T(8,128)S(1)} %pad_maximum_fusion.1.gram_ref, f32[512,512]{1,0:T(8,128)S(1)} %copy-done.2), custom_call_target="tpu_custom_call" | custom-call | flops 1000000 | bytes 65536 | tf_op jit(solution)/shard_map/factor/pallas_call | solution.py:388
  117.9 5.6 %finish_near.1.refs_2_ = f32[8,256,512]{2,1,0:T(8,128)} custom-call(s32[12]{0:T(128)S(1)} %convert_element_type.11.slot_ref, bf16[512,512]{1,0:T(8,128)(2,1)S(1)} %get-tuple-element.49.head_ref, bf16[512,512]{1,0:T(8,128)(2,1)S(1)} %get-tuple-element.50.tail_ref, f32[2,256,512]{2,1,0:T(8,128)S(1)} %copy-done.3, f32[2,2,256,512]{3,2,1,0:T(8,128)S(1)} %copy-done.1, ...), custom_call_target="tpu_custom_call" | custom-call | flops 1000000 | bytes 65536 | tf_op jit(solution)/shard_map/finish_near/pallas_call | solution.py:445
  (71 shorter events, 25.9 us)
Async XLA Ops:
  5.0 14.7 %collective-permute-start = (f32[2,2,256,512]{3,2,1,0:T(8,128)}, f32[2,2,256,512]{3,2,1,0:T(8,128)S(1)}, u32[]{:S(2)}, u32[]{:S(2)}) collective-permute-start(f32[2,2,256,512]{3,2,1,0:T(8,128)} %get-tuple-element.38), channel_id=1, source_target_pairs={{0,16},{16,0},{32,48},{48,32},{64,80},{80,64},{96,112},{112,96},{1... | collective-permute-start | bytes 6291464 | tf_op jit(solution)/shard_map/ppermute | solution.py:475
  8.2 50.5 %collective-permute-start.12 = (f32[2,2,256,512]{3,2,1,0:T(8,128)}, f32[2,2,256,512]{3,2,1,0:T(8,128)}, u32[]{:S(2)}, u32[]{:S(2)}) collective-permute-start(f32[2,2,256,512]{3,2,1,0:T(8,128)} %get-tuple-element.43), channel_id=1, source_target_pairs={{0,32},{16,48},{32,64},{48,80},{64,96},{80,112},{96,0},{112,16},{1... | collective-permute-start | bytes 6291464 | tf_op jit(solution)/shard_map/ppermute | solution.py:472
  10.3 48.4 %collective-permute-start.13 = (f32[2,2,256,512]{3,2,1,0:T(8,128)}, f32[2,2,256,512]{3,2,1,0:T(8,128)}, u32[]{:S(2)}, u32[]{:S(2)}) collective-permute-start(f32[2,2,256,512]{3,2,1,0:T(8,128)} %get-tuple-element.44), channel_id=1, source_target_pairs={{0,96},{16,112},{32,0},{48,16},{64,32},{80,48},{96,64},{112,80},{1... | collective-permute-start | bytes 6291464 | tf_op jit(solution)/shard_map/ppermute | solution.py:472
  19.7 32.6 %copy-start = (f32[2,2,256,512]{3,2,1,0:T(8,128)}, f32[2,2,256,512]{3,2,1,0:T(8,128)S(1)}, u32[]{:S(2)}) copy-start(f32[2,2,256,512]{3,2,1,0:T(8,128)S(1)} %collective-permute-done.refs_1_) | copy-start | bytes 6291460
  21.1 7.1 %collective-permute-start.1 = (f32[384,256]{1,0:T(8,128)S(1)}, f32[384,256]{1,0:T(8,128)S(1)}, u32[]{:S(2)}, u32[]{:S(2)}) collective-permute-start(f32[384,256]{1,0:T(8,128)S(1)} %dynamic-slice_bitcast_fusion), channel_id=1, source_target_pairs={{0,16},{16,0},{32,48},{48,32},{64,80},{80,64},{96,112},{112,96},{1... | collective-permute-start | bytes 1179656 | tf_op jit(solution)/shard_map/ppermute | solution.py:256
  29.3 7.2 %collective-permute-start.2 = (f32[96,256]{1,0:T(8,128)S(1)}, f32[96,256]{1,0:T(8,128)S(1)}, u32[]{:S(2)}, u32[]{:S(2)}) collective-permute-start(f32[96,256]{1,0:T(8,128)S(1)} %get-tuple-element.62), channel_id=1, source_target_pairs={{0,1},{1,2},{2,3},{3,0},{4,5},{5,6},{6,7},{7,4},{8,9},{9,10},{10,1... | collective-permute-start | bytes 294920 | tf_op jit(solution)/shard_map/ppermute | solution.py:256
  30.8 5.7 %collective-permute-start.4 = (f32[96,256]{1,0:T(8,128)S(1)}, f32[96,256]{1,0:T(8,128)S(1)}, u32[]{:S(2)}, u32[]{:S(2)}) collective-permute-start(f32[96,256]{1,0:T(8,128)S(1)} %get-tuple-element.63), channel_id=1, source_target_pairs={{0,3},{1,0},{2,1},{3,2},{4,7},{5,4},{6,5},{7,6},{8,11},{9,8},{10,9... | collective-permute-start | bytes 294920 | tf_op jit(solution)/shard_map/ppermute | solution.py:256
  33.6 5.7 %collective-permute-start.3 = (f32[96,256]{1,0:T(8,128)S(1)}, f32[96,256]{1,0:T(8,128)S(1)}, u32[]{:S(2)}, u32[]{:S(2)}) collective-permute-start(f32[96,256]{1,0:T(8,128)S(1)} %get-tuple-element.64), channel_id=1, source_target_pairs={{0,2},{1,3},{2,0},{3,1},{4,6},{5,7},{6,4},{7,5},{8,10},{9,11},{10,... | collective-permute-start | bytes 294920 | tf_op jit(solution)/shard_map/ppermute | solution.py:256
  39.3 5.0 %collective-permute-start.5 = (f32[24,256]{1,0:T(8,128)S(1)}, f32[24,256]{1,0:T(8,128)S(1)}, u32[]{:S(2)}, u32[]{:S(2)}) collective-permute-start(f32[24,256]{1,0:T(8,128)S(1)} %get-tuple-element.69), channel_id=1, source_target_pairs={{0,4},{1,5},{2,6},{3,7},{4,8},{5,9},{6,10},{7,11},{8,12},{9,13},{1... | collective-permute-start | bytes 73736 | tf_op jit(solution)/shard_map/ppermute | solution.py:256
  39.4 6.4 %collective-permute-start.7 = (f32[24,256]{1,0:T(8,128)S(1)}, f32[24,256]{1,0:T(8,128)S(1)}, u32[]{:S(2)}, u32[]{:S(2)}) collective-permute-start(f32[24,256]{1,0:T(8,128)S(1)} %get-tuple-element.70), channel_id=1, source_target_pairs={{0,12},{1,13},{2,14},{3,15},{4,0},{5,1},{6,2},{7,3},{8,4},{9,5},{1... | collective-permute-start | bytes 73736 | tf_op jit(solution)/shard_map/ppermute | solution.py:256
  42.8 4.2 %collective-permute-start.6 = (f32[24,256]{1,0:T(8,128)S(1)}, f32[24,256]{1,0:T(8,128)S(1)}, u32[]{:S(2)}, u32[]{:S(2)}) collective-permute-start(f32[24,256]{1,0:T(8,128)S(1)} %get-tuple-element.71), channel_id=1, source_target_pairs={{0,8},{1,9},{2,10},{3,11},{4,12},{5,13},{6,14},{7,15},{8,0},{9,1},... | collective-permute-start | bytes 73736 | tf_op jit(solution)/shard_map/ppermute | solution.py:256
  44.3 2.7 %collective-permute-start.8 = (f32[8,128]{1,0:T(8,128)S(1)}, f32[8,128]{1,0:T(8,128)S(1)}, u32[]{:S(2)}, u32[]{:S(2)}) collective-permute-start(f32[8,128]{1,0:T(8,128)S(1)} %scatter.4), channel_id=1, source_target_pairs={{0,16},{16,0},{32,48},{48,32},{64,80},{80,64},{96,112},{112,96},{1... | collective-permute-start | bytes 12296 | tf_op jit(solution)/shard_map/ppermute | solution.py:475
  47.0 12.4 %collective-permute-start.11 = (f32[32,256]{1,0:T(8,128)S(1)}, f32[32,256]{1,0:T(8,128)S(1)}, u32[]{:S(2)}, u32[]{:S(2)}) collective-permute-start(f32[32,256]{1,0:T(8,128)S(1)} %maximum_maximum_fusion), channel_id=1, source_target_pairs={{0,32},{16,48},{32,64},{48,80},{64,96},{80,112},{96,0},{112,16},{1... | collective-permute-start | bytes 98312 | tf_op jit(solution)/shard_map/ppermute | solution.py:270
  47.2 13.3 %collective-permute-start.10 = (f32[32,256]{1,0:T(8,128)S(1)}, f32[32,256]{1,0:T(8,128)S(1)}, u32[]{:S(2)}, u32[]{:S(2)}) collective-permute-start(f32[32,256]{1,0:T(8,128)S(1)} %maximum_maximum_fusion), channel_id=1, source_target_pairs={{0,64},{16,80},{32,96},{48,112},{64,0},{80,16},{96,32},{112,48},{1... | collective-permute-start | bytes 98312 | tf_op jit(solution)/shard_map/ppermute | solution.py:270
  50.9 9.7 %collective-permute-start.9 = (f32[32,256]{1,0:T(8,128)S(1)}, f32[32,256]{1,0:T(8,128)S(1)}, u32[]{:S(2)}, u32[]{:S(2)}) collective-permute-start(f32[32,256]{1,0:T(8,128)S(1)} %maximum_maximum_fusion), channel_id=1, source_target_pairs={{0,96},{16,112},{32,0},{48,16},{64,32},{80,48},{96,64},{112,80},{1... | collective-permute-start | bytes 98312 | tf_op jit(solution)/shard_map/ppermute | solution.py:270
  64.7 53.2 %collective-permute-start.22 = (f32[2,2,256,512]{3,2,1,0:T(8,128)}, f32[2,2,256,512]{3,2,1,0:T(8,128)S(1)}, u32[]{:S(2)}, u32[]{:S(2)}) collective-permute-start(f32[2,2,256,512]{3,2,1,0:T(8,128)} %pad_maximum_fusion), channel_id=1, source_target_pairs={{0,16},{16,0},{32,48},{48,32},{64,80},{80,64},{96,112},{112,96},{1... | collective-permute-start | bytes 6291464 | tf_op jit(solution)/shard_map/ppermute | solution.py:475
  66.2 57.2 %collective-permute-start.21 = (f32[2,2,256,512]{3,2,1,0:T(8,128)}, f32[2,2,256,512]{3,2,1,0:T(8,128)}, u32[]{:S(2)}, u32[]{:S(2)}) collective-permute-start(f32[2,2,256,512]{3,2,1,0:T(8,128)} %slice_dynamic-update-slice_fusion), channel_id=1, source_target_pairs={{0,64},{16,80},{32,96},{48,112},{64,0},{80,16},{96,32},{112,48},{1... | collective-permute-start | bytes 6291464 | tf_op jit(solution)/shard_map/ppermute | solution.py:472
  67.7 3.1 %collective-permute-start.16 = (f32[24,256]{1,0:T(8,128)S(1)}, f32[24,256]{1,0:T(8,128)S(1)}, u32[]{:S(2)}, u32[]{:S(2)}) collective-permute-start(f32[24,256]{1,0:T(8,128)S(1)} %select_add_fusion), channel_id=1, source_target_pairs={{0,12},{1,13},{2,14},{3,15},{4,0},{5,1},{6,2},{7,3},{8,4},{9,5},{1... | collective-permute-start | bytes 73736 | tf_op jit(solution)/shard_map/ppermute | solution.py:270
  69.9 4.6 %collective-permute-start.15 = (f32[24,256]{1,0:T(8,128)S(1)}, f32[24,256]{1,0:T(8,128)S(1)}, u32[]{:S(2)}, u32[]{:S(2)}) collective-permute-start(f32[24,256]{1,0:T(8,128)S(1)} %select_add_fusion), channel_id=1, source_target_pairs={{0,8},{1,9},{2,10},{3,11},{4,12},{5,13},{6,14},{7,15},{8,0},{9,1},... | collective-permute-start | bytes 73736 | tf_op jit(solution)/shard_map/ppermute | solution.py:270
  69.9 4.6 %collective-permute-start.14 = (f32[24,256]{1,0:T(8,128)S(1)}, f32[24,256]{1,0:T(8,128)S(1)}, u32[]{:S(2)}, u32[]{:S(2)}) collective-permute-start(f32[24,256]{1,0:T(8,128)S(1)} %select_add_fusion), channel_id=1, source_target_pairs={{0,4},{1,5},{2,6},{3,7},{4,8},{5,9},{6,10},{7,11},{8,12},{9,13},{1... | collective-permute-start | bytes 73736 | tf_op jit(solution)/shard_map/ppermute | solution.py:270
  74.5 6.0 %collective-permute-start.19 = (f32[96,256]{1,0:T(8,128)S(1)}, f32[96,256]{1,0:T(8,128)S(1)}, u32[]{:S(2)}, u32[]{:S(2)}) collective-permute-start(f32[96,256]{1,0:T(8,128)S(1)} %pad_maximum_fusion.3), channel_id=1, source_target_pairs={{0,3},{1,0},{2,1},{3,2},{4,7},{5,4},{6,5},{7,6},{8,11},{9,8},{10,9... | collective-permute-start | bytes 294920 | tf_op jit(solution)/shard_map/ppermute | solution.py:270
  78.3 5.4 %collective-permute-start.18 = (f32[96,256]{1,0:T(8,128)S(1)}, f32[96,256]{1,0:T(8,128)S(1)}, u32[]{:S(2)}, u32[]{:S(2)}) collective-permute-start(f32[96,256]{1,0:T(8,128)S(1)} %pad_maximum_fusion.3), channel_id=1, source_target_pairs={{0,2},{1,3},{2,0},{3,1},{4,6},{5,7},{6,4},{7,5},{8,10},{9,11},{10,... | collective-permute-start | bytes 294920 | tf_op jit(solution)/shard_map/ppermute | solution.py:270
  78.9 5.9 %collective-permute-start.17 = (f32[96,256]{1,0:T(8,128)S(1)}, f32[96,256]{1,0:T(8,128)S(1)}, u32[]{:S(2)}, u32[]{:S(2)}) collective-permute-start(f32[96,256]{1,0:T(8,128)S(1)} %pad_maximum_fusion.3), channel_id=1, source_target_pairs={{0,1},{1,2},{2,3},{3,0},{4,5},{5,6},{6,7},{7,4},{8,9},{9,10},{10,1... | collective-permute-start | bytes 294920 | tf_op jit(solution)/shard_map/ppermute | solution.py:270
  85.6 7.6 %collective-permute-start.20 = (f32[384,256]{1,0:T(8,128)}, f32[384,256]{1,0:T(8,128)}, u32[]{:S(2)}, u32[]{:S(2)}) collective-permute-start(f32[384,256]{1,0:T(8,128)} %pad_maximum_fusion.2), channel_id=1, source_target_pairs={{0,16},{16,0},{32,48},{48,32},{64,80},{80,64},{96,112},{112,96},{1... | collective-permute-start | bytes 1179656 | tf_op jit(solution)/shard_map/ppermute | solution.py:270
  (8 other events, 124.2 us)

commit v5 on v4

--- a/solution.py
+++ b/solution.py
@@ -350,8 +350,17 @@
     return jnp.concatenate(upper, 0), jnp.concatenate(strips, 0)
 
 
-def factor_kernel(row_count, gram_ref, inverse_ref, factor_ref, head_ref, tail_ref, work):
+def factor_kernel(row_count, inverse_ref, *refs):
+    *pieces, factor_ref, head_ref, tail_ref, gram_ref, work = refs
     size = work.shape[0]
+    core = lax.rem(lax.axis_index("scene"), 2)
+    ring = len(pieces) // 2
+    x = lax.rem(lax.axis_index("rows"), ring)
+    height = pieces[0].shape[0]
+    for i, piece in enumerate(pieces):
+        half = core if i < ring else 1 - core
+        row = (half * ring + lax.rem(x + i % ring, ring)) * height
+        gram_ref[pl.ds(pl.multiple_of(row, 8), height), :] = piece[...]
     work[:HALF, :HALF] = gram_ref[:HALF, :] / row_count
     work[:HALF, HALF:] = gram_ref[HALF : 2 * HALF, :] / row_count
     work[HALF:, HALF:] = gram_ref[2 * HALF :, :] / row_count
@@ -382,7 +391,7 @@
     head_ref[...], tail_ref[...] = split(dot32(inverse_ref[...], inverse, 1, 1))
 
 
-def factor(gram_sum, inverse_factor, row_count):
+def factor(pieces, inverse_factor, row_count):
     vmem = pl.BlockSpec(memory_space=pltpu.VMEM)
     size = inverse_factor.shape[0]
     return pl.pallas_call(
@@ -392,75 +401,99 @@
             jax.ShapeDtypeStruct((size, size), jnp.bfloat16),
             jax.ShapeDtypeStruct((size, size), jnp.bfloat16),
         ),
-        in_specs=[vmem, vmem],
+        in_specs=[vmem] * (1 + len(pieces)),
         out_specs=(vmem, vmem, vmem),
-        scratch_shapes=[pltpu.VMEM((size, size), jnp.float32)],
+        scratch_shapes=[
+            pltpu.VMEM((3 * HALF, HALF), jnp.float32),
+            pltpu.VMEM((size, size), jnp.float32),
+        ],
         compiler_params=pltpu.CompilerParams(vmem_limit_bytes=24 << 20),
         cost_estimate=pl.CostEstimate(
             flops=1_000_000, bytes_accessed=1 << 16, transcendentals=0
         ),
         name="factor",
-    )(gram_sum, inverse_factor)
-
-
-def finish_kernel(pairs, slot_ref, head_ref, tail_ref, *refs):
-    out_ref, tiles, results, slots, in_sems, out_sems = refs[-6:]
-    count = jnp.int32(0)
-    for p, place in enumerate(pairs):
-        source = refs[p].at[place] if place is not None else refs[p]
+    )(inverse_factor, *pieces)
+
+
+def finish_kernel(places, slot_ref, head_ref, tail_ref, *refs):
+    *received, out_ref, tiles, results, in_sems, out_sems = refs
+    for p, place in enumerate(places):
+        source = received[p] if place is None else received[p].at[place]
         for rank in range(PAIR):
             slot = slot_ref[PAIR * p + rank]
 
             @pl.when(slot >= 0)
-            def _(source=source, rank=rank, slot=slot, count=count):
-                slots[count] = slot
-                pltpu.make_async_copy(source.at[rank], tiles.at[count], in_sems.at[count]).start()
-
-            count = count + jnp.where(slot >= 0, 1, 0)
-
-    def result_copy(j, slot):
-        return pltpu.make_async_copy(results.at[j], out_ref.at[slot], out_sems.at[j])
-
-    @pl.loop(0, count)
-    def _(j):
-        pltpu.make_async_copy(out_ref.at[0], tiles.at[j], in_sems.at[j]).wait()
-        head, tail = split(tiles[j])
-        results[j, :, :HALF] = dot_split(
+            def _():
+                pltpu.make_async_copy(source.at[rank], tiles.at[slot], in_sems.at[slot]).start()
+
+    def result_copy(j):
+        return pltpu.make_async_copy(results.at[j], out_ref.at[j], out_sems.at[j])
+
+    rows, columns = tiles.shape[1:]
+    for j in range(0, OWN_TILES, 2):
+        for i in (j, j + 1):
+            pltpu.make_async_copy(out_ref.at[i], tiles.at[i], in_sems.at[i]).wait()
+        head, tail = split(tiles[j : j + 2].reshape(2 * rows, columns))
+        left = dot_split(
             (head[:, :HALF], tail[:, :HALF]), (head_ref[:HALF, :HALF], tail_ref[:HALF, :HALF])
         )
-        results[j, :, HALF:] = dot_split((head, tail), (head_ref[:, HALF:], tail_ref[:, HALF:]))
-        result_copy(j, slots[j]).start()
-
-    @pl.loop(0, count)
-    def _(j):
-        result_copy(j, 0).wait()
-
-
-def finish(slots, head, tail, received, pairs, before, name):
+        right = dot_split((head, tail), (head_ref[:, HALF:], tail_ref[:, HALF:]))
+        results[j : j + 2, :, :HALF] = left.reshape(2, rows, HALF)
+        results[j : j + 2, :, HALF:] = right.reshape(2, rows, HALF)
+        for i in (j, j + 1):
+            result_copy(i).start()
+
+    for j in range(OWN_TILES):
+        result_copy(j).wait()
+
+
+def finish(slots, head, tail, received, places):
     rows, columns = received[0].shape[-2:]
-    most = min(PAIR * len(pairs), OWN_TILES)
     hbm = pl.BlockSpec(memory_space=pl.ANY)
     vmem = pl.BlockSpec(memory_space=pltpu.VMEM)
-    operands = [slots, head, tail, *received] + ([] if before is None else [before])
     return pl.pallas_call(
-        functools.partial(finish_kernel, pairs),
+        functools.partial(finish_kernel, places),
         out_shape=jax.ShapeDtypeStruct((OWN_TILES, rows, columns), jnp.float32),
-        in_specs=[pl.BlockSpec(memory_space=pltpu.SMEM), vmem, vmem] + [hbm] * (len(operands) - 3),
+        in_specs=[pl.BlockSpec(memory_space=pltpu.SMEM), vmem, vmem] + [hbm] * len(received),
         out_specs=hbm,
-        input_output_aliases={} if before is None else {len(operands) - 1: 0},
         scratch_shapes=[
-            pltpu.VMEM((most, rows, columns), jnp.float32),
-            pltpu.VMEM((most, rows, columns), jnp.float32),
-            pltpu.SMEM((most,), jnp.int32),
-            pltpu.SemaphoreType.DMA((most,)),
-            pltpu.SemaphoreType.DMA((most,)),
+            pltpu.VMEM((OWN_TILES, rows, columns), jnp.float32),
+            pltpu.VMEM((OWN_TILES, rows, columns), jnp.float32),
+            pltpu.SemaphoreType.DMA((OWN_TILES,)),
+            pltpu.SemaphoreType.DMA((OWN_TILES,)),
         ],
-        compiler_params=pltpu.CompilerParams(vmem_limit_bytes=32 << 20),
+        compiler_params=pltpu.CompilerParams(vmem_limit_bytes=48 << 20),
         cost_estimate=pl.CostEstimate(
             flops=1_000_000, bytes_accessed=1 << 16, transcendentals=0
         ),
-        name=name,
-    )(*operands)
+        name="finish",
+    )(slots, head, tail, *received)
+
+
+def second_pairs_kernel(first_ref, second_ref, out_ref, sems):
+    copies = [
+        pltpu.make_async_copy(ref.at[1], out_ref.at[i], sems.at[i])
+        for i, ref in enumerate((first_ref, second_ref))
+    ]
+    for copy in copies:
+        copy.start()
+    for copy in copies:
+        copy.wait()
+
+
+def second_pairs(first, second):
+    hbm = pl.BlockSpec(memory_space=pl.ANY)
+    return pl.pallas_call(
+        second_pairs_kernel,
+        out_shape=jax.ShapeDtypeStruct(first.shape, first.dtype),
+        in_specs=[hbm, hbm],
+        out_specs=pl.BlockSpec(memory_space=pltpu.VMEM),
+        scratch_shapes=[pltpu.SemaphoreType.DMA((2,))],
+        cost_estimate=pl.CostEstimate(
+            flops=1_000_000, bytes_accessed=1 << 16, transcendentals=0
+        ),
+        name="second_pairs",
+    )(first, second)
 
 
 def shards(observations, inverse_factor, tile_count, tile_owner, tile_slot):
@@ -493,28 +526,21 @@
     )
     far_in = along_z(far, 2)
     value = sum_in_order([part[:height] for part in parts], "scene", 2)
-    for axis, span, stride in reversed(stages):
-        value = gather(value, axis, span, stride)
-    passed_on = other_core(jnp.concatenate([from_below[1:], from_above[1:]], 0))
-    upper, head, tail = factor(value, inverse_factor, scenes * rows * OWN_TILES * tile_rows)
+    (x_axis, x_span, x_stride), (y_axis, y_span, y_stride) = stages[1:]
+    value = gather(value, y_axis, y_span, y_stride)
+    pieces = from_ahead(value, x_axis, x_span, x_stride)
+    pieces = pieces + [other_core(piece) for piece in pieces]
+    passed_on = other_core(second_pairs(from_below, from_above))
+    upper, head, tail = factor(pieces, inverse_factor, scenes * rows * OWN_TILES * tile_rows)
 
     def slots_of(ahead, other):
         start = 128 * other + 2 * PAIR * ((chips - ahead) % chips) + PAIR * other
         return parts[ahead][height, start : start + PAIR]
 
-    near = [(0, 0), (0, 1), (3, 0), (1, 0), (3, 1), (1, 1)]
-    near_slots = jnp.concatenate([slots_of(*source) for source in near]).astype(jnp.int32)
-    far_slots = jnp.concatenate([slots_of(2, 0), slots_of(2, 1)]).astype(jnp.int32)
-    out = finish(
-        near_slots,
-        head,
-        tail,
-        [own, crossed, from_below, from_above, passed_on, passed_on],
-        (None, 0, 0, 0, 0, 1),
-        None,
-        "finish_near",
-    )
-    return finish(far_slots, head, tail, [far_in, far_in], (0, 1), out, "finish_far"), upper
+    sources = [(0, 0), (0, 1), (3, 0), (1, 0), (3, 1), (1, 1), (2, 0), (2, 1)]
+    slots = jnp.concatenate([slots_of(*source) for source in sources]).astype(jnp.int32)
+    received = [own, crossed, from_below, from_above, passed_on, passed_on, far_in, far_in]
+    return finish(slots, head, tail, received, (None, 0, 0, 0, 0, 1, 0, 1)), upper
 
 
 def solution(mesh):

time: 126 us -> 124 us (0.984)
  Pallas kernels: 40.3 us -> 49.7 us
  waiting for transfers between devices: 25.3 us -> 19.9 us
  other arithmetic: 5.87 us -> 1.9 us
  local copies, waits for them, and re-layouts: 9 us -> 5.64 us
  starting transfers between devices: 42.1 us -> 44.7 us
    pallas_call x2, Pallas kernels: 6.21 us -> 12 us  [the longest x1 9.14 us: finish(): pl.pallas_call(functools.partial(finish_kernel, places), out_shape=jax.Sh...]
    ppermute x10 -> x9, waiting for transfers between devices: 11.5 us -> 7.66 us  [from_ahead(): lax.ppermute(value, axis, ring_pairs(size, span, stride, span - ahead))]
    slice x2 -> x0, local copies, waits for them, and re-layouts: 2.61 us -> none  [shards(): passed_on = other_core(jnp.concatenate([from_below[1:], from_above[1:]], 0))]
    pallas_call x1, Pallas kernels: 6.87 us -> 9.42 us  [gram(): pl.pallas_call(gram_kernel, out_shape=(jax.ShapeDtypeStruct((3 * HALF, HA...]
    ppermute x7, waiting for transfers between devices: 7.47 us -> 5.74 us  [scatter_sum(): lax.ppermute(sent, axis, ring_pairs(size, span, stride, shift))]
    ppermute x3 -> x7, starting transfers between devices: 6.27 us -> 7.94 us  [other_core(): return lax.ppermute(value, 'scene', ring_pairs(scenes, 2, 1, 1))]
    concatenate x1 -> x0, other arithmetic: 1.49 us -> none  [shards(): passed_on = other_core(jnp.concatenate([from_below[1:], from_above[1:]], 0))]
    ppermute x10 -> x9, starting transfers between devices: 13.9 us -> 14.6 us  [from_ahead(): lax.ppermute(value, axis, ring_pairs(size, span, stride, span - ahead))]
  transfers between devices with their start and end apart: 23 -> 26, of which waited for: 13 -> 14; matrix products, arithmetic and copies ran while one was open for 9% -> 6% of each run, Pallas kernels for 29% -> 28%
where the time goes in v5:
time: 124 us; the launch traced here: 123 us
  Pallas kernels  49.7 us (40%)
  starting transfers between devices  44.7 us (36%)
  waiting for transfers between devices  19.9 us (16%)
  local copies, waits for them, and re-layouts  5.64 us (5%)
  other arithmetic  1.9 us (2%)
  between operations  1.66 us (1%)
    pallas_call x1, Pallas kernels, factor(): pl.pallas_call(functools.partial(factor_kernel, row_count), out_shape=(ja...  24.6 us
    ppermute x7, starting transfers between devices, scatter_sum(): lax.ppermute(sent, axis, ring_pairs(size, span, stride, shift))  15.1 us
    ppermute x9, starting transfers between devices, from_ahead(): lax.ppermute(value, axis, ring_pairs(size, span, stride, span - ahead))  14.6 us
    pallas_call x1, Pallas kernels, gram(): pl.pallas_call(gram_kernel, out_shape=(jax.ShapeDtypeStruct((3 * HALF, HA...  9.42 us
    pallas_call x1, Pallas kernels, finish(): pl.pallas_call(functools.partial(finish_kernel, places), out_shape=jax.Sh...  9.14 us
    ppermute x7, starting transfers between devices, other_core(): return lax.ppermute(value, 'scene', ring_pairs(scenes, 2, 1, 1))  7.94 us
    ppermute x9, waiting for transfers between devices, from_ahead(): lax.ppermute(value, axis, ring_pairs(size, span, stride, span - ahead))  7.66 us
    ppermute x3, starting transfers between devices, along_z(): return lax.ppermute(value, 'scene', ring_pairs(scenes, chips, 2, up))  7.05 us
  transfers between devices with their start and end apart: 26, of which 14 were waited for; matrix products, arithmetic and copies ran while one was open for 6% of the time, Pallas kernels for 28%

profile of v5, /device:TPU:1, one launch (start us, length us, event | category | flops | bytes accessed | tf_op | source)
XLA Modules:
  0.0 123.4 jit_solution(1982209486947817737)
XLA Ops:
  1.3 3.6 %pack.1 = (f32[2,2,256,512]{3,2,1,0:T(8,128)}, f32[2,2,256,512]{3,2,1,0:T(8,128)}, f32[2,2,256,512]{3,2,1,0:T(8,128)}, s32[16]{0:T(128)}, s32[16]{0:T(128)}) custom-call(s32[1]{0:T(128)S(6)} %copy.8.count_ref, s32[16]{0:T(128)} %owner_ref.1, s32[16]{0:T(128)} %slot_ref.1, f32[16,256,512]{2,1,0:T(8,128)} %tile_ref), custom_call_target="tpu_custom_call" | custom-call | bytes 8388608 | tf_op jit(solution)/shard_map/pack/pallas_call | solution.py:123
  4.9 1.7 %collective-permute-start = (f32[2,2,256,512]{3,2,1,0:T(8,128)}, f32[2,2,256,512]{3,2,1,0:T(8,128)S(1)}, u32[]{:S(2)}, u32[]{:S(2)}) collective-permute-start(f32[2,2,256,512]{3,2,1,0:T(8,128)} %get-tuple-element.38), channel_id=1, source_target_pairs={{0,16},{16,0},{32,48},{48,32},{64,80},{80,64},{96,112},{112,96},{1... | collective-permute-start | bytes 6291464 | tf_op jit(solution)/shard_map/ppermute | solution.py:508
  6.5 4.1 %collective-permute-start.12 = (f32[2,2,256,512]{3,2,1,0:T(8,128)}, f32[2,2,256,512]{3,2,1,0:T(8,128)}, u32[]{:S(2)}, u32[]{:S(2)}) collective-permute-start(f32[2,2,256,512]{3,2,1,0:T(8,128)} %get-tuple-element.43), channel_id=1, source_target_pairs={{0,32},{16,48},{32,64},{48,80},{64,96},{80,112},{96,0},{112,16},{1... | collective-permute-start | bytes 6291464 | tf_op jit(solution)/shard_map/ppermute | solution.py:505
  10.6 1.5 %collective-permute-start.13 = (f32[2,2,256,512]{3,2,1,0:T(8,128)}, f32[2,2,256,512]{3,2,1,0:T(8,128)}, u32[]{:S(2)}, u32[]{:S(2)}) collective-permute-start(f32[2,2,256,512]{3,2,1,0:T(8,128)} %get-tuple-element.44), channel_id=1, source_target_pairs={{0,96},{16,112},{32,0},{48,16},{64,32},{80,48},{96,64},{112,80},{1... | collective-permute-start | bytes 6291464 | tf_op jit(solution)/shard_map/ppermute | solution.py:505
  12.1 9.4 %gram.1 = (f32[768,256]{1,0:T(8,128)}, f32[2,256,512]{2,1,0:T(8,128)}, f32[2,2,256,512]{3,2,1,0:T(8,128)}) custom-call(s32[1]{0:T(128)S(6)} %copy.8.count_ref, s32[16]{0:T(128)} %get-tuple-element.35.seat_ref, f32[16,256,512]{2,1,0:T(8,128)} %tile_ref, f32[512,512]{1,0:T(8,128)} %inverse_ref.3), custom_call_target="tpu_custom_call" | custom-call | flops 1000000 | bytes 65536 | tf_op jit(solution)/shard_map/gram/pallas_call | solution.py:203
  22.8 1.6 %collective-permute-done.1 = f32[384,256]{1,0:T(8,128)S(1)} collective-permute-done((f32[384,256]{1,0:T(8,128)S(1)}, f32[384,256]{1,0:T(8,128)S(1)}, u32[]{:S(2)}, u32[]{:S(2)}) %collective-permute-start.1) | collective-permute-done | bytes 393248 | tf_op jit(solution)/shard_map/ppermute | solution.py:256
  25.5 2.3 %collective-permute-start.2 = (f32[96,256]{1,0:T(8,128)S(1)}, f32[96,256]{1,0:T(8,128)S(1)}, u32[]{:S(2)}, u32[]{:S(2)}) collective-permute-start(f32[96,256]{1,0:T(8,128)S(1)} %get-tuple-element.56), channel_id=1, source_target_pairs={{0,1},{1,2},{2,3},{3,0},{4,5},{5,6},{6,7},{7,4},{8,9},{9,10},{10,1... | collective-permute-start | bytes 294920 | tf_op jit(solution)/shard_map/ppermute | solution.py:256
  28.2 2.8 %collective-permute-start.3 = (f32[96,256]{1,0:T(8,128)S(1)}, f32[96,256]{1,0:T(8,128)S(1)}, u32[]{:S(2)}, u32[]{:S(2)}) collective-permute-start(f32[96,256]{1,0:T(8,128)S(1)} %get-tuple-element.58), channel_id=1, source_target_pairs={{0,2},{1,3},{2,0},{3,1},{4,6},{5,7},{6,4},{7,5},{8,10},{9,11},{10,... | collective-permute-start | bytes 294920 | tf_op jit(solution)/shard_map/ppermute | solution.py:256
  31.7 2.6 %collective-permute-done.3 = f32[96,256]{1,0:T(8,128)S(1)} collective-permute-done((f32[96,256]{1,0:T(8,128)S(1)}, f32[96,256]{1,0:T(8,128)S(1)}, u32[]{:S(2)}, u32[]{:S(2)}) %collective-permute-start.3) | collective-permute-done | bytes 98336 | tf_op jit(solution)/shard_map/ppermute | solution.py:256
  34.4 4.9 %collective-permute-start.5 = (f32[24,256]{1,0:T(8,128)S(1)}, f32[24,256]{1,0:T(8,128)S(1)}, u32[]{:S(2)}, u32[]{:S(2)}) collective-permute-start(f32[24,256]{1,0:T(8,128)S(1)} %get-tuple-element.63), channel_id=1, source_target_pairs={{0,4},{1,5},{2,6},{3,7},{4,8},{5,9},{6,10},{7,11},{8,12},{9,13},{1... | collective-permute-start | bytes 73736 | tf_op jit(solution)/shard_map/ppermute | solution.py:256
  39.3 3.1 %collective-permute-start.7 = (f32[24,256]{1,0:T(8,128)S(1)}, f32[24,256]{1,0:T(8,128)S(1)}, u32[]{:S(2)}, u32[]{:S(2)}) collective-permute-start(f32[24,256]{1,0:T(8,128)S(1)} %get-tuple-element.64), channel_id=1, source_target_pairs={{0,12},{1,13},{2,14},{3,15},{4,0},{5,1},{6,2},{7,3},{8,4},{9,5},{1... | collective-permute-start | bytes 73736 | tf_op jit(solution)/shard_map/ppermute | solution.py:256
  43.9 2.1 %collective-permute-start.8 = (f32[8,128]{1,0:T(8,128)S(1)}, f32[8,128]{1,0:T(8,128)S(1)}, u32[]{:S(2)}, u32[]{:S(2)}) collective-permute-start(f32[8,128]{1,0:T(8,128)S(1)} %scatter.4), channel_id=1, source_target_pairs={{0,16},{16,0},{32,48},{48,32},{64,80},{80,64},{96,112},{112,96},{1... | collective-permute-start | bytes 12296 | tf_op jit(solution)/shard_map/ppermute | solution.py:508
  46.9 2.7 %collective-permute-start.10 = (f32[32,256]{1,0:T(8,128)S(1)}, f32[32,256]{1,0:T(8,128)S(1)}, u32[]{:S(2)}, u32[]{:S(2)}) collective-permute-start(f32[32,256]{1,0:T(8,128)S(1)} %maximum_maximum_fusion), channel_id=1, source_target_pairs={{0,64},{16,80},{32,96},{48,112},{64,0},{80,16},{96,32},{112,48},{1... | collective-permute-start | bytes 98312 | tf_op jit(solution)/shard_map/ppermute | solution.py:270
  49.6 1.9 %collective-permute-start.9 = (f32[32,256]{1,0:T(8,128)S(1)}, f32[32,256]{1,0:T(8,128)S(1)}, u32[]{:S(2)}, u32[]{:S(2)}) collective-permute-start(f32[32,256]{1,0:T(8,128)S(1)} %maximum_maximum_fusion), channel_id=1, source_target_pairs={{0,96},{16,112},{32,0},{48,16},{64,32},{80,48},{96,64},{112,80},{1... | collective-permute-start | bytes 98312 | tf_op jit(solution)/shard_map/ppermute | solution.py:270
  52.6 5.8 %collective-permute-done.12.first_ref.refs_2_ = f32[2,2,256,512]{3,2,1,0:T(8,128)} collective-permute-done((f32[2,2,256,512]{3,2,1,0:T(8,128)}, f32[2,2,256,512]{3,2,1,0:T(8,128)}, u32[]{:S(2)}, u32[]{:S(2)}) %collective-permute-start.12) | collective-permute-done | bytes 2097184 | tf_op jit(solution)/shard_map/ppermute | solution.py:505
  60.4 2.9 %second_pairs.1 = f32[2,2,256,512]{3,2,1,0:T(8,128)} custom-call(f32[2,2,256,512]{3,2,1,0:T(8,128)} %collective-permute-done.12.first_ref.refs_2_, f32[2,2,256,512]{3,2,1,0:T(8,128)} %collective-permute-done.13.second_ref.refs_3_), custom_call_target="tpu_custom_call" | custom-call | flops 1000000 | bytes 65536 | tf_op jit(solution)/shard_map/second_pairs/pallas_call | solution.py:486
  64.5 1.5 %collective-permute-start.25 = (f32[2,2,256,512]{3,2,1,0:T(8,128)}, f32[2,2,256,512]{3,2,1,0:T(8,128)}, u32[]{:S(2)}, u32[]{:S(2)}) collective-permute-start(f32[2,2,256,512]{3,2,1,0:T(8,128)} %slice_dynamic-update-slice_fusion), channel_id=1, source_target_pairs={{0,64},{16,80},{32,96},{48,112},{64,0},{80,16},{96,32},{112,48},{1... | collective-permute-start | bytes 6291464 | tf_op jit(solution)/shard_map/ppermute | solution.py:505
  66.0 2.4 %collective-permute-start.16 = (f32[24,256]{1,0:T(8,128)S(1)}, f32[24,256]{1,0:T(8,128)S(1)}, u32[]{:S(2)}, u32[]{:S(2)}) collective-permute-start(f32[24,256]{1,0:T(8,128)S(1)} %select_add_fusion), channel_id=1, source_target_pairs={{0,12},{1,13},{2,14},{3,15},{4,0},{5,1},{6,2},{7,3},{8,4},{9,5},{1... | collective-permute-start | bytes 73736 | tf_op jit(solution)/shard_map/ppermute | solution.py:270
  70.4 2.7 %collective-permute-done.15 = f32[24,256]{1,0:T(8,128)S(1)} collective-permute-done((f32[24,256]{1,0:T(8,128)S(1)}, f32[24,256]{1,0:T(8,128)S(1)}, u32[]{:S(2)}, u32[]{:S(2)}) %collective-permute-start.15) | collective-permute-done | bytes 24608 | tf_op jit(solution)/shard_map/ppermute | solution.py:270
  73.9 1.5 %collective-permute-start.20 = (f32[96,256]{1,0:T(8,128)S(1)}, f32[96,256]{1,0:T(8,128)S(1)}, u32[]{:S(2)}, u32[]{:S(2)}) collective-permute-start(f32[96,256]{1,0:T(8,128)S(1)} %pad_maximum_fusion.refs_0_), channel_id=1, source_target_pairs={{0,16},{16,0},{32,48},{48,32},{64,80},{80,64},{96,112},{112,96},{1... | collective-permute-start | bytes 294920 | tf_op jit(solution)/shard_map/ppermute | solution.py:508
  76.4 3.7 %collective-permute-start.18 = (f32[96,256]{1,0:T(8,128)S(1)}, f32[96,256]{1,0:T(8,128)S(1)}, u32[]{:S(2)}, u32[]{:S(2)}) collective-permute-start(f32[96,256]{1,0:T(8,128)S(1)} %pad_maximum_fusion.refs_0_), channel_id=1, source_target_pairs={{0,2},{1,3},{2,0},{3,1},{4,6},{5,7},{6,4},{7,5},{8,10},{9,11},{10,... | collective-permute-start | bytes 294920 | tf_op jit(solution)/shard_map/ppermute | solution.py:270
  82.9 2.4 %collective-permute-done.18.refs_2_ = f32[96,256]{1,0:T(8,128)S(1)} collective-permute-done((f32[96,256]{1,0:T(8,128)S(1)}, f32[96,256]{1,0:T(8,128)S(1)}, u32[]{:S(2)}, u32[]{:S(2)}) %collective-permute-start.18) | collective-permute-done | bytes 98336 | tf_op jit(solution)/shard_map/ppermute | solution.py:270
  89.5 24.6 %factor.1 = (f32[512,512]{1,0:T(8,128)}, bf16[512,512]{1,0:T(8,128)(2,1)S(1)}, bf16[512,512]{1,0:T(8,128)(2,1)S(1)}) custom-call(f32[512,512]{1,0:T(8,128)S(1)} %copy-done, f32[96,256]{1,0:T(8,128)S(1)} %pad_maximum_fusion.refs_0_, f32[96,256]{1,0:T(8,128)} %collective-permute-done.17.refs_1_, f32[96,256]{1,0:T(8,128)S(1)} %collective-permute-done.18.refs_2_, ...), custom_call_target="tpu_custom_call" | custom-call | flops 1000000 | bytes 65536 | tf_op jit(solution)/shard_map/factor/pallas_call | solution.py:397
  114.1 9.1 %finish.1 = f32[8,256,512]{2,1,0:T(8,128)} custom-call(s32[16]{0:T(128)S(1)} %convert_element_type.7.slot_ref, bf16[512,512]{1,0:T(8,128)(2,1)S(1)} %get-tuple-element.49.head_ref, bf16[512,512]{1,0:T(8,128)(2,1)S(1)} %get-tuple-element.50.tail_ref, f32[2,256,512]{2,1,0:T(8,128)S(1)} %copy-done.1, f32[2,2,256,512]{3,2,1,0:T(8,128)S(1)} %collective-permute-done.refs_1_, ...), custom_call_target="tpu_custom_call" | custom-call | flops 1000000 | bytes 65536 | tf_op jit(solution)/shard_map/finish/pallas_call | solution.py:454
  (64 shorter events, 20.9 us)
Async XLA Ops:
  4.9 16.7 %collective-permute-start = (f32[2,2,256,512]{3,2,1,0:T(8,128)}, f32[2,2,256,512]{3,2,1,0:T(8,128)S(1)}, u32[]{:S(2)}, u32[]{:S(2)}) collective-permute-start(f32[2,2,256,512]{3,2,1,0:T(8,128)} %get-tuple-element.38), channel_id=1, source_target_pairs={{0,16},{16,0},{32,48},{48,32},{64,80},{80,64},{96,112},{112,96},{1... | collective-permute-start | bytes 6291464 | tf_op jit(solution)/shard_map/ppermute | solution.py:508
  6.5 51.8 %collective-permute-start.12 = (f32[2,2,256,512]{3,2,1,0:T(8,128)}, f32[2,2,256,512]{3,2,1,0:T(8,128)}, u32[]{:S(2)}, u32[]{:S(2)}) collective-permute-start(f32[2,2,256,512]{3,2,1,0:T(8,128)} %get-tuple-element.43), channel_id=1, source_target_pairs={{0,32},{16,48},{32,64},{48,80},{64,96},{80,112},{96,0},{112,16},{1... | collective-permute-start | bytes 6291464 | tf_op jit(solution)/shard_map/ppermute | solution.py:505
  10.6 48.3 %collective-permute-start.13 = (f32[2,2,256,512]{3,2,1,0:T(8,128)}, f32[2,2,256,512]{3,2,1,0:T(8,128)}, u32[]{:S(2)}, u32[]{:S(2)}) collective-permute-start(f32[2,2,256,512]{3,2,1,0:T(8,128)} %get-tuple-element.44), channel_id=1, source_target_pairs={{0,96},{16,112},{32,0},{48,16},{64,32},{80,48},{96,64},{112,80},{1... | collective-permute-start | bytes 6291464 | tf_op jit(solution)/shard_map/ppermute | solution.py:505
  25.5 5.6 %collective-permute-start.2 = (f32[96,256]{1,0:T(8,128)S(1)}, f32[96,256]{1,0:T(8,128)S(1)}, u32[]{:S(2)}, u32[]{:S(2)}) collective-permute-start(f32[96,256]{1,0:T(8,128)S(1)} %get-tuple-element.56), channel_id=1, source_target_pairs={{0,1},{1,2},{2,3},{3,0},{4,5},{5,6},{6,7},{7,4},{8,9},{9,10},{10,1... | collective-permute-start | bytes 294920 | tf_op jit(solution)/shard_map/ppermute | solution.py:256
  27.8 3.9 %collective-permute-start.4 = (f32[96,256]{1,0:T(8,128)S(1)}, f32[96,256]{1,0:T(8,128)S(1)}, u32[]{:S(2)}, u32[]{:S(2)}) collective-permute-start(f32[96,256]{1,0:T(8,128)S(1)} %get-tuple-element.57), channel_id=1, source_target_pairs={{0,3},{1,0},{2,1},{3,2},{4,7},{5,4},{6,5},{7,6},{8,11},{9,8},{10,9... | collective-permute-start | bytes 294920 | tf_op jit(solution)/shard_map/ppermute | solution.py:256
  28.2 6.1 %collective-permute-start.3 = (f32[96,256]{1,0:T(8,128)S(1)}, f32[96,256]{1,0:T(8,128)S(1)}, u32[]{:S(2)}, u32[]{:S(2)}) collective-permute-start(f32[96,256]{1,0:T(8,128)S(1)} %get-tuple-element.58), channel_id=1, source_target_pairs={{0,2},{1,3},{2,0},{3,1},{4,6},{5,7},{6,4},{7,5},{8,10},{9,11},{10,... | collective-permute-start | bytes 294920 | tf_op jit(solution)/shard_map/ppermute | solution.py:256
  34.4 9.6 %collective-permute-start.5 = (f32[24,256]{1,0:T(8,128)S(1)}, f32[24,256]{1,0:T(8,128)S(1)}, u32[]{:S(2)}, u32[]{:S(2)}) collective-permute-start(f32[24,256]{1,0:T(8,128)S(1)} %get-tuple-element.63), channel_id=1, source_target_pairs={{0,4},{1,5},{2,6},{3,7},{4,8},{5,9},{6,10},{7,11},{8,12},{9,13},{1... | collective-permute-start | bytes 73736 | tf_op jit(solution)/shard_map/ppermute | solution.py:256
  39.3 6.7 %collective-permute-start.7 = (f32[24,256]{1,0:T(8,128)S(1)}, f32[24,256]{1,0:T(8,128)S(1)}, u32[]{:S(2)}, u32[]{:S(2)}) collective-permute-start(f32[24,256]{1,0:T(8,128)S(1)} %get-tuple-element.64), channel_id=1, source_target_pairs={{0,12},{1,13},{2,14},{3,15},{4,0},{5,1},{6,2},{7,3},{8,4},{9,5},{1... | collective-permute-start | bytes 73736 | tf_op jit(solution)/shard_map/ppermute | solution.py:256
  42.4 4.3 %collective-permute-start.6 = (f32[24,256]{1,0:T(8,128)S(1)}, f32[24,256]{1,0:T(8,128)S(1)}, u32[]{:S(2)}, u32[]{:S(2)}) collective-permute-start(f32[24,256]{1,0:T(8,128)S(1)} %get-tuple-element.65), channel_id=1, source_target_pairs={{0,8},{1,9},{2,10},{3,11},{4,12},{5,13},{6,14},{7,15},{8,0},{9,1},... | collective-permute-start | bytes 73736 | tf_op jit(solution)/shard_map/ppermute | solution.py:256
  46.8 12.1 %collective-permute-start.11 = (f32[32,256]{1,0:T(8,128)S(1)}, f32[32,256]{1,0:T(8,128)S(1)}, u32[]{:S(2)}, u32[]{:S(2)}) collective-permute-start(f32[32,256]{1,0:T(8,128)S(1)} %maximum_maximum_fusion), channel_id=1, source_target_pairs={{0,32},{16,48},{32,64},{48,80},{64,96},{80,112},{96,0},{112,16},{1... | collective-permute-start | bytes 98312 | tf_op jit(solution)/shard_map/ppermute | solution.py:270
  46.9 13.4 %collective-permute-start.10 = (f32[32,256]{1,0:T(8,128)S(1)}, f32[32,256]{1,0:T(8,128)S(1)}, u32[]{:S(2)}, u32[]{:S(2)}) collective-permute-start(f32[32,256]{1,0:T(8,128)S(1)} %maximum_maximum_fusion), channel_id=1, source_target_pairs={{0,64},{16,80},{32,96},{48,112},{64,0},{80,16},{96,32},{112,48},{1... | collective-permute-start | bytes 98312 | tf_op jit(solution)/shard_map/ppermute | solution.py:270
  49.6 10.7 %collective-permute-start.9 = (f32[32,256]{1,0:T(8,128)S(1)}, f32[32,256]{1,0:T(8,128)S(1)}, u32[]{:S(2)}, u32[]{:S(2)}) collective-permute-start(f32[32,256]{1,0:T(8,128)S(1)} %maximum_maximum_fusion), channel_id=1, source_target_pairs={{0,96},{16,112},{32,0},{48,16},{64,32},{80,48},{96,64},{112,80},{1... | collective-permute-start | bytes 98312 | tf_op jit(solution)/shard_map/ppermute | solution.py:270
  63.3 50.8 %collective-permute-start.24 = (f32[2,2,256,512]{3,2,1,0:T(8,128)}, f32[2,2,256,512]{3,2,1,0:T(8,128)}, u32[]{:S(2)}, u32[]{:S(2)}) collective-permute-start(f32[2,2,256,512]{3,2,1,0:T(8,128)} %second_pairs.1), channel_id=1, source_target_pairs={{0,16},{16,0},{32,48},{48,32},{64,80},{80,64},{96,112},{112,96},{1... | collective-permute-start | bytes 6291464 | tf_op jit(solution)/shard_map/ppermute | solution.py:508
  64.5 49.6 %collective-permute-start.25 = (f32[2,2,256,512]{3,2,1,0:T(8,128)}, f32[2,2,256,512]{3,2,1,0:T(8,128)}, u32[]{:S(2)}, u32[]{:S(2)}) collective-permute-start(f32[2,2,256,512]{3,2,1,0:T(8,128)} %slice_dynamic-update-slice_fusion), channel_id=1, source_target_pairs={{0,64},{16,80},{32,96},{48,112},{64,0},{80,16},{96,32},{112,48},{1... | collective-permute-start | bytes 6291464 | tf_op jit(solution)/shard_map/ppermute | solution.py:505
  66.0 4.3 %collective-permute-start.16 = (f32[24,256]{1,0:T(8,128)S(1)}, f32[24,256]{1,0:T(8,128)S(1)}, u32[]{:S(2)}, u32[]{:S(2)}) collective-permute-start(f32[24,256]{1,0:T(8,128)S(1)} %select_add_fusion), channel_id=1, source_target_pairs={{0,12},{1,13},{2,14},{3,15},{4,0},{5,1},{6,2},{7,3},{8,4},{9,5},{1... | collective-permute-start | bytes 73736 | tf_op jit(solution)/shard_map/ppermute | solution.py:270
  68.5 4.6 %collective-permute-start.15 = (f32[24,256]{1,0:T(8,128)S(1)}, f32[24,256]{1,0:T(8,128)S(1)}, u32[]{:S(2)}, u32[]{:S(2)}) collective-permute-start(f32[24,256]{1,0:T(8,128)S(1)} %select_add_fusion), channel_id=1, source_target_pairs={{0,8},{1,9},{2,10},{3,11},{4,12},{5,13},{6,14},{7,15},{8,0},{9,1},... | collective-permute-start | bytes 73736 | tf_op jit(solution)/shard_map/ppermute | solution.py:270
  69.6 4.3 %collective-permute-start.14 = (f32[24,256]{1,0:T(8,128)S(1)}, f32[24,256]{1,0:T(8,128)S(1)}, u32[]{:S(2)}, u32[]{:S(2)}) collective-permute-start(f32[24,256]{1,0:T(8,128)S(1)} %select_add_fusion), channel_id=1, source_target_pairs={{0,4},{1,5},{2,6},{3,7},{4,8},{5,9},{6,10},{7,11},{8,12},{9,13},{1... | collective-permute-start | bytes 73736 | tf_op jit(solution)/shard_map/ppermute | solution.py:270
  73.9 6.2 %collective-permute-start.20 = (f32[96,256]{1,0:T(8,128)S(1)}, f32[96,256]{1,0:T(8,128)S(1)}, u32[]{:S(2)}, u32[]{:S(2)}) collective-permute-start(f32[96,256]{1,0:T(8,128)S(1)} %pad_maximum_fusion.refs_0_), channel_id=1, source_target_pairs={{0,16},{16,0},{32,48},{48,32},{64,80},{80,64},{96,112},{112,96},{1... | collective-permute-start | bytes 294920 | tf_op jit(solution)/shard_map/ppermute | solution.py:508
  75.4 6.8 %collective-permute-start.19 = (f32[96,256]{1,0:T(8,128)S(1)}, f32[96,256]{1,0:T(8,128)S(1)}, u32[]{:S(2)}, u32[]{:S(2)}) collective-permute-start(f32[96,256]{1,0:T(8,128)S(1)} %pad_maximum_fusion.refs_0_), channel_id=1, source_target_pairs={{0,1},{1,2},{2,3},{3,0},{4,5},{5,6},{6,7},{7,4},{8,9},{9,10},{10,1... | collective-permute-start | bytes 294920 | tf_op jit(solution)/shard_map/ppermute | solution.py:270
  76.4 8.8 %collective-permute-start.18 = (f32[96,256]{1,0:T(8,128)S(1)}, f32[96,256]{1,0:T(8,128)S(1)}, u32[]{:S(2)}, u32[]{:S(2)}) collective-permute-start(f32[96,256]{1,0:T(8,128)S(1)} %pad_maximum_fusion.refs_0_), channel_id=1, source_target_pairs={{0,2},{1,3},{2,0},{3,1},{4,6},{5,7},{6,4},{7,5},{8,10},{9,11},{10,... | collective-permute-start | bytes 294920 | tf_op jit(solution)/shard_map/ppermute | solution.py:270
  80.2 5.9 %collective-permute-start.17 = (f32[96,256]{1,0:T(8,128)S(1)}, f32[96,256]{1,0:T(8,128)}, u32[]{:S(2)}, u32[]{:S(2)}) collective-permute-start(f32[96,256]{1,0:T(8,128)S(1)} %pad_maximum_fusion.refs_0_), channel_id=1, source_target_pairs={{0,3},{1,0},{2,1},{3,2},{4,7},{5,4},{6,5},{7,6},{8,11},{9,8},{10,9... | collective-permute-start | bytes 294920 | tf_op jit(solution)/shard_map/ppermute | solution.py:270
  82.1 7.3 %collective-permute-start.23 = (f32[96,256]{1,0:T(8,128)S(1)}, f32[96,256]{1,0:T(8,128)}, u32[]{:S(2)}, u32[]{:S(2)}) collective-permute-start(f32[96,256]{1,0:T(8,128)S(1)} %collective-permute-done.19.refs_3_), channel_id=1, source_target_pairs={{0,16},{16,0},{32,48},{48,32},{64,80},{80,64},{96,112},{112,96},{1... | collective-permute-start | bytes 294920 | tf_op jit(solution)/shard_map/ppermute | solution.py:508
  85.3 4.2 %collective-permute-start.22 = (f32[96,256]{1,0:T(8,128)S(1)}, f32[96,256]{1,0:T(8,128)}, u32[]{:S(2)}, u32[]{:S(2)}) collective-permute-start(f32[96,256]{1,0:T(8,128)S(1)} %collective-permute-done.18.refs_2_), channel_id=1, source_target_pairs={{0,16},{16,0},{32,48},{48,32},{64,80},{80,64},{96,112},{112,96},{1... | collective-permute-start | bytes 294920 | tf_op jit(solution)/shard_map/ppermute | solution.py:508
  86.0 3.5 %collective-permute-start.21 = (f32[96,256]{1,0:T(8,128)}, f32[96,256]{1,0:T(8,128)}, u32[]{:S(2)}, u32[]{:S(2)}) collective-permute-start(f32[96,256]{1,0:T(8,128)} %collective-permute-done.17.refs_1_), channel_id=1, source_target_pairs={{0,16},{16,0},{32,48},{48,32},{64,80},{80,64},{96,112},{112,96},{1... | collective-permute-start | bytes 294920 | tf_op jit(solution)/shard_map/ppermute | solution.py:508
  (9 other events, 126.7 us)

commit v6 on v4

--- a/solution.py
+++ b/solution.py
@@ -350,8 +350,17 @@
     return jnp.concatenate(upper, 0), jnp.concatenate(strips, 0)
 
 
-def factor_kernel(row_count, gram_ref, inverse_ref, factor_ref, head_ref, tail_ref, work):
+def factor_kernel(row_count, inverse_ref, *refs):
+    *pieces, factor_ref, head_ref, tail_ref, gram_ref, work = refs
     size = work.shape[0]
+    core = lax.rem(lax.axis_index("scene"), 2)
+    ring = len(pieces) // 2
+    x = lax.rem(lax.axis_index("rows"), ring)
+    height = pieces[0].shape[0]
+    for i, piece in enumerate(pieces):
+        half = core if i < ring else 1 - core
+        row = (half * ring + lax.rem(x + i % ring, ring)) * height
+        gram_ref[pl.ds(pl.multiple_of(row, 8), height), :] = piece[...]
     work[:HALF, :HALF] = gram_ref[:HALF, :] / row_count
     work[:HALF, HALF:] = gram_ref[HALF : 2 * HALF, :] / row_count
     work[HALF:, HALF:] = gram_ref[2 * HALF :, :] / row_count
@@ -382,7 +391,7 @@
     head_ref[...], tail_ref[...] = split(dot32(inverse_ref[...], inverse, 1, 1))
 
 
-def factor(gram_sum, inverse_factor, row_count):
+def factor(pieces, inverse_factor, row_count):
     vmem = pl.BlockSpec(memory_space=pltpu.VMEM)
     size = inverse_factor.shape[0]
     return pl.pallas_call(
@@ -392,15 +401,18 @@
             jax.ShapeDtypeStruct((size, size), jnp.bfloat16),
             jax.ShapeDtypeStruct((size, size), jnp.bfloat16),
         ),
-        in_specs=[vmem, vmem],
+        in_specs=[vmem] * (1 + len(pieces)),
         out_specs=(vmem, vmem, vmem),
-        scratch_shapes=[pltpu.VMEM((size, size), jnp.float32)],
+        scratch_shapes=[
+            pltpu.VMEM((3 * HALF, HALF), jnp.float32),
+            pltpu.VMEM((size, size), jnp.float32),
+        ],
         compiler_params=pltpu.CompilerParams(vmem_limit_bytes=24 << 20),
         cost_estimate=pl.CostEstimate(
             flops=1_000_000, bytes_accessed=1 << 16, transcendentals=0
         ),
         name="factor",
-    )(gram_sum, inverse_factor)
+    )(inverse_factor, *pieces)
 
 
 def finish_kernel(pairs, slot_ref, head_ref, tail_ref, *refs):
@@ -455,12 +467,38 @@
             pltpu.SemaphoreType.DMA((most,)),
             pltpu.SemaphoreType.DMA((most,)),
         ],
-        compiler_params=pltpu.CompilerParams(vmem_limit_bytes=32 << 20),
+        compiler_params=pltpu.CompilerParams(vmem_limit_bytes=24 << 20),
         cost_estimate=pl.CostEstimate(
             flops=1_000_000, bytes_accessed=1 << 16, transcendentals=0
         ),
         name=name,
     )(*operands)
+
+
+def second_pairs_kernel(first_ref, second_ref, out_ref, sems):
+    copies = [
+        pltpu.make_async_copy(ref.at[1], out_ref.at[i], sems.at[i])
+        for i, ref in enumerate((first_ref, second_ref))
+    ]
+    for copy in copies:
+        copy.start()
+    for copy in copies:
+        copy.wait()
+
+
+def second_pairs(first, second):
+    hbm = pl.BlockSpec(memory_space=pl.ANY)
+    return pl.pallas_call(
+        second_pairs_kernel,
+        out_shape=jax.ShapeDtypeStruct(first.shape, first.dtype),
+        in_specs=[hbm, hbm],
+        out_specs=pl.BlockSpec(memory_space=pltpu.VMEM),
+        scratch_shapes=[pltpu.SemaphoreType.DMA((2,))],
+        cost_estimate=pl.CostEstimate(
+            flops=1_000_000, bytes_accessed=1 << 16, transcendentals=0
+        ),
+        name="second_pairs",
+    )(first, second)
 
 
 def shards(observations, inverse_factor, tile_count, tile_owner, tile_slot):
@@ -493,28 +531,26 @@
     )
     far_in = along_z(far, 2)
     value = sum_in_order([part[:height] for part in parts], "scene", 2)
-    for axis, span, stride in reversed(stages):
-        value = gather(value, axis, span, stride)
-    passed_on = other_core(jnp.concatenate([from_below[1:], from_above[1:]], 0))
-    upper, head, tail = factor(value, inverse_factor, scenes * rows * OWN_TILES * tile_rows)
 
     def slots_of(ahead, other):
         start = 128 * other + 2 * PAIR * ((chips - ahead) % chips) + PAIR * other
         return parts[ahead][height, start : start + PAIR]
 
-    near = [(0, 0), (0, 1), (3, 0), (1, 0), (3, 1), (1, 1)]
-    near_slots = jnp.concatenate([slots_of(*source) for source in near]).astype(jnp.int32)
-    far_slots = jnp.concatenate([slots_of(2, 0), slots_of(2, 1)]).astype(jnp.int32)
-    out = finish(
-        near_slots,
-        head,
-        tail,
-        [own, crossed, from_below, from_above, passed_on, passed_on],
-        (None, 0, 0, 0, 0, 1),
-        None,
-        "finish_near",
-    )
-    return finish(far_slots, head, tail, [far_in, far_in], (0, 1), out, "finish_far"), upper
+    sources = [(0, 0), (0, 1), (3, 0), (1, 0), (3, 1), (1, 1), (2, 0), (2, 1)]
+    slots = jnp.concatenate([slots_of(*source) for source in sources]).astype(jnp.int32)
+    value, from_below, from_above = lax.optimization_barrier((value, from_below, from_above))
+    passed_on = other_core(second_pairs(from_below, from_above))
+    (x_axis, x_span, x_stride), (y_axis, y_span, y_stride) = stages[1:]
+    value = gather(value, y_axis, y_span, y_stride)
+    value, slots = lax.optimization_barrier((value, slots))
+    pieces = from_ahead(value, x_axis, x_span, x_stride)
+    pieces = pieces + [other_core(piece) for piece in pieces]
+    upper, head, tail = factor(pieces, inverse_factor, scenes * rows * OWN_TILES * tile_rows)
+    near = [own, crossed, from_below, from_above, passed_on, passed_on]
+    first = PAIR * len(near)
+    out = finish(slots[:first], head, tail, near, (None, 0, 0, 0, 0, 1), None, "finish_near")
+    far = [far_in, far_in]
+    return finish(slots[first:], head, tail, far, (0, 1), out, "finish_far"), upper
 
 
 def solution(mesh):

time: 126 us -> 120 us (0.952)
  Pallas kernels: 40.3 us -> 53.1 us
  waiting for transfers between devices: 25.3 us -> 14.8 us
  other arithmetic: 5.87 us -> 1.14 us
  local copies, waits for them, and re-layouts: 9 us -> 5.06 us
    ppermute x10 -> x9, waiting for transfers between devices: 11.5 us -> 2.71 us  [from_ahead(): lax.ppermute(value, axis, ring_pairs(size, span, stride, span - ahead))]
    pallas_call x1, Pallas kernels: 6.87 us -> 14.5 us  [gram(): pl.pallas_call(gram_kernel, out_shape=(jax.ShapeDtypeStruct((3 * HALF, HA...]
    ppermute x3 -> x7, starting transfers between devices: 6.27 us -> 12.6 us  [other_core(): return lax.ppermute(value, 'scene', ring_pairs(scenes, 2, 1, 1))]
    ppermute x7, starting transfers between devices: 15.8 us -> 9.69 us  [scatter_sum(): lax.ppermute(sent, axis, ring_pairs(size, span, stride, shift))]
    pallas_call x0 -> x1, Pallas kernels: none -> 3 us  [second_pairs(): pl.pallas_call(second_pairs_kernel, out_shape=jax.ShapeDtypeStruct(first....]
    ppermute x3, waiting for transfers between devices: 6.35 us -> 3.77 us  [along_z(): return lax.ppermute(value, 'scene', ring_pairs(scenes, chips, 2, up))]
    slice x2 -> x1, local copies, waits for them, and re-layouts: 2.61 us -> 0.07 us  [shards(): slots[first:]]
    squeeze x2, local copies, waits for them, and re-layouts: 2.65 us -> 0.14 us  [slots_of(): return parts[ahead][height, start:start + PAIR]]
  transfers between devices with their start and end apart: 23 -> 26, of which waited for: 13 -> 13; matrix products, arithmetic and copies ran while one was open for 9% -> 4% of each run, Pallas kernels for 29% -> 37%
where the time goes in v6:
time: 120 us; the launch traced here: 118 us
  Pallas kernels  53.1 us (44%)
  starting transfers between devices  42.1 us (35%)
  waiting for transfers between devices  14.8 us (12%)
  local copies, waits for them, and re-layouts  5.06 us (4%)
  between operations  1.63 us (1%)
    pallas_call x1, Pallas kernels, factor(): pl.pallas_call(functools.partial(factor_kernel, row_count), out_shape=(ja...  23.4 us
    ppermute x9, starting transfers between devices, from_ahead(): lax.ppermute(value, axis, ring_pairs(size, span, stride, span - ahead))  15.3 us
    pallas_call x1, Pallas kernels, gram(): pl.pallas_call(gram_kernel, out_shape=(jax.ShapeDtypeStruct((3 * HALF, HA...  14.5 us
    ppermute x7, starting transfers between devices, other_core(): return lax.ppermute(value, 'scene', ring_pairs(scenes, 2, 1, 1))  12.6 us
    ppermute x7, starting transfers between devices, scatter_sum(): lax.ppermute(sent, axis, ring_pairs(size, span, stride, shift))  9.69 us
    ppermute x7, waiting for transfers between devices, scatter_sum(): lax.ppermute(sent, axis, ring_pairs(size, span, stride, shift))  6.82 us
    pallas_call x2, Pallas kernels, finish(): pl.pallas_call(functools.partial(finish_kernel, pairs), out_shape=jax.Sha...  6.19 us
    pallas_call x1, Pallas kernels, pack(): pl.pallas_call(pack_kernel, out_shape=(two_pairs, two_pairs, two_pairs, t...  6.03 us
  transfers between devices with their start and end apart: 26, of which 13 were waited for; matrix products, arithmetic and copies ran while one was open for 4% of the time, Pallas kernels for 37%

profile of v6, /device:TPU:1, one launch (start us, length us, event | category | flops | bytes accessed | tf_op | source)
XLA Modules:
  0.0 117.8 jit_solution(10984446286599032805)
XLA Ops:
  1.3 6.0 %pack.1 = (f32[2,2,256,512]{3,2,1,0:T(8,128)}, f32[2,2,256,512]{3,2,1,0:T(8,128)}, f32[2,2,256,512]{3,2,1,0:T(8,128)}, s32[16]{0:T(128)}, s32[16]{0:T(128)}) custom-call(s32[1]{0:T(128)S(6)} %copy.10.count_ref, s32[16]{0:T(128)} %owner_ref.1, s32[16]{0:T(128)} %slot_ref.1, f32[16,256,512]{2,1,0:T(8,128)} %tile_ref), custom_call_target="tpu_custom_call" | custom-call | bytes 8388608 | tf_op jit(solution)/shard_map/pack/pallas_call | solution.py:123
  7.3 2.2 %collective-permute-start = (f32[2,2,256,512]{3,2,1,0:T(8,128)}, f32[2,2,256,512]{3,2,1,0:T(8,128)}, u32[]{:S(2)}, u32[]{:S(2)}) collective-permute-start(f32[2,2,256,512]{3,2,1,0:T(8,128)} %get-tuple-element.43), channel_id=1, source_target_pairs={{0,16},{16,0},{32,48},{48,32},{64,80},{80,64},{96,112},{112,96},{1... | collective-permute-start | bytes 6291464 | tf_op jit(solution)/shard_map/ppermute | solution.py:513
  9.5 2.7 %collective-permute-start.13 = (f32[2,2,256,512]{3,2,1,0:T(8,128)}, f32[2,2,256,512]{3,2,1,0:T(8,128)}, u32[]{:S(2)}, u32[]{:S(2)}) collective-permute-start(f32[2,2,256,512]{3,2,1,0:T(8,128)} %get-tuple-element.49), channel_id=1, source_target_pairs={{0,96},{16,112},{32,0},{48,16},{64,32},{80,48},{96,64},{112,80},{1... | collective-permute-start | bytes 6291464 | tf_op jit(solution)/shard_map/ppermute | solution.py:510
  12.2 14.5 %gram.1 = (f32[768,256]{1,0:T(8,128)}, f32[2,256,512]{2,1,0:T(8,128)}, f32[2,2,256,512]{3,2,1,0:T(8,128)}) custom-call(s32[1]{0:T(128)S(6)} %copy.10.count_ref, s32[16]{0:T(128)} %get-tuple-element.40.seat_ref, f32[16,256,512]{2,1,0:T(8,128)} %tile_ref, f32[512,512]{1,0:T(8,128)} %inverse_ref.3), custom_call_target="tpu_custom_call" | custom-call | flops 1000000 | bytes 65536 | tf_op jit(solution)/shard_map/gram/pallas_call | solution.py:203
  31.0 2.8 %collective-permute-start.3 = (f32[96,256]{1,0:T(8,128)S(1)}, f32[96,256]{1,0:T(8,128)S(1)}, u32[]{:S(2)}, u32[]{:S(2)}) collective-permute-start(f32[96,256]{1,0:T(8,128)S(1)} %get-tuple-element.68), channel_id=1, source_target_pairs={{0,2},{1,3},{2,0},{3,1},{4,6},{5,7},{6,4},{7,5},{8,10},{9,11},{10,... | collective-permute-start | bytes 294920 | tf_op jit(solution)/shard_map/ppermute | solution.py:256
  33.8 2.4 %collective-permute-done.2 = f32[96,256]{1,0:T(8,128)S(1)} collective-permute-done((f32[96,256]{1,0:T(8,128)S(1)}, f32[96,256]{1,0:T(8,128)S(1)}, u32[]{:S(2)}, u32[]{:S(2)}) %collective-permute-start.2) | collective-permute-done | bytes 98336 | tf_op jit(solution)/shard_map/ppermute | solution.py:256
  36.2 2.5 %collective-permute-done.3 = f32[96,256]{1,0:T(8,128)S(1)} collective-permute-done((f32[96,256]{1,0:T(8,128)S(1)}, f32[96,256]{1,0:T(8,128)S(1)}, u32[]{:S(2)}, u32[]{:S(2)}) %collective-permute-start.3) | collective-permute-done | bytes 98336 | tf_op jit(solution)/shard_map/ppermute | solution.py:256
  38.9 5.1 %collective-permute-start.6 = (f32[24,256]{1,0:T(8,128)S(1)}, f32[24,256]{1,0:T(8,128)S(1)}, u32[]{:S(2)}, u32[]{:S(2)}) collective-permute-start(f32[24,256]{1,0:T(8,128)S(1)} %get-tuple-element.75), channel_id=1, source_target_pairs={{0,8},{1,9},{2,10},{3,11},{4,12},{5,13},{6,14},{7,15},{8,0},{9,1},... | collective-permute-start | bytes 73736 | tf_op jit(solution)/shard_map/ppermute | solution.py:256
  44.9 1.6 %collective-permute-start.8 = (f32[8,128]{1,0:T(8,128)S(1)}, f32[8,128]{1,0:T(8,128)S(1)}, u32[]{:S(2)}, u32[]{:S(2)}) collective-permute-start(f32[8,128]{1,0:T(8,128)S(1)} %scatter.4), channel_id=1, source_target_pairs={{0,16},{16,0},{32,48},{48,32},{64,80},{80,64},{96,112},{112,96},{1... | collective-permute-start | bytes 12296 | tf_op jit(solution)/shard_map/ppermute | solution.py:513
  47.3 2.1 %collective-permute-start.10 = (f32[32,256]{1,0:T(8,128)S(1)}, f32[32,256]{1,0:T(8,128)S(1)}, u32[]{:S(2)}, u32[]{:S(2)}) collective-permute-start(f32[32,256]{1,0:T(8,128)S(1)} %maximum_maximum_fusion), channel_id=1, source_target_pairs={{0,64},{16,80},{32,96},{48,112},{64,0},{80,16},{96,32},{112,48},{1... | collective-permute-start | bytes 98312 | tf_op jit(solution)/shard_map/ppermute | solution.py:270
  50.2 1.9 %collective-permute-start.9 = (f32[32,256]{1,0:T(8,128)S(1)}, f32[32,256]{1,0:T(8,128)S(1)}, u32[]{:S(2)}, u32[]{:S(2)}) collective-permute-start(f32[32,256]{1,0:T(8,128)S(1)} %maximum_maximum_fusion), channel_id=1, source_target_pairs={{0,96},{16,112},{32,0},{48,16},{64,32},{80,48},{96,64},{112,80},{1... | collective-permute-start | bytes 98312 | tf_op jit(solution)/shard_map/ppermute | solution.py:270
  52.1 2.3 %slice_dynamic-update-slice_fusion = f32[2,2,256,512]{3,2,1,0:T(8,128)} fusion(f32[2,2,256,512]{3,2,1,0:T(8,128)} %get-tuple-element.46, f32[2,2,256,512]{3,2,1,0:T(8,128)} %collective-permute-done.refs_1_), kind=kLoop, calls=%fused_computation | loop fusion | bytes 2097152 | tf_op jit(solution)/shard_map/dynamic_update_slice | solution.py:528
  54.4 3.8 %collective-permute-done.12.first_ref.refs_2_ = f32[2,2,256,512]{3,2,1,0:T(8,128)S(1)} collective-permute-done((f32[2,2,256,512]{3,2,1,0:T(8,128)}, f32[2,2,256,512]{3,2,1,0:T(8,128)S(1)}, u32[]{:S(2)}, u32[]{:S(2)}) %collective-permute-start.12) | collective-permute-done | bytes 2097184 | tf_op jit(solution)/shard_map/ppermute | solution.py:510
  59.5 3.0 %second_pairs.1 = f32[2,2,256,512]{3,2,1,0:T(8,128)} custom-call(f32[2,2,256,512]{3,2,1,0:T(8,128)} %copy-done, f32[2,2,256,512]{3,2,1,0:T(8,128)} %collective-permute-done.13.second_ref.refs_3_), custom_call_target="tpu_custom_call" | custom-call | flops 1000000 | bytes 65536 | tf_op jit(solution)/shard_map/second_pairs/pallas_call | solution.py:491
  62.5 1.8 %collective-permute-start.25 = (f32[2,2,256,512]{3,2,1,0:T(8,128)}, f32[2,2,256,512]{3,2,1,0:T(8,128)}, u32[]{:S(2)}, u32[]{:S(2)}) collective-permute-start(f32[2,2,256,512]{3,2,1,0:T(8,128)} %second_pairs.1), channel_id=1, source_target_pairs={{0,16},{16,0},{32,48},{48,32},{64,80},{80,64},{96,112},{112,96},{1... | collective-permute-start | bytes 6291464 | tf_op jit(solution)/shard_map/ppermute | solution.py:513
  64.3 1.8 %collective-permute-start.24 = (f32[2,2,256,512]{3,2,1,0:T(8,128)}, f32[2,2,256,512]{3,2,1,0:T(8,128)}, u32[]{:S(2)}, u32[]{:S(2)}) collective-permute-start(f32[2,2,256,512]{3,2,1,0:T(8,128)} %slice_dynamic-update-slice_fusion), channel_id=1, source_target_pairs={{0,64},{16,80},{32,96},{48,112},{64,0},{80,16},{96,32},{112,48},{1... | collective-permute-start | bytes 6291464 | tf_op jit(solution)/shard_map/ppermute | solution.py:510
  66.1 1.6 %collective-permute-start.14 = (f32[24,256]{1,0:T(8,128)S(1)}, f32[24,256]{1,0:T(8,128)S(1)}, u32[]{:S(2)}, u32[]{:S(2)}) collective-permute-start(f32[24,256]{1,0:T(8,128)S(1)} %select_add_fusion), channel_id=1, source_target_pairs={{0,4},{1,5},{2,6},{3,7},{4,8},{5,9},{6,10},{7,11},{8,12},{9,13},{1... | collective-permute-start | bytes 73736 | tf_op jit(solution)/shard_map/ppermute | solution.py:270
  67.6 2.2 %collective-permute-start.15 = (f32[24,256]{1,0:T(8,128)S(1)}, f32[24,256]{1,0:T(8,128)S(1)}, u32[]{:S(2)}, u32[]{:S(2)}) collective-permute-start(f32[24,256]{1,0:T(8,128)S(1)} %select_add_fusion), channel_id=1, source_target_pairs={{0,8},{1,9},{2,10},{3,11},{4,12},{5,13},{6,14},{7,15},{8,0},{9,1},... | collective-permute-start | bytes 73736 | tf_op jit(solution)/shard_map/ppermute | solution.py:270
  69.9 2.1 %collective-permute-start.16 = (f32[24,256]{1,0:T(8,128)S(1)}, f32[24,256]{1,0:T(8,128)S(1)}, u32[]{:S(2)}, u32[]{:S(2)}) collective-permute-start(f32[24,256]{1,0:T(8,128)S(1)} %select_add_fusion), channel_id=1, source_target_pairs={{0,12},{1,13},{2,14},{3,15},{4,0},{5,1},{6,2},{7,3},{8,4},{9,5},{1... | collective-permute-start | bytes 73736 | tf_op jit(solution)/shard_map/ppermute | solution.py:270
  73.0 3.4 %collective-permute-start.17 = (f32[96,256]{1,0:T(8,128)S(1)}, f32[96,256]{1,0:T(8,128)S(1)}, u32[]{:S(2)}, u32[]{:S(2)}) collective-permute-start(f32[96,256]{1,0:T(8,128)S(1)} %pad_maximum_fusion.refs_0_), channel_id=1, source_target_pairs={{0,3},{1,0},{2,1},{3,2},{4,7},{5,4},{6,5},{7,6},{8,11},{9,8},{10,9... | collective-permute-start | bytes 294920 | tf_op jit(solution)/shard_map/ppermute | solution.py:270
  78.0 3.2 %collective-permute-start.20 = (f32[96,256]{1,0:T(8,128)S(1)}, f32[96,256]{1,0:T(8,128)S(1)}, u32[]{:S(2)}, u32[]{:S(2)}) collective-permute-start(f32[96,256]{1,0:T(8,128)S(1)} %pad_maximum_fusion.refs_0_), channel_id=1, source_target_pairs={{0,16},{16,0},{32,48},{48,32},{64,80},{80,64},{96,112},{112,96},{1... | collective-permute-start | bytes 294920 | tf_op jit(solution)/shard_map/ppermute | solution.py:513
  81.7 2.7 %collective-permute-start.21 = (f32[96,256]{1,0:T(8,128)S(1)}, f32[96,256]{1,0:T(8,128)S(1)}, u32[]{:S(2)}, u32[]{:S(2)}) collective-permute-start(f32[96,256]{1,0:T(8,128)S(1)} %collective-permute-done.17.refs_1_), channel_id=1, source_target_pairs={{0,16},{16,0},{32,48},{48,32},{64,80},{80,64},{96,112},{112,96},{1... | collective-permute-start | bytes 294920 | tf_op jit(solution)/shard_map/ppermute | solution.py:513
  86.8 23.4 %factor.1 = (f32[512,512]{1,0:T(8,128)}, bf16[512,512]{1,0:T(8,128)(2,1)S(1)}, bf16[512,512]{1,0:T(8,128)(2,1)S(1)}) custom-call(f32[512,512]{1,0:T(8,128)S(1)} %copy-done.2, f32[96,256]{1,0:T(8,128)S(1)} %pad_maximum_fusion.refs_0_, f32[96,256]{1,0:T(8,128)S(1)} %collective-permute-done.17.refs_1_, f32[96,256]{1,0:T(8,128)S(1)} %collective-permute-done.18.refs_2_, ...), custom_call_target="tpu_custom_call" | custom-call | flops 1000000 | bytes 65536 | tf_op jit(solution)/shard_map/factor/pallas_call | solution.py:397
  111.5 5.5 %finish_near.1.refs_2_ = f32[8,256,512]{2,1,0:T(8,128)} custom-call(s32[12]{0:T(128)S(1)} %bitcast.50, bf16[512,512]{1,0:T(8,128)(2,1)S(1)} %get-tuple-element.59.head_ref, bf16[512,512]{1,0:T(8,128)(2,1)S(1)} %get-tuple-element.60.tail_ref, f32[2,256,512]{2,1,0:T(8,128)S(1)} %copy-done.3, f32[2,2,256,512]{3,2,1,0:T(8,128)} %collective-permute-done.refs_1_, ...), custom_call_target="tpu_custom_call" | custom-call | flops 1000000 | bytes 65536 | tf_op jit(solution)/shard_map/finish_near/pallas_call | solution.py:457
  (62 shorter events, 15.6 us)
Async XLA Ops:
  7.3 19.4 %collective-permute-start = (f32[2,2,256,512]{3,2,1,0:T(8,128)}, f32[2,2,256,512]{3,2,1,0:T(8,128)}, u32[]{:S(2)}, u32[]{:S(2)}) collective-permute-start(f32[2,2,256,512]{3,2,1,0:T(8,128)} %get-tuple-element.43), channel_id=1, source_target_pairs={{0,16},{16,0},{32,48},{48,32},{64,80},{80,64},{96,112},{112,96},{1... | collective-permute-start | bytes 6291464 | tf_op jit(solution)/shard_map/ppermute | solution.py:513
  9.5 48.6 %collective-permute-start.12 = (f32[2,2,256,512]{3,2,1,0:T(8,128)}, f32[2,2,256,512]{3,2,1,0:T(8,128)S(1)}, u32[]{:S(2)}, u32[]{:S(2)}) collective-permute-start(f32[2,2,256,512]{3,2,1,0:T(8,128)} %get-tuple-element.48), channel_id=1, source_target_pairs={{0,32},{16,48},{32,64},{48,80},{64,96},{80,112},{96,0},{112,16},{1... | collective-permute-start | bytes 6291464 | tf_op jit(solution)/shard_map/ppermute | solution.py:510
  9.5 48.6 %collective-permute-start.13 = (f32[2,2,256,512]{3,2,1,0:T(8,128)}, f32[2,2,256,512]{3,2,1,0:T(8,128)}, u32[]{:S(2)}, u32[]{:S(2)}) collective-permute-start(f32[2,2,256,512]{3,2,1,0:T(8,128)} %get-tuple-element.49), channel_id=1, source_target_pairs={{0,96},{16,112},{32,0},{48,16},{64,32},{80,48},{96,64},{112,80},{1... | collective-permute-start | bytes 6291464 | tf_op jit(solution)/shard_map/ppermute | solution.py:510
  27.7 2.1 %collective-permute-start.1 = (f32[384,256]{1,0:T(8,128)S(1)}, f32[384,256]{1,0:T(8,128)S(1)}, u32[]{:S(2)}, u32[]{:S(2)}) collective-permute-start(f32[384,256]{1,0:T(8,128)S(1)} %dynamic-slice_bitcast_fusion), channel_id=1, source_target_pairs={{0,16},{16,0},{32,48},{48,32},{64,80},{80,64},{96,112},{112,96},{1... | collective-permute-start | bytes 1179656 | tf_op jit(solution)/shard_map/ppermute | solution.py:256
  30.9 5.3 %collective-permute-start.2 = (f32[96,256]{1,0:T(8,128)S(1)}, f32[96,256]{1,0:T(8,128)S(1)}, u32[]{:S(2)}, u32[]{:S(2)}) collective-permute-start(f32[96,256]{1,0:T(8,128)S(1)} %get-tuple-element.66), channel_id=1, source_target_pairs={{0,1},{1,2},{2,3},{3,0},{4,5},{5,6},{6,7},{7,4},{8,9},{9,10},{10,1... | collective-permute-start | bytes 294920 | tf_op jit(solution)/shard_map/ppermute | solution.py:256
  31.0 7.7 %collective-permute-start.3 = (f32[96,256]{1,0:T(8,128)S(1)}, f32[96,256]{1,0:T(8,128)S(1)}, u32[]{:S(2)}, u32[]{:S(2)}) collective-permute-start(f32[96,256]{1,0:T(8,128)S(1)} %get-tuple-element.68), channel_id=1, source_target_pairs={{0,2},{1,3},{2,0},{3,1},{4,6},{5,7},{6,4},{7,5},{8,10},{9,11},{10,... | collective-permute-start | bytes 294920 | tf_op jit(solution)/shard_map/ppermute | solution.py:256
  33.8 4.9 %collective-permute-start.4 = (f32[96,256]{1,0:T(8,128)S(1)}, f32[96,256]{1,0:T(8,128)S(1)}, u32[]{:S(2)}, u32[]{:S(2)}) collective-permute-start(f32[96,256]{1,0:T(8,128)S(1)} %get-tuple-element.67), channel_id=1, source_target_pairs={{0,3},{1,0},{2,1},{3,2},{4,7},{5,4},{6,5},{7,6},{8,11},{9,8},{10,9... | collective-permute-start | bytes 294920 | tf_op jit(solution)/shard_map/ppermute | solution.py:256
  38.8 6.1 %collective-permute-start.5 = (f32[24,256]{1,0:T(8,128)S(1)}, f32[24,256]{1,0:T(8,128)S(1)}, u32[]{:S(2)}, u32[]{:S(2)}) collective-permute-start(f32[24,256]{1,0:T(8,128)S(1)} %get-tuple-element.73), channel_id=1, source_target_pairs={{0,4},{1,5},{2,6},{3,7},{4,8},{5,9},{6,10},{7,11},{8,12},{9,13},{1... | collective-permute-start | bytes 73736 | tf_op jit(solution)/shard_map/ppermute | solution.py:256
  38.9 7.6 %collective-permute-start.6 = (f32[24,256]{1,0:T(8,128)S(1)}, f32[24,256]{1,0:T(8,128)S(1)}, u32[]{:S(2)}, u32[]{:S(2)}) collective-permute-start(f32[24,256]{1,0:T(8,128)S(1)} %get-tuple-element.75), channel_id=1, source_target_pairs={{0,8},{1,9},{2,10},{3,11},{4,12},{5,13},{6,14},{7,15},{8,0},{9,1},... | collective-permute-start | bytes 73736 | tf_op jit(solution)/shard_map/ppermute | solution.py:256
  44.0 3.1 %collective-permute-start.7 = (f32[24,256]{1,0:T(8,128)S(1)}, f32[24,256]{1,0:T(8,128)S(1)}, u32[]{:S(2)}, u32[]{:S(2)}) collective-permute-start(f32[24,256]{1,0:T(8,128)S(1)} %get-tuple-element.74), channel_id=1, source_target_pairs={{0,12},{1,13},{2,14},{3,15},{4,0},{5,1},{6,2},{7,3},{8,4},{9,5},{1... | collective-permute-start | bytes 73736 | tf_op jit(solution)/shard_map/ppermute | solution.py:256
  44.9 2.5 %collective-permute-start.8 = (f32[8,128]{1,0:T(8,128)S(1)}, f32[8,128]{1,0:T(8,128)S(1)}, u32[]{:S(2)}, u32[]{:S(2)}) collective-permute-start(f32[8,128]{1,0:T(8,128)S(1)} %scatter.4), channel_id=1, source_target_pairs={{0,16},{16,0},{32,48},{48,32},{64,80},{80,64},{96,112},{112,96},{1... | collective-permute-start | bytes 12296 | tf_op jit(solution)/shard_map/ppermute | solution.py:513
  47.3 11.9 %collective-permute-start.10 = (f32[32,256]{1,0:T(8,128)S(1)}, f32[32,256]{1,0:T(8,128)S(1)}, u32[]{:S(2)}, u32[]{:S(2)}) collective-permute-start(f32[32,256]{1,0:T(8,128)S(1)} %maximum_maximum_fusion), channel_id=1, source_target_pairs={{0,64},{16,80},{32,96},{48,112},{64,0},{80,16},{96,32},{112,48},{1... | collective-permute-start | bytes 98312 | tf_op jit(solution)/shard_map/ppermute | solution.py:270
  49.4 9.9 %collective-permute-start.11 = (f32[32,256]{1,0:T(8,128)S(1)}, f32[32,256]{1,0:T(8,128)S(1)}, u32[]{:S(2)}, u32[]{:S(2)}) collective-permute-start(f32[32,256]{1,0:T(8,128)S(1)} %maximum_maximum_fusion), channel_id=1, source_target_pairs={{0,32},{16,48},{32,64},{48,80},{64,96},{80,112},{96,0},{112,16},{1... | collective-permute-start | bytes 98312 | tf_op jit(solution)/shard_map/ppermute | solution.py:270
  50.2 9.1 %collective-permute-start.9 = (f32[32,256]{1,0:T(8,128)S(1)}, f32[32,256]{1,0:T(8,128)S(1)}, u32[]{:S(2)}, u32[]{:S(2)}) collective-permute-start(f32[32,256]{1,0:T(8,128)S(1)} %maximum_maximum_fusion), channel_id=1, source_target_pairs={{0,96},{16,112},{32,0},{48,16},{64,32},{80,48},{96,64},{112,80},{1... | collective-permute-start | bytes 98312 | tf_op jit(solution)/shard_map/ppermute | solution.py:270
  62.5 47.8 %collective-permute-start.25 = (f32[2,2,256,512]{3,2,1,0:T(8,128)}, f32[2,2,256,512]{3,2,1,0:T(8,128)}, u32[]{:S(2)}, u32[]{:S(2)}) collective-permute-start(f32[2,2,256,512]{3,2,1,0:T(8,128)} %second_pairs.1), channel_id=1, source_target_pairs={{0,16},{16,0},{32,48},{48,32},{64,80},{80,64},{96,112},{112,96},{1... | collective-permute-start | bytes 6291464 | tf_op jit(solution)/shard_map/ppermute | solution.py:513
  64.3 52.8 %collective-permute-start.24 = (f32[2,2,256,512]{3,2,1,0:T(8,128)}, f32[2,2,256,512]{3,2,1,0:T(8,128)}, u32[]{:S(2)}, u32[]{:S(2)}) collective-permute-start(f32[2,2,256,512]{3,2,1,0:T(8,128)} %slice_dynamic-update-slice_fusion), channel_id=1, source_target_pairs={{0,64},{16,80},{32,96},{48,112},{64,0},{80,16},{96,32},{112,48},{1... | collective-permute-start | bytes 6291464 | tf_op jit(solution)/shard_map/ppermute | solution.py:510
  66.1 6.1 %collective-permute-start.14 = (f32[24,256]{1,0:T(8,128)S(1)}, f32[24,256]{1,0:T(8,128)S(1)}, u32[]{:S(2)}, u32[]{:S(2)}) collective-permute-start(f32[24,256]{1,0:T(8,128)S(1)} %select_add_fusion), channel_id=1, source_target_pairs={{0,4},{1,5},{2,6},{3,7},{4,8},{5,9},{6,10},{7,11},{8,12},{9,13},{1... | collective-permute-start | bytes 73736 | tf_op jit(solution)/shard_map/ppermute | solution.py:270
  67.6 4.7 %collective-permute-start.15 = (f32[24,256]{1,0:T(8,128)S(1)}, f32[24,256]{1,0:T(8,128)S(1)}, u32[]{:S(2)}, u32[]{:S(2)}) collective-permute-start(f32[24,256]{1,0:T(8,128)S(1)} %select_add_fusion), channel_id=1, source_target_pairs={{0,8},{1,9},{2,10},{3,11},{4,12},{5,13},{6,14},{7,15},{8,0},{9,1},... | collective-permute-start | bytes 73736 | tf_op jit(solution)/shard_map/ppermute | solution.py:270
  69.9 3.1 %collective-permute-start.16 = (f32[24,256]{1,0:T(8,128)S(1)}, f32[24,256]{1,0:T(8,128)S(1)}, u32[]{:S(2)}, u32[]{:S(2)}) collective-permute-start(f32[24,256]{1,0:T(8,128)S(1)} %select_add_fusion), channel_id=1, source_target_pairs={{0,12},{1,13},{2,14},{3,15},{4,0},{5,1},{6,2},{7,3},{8,4},{9,5},{1... | collective-permute-start | bytes 73736 | tf_op jit(solution)/shard_map/ppermute | solution.py:270
  73.0 5.0 %collective-permute-start.17 = (f32[96,256]{1,0:T(8,128)S(1)}, f32[96,256]{1,0:T(8,128)S(1)}, u32[]{:S(2)}, u32[]{:S(2)}) collective-permute-start(f32[96,256]{1,0:T(8,128)S(1)} %pad_maximum_fusion.refs_0_), channel_id=1, source_target_pairs={{0,3},{1,0},{2,1},{3,2},{4,7},{5,4},{6,5},{7,6},{8,11},{9,8},{10,9... | collective-permute-start | bytes 294920 | tf_op jit(solution)/shard_map/ppermute | solution.py:270
  76.4 5.4 %collective-permute-start.18 = (f32[96,256]{1,0:T(8,128)S(1)}, f32[96,256]{1,0:T(8,128)S(1)}, u32[]{:S(2)}, u32[]{:S(2)}) collective-permute-start(f32[96,256]{1,0:T(8,128)S(1)} %pad_maximum_fusion.refs_0_), channel_id=1, source_target_pairs={{0,2},{1,3},{2,0},{3,1},{4,6},{5,7},{6,4},{7,5},{8,10},{9,11},{10,... | collective-permute-start | bytes 294920 | tf_op jit(solution)/shard_map/ppermute | solution.py:270
  77.1 7.4 %collective-permute-start.19 = (f32[96,256]{1,0:T(8,128)S(1)}, f32[96,256]{1,0:T(8,128)S(1)}, u32[]{:S(2)}, u32[]{:S(2)}) collective-permute-start(f32[96,256]{1,0:T(8,128)S(1)} %pad_maximum_fusion.refs_0_), channel_id=1, source_target_pairs={{0,1},{1,2},{2,3},{3,0},{4,5},{5,6},{6,7},{7,4},{8,9},{9,10},{10,1... | collective-permute-start | bytes 294920 | tf_op jit(solution)/shard_map/ppermute | solution.py:270
  78.0 7.5 %collective-permute-start.20 = (f32[96,256]{1,0:T(8,128)S(1)}, f32[96,256]{1,0:T(8,128)S(1)}, u32[]{:S(2)}, u32[]{:S(2)}) collective-permute-start(f32[96,256]{1,0:T(8,128)S(1)} %pad_maximum_fusion.refs_0_), channel_id=1, source_target_pairs={{0,16},{16,0},{32,48},{48,32},{64,80},{80,64},{96,112},{112,96},{1... | collective-permute-start | bytes 294920 | tf_op jit(solution)/shard_map/ppermute | solution.py:513
  81.7 3.8 %collective-permute-start.21 = (f32[96,256]{1,0:T(8,128)S(1)}, f32[96,256]{1,0:T(8,128)S(1)}, u32[]{:S(2)}, u32[]{:S(2)}) collective-permute-start(f32[96,256]{1,0:T(8,128)S(1)} %collective-permute-done.17.refs_1_), channel_id=1, source_target_pairs={{0,16},{16,0},{32,48},{48,32},{64,80},{80,64},{96,112},{112,96},{1... | collective-permute-start | bytes 294920 | tf_op jit(solution)/shard_map/ppermute | solution.py:513
  (7 other events, 99.1 us)

commit v7 on v6

--- a/solution.py
+++ b/solution.py
@@ -475,10 +475,10 @@
     )(*operands)
 
 
-def second_pairs_kernel(first_ref, second_ref, out_ref, sems):
+def second_pairs_kernel(first_ref, second_ref, first_out, second_out, sems):
     copies = [
-        pltpu.make_async_copy(ref.at[1], out_ref.at[i], sems.at[i])
-        for i, ref in enumerate((first_ref, second_ref))
+        pltpu.make_async_copy(first_ref.at[1], first_out, sems.at[0]),
+        pltpu.make_async_copy(second_ref.at[1], second_out, sems.at[1]),
     ]
     for copy in copies:
         copy.start()
@@ -490,9 +490,9 @@
     hbm = pl.BlockSpec(memory_space=pl.ANY)
     return pl.pallas_call(
         second_pairs_kernel,
-        out_shape=jax.ShapeDtypeStruct(first.shape, first.dtype),
+        out_shape=(jax.ShapeDtypeStruct(first.shape[1:], first.dtype),) * 2,
         in_specs=[hbm, hbm],
-        out_specs=pl.BlockSpec(memory_space=pltpu.VMEM),
+        out_specs=(pl.BlockSpec(memory_space=pltpu.VMEM),) * 2,
         scratch_shapes=[pltpu.SemaphoreType.DMA((2,))],
         cost_estimate=pl.CostEstimate(
             flops=1_000_000, bytes_accessed=1 << 16, transcendentals=0
@@ -539,16 +539,16 @@
     sources = [(0, 0), (0, 1), (3, 0), (1, 0), (3, 1), (1, 1), (2, 0), (2, 1)]
     slots = jnp.concatenate([slots_of(*source) for source in sources]).astype(jnp.int32)
     value, from_below, from_above = lax.optimization_barrier((value, from_below, from_above))
-    passed_on = other_core(second_pairs(from_below, from_above))
+    passed_up, passed_down = (other_core(pair) for pair in second_pairs(from_below, from_above))
     (x_axis, x_span, x_stride), (y_axis, y_span, y_stride) = stages[1:]
     value = gather(value, y_axis, y_span, y_stride)
     value, slots = lax.optimization_barrier((value, slots))
     pieces = from_ahead(value, x_axis, x_span, x_stride)
     pieces = pieces + [other_core(piece) for piece in pieces]
     upper, head, tail = factor(pieces, inverse_factor, scenes * rows * OWN_TILES * tile_rows)
-    near = [own, crossed, from_below, from_above, passed_on, passed_on]
+    near = [own, crossed, from_below, from_above, passed_up, passed_down]
     first = PAIR * len(near)
-    out = finish(slots[:first], head, tail, near, (None, 0, 0, 0, 0, 1), None, "finish_near")
+    out = finish(slots[:first], head, tail, near, (None, 0, 0, 0, None, None), None, "finish_near")
     far = [far_in, far_in]
     return finish(slots[first:], head, tail, far, (0, 1), out, "finish_far"), upper
 

time: 120 us -> 125 us (1.042)
  starting transfers between devices: 42.1 us -> 51.3 us
  Pallas kernels: 53.1 us -> 45.8 us
  waiting for transfers between devices: 14.8 us -> 18.9 us
    ppermute x7, starting transfers between devices: 9.69 us -> 19.5 us  [scatter_sum(): lax.ppermute(sent, axis, ring_pairs(size, span, stride, shift))]
    pallas_call x1, Pallas kernels: 14.5 us -> 6.87 us  [gram(): pl.pallas_call(gram_kernel, out_shape=(jax.ShapeDtypeStruct((3 * HALF, HA...]
    ppermute x9, waiting for transfers between devices: 2.71 us -> 8.36 us  [from_ahead(): lax.ppermute(value, axis, ring_pairs(size, span, stride, span - ahead))]
    ppermute x3, starting transfers between devices: 4.51 us -> 7.93 us  [along_z(): return lax.ppermute(value, 'scene', ring_pairs(scenes, chips, 2, up))]
    ppermute x7, waiting for transfers between devices: 6.82 us -> 3.88 us  [scatter_sum(): lax.ppermute(sent, axis, ring_pairs(size, span, stride, shift))]
    pallas_call x2, Pallas kernels: 6.19 us -> 8.87 us  [finish(): pl.pallas_call(functools.partial(finish_kernel, pairs), out_shape=jax.Sha...]
    pallas_call x1, Pallas kernels: 6.03 us -> 3.64 us  [pack(): pl.pallas_call(pack_kernel, out_shape=(two_pairs, two_pairs, two_pairs, t...]
    ppermute x7 -> x8, starting transfers between devices: 12.6 us -> 10.6 us  [other_core(): return lax.ppermute(value, 'scene', ring_pairs(scenes, 2, 1, 1))]
  transfers between devices with their start and end apart: 26 -> 27, of which waited for: 13 -> 13; matrix products, arithmetic and copies ran while one was open for 4% -> 4% of each run, Pallas kernels for 37% -> 31%
where the time goes in v7:
time: 125 us; the launch traced here: 124 us
  starting transfers between devices  51.3 us (41%)
  Pallas kernels  45.8 us (37%)
  waiting for transfers between devices  18.9 us (15%)
  local copies, waits for them, and re-layouts  4.9 us (4%)
  between operations  1.64 us (1%)
    pallas_call x1, Pallas kernels, factor(): pl.pallas_call(functools.partial(factor_kernel, row_count), out_shape=(ja...  23.4 us
    ppermute x7, starting transfers between devices, scatter_sum(): lax.ppermute(sent, axis, ring_pairs(size, span, stride, shift))  19.5 us
    ppermute x9, starting transfers between devices, from_ahead(): lax.ppermute(value, axis, ring_pairs(size, span, stride, span - ahead))  13.3 us
    ppermute x8, starting transfers between devices, other_core(): return lax.ppermute(value, 'scene', ring_pairs(scenes, 2, 1, 1))  10.6 us
    pallas_call x2, Pallas kernels, finish(): pl.pallas_call(functools.partial(finish_kernel, pairs), out_shape=jax.Sha...  8.87 us
    ppermute x9, waiting for transfers between devices, from_ahead(): lax.ppermute(value, axis, ring_pairs(size, span, stride, span - ahead))  8.36 us
    ppermute x3, starting transfers between devices, along_z(): return lax.ppermute(value, 'scene', ring_pairs(scenes, chips, 2, up))  7.93 us
    pallas_call x1, Pallas kernels, gram(): pl.pallas_call(gram_kernel, out_shape=(jax.ShapeDtypeStruct((3 * HALF, HA...  6.87 us
  transfers between devices with their start and end apart: 27, of which 13 were waited for; matrix products, arithmetic and copies ran while one was open for 4% of the time, Pallas kernels for 31%

profile of v7, /device:TPU:1, one launch (start us, length us, event | category | flops | bytes accessed | tf_op | source)
XLA Modules:
  0.0 123.7 jit_solution(2413576548662157277)
XLA Ops:
  1.3 3.6 %pack.1 = (f32[2,2,256,512]{3,2,1,0:T(8,128)}, f32[2,2,256,512]{3,2,1,0:T(8,128)}, f32[2,2,256,512]{3,2,1,0:T(8,128)}, s32[16]{0:T(128)}, s32[16]{0:T(128)}) custom-call(s32[1]{0:T(128)S(6)} %copy.10.count_ref, s32[16]{0:T(128)} %owner_ref.1, s32[16]{0:T(128)} %slot_ref.1, f32[16,256,512]{2,1,0:T(8,128)} %tile_ref), custom_call_target="tpu_custom_call" | custom-call | bytes 8388608 | tf_op jit(solution)/shard_map/pack/pallas_call | solution.py:123
  4.9 2.0 %collective-permute-start = (f32[2,2,256,512]{3,2,1,0:T(8,128)}, f32[2,2,256,512]{3,2,1,0:T(8,128)}, u32[]{:S(2)}, u32[]{:S(2)}) collective-permute-start(f32[2,2,256,512]{3,2,1,0:T(8,128)} %get-tuple-element.45), channel_id=1, source_target_pairs={{0,16},{16,0},{32,48},{48,32},{64,80},{80,64},{96,112},{112,96},{1... | collective-permute-start | bytes 6291464 | tf_op jit(solution)/shard_map/ppermute | solution.py:513
  6.9 3.8 %collective-permute-start.12 = (f32[2,2,256,512]{3,2,1,0:T(8,128)}, f32[2,2,256,512]{3,2,1,0:T(8,128)S(1)}, u32[]{:S(2)}, u32[]{:S(2)}) collective-permute-start(f32[2,2,256,512]{3,2,1,0:T(8,128)} %get-tuple-element.50), channel_id=1, source_target_pairs={{0,32},{16,48},{32,64},{48,80},{64,96},{80,112},{96,0},{112,16},{1... | collective-permute-start | bytes 6291464 | tf_op jit(solution)/shard_map/ppermute | solution.py:510
  10.7 1.9 %collective-permute-start.13 = (f32[2,2,256,512]{3,2,1,0:T(8,128)}, f32[2,2,256,512]{3,2,1,0:T(8,128)}, u32[]{:S(2)}, u32[]{:S(2)}) collective-permute-start(f32[2,2,256,512]{3,2,1,0:T(8,128)} %get-tuple-element.51), channel_id=1, source_target_pairs={{0,96},{16,112},{32,0},{48,16},{64,32},{80,48},{96,64},{112,80},{1... | collective-permute-start | bytes 6291464 | tf_op jit(solution)/shard_map/ppermute | solution.py:510
  12.6 6.9 %gram.1 = (f32[768,256]{1,0:T(8,128)}, f32[2,256,512]{2,1,0:T(8,128)}, f32[2,2,256,512]{3,2,1,0:T(8,128)}) custom-call(s32[1]{0:T(128)S(6)} %copy.10.count_ref, s32[16]{0:T(128)} %get-tuple-element.42.seat_ref, f32[16,256,512]{2,1,0:T(8,128)} %tile_ref, f32[512,512]{1,0:T(8,128)} %inverse_ref.3), custom_call_target="tpu_custom_call" | custom-call | flops 1000000 | bytes 65536 | tf_op jit(solution)/shard_map/gram/pallas_call | solution.py:203
  20.5 5.6 %collective-permute-start.1 = (f32[384,256]{1,0:T(8,128)S(1)}, f32[384,256]{1,0:T(8,128)S(1)}, u32[]{:S(2)}, u32[]{:S(2)}) collective-permute-start(f32[384,256]{1,0:T(8,128)S(1)} %dynamic-slice_bitcast_fusion), channel_id=1, source_target_pairs={{0,16},{16,0},{32,48},{48,32},{64,80},{80,64},{96,112},{112,96},{1... | collective-permute-start | bytes 1179656 | tf_op jit(solution)/shard_map/ppermute | solution.py:256
  28.6 4.5 %collective-permute-start.2 = (f32[96,256]{1,0:T(8,128)S(1)}, f32[96,256]{1,0:T(8,128)S(1)}, u32[]{:S(2)}, u32[]{:S(2)}) collective-permute-start(f32[96,256]{1,0:T(8,128)S(1)} %get-tuple-element.70), channel_id=1, source_target_pairs={{0,1},{1,2},{2,3},{3,0},{4,5},{5,6},{6,7},{7,4},{8,9},{9,10},{10,1... | collective-permute-start | bytes 294920 | tf_op jit(solution)/shard_map/ppermute | solution.py:256
  34.0 2.0 %collective-permute-start.4 = (f32[96,256]{1,0:T(8,128)S(1)}, f32[96,256]{1,0:T(8,128)S(1)}, u32[]{:S(2)}, u32[]{:S(2)}) collective-permute-start(f32[96,256]{1,0:T(8,128)S(1)} %get-tuple-element.71), channel_id=1, source_target_pairs={{0,3},{1,0},{2,1},{3,2},{4,7},{5,4},{6,5},{7,6},{8,11},{9,8},{10,9... | collective-permute-start | bytes 294920 | tf_op jit(solution)/shard_map/ppermute | solution.py:256
  36.0 2.5 %collective-permute-done.3 = f32[96,256]{1,0:T(8,128)S(1)} collective-permute-done((f32[96,256]{1,0:T(8,128)S(1)}, f32[96,256]{1,0:T(8,128)S(1)}, u32[]{:S(2)}, u32[]{:S(2)}) %collective-permute-start.3) | collective-permute-done | bytes 98336 | tf_op jit(solution)/shard_map/ppermute | solution.py:256
  38.6 2.2 %collective-permute-start.5 = (f32[24,256]{1,0:T(8,128)S(1)}, f32[24,256]{1,0:T(8,128)S(1)}, u32[]{:S(2)}, u32[]{:S(2)}) collective-permute-start(f32[24,256]{1,0:T(8,128)S(1)} %get-tuple-element.77), channel_id=1, source_target_pairs={{0,4},{1,5},{2,6},{3,7},{4,8},{5,9},{6,10},{7,11},{8,12},{9,13},{1... | collective-permute-start | bytes 73736 | tf_op jit(solution)/shard_map/ppermute | solution.py:256
  40.8 2.3 %collective-permute-start.6 = (f32[24,256]{1,0:T(8,128)S(1)}, f32[24,256]{1,0:T(8,128)S(1)}, u32[]{:S(2)}, u32[]{:S(2)}) collective-permute-start(f32[24,256]{1,0:T(8,128)S(1)} %get-tuple-element.79), channel_id=1, source_target_pairs={{0,8},{1,9},{2,10},{3,11},{4,12},{5,13},{6,14},{7,15},{8,0},{9,1},... | collective-permute-start | bytes 73736 | tf_op jit(solution)/shard_map/ppermute | solution.py:256
  43.0 2.0 %collective-permute-start.7 = (f32[24,256]{1,0:T(8,128)S(1)}, f32[24,256]{1,0:T(8,128)S(1)}, u32[]{:S(2)}, u32[]{:S(2)}) collective-permute-start(f32[24,256]{1,0:T(8,128)S(1)} %get-tuple-element.78), channel_id=1, source_target_pairs={{0,12},{1,13},{2,14},{3,15},{4,0},{5,1},{6,2},{7,3},{8,4},{9,5},{1... | collective-permute-start | bytes 73736 | tf_op jit(solution)/shard_map/ppermute | solution.py:256
  45.0 2.1 %collective-permute-start.8 = (f32[8,128]{1,0:T(8,128)S(1)}, f32[8,128]{1,0:T(8,128)S(1)}, u32[]{:S(2)}, u32[]{:S(2)}) collective-permute-start(f32[8,128]{1,0:T(8,128)S(1)} %scatter.4), channel_id=1, source_target_pairs={{0,16},{16,0},{32,48},{48,32},{64,80},{80,64},{96,112},{112,96},{1... | collective-permute-start | bytes 12296 | tf_op jit(solution)/shard_map/ppermute | solution.py:513
  50.2 2.3 %collective-permute-start.9 = (f32[32,256]{1,0:T(8,128)S(1)}, f32[32,256]{1,0:T(8,128)S(1)}, u32[]{:S(2)}, u32[]{:S(2)}) collective-permute-start(f32[32,256]{1,0:T(8,128)S(1)} %maximum_maximum_fusion), channel_id=1, source_target_pairs={{0,96},{16,112},{32,0},{48,16},{64,32},{80,48},{96,64},{112,80},{1... | collective-permute-start | bytes 98312 | tf_op jit(solution)/shard_map/ppermute | solution.py:270
  52.4 2.3 %slice_dynamic-update-slice_fusion = f32[2,2,256,512]{3,2,1,0:T(8,128)} fusion(f32[2,2,256,512]{3,2,1,0:T(8,128)} %get-tuple-element.48, f32[2,2,256,512]{3,2,1,0:T(8,128)} %collective-permute-done.refs_1_), kind=kLoop, calls=%fused_computation | loop fusion | bytes 2097152 | tf_op jit(solution)/shard_map/dynamic_update_slice | solution.py:528
  54.7 4.0 %collective-permute-done.12.first_ref.refs_2_ = f32[2,2,256,512]{3,2,1,0:T(8,128)S(1)} collective-permute-done((f32[2,2,256,512]{3,2,1,0:T(8,128)}, f32[2,2,256,512]{3,2,1,0:T(8,128)S(1)}, u32[]{:S(2)}, u32[]{:S(2)}) %collective-permute-start.12) | collective-permute-done | bytes 2097184 | tf_op jit(solution)/shard_map/ppermute | solution.py:510
  60.1 2.2 %collective-permute-start.24 = (f32[2,2,256,512]{3,2,1,0:T(8,128)}, f32[2,2,256,512]{3,2,1,0:T(8,128)}, u32[]{:S(2)}, u32[]{:S(2)}) collective-permute-start(f32[2,2,256,512]{3,2,1,0:T(8,128)} %slice_dynamic-update-slice_fusion), channel_id=1, source_target_pairs={{0,64},{16,80},{32,96},{48,112},{64,0},{80,16},{96,32},{112,48},{1... | collective-permute-start | bytes 6291464 | tf_op jit(solution)/shard_map/ppermute | solution.py:510
  62.4 3.0 %second_pairs.1 = (f32[2,256,512]{2,1,0:T(8,128)}, f32[2,256,512]{2,1,0:T(8,128)}) custom-call(f32[2,2,256,512]{3,2,1,0:T(8,128)} %copy-done, f32[2,2,256,512]{3,2,1,0:T(8,128)} %collective-permute-done.13.second_ref.refs_3_), custom_call_target="tpu_custom_call" | custom-call | flops 1000000 | bytes 65536 | tf_op jit(solution)/shard_map/second_pairs/pallas_call | solution.py:491
  74.4 2.6 %collective-permute-start.17 = (f32[96,256]{1,0:T(8,128)S(1)}, f32[96,256]{1,0:T(8,128)S(1)}, u32[]{:S(2)}, u32[]{:S(2)}) collective-permute-start(f32[96,256]{1,0:T(8,128)S(1)} %pad_maximum_fusion.refs_0_), channel_id=1, source_target_pairs={{0,3},{1,0},{2,1},{3,2},{4,7},{5,4},{6,5},{7,6},{8,11},{9,8},{10,9... | collective-permute-start | bytes 294920 | tf_op jit(solution)/shard_map/ppermute | solution.py:270
  80.3 2.1 %collective-permute-done.18.refs_2_ = f32[96,256]{1,0:T(8,128)S(1)} collective-permute-done((f32[96,256]{1,0:T(8,128)S(1)}, f32[96,256]{1,0:T(8,128)S(1)}, u32[]{:S(2)}, u32[]{:S(2)}) %collective-permute-start.18) | collective-permute-done | bytes 98336 | tf_op jit(solution)/shard_map/ppermute | solution.py:270
  82.4 2.8 %collective-permute-start.20 = (f32[96,256]{1,0:T(8,128)S(1)}, f32[96,256]{1,0:T(8,128)S(1)}, u32[]{:S(2)}, u32[]{:S(2)}) collective-permute-start(f32[96,256]{1,0:T(8,128)S(1)} %pad_maximum_fusion.refs_0_), channel_id=1, source_target_pairs={{0,16},{16,0},{32,48},{48,32},{64,80},{80,64},{96,112},{112,96},{1... | collective-permute-start | bytes 294920 | tf_op jit(solution)/shard_map/ppermute | solution.py:513
  89.9 23.4 %factor.1 = (f32[512,512]{1,0:T(8,128)}, bf16[512,512]{1,0:T(8,128)(2,1)S(1)}, bf16[512,512]{1,0:T(8,128)(2,1)S(1)}) custom-call(f32[512,512]{1,0:T(8,128)S(1)} %copy-done.2, f32[96,256]{1,0:T(8,128)S(1)} %pad_maximum_fusion.refs_0_, f32[96,256]{1,0:T(8,128)S(1)} %collective-permute-done.17.refs_1_, f32[96,256]{1,0:T(8,128)S(1)} %collective-permute-done.18.refs_2_, ...), custom_call_target="tpu_custom_call" | custom-call | flops 1000000 | bytes 65536 | tf_op jit(solution)/shard_map/factor/pallas_call | solution.py:397
  114.6 5.0 %finish_near.1.refs_2_ = f32[8,256,512]{2,1,0:T(8,128)} custom-call(s32[12]{0:T(128)S(1)} %bitcast.50, bf16[512,512]{1,0:T(8,128)(2,1)S(1)} %get-tuple-element.61.head_ref, bf16[512,512]{1,0:T(8,128)(2,1)S(1)} %get-tuple-element.62.tail_ref, f32[2,256,512]{2,1,0:T(8,128)S(1)} %copy-done.3, f32[2,2,256,512]{3,2,1,0:T(8,128)} %collective-permute-done.refs_1_, ...), custom_call_target="tpu_custom_call" | custom-call | flops 1000000 | bytes 65536 | tf_op jit(solution)/shard_map/finish_near/pallas_call | solution.py:457
  119.6 3.9 %finish_far.1 = f32[8,256,512]{2,1,0:T(8,128)} custom-call(s32[4]{0:T(128)S(1)} %slice.74.slot_ref, bf16[512,512]{1,0:T(8,128)(2,1)S(1)} %get-tuple-element.61.head_ref, bf16[512,512]{1,0:T(8,128)(2,1)S(1)} %get-tuple-element.62.tail_ref, f32[2,2,256,512]{3,2,1,0:T(8,128)} %collective-permute-done.24.refs_0_.refs_1_, ...), custom_call_target="tpu_custom_call", output_to_operand_aliasing={{}: (5, {})} | custom-call | flops 1000000 | bytes 65536 | tf_op jit(solution)/shard_map/finish_far/pallas_call | solution.py:457
  (64 shorter events, 27.1 us)
Async XLA Ops:
  4.9 14.6 %collective-permute-start = (f32[2,2,256,512]{3,2,1,0:T(8,128)}, f32[2,2,256,512]{3,2,1,0:T(8,128)}, u32[]{:S(2)}, u32[]{:S(2)}) collective-permute-start(f32[2,2,256,512]{3,2,1,0:T(8,128)} %get-tuple-element.45), channel_id=1, source_target_pairs={{0,16},{16,0},{32,48},{48,32},{64,80},{80,64},{96,112},{112,96},{1... | collective-permute-start | bytes 6291464 | tf_op jit(solution)/shard_map/ppermute | solution.py:513
  6.9 51.8 %collective-permute-start.12 = (f32[2,2,256,512]{3,2,1,0:T(8,128)}, f32[2,2,256,512]{3,2,1,0:T(8,128)S(1)}, u32[]{:S(2)}, u32[]{:S(2)}) collective-permute-start(f32[2,2,256,512]{3,2,1,0:T(8,128)} %get-tuple-element.50), channel_id=1, source_target_pairs={{0,32},{16,48},{32,64},{48,80},{64,96},{80,112},{96,0},{112,16},{1... | collective-permute-start | bytes 6291464 | tf_op jit(solution)/shard_map/ppermute | solution.py:510
  10.7 48.1 %collective-permute-start.13 = (f32[2,2,256,512]{3,2,1,0:T(8,128)}, f32[2,2,256,512]{3,2,1,0:T(8,128)}, u32[]{:S(2)}, u32[]{:S(2)}) collective-permute-start(f32[2,2,256,512]{3,2,1,0:T(8,128)} %get-tuple-element.51), channel_id=1, source_target_pairs={{0,96},{16,112},{32,0},{48,16},{64,32},{80,48},{96,64},{112,80},{1... | collective-permute-start | bytes 6291464 | tf_op jit(solution)/shard_map/ppermute | solution.py:510
  20.5 7.0 %collective-permute-start.1 = (f32[384,256]{1,0:T(8,128)S(1)}, f32[384,256]{1,0:T(8,128)S(1)}, u32[]{:S(2)}, u32[]{:S(2)}) collective-permute-start(f32[384,256]{1,0:T(8,128)S(1)} %dynamic-slice_bitcast_fusion), channel_id=1, source_target_pairs={{0,16},{16,0},{32,48},{48,32},{64,80},{80,64},{96,112},{112,96},{1... | collective-permute-start | bytes 1179656 | tf_op jit(solution)/shard_map/ppermute | solution.py:256
  28.6 7.4 %collective-permute-start.2 = (f32[96,256]{1,0:T(8,128)S(1)}, f32[96,256]{1,0:T(8,128)S(1)}, u32[]{:S(2)}, u32[]{:S(2)}) collective-permute-start(f32[96,256]{1,0:T(8,128)S(1)} %get-tuple-element.70), channel_id=1, source_target_pairs={{0,1},{1,2},{2,3},{3,0},{4,5},{5,6},{6,7},{7,4},{8,9},{9,10},{10,1... | collective-permute-start | bytes 294920 | tf_op jit(solution)/shard_map/ppermute | solution.py:256
  33.1 5.4 %collective-permute-start.3 = (f32[96,256]{1,0:T(8,128)S(1)}, f32[96,256]{1,0:T(8,128)S(1)}, u32[]{:S(2)}, u32[]{:S(2)}) collective-permute-start(f32[96,256]{1,0:T(8,128)S(1)} %get-tuple-element.72), channel_id=1, source_target_pairs={{0,2},{1,3},{2,0},{3,1},{4,6},{5,7},{6,4},{7,5},{8,10},{9,11},{10,... | collective-permute-start | bytes 294920 | tf_op jit(solution)/shard_map/ppermute | solution.py:256
  34.0 4.5 %collective-permute-start.4 = (f32[96,256]{1,0:T(8,128)S(1)}, f32[96,256]{1,0:T(8,128)S(1)}, u32[]{:S(2)}, u32[]{:S(2)}) collective-permute-start(f32[96,256]{1,0:T(8,128)S(1)} %get-tuple-element.71), channel_id=1, source_target_pairs={{0,3},{1,0},{2,1},{3,2},{4,7},{5,4},{6,5},{7,6},{8,11},{9,8},{10,9... | collective-permute-start | bytes 294920 | tf_op jit(solution)/shard_map/ppermute | solution.py:256
  38.6 6.5 %collective-permute-start.5 = (f32[24,256]{1,0:T(8,128)S(1)}, f32[24,256]{1,0:T(8,128)S(1)}, u32[]{:S(2)}, u32[]{:S(2)}) collective-permute-start(f32[24,256]{1,0:T(8,128)S(1)} %get-tuple-element.77), channel_id=1, source_target_pairs={{0,4},{1,5},{2,6},{3,7},{4,8},{5,9},{6,10},{7,11},{8,12},{9,13},{1... | collective-permute-start | bytes 73736 | tf_op jit(solution)/shard_map/ppermute | solution.py:256
  40.8 6.4 %collective-permute-start.6 = (f32[24,256]{1,0:T(8,128)S(1)}, f32[24,256]{1,0:T(8,128)S(1)}, u32[]{:S(2)}, u32[]{:S(2)}) collective-permute-start(f32[24,256]{1,0:T(8,128)S(1)} %get-tuple-element.79), channel_id=1, source_target_pairs={{0,8},{1,9},{2,10},{3,11},{4,12},{5,13},{6,14},{7,15},{8,0},{9,1},... | collective-permute-start | bytes 73736 | tf_op jit(solution)/shard_map/ppermute | solution.py:256
  43.0 4.1 %collective-permute-start.7 = (f32[24,256]{1,0:T(8,128)S(1)}, f32[24,256]{1,0:T(8,128)S(1)}, u32[]{:S(2)}, u32[]{:S(2)}) collective-permute-start(f32[24,256]{1,0:T(8,128)S(1)} %get-tuple-element.78), channel_id=1, source_target_pairs={{0,12},{1,13},{2,14},{3,15},{4,0},{5,1},{6,2},{7,3},{8,4},{9,5},{1... | collective-permute-start | bytes 73736 | tf_op jit(solution)/shard_map/ppermute | solution.py:256
  45.0 2.9 %collective-permute-start.8 = (f32[8,128]{1,0:T(8,128)S(1)}, f32[8,128]{1,0:T(8,128)S(1)}, u32[]{:S(2)}, u32[]{:S(2)}) collective-permute-start(f32[8,128]{1,0:T(8,128)S(1)} %scatter.4), channel_id=1, source_target_pairs={{0,16},{16,0},{32,48},{48,32},{64,80},{80,64},{96,112},{112,96},{1... | collective-permute-start | bytes 12296 | tf_op jit(solution)/shard_map/ppermute | solution.py:513
  48.0 12.1 %collective-permute-start.10 = (f32[32,256]{1,0:T(8,128)S(1)}, f32[32,256]{1,0:T(8,128)S(1)}, u32[]{:S(2)}, u32[]{:S(2)}) collective-permute-start(f32[32,256]{1,0:T(8,128)S(1)} %maximum_maximum_fusion), channel_id=1, source_target_pairs={{0,64},{16,80},{32,96},{48,112},{64,0},{80,16},{96,32},{112,48},{1... | collective-permute-start | bytes 98312 | tf_op jit(solution)/shard_map/ppermute | solution.py:270
  49.8 10.4 %collective-permute-start.11 = (f32[32,256]{1,0:T(8,128)S(1)}, f32[32,256]{1,0:T(8,128)S(1)}, u32[]{:S(2)}, u32[]{:S(2)}) collective-permute-start(f32[32,256]{1,0:T(8,128)S(1)} %maximum_maximum_fusion), channel_id=1, source_target_pairs={{0,32},{16,48},{32,64},{48,80},{64,96},{80,112},{96,0},{112,16},{1... | collective-permute-start | bytes 98312 | tf_op jit(solution)/shard_map/ppermute | solution.py:270
  50.2 9.9 %collective-permute-start.9 = (f32[32,256]{1,0:T(8,128)S(1)}, f32[32,256]{1,0:T(8,128)S(1)}, u32[]{:S(2)}, u32[]{:S(2)}) collective-permute-start(f32[32,256]{1,0:T(8,128)S(1)} %maximum_maximum_fusion), channel_id=1, source_target_pairs={{0,96},{16,112},{32,0},{48,16},{64,32},{80,48},{96,64},{112,80},{1... | collective-permute-start | bytes 98312 | tf_op jit(solution)/shard_map/ppermute | solution.py:270
  60.1 59.4 %collective-permute-start.24 = (f32[2,2,256,512]{3,2,1,0:T(8,128)}, f32[2,2,256,512]{3,2,1,0:T(8,128)}, u32[]{:S(2)}, u32[]{:S(2)}) collective-permute-start(f32[2,2,256,512]{3,2,1,0:T(8,128)} %slice_dynamic-update-slice_fusion), channel_id=1, source_target_pairs={{0,64},{16,80},{32,96},{48,112},{64,0},{80,16},{96,32},{112,48},{1... | collective-permute-start | bytes 6291464 | tf_op jit(solution)/shard_map/ppermute | solution.py:510
  65.5 47.9 %collective-permute-start.25 = (f32[2,256,512]{2,1,0:T(8,128)}, f32[2,256,512]{2,1,0:T(8,128)}, u32[]{:S(2)}, u32[]{:S(2)}) collective-permute-start(f32[2,256,512]{2,1,0:T(8,128)} %get-tuple-element.67), channel_id=1, source_target_pairs={{0,16},{16,0},{32,48},{48,32},{64,80},{80,64},{96,112},{112,96},{1... | collective-permute-start | bytes 3145736 | tf_op jit(solution)/shard_map/ppermute | solution.py:513
  66.9 46.5 %collective-permute-start.26 = (f32[2,256,512]{2,1,0:T(8,128)}, f32[2,256,512]{2,1,0:T(8,128)}, u32[]{:S(2)}, u32[]{:S(2)}) collective-permute-start(f32[2,256,512]{2,1,0:T(8,128)} %get-tuple-element.68), channel_id=1, source_target_pairs={{0,16},{16,0},{32,48},{48,32},{64,80},{80,64},{96,112},{112,96},{1... | collective-permute-start | bytes 3145736 | tf_op jit(solution)/shard_map/ppermute | solution.py:513
  67.0 4.3 %collective-permute-start.14 = (f32[24,256]{1,0:T(8,128)S(1)}, f32[24,256]{1,0:T(8,128)S(1)}, u32[]{:S(2)}, u32[]{:S(2)}) collective-permute-start(f32[24,256]{1,0:T(8,128)S(1)} %select_add_fusion), channel_id=1, source_target_pairs={{0,4},{1,5},{2,6},{3,7},{4,8},{5,9},{6,10},{7,11},{8,12},{9,13},{1... | collective-permute-start | bytes 73736 | tf_op jit(solution)/shard_map/ppermute | solution.py:270
  68.5 4.6 %collective-permute-start.15 = (f32[24,256]{1,0:T(8,128)S(1)}, f32[24,256]{1,0:T(8,128)S(1)}, u32[]{:S(2)}, u32[]{:S(2)}) collective-permute-start(f32[24,256]{1,0:T(8,128)S(1)} %select_add_fusion), channel_id=1, source_target_pairs={{0,8},{1,9},{2,10},{3,11},{4,12},{5,13},{6,14},{7,15},{8,0},{9,1},... | collective-permute-start | bytes 73736 | tf_op jit(solution)/shard_map/ppermute | solution.py:270
  71.3 3.1 %collective-permute-start.16 = (f32[24,256]{1,0:T(8,128)S(1)}, f32[24,256]{1,0:T(8,128)S(1)}, u32[]{:S(2)}, u32[]{:S(2)}) collective-permute-start(f32[24,256]{1,0:T(8,128)S(1)} %select_add_fusion), channel_id=1, source_target_pairs={{0,12},{1,13},{2,14},{3,15},{4,0},{5,1},{6,2},{7,3},{8,4},{9,5},{1... | collective-permute-start | bytes 73736 | tf_op jit(solution)/shard_map/ppermute | solution.py:270
  74.4 4.5 %collective-permute-start.17 = (f32[96,256]{1,0:T(8,128)S(1)}, f32[96,256]{1,0:T(8,128)S(1)}, u32[]{:S(2)}, u32[]{:S(2)}) collective-permute-start(f32[96,256]{1,0:T(8,128)S(1)} %pad_maximum_fusion.refs_0_), channel_id=1, source_target_pairs={{0,3},{1,0},{2,1},{3,2},{4,7},{5,4},{6,5},{7,6},{8,11},{9,8},{10,9... | collective-permute-start | bytes 294920 | tf_op jit(solution)/shard_map/ppermute | solution.py:270
  77.0 5.4 %collective-permute-start.18 = (f32[96,256]{1,0:T(8,128)S(1)}, f32[96,256]{1,0:T(8,128)S(1)}, u32[]{:S(2)}, u32[]{:S(2)}) collective-permute-start(f32[96,256]{1,0:T(8,128)S(1)} %pad_maximum_fusion.refs_0_), channel_id=1, source_target_pairs={{0,2},{1,3},{2,0},{3,1},{4,6},{5,7},{6,4},{7,5},{8,10},{9,11},{10,... | collective-permute-start | bytes 294920 | tf_op jit(solution)/shard_map/ppermute | solution.py:270
  78.9 7.0 %collective-permute-start.19 = (f32[96,256]{1,0:T(8,128)S(1)}, f32[96,256]{1,0:T(8,128)S(1)}, u32[]{:S(2)}, u32[]{:S(2)}) collective-permute-start(f32[96,256]{1,0:T(8,128)S(1)} %pad_maximum_fusion.refs_0_), channel_id=1, source_target_pairs={{0,1},{1,2},{2,3},{3,0},{4,5},{5,6},{6,7},{7,4},{8,9},{9,10},{10,1... | collective-permute-start | bytes 294920 | tf_op jit(solution)/shard_map/ppermute | solution.py:270
  82.4 5.3 %collective-permute-start.20 = (f32[96,256]{1,0:T(8,128)S(1)}, f32[96,256]{1,0:T(8,128)S(1)}, u32[]{:S(2)}, u32[]{:S(2)}) collective-permute-start(f32[96,256]{1,0:T(8,128)S(1)} %pad_maximum_fusion.refs_0_), channel_id=1, source_target_pairs={{0,16},{16,0},{32,48},{48,32},{64,80},{80,64},{96,112},{112,96},{1... | collective-permute-start | bytes 294920 | tf_op jit(solution)/shard_map/ppermute | solution.py:513
  (8 other events, 111.3 us)

commit v8 on v6

--- a/solution.py
+++ b/solution.py
@@ -12,6 +12,7 @@
 PIVOT = 8
 HALF = 256
 PAIR = 2
+SPARE = 8
 GROUP = 4
 
 
@@ -142,8 +143,11 @@
     step = pl.program_id(0)
     tiles = tile_ref.shape[0]
 
+    height = tile_ref.shape[1]
+
     def kept(i, target, rank):
-        return pltpu.make_async_copy(tile_ref.at[i], target.at[rank], sems.at[i])
+        rows = pl.ds(pl.multiple_of(rank * height, 8), height)
+        return pltpu.make_async_copy(tile_ref.at[i], target.at[rows], sems.at[i])
 
     @pl.when(step == 0)
     def _():
@@ -154,7 +158,7 @@
         cross[...] = jnp.zeros_like(cross)
 
     for i in range(tiles):
-        for pair, target in ((0, own_ref), (4, far_ref.at[0])):
+        for pair, target in ((0, own_ref), (4, far_ref)):
             seat = seat_ref[tiles * step + i]
 
             @pl.when((tiles * step + i < count_ref[0]) & (seat // PAIR == pair))
@@ -198,14 +202,14 @@
 
 def gram(tiles, inverse_factor, tile_count, seats):
     capacity, rows, columns = tiles.shape
-    pair = jax.ShapeDtypeStruct((PAIR, rows, columns), jnp.float32)
+    pair = jax.ShapeDtypeStruct((PAIR * rows, columns), jnp.float32)
     hbm = pl.BlockSpec(memory_space=pl.ANY)
     return pl.pallas_call(
         gram_kernel,
         out_shape=(
             jax.ShapeDtypeStruct((3 * HALF, HALF), jnp.float32),
             pair,
-            jax.ShapeDtypeStruct((2, PAIR, rows, columns), jnp.float32),
+            jax.ShapeDtypeStruct((2 * PAIR * rows + SPARE, columns), jnp.float32),
         ),
         grid_spec=pltpu.PrefetchScalarGridSpec(
             num_scalar_prefetch=2,
@@ -419,14 +423,19 @@
     out_ref, tiles, results, slots, in_sems, out_sems = refs[-6:]
     count = jnp.int32(0)
     for p, place in enumerate(pairs):
-        source = refs[p].at[place] if place is not None else refs[p]
+        flat = len(refs[p].shape) == 2
+        first = PAIR * place if flat else 0
+        source = refs[p] if flat else refs[p].at[place]
+        height = tiles.shape[1]
         for rank in range(PAIR):
             slot = slot_ref[PAIR * p + rank]
 
             @pl.when(slot >= 0)
-            def _(source=source, rank=rank, slot=slot, count=count):
+            def _(source=source, rank=rank, slot=slot, count=count, first=first):
                 slots[count] = slot
-                pltpu.make_async_copy(source.at[rank], tiles.at[count], in_sems.at[count]).start()
+                rows = pl.ds((first + rank) * height, height)
+                own_rows = source.at[rows] if len(source.shape) == 2 else source.at[rank]
+                pltpu.make_async_copy(own_rows, tiles.at[count], in_sems.at[count]).start()
 
             count = count + jnp.where(slot >= 0, 1, 0)
 
@@ -448,8 +457,8 @@
         result_copy(j, 0).wait()
 
 
-def finish(slots, head, tail, received, pairs, before, name):
-    rows, columns = received[0].shape[-2:]
+def finish(slots, head, tail, received, pairs, before, name, rows):
+    columns = received[0].shape[-1]
     most = min(PAIR * len(pairs), OWN_TILES)
     hbm = pl.BlockSpec(memory_space=pl.ANY)
     vmem = pl.BlockSpec(memory_space=pltpu.VMEM)
@@ -525,7 +534,9 @@
         value = scatter_sum(value, axis, span, stride)
     height = value.shape[0]
     parts = from_ahead(jnp.concatenate([value, tables], 0), "scene", chips, 2)
-    far = lax.dynamic_update_slice_in_dim(far, crossed[1:], 1, 0)
+    far = lax.dynamic_update_slice_in_dim(
+        far, crossed[1].reshape(PAIR * tile_rows, columns), PAIR * tile_rows, 0
+    )
     *parts, far, from_below, from_above = lax.optimization_barrier(
         (*parts, far, from_below, from_above)
     )
@@ -548,9 +559,9 @@
     upper, head, tail = factor(pieces, inverse_factor, scenes * rows * OWN_TILES * tile_rows)
     near = [own, crossed, from_below, from_above, passed_on, passed_on]
     first = PAIR * len(near)
-    out = finish(slots[:first], head, tail, near, (None, 0, 0, 0, 0, 1), None, "finish_near")
+    out = finish(slots[:first], head, tail, near, (0, 0, 0, 0, 0, 1), None, "finish_near", tile_rows)
     far = [far_in, far_in]
-    return finish(slots[first:], head, tail, far, (0, 1), out, "finish_far"), upper
+    return finish(slots[first:], head, tail, far, (0, 1), out, "finish_far", tile_rows), upper
 
 
 def solution(mesh):

time: 120 us -> 119 us (level); the launches traced: 118 us -> 120 us
  starting transfers between devices: 42.1 us -> 51.3 us
  Pallas kernels: 53.1 us -> 44.5 us
  waiting for transfers between devices: 14.8 us -> 16.3 us
    ppermute x7, starting transfers between devices: 9.69 us -> 18.3 us  [scatter_sum(): lax.ppermute(sent, axis, ring_pairs(size, span, stride, shift))]
    pallas_call x1, Pallas kernels: 14.5 us -> 6.9 us  [gram(): pl.pallas_call(gram_kernel, out_shape=(jax.ShapeDtypeStruct((3 * HALF, HA...]
    ppermute x3, starting transfers between devices: 4.51 us -> 8.6 us  [along_z(): return lax.ppermute(value, 'scene', ring_pairs(scenes, chips, 2, up))]
    pallas_call x1, Pallas kernels: 6.03 us -> 3.21 us  [pack(): pl.pallas_call(pack_kernel, out_shape=(two_pairs, two_pairs, two_pairs, t...]
    ppermute x7, waiting for transfers between devices: 6.82 us -> 4.26 us  [scatter_sum(): lax.ppermute(sent, axis, ring_pairs(size, span, stride, shift))]
    ppermute x9, waiting for transfers between devices: 2.71 us -> 5.21 us  [from_ahead(): lax.ppermute(value, axis, ring_pairs(size, span, stride, span - ahead))]
    ppermute x9, starting transfers between devices: 15.3 us -> 13.1 us  [from_ahead(): lax.ppermute(value, axis, ring_pairs(size, span, stride, span - ahead))]
    pallas_call x2, Pallas kernels: 6.19 us -> 7.92 us  [finish(): pl.pallas_call(functools.partial(finish_kernel, pairs), out_shape=jax.Sha...]
  transfers between devices with their start and end apart: 26 -> 26, of which waited for: 13 -> 11; matrix products, arithmetic and copies ran while one was open for 4% -> 4% of each run, Pallas kernels for 37% -> 32%
where the time goes in v8:
time: 119 us; the launch traced here: 120 us
  starting transfers between devices  51.3 us (43%)
  Pallas kernels  44.5 us (37%)
  waiting for transfers between devices  16.3 us (14%)
  local copies, waits for them, and re-layouts  5.01 us (4%)
  between operations  1.74 us (1%)
    pallas_call x1, Pallas kernels, factor(): pl.pallas_call(functools.partial(factor_kernel, row_count), out_shape=(ja...  23.4 us
    ppermute x7, starting transfers between devices, scatter_sum(): lax.ppermute(sent, axis, ring_pairs(size, span, stride, shift))  18.3 us
    ppermute x9, starting transfers between devices, from_ahead(): lax.ppermute(value, axis, ring_pairs(size, span, stride, span - ahead))  13.1 us
    ppermute x7, starting transfers between devices, other_core(): return lax.ppermute(value, 'scene', ring_pairs(scenes, 2, 1, 1))  11.3 us
    ppermute x3, starting transfers between devices, along_z(): return lax.ppermute(value, 'scene', ring_pairs(scenes, chips, 2, up))  8.6 us
    pallas_call x2, Pallas kernels, finish(): pl.pallas_call(functools.partial(finish_kernel, pairs), out_shape=jax.Sha...  7.92 us
    pallas_call x1, Pallas kernels, gram(): pl.pallas_call(gram_kernel, out_shape=(jax.ShapeDtypeStruct((3 * HALF, HA...  6.9 us
    ppermute x9, waiting for transfers between devices, from_ahead(): lax.ppermute(value, axis, ring_pairs(size, span, stride, span - ahead))  5.21 us
  transfers between devices with their start and end apart: 26, of which 11 were waited for; matrix products, arithmetic and copies ran while one was open for 4% of the time, Pallas kernels for 32%

profile of v8, /device:TPU:1, one launch (start us, length us, event | category | flops | bytes accessed | tf_op | source)
XLA Modules:
  0.0 119.9 jit_solution(14927882124535044409)
XLA Ops:
  1.3 3.2 %pack.1 = (f32[2,2,256,512]{3,2,1,0:T(8,128)}, f32[2,2,256,512]{3,2,1,0:T(8,128)}, f32[2,2,256,512]{3,2,1,0:T(8,128)}, s32[16]{0:T(128)}, s32[16]{0:T(128)}) custom-call(s32[1]{0:T(128)S(6)} %copy.10.count_ref, s32[16]{0:T(128)} %owner_ref.1, s32[16]{0:T(128)} %slot_ref.1, f32[16,256,512]{2,1,0:T(8,128)} %tile_ref), custom_call_target="tpu_custom_call" | custom-call | bytes 8388608 | tf_op jit(solution)/shard_map/pack/pallas_call | solution.py:124
  4.5 1.9 %collective-permute-start = (f32[2,2,256,512]{3,2,1,0:T(8,128)}, f32[2,2,256,512]{3,2,1,0:T(8,128)}, u32[]{:S(2)}, u32[]{:S(2)}) collective-permute-start(f32[2,2,256,512]{3,2,1,0:T(8,128)} %get-tuple-element.43), channel_id=1, source_target_pairs={{0,16},{16,0},{32,48},{48,32},{64,80},{80,64},{96,112},{112,96},{1... | collective-permute-start | bytes 6291464 | tf_op jit(solution)/shard_map/ppermute | solution.py:522
  6.4 3.5 %collective-permute-start.12 = (f32[2,2,256,512]{3,2,1,0:T(8,128)}, f32[2,2,256,512]{3,2,1,0:T(8,128)S(1)}, u32[]{:S(2)}, u32[]{:S(2)}) collective-permute-start(f32[2,2,256,512]{3,2,1,0:T(8,128)} %get-tuple-element.48), channel_id=1, source_target_pairs={{0,32},{16,48},{32,64},{48,80},{64,96},{80,112},{96,0},{112,16},{1... | collective-permute-start | bytes 6291464 | tf_op jit(solution)/shard_map/ppermute | solution.py:519
  9.9 2.9 %collective-permute-start.13 = (f32[2,2,256,512]{3,2,1,0:T(8,128)}, f32[2,2,256,512]{3,2,1,0:T(8,128)}, u32[]{:S(2)}, u32[]{:S(2)}) collective-permute-start(f32[2,2,256,512]{3,2,1,0:T(8,128)} %get-tuple-element.49), channel_id=1, source_target_pairs={{0,96},{16,112},{32,0},{48,16},{64,32},{80,48},{96,64},{112,80},{1... | collective-permute-start | bytes 6291464 | tf_op jit(solution)/shard_map/ppermute | solution.py:519
  12.8 6.9 %gram.1 = (f32[768,256]{1,0:T(8,128)}, f32[512,512]{1,0:T(8,128)}, f32[1032,512]{1,0:T(8,128)}) custom-call(s32[1]{0:T(128)S(6)} %copy.10.count_ref, s32[16]{0:T(128)} %get-tuple-element.40.seat_ref, f32[16,256,512]{2,1,0:T(8,128)} %tile_ref, f32[512,512]{1,0:T(8,128)} %inverse_ref.3), custom_call_target="tpu_custom_call" | custom-call | flops 1000000 | bytes 65536 | tf_op jit(solution)/shard_map/gram/pallas_call | solution.py:207
  20.8 3.2 %collective-permute-start.1 = (f32[384,256]{1,0:T(8,128)S(1)}, f32[384,256]{1,0:T(8,128)S(1)}, u32[]{:S(2)}, u32[]{:S(2)}) collective-permute-start(f32[384,256]{1,0:T(8,128)S(1)} %dynamic-slice_bitcast_fusion), channel_id=1, source_target_pairs={{0,16},{16,0},{32,48},{48,32},{64,80},{80,64},{96,112},{112,96},{1... | collective-permute-start | bytes 1179656 | tf_op jit(solution)/shard_map/ppermute | solution.py:260
  27.5 6.5 %collective-permute-start.3 = (f32[96,256]{1,0:T(8,128)S(1)}, f32[96,256]{1,0:T(8,128)S(1)}, u32[]{:S(2)}, u32[]{:S(2)}) collective-permute-start(f32[96,256]{1,0:T(8,128)S(1)} %get-tuple-element.68), channel_id=1, source_target_pairs={{0,2},{1,3},{2,0},{3,1},{4,6},{5,7},{6,4},{7,5},{8,10},{9,11},{10,... | collective-permute-start | bytes 294920 | tf_op jit(solution)/shard_map/ppermute | solution.py:260
  34.0 2.0 %collective-permute-start.4 = (f32[96,256]{1,0:T(8,128)S(1)}, f32[96,256]{1,0:T(8,128)S(1)}, u32[]{:S(2)}, u32[]{:S(2)}) collective-permute-start(f32[96,256]{1,0:T(8,128)S(1)} %get-tuple-element.67), channel_id=1, source_target_pairs={{0,3},{1,0},{2,1},{3,2},{4,7},{5,4},{6,5},{7,6},{8,11},{9,8},{10,9... | collective-permute-start | bytes 294920 | tf_op jit(solution)/shard_map/ppermute | solution.py:260
  36.0 2.9 %collective-permute-done.3 = f32[96,256]{1,0:T(8,128)S(1)} collective-permute-done((f32[96,256]{1,0:T(8,128)S(1)}, f32[96,256]{1,0:T(8,128)S(1)}, u32[]{:S(2)}, u32[]{:S(2)}) %collective-permute-start.3) | collective-permute-done | bytes 98336 | tf_op jit(solution)/shard_map/ppermute | solution.py:260
  40.7 3.8 %collective-permute-start.6 = (f32[24,256]{1,0:T(8,128)S(1)}, f32[24,256]{1,0:T(8,128)S(1)}, u32[]{:S(2)}, u32[]{:S(2)}) collective-permute-start(f32[24,256]{1,0:T(8,128)S(1)} %get-tuple-element.75), channel_id=1, source_target_pairs={{0,8},{1,9},{2,10},{3,11},{4,12},{5,13},{6,14},{7,15},{8,0},{9,1},... | collective-permute-start | bytes 73736 | tf_op jit(solution)/shard_map/ppermute | solution.py:260
  50.7 2.1 %collective-permute-start.9 = (f32[32,256]{1,0:T(8,128)S(1)}, f32[32,256]{1,0:T(8,128)S(1)}, u32[]{:S(2)}, u32[]{:S(2)}) collective-permute-start(f32[32,256]{1,0:T(8,128)S(1)} %maximum_maximum_fusion), channel_id=1, source_target_pairs={{0,96},{16,112},{32,0},{48,16},{64,32},{80,48},{96,64},{112,80},{1... | collective-permute-start | bytes 98312 | tf_op jit(solution)/shard_map/ppermute | solution.py:274
  53.8 4.8 %collective-permute-done.12.first_ref.refs_2_ = f32[2,2,256,512]{3,2,1,0:T(8,128)S(1)} collective-permute-done((f32[2,2,256,512]{3,2,1,0:T(8,128)}, f32[2,2,256,512]{3,2,1,0:T(8,128)S(1)}, u32[]{:S(2)}, u32[]{:S(2)}) %collective-permute-start.12) | collective-permute-done | bytes 2097184 | tf_op jit(solution)/shard_map/ppermute | solution.py:519
  59.9 2.2 %collective-permute-start.24 = (f32[1032,512]{1,0:T(8,128)}, f32[1032,512]{1,0:T(8,128)S(1)}, u32[]{:S(2)}, u32[]{:S(2)}) collective-permute-start(f32[1032,512]{1,0:T(8,128)} %constant_dynamic-update-slice_fusion), channel_id=1, source_target_pairs={{0,64},{16,80},{32,96},{48,112},{64,0},{80,16},{96,32},{112,48},{1... | collective-permute-start | bytes 6340616 | tf_op jit(solution)/shard_map/ppermute | solution.py:519
  62.1 3.0 %second_pairs.1 = f32[2,2,256,512]{3,2,1,0:T(8,128)} custom-call(f32[2,2,256,512]{3,2,1,0:T(8,128)} %copy-done, f32[2,2,256,512]{3,2,1,0:T(8,128)} %collective-permute-done.13.second_ref.refs_3_), custom_call_target="tpu_custom_call" | custom-call | flops 1000000 | bytes 65536 | tf_op jit(solution)/shard_map/second_pairs/pallas_call | solution.py:500
  65.2 1.8 %collective-permute-start.25 = (f32[2,2,256,512]{3,2,1,0:T(8,128)}, f32[2,2,256,512]{3,2,1,0:T(8,128)}, u32[]{:S(2)}, u32[]{:S(2)}) collective-permute-start(f32[2,2,256,512]{3,2,1,0:T(8,128)} %second_pairs.1), channel_id=1, source_target_pairs={{0,16},{16,0},{32,48},{48,32},{64,80},{80,64},{96,112},{112,96},{1... | collective-permute-start | bytes 6291464 | tf_op jit(solution)/shard_map/ppermute | solution.py:522
  67.0 1.9 %collective-permute-start.14 = (f32[24,256]{1,0:T(8,128)S(1)}, f32[24,256]{1,0:T(8,128)S(1)}, u32[]{:S(2)}, u32[]{:S(2)}) collective-permute-start(f32[24,256]{1,0:T(8,128)S(1)} %select_add_fusion), channel_id=1, source_target_pairs={{0,4},{1,5},{2,6},{3,7},{4,8},{5,9},{6,10},{7,11},{8,12},{9,13},{1... | collective-permute-start | bytes 73736 | tf_op jit(solution)/shard_map/ppermute | solution.py:274
  71.5 1.8 %collective-permute-done.15 = f32[24,256]{1,0:T(8,128)S(1)} collective-permute-done((f32[24,256]{1,0:T(8,128)S(1)}, f32[24,256]{1,0:T(8,128)S(1)}, u32[]{:S(2)}, u32[]{:S(2)}) %collective-permute-start.15) | collective-permute-done | bytes 24608 | tf_op jit(solution)/shard_map/ppermute | solution.py:274
  73.4 3.7 %collective-permute-start.17 = (f32[96,256]{1,0:T(8,128)S(1)}, f32[96,256]{1,0:T(8,128)S(1)}, u32[]{:S(2)}, u32[]{:S(2)}) collective-permute-start(f32[96,256]{1,0:T(8,128)S(1)} %pad_maximum_fusion.refs_0_), channel_id=1, source_target_pairs={{0,3},{1,0},{2,1},{3,2},{4,7},{5,4},{6,5},{7,6},{8,11},{9,8},{10,9... | collective-permute-start | bytes 294920 | tf_op jit(solution)/shard_map/ppermute | solution.py:274
  77.8 1.9 %collective-permute-done.17.refs_1_ = f32[96,256]{1,0:T(8,128)S(1)} collective-permute-done((f32[96,256]{1,0:T(8,128)S(1)}, f32[96,256]{1,0:T(8,128)S(1)}, u32[]{:S(2)}, u32[]{:S(2)}) %collective-permute-start.17) | collective-permute-done | bytes 98336 | tf_op jit(solution)/shard_map/ppermute | solution.py:274
  79.7 2.5 %collective-permute-start.20 = (f32[96,256]{1,0:T(8,128)S(1)}, f32[96,256]{1,0:T(8,128)S(1)}, u32[]{:S(2)}, u32[]{:S(2)}) collective-permute-start(f32[96,256]{1,0:T(8,128)S(1)} %pad_maximum_fusion.refs_0_), channel_id=1, source_target_pairs={{0,16},{16,0},{32,48},{48,32},{64,80},{80,64},{96,112},{112,96},{1... | collective-permute-start | bytes 294920 | tf_op jit(solution)/shard_map/ppermute | solution.py:522
  82.4 2.8 %collective-permute-start.21 = (f32[96,256]{1,0:T(8,128)S(1)}, f32[96,256]{1,0:T(8,128)S(1)}, u32[]{:S(2)}, u32[]{:S(2)}) collective-permute-start(f32[96,256]{1,0:T(8,128)S(1)} %collective-permute-done.17.refs_1_), channel_id=1, source_target_pairs={{0,16},{16,0},{32,48},{48,32},{64,80},{80,64},{96,112},{112,96},{1... | collective-permute-start | bytes 294920 | tf_op jit(solution)/shard_map/ppermute | solution.py:522
  87.1 23.4 %factor.1 = (f32[512,512]{1,0:T(8,128)}, bf16[512,512]{1,0:T(8,128)(2,1)S(1)}, bf16[512,512]{1,0:T(8,128)(2,1)S(1)}) custom-call(f32[512,512]{1,0:T(8,128)S(1)} %copy-done.2, f32[96,256]{1,0:T(8,128)S(1)} %pad_maximum_fusion.refs_0_, f32[96,256]{1,0:T(8,128)S(1)} %collective-permute-done.17.refs_1_, f32[96,256]{1,0:T(8,128)S(1)} %collective-permute-done.18.refs_2_, ...), custom_call_target="tpu_custom_call" | custom-call | flops 1000000 | bytes 65536 | tf_op jit(solution)/shard_map/factor/pallas_call | solution.py:401
  111.8 5.4 %finish_near.1.refs_2_ = f32[8,256,512]{2,1,0:T(8,128)} custom-call(s32[12]{0:T(128)S(1)} %bitcast.51, bf16[512,512]{1,0:T(8,128)(2,1)S(1)} %get-tuple-element.59.head_ref, bf16[512,512]{1,0:T(8,128)(2,1)S(1)} %get-tuple-element.60.tail_ref, f32[512,512]{1,0:T(8,128)S(1)} %copy-done.3, f32[2,2,256,512]{3,2,1,0:T(8,128)} %collective-permute-done.refs_1_, ...), custom_call_target="tpu_custom_call" | custom-call | flops 1000000 | bytes 65536 | tf_op jit(solution)/shard_map/finish_near/pallas_call | solution.py:466
  117.3 2.5 %finish_far.1 = f32[8,256,512]{2,1,0:T(8,128)} custom-call(s32[4]{0:T(128)S(1)} %slice.74.slot_ref, bf16[512,512]{1,0:T(8,128)(2,1)S(1)} %get-tuple-element.59.head_ref, bf16[512,512]{1,0:T(8,128)(2,1)S(1)} %get-tuple-element.60.tail_ref, f32[1032,512]{1,0:T(8,128)S(1)} %collective-permute-done.24.refs_0_.refs_1_, ...), custom_call_target="tpu_custom_call", output_to_operand_aliasing={{}: (5, {})} | custom-call | flops 1000000 | bytes 65536 | tf_op jit(solution)/shard_map/finish_far/pallas_call | solution.py:466
  (63 shorter events, 21.4 us)
Async XLA Ops:
  4.5 15.2 %collective-permute-start = (f32[2,2,256,512]{3,2,1,0:T(8,128)}, f32[2,2,256,512]{3,2,1,0:T(8,128)}, u32[]{:S(2)}, u32[]{:S(2)}) collective-permute-start(f32[2,2,256,512]{3,2,1,0:T(8,128)} %get-tuple-element.43), channel_id=1, source_target_pairs={{0,16},{16,0},{32,48},{48,32},{64,80},{80,64},{96,112},{112,96},{1... | collective-permute-start | bytes 6291464 | tf_op jit(solution)/shard_map/ppermute | solution.py:522
  6.4 52.2 %collective-permute-start.12 = (f32[2,2,256,512]{3,2,1,0:T(8,128)}, f32[2,2,256,512]{3,2,1,0:T(8,128)S(1)}, u32[]{:S(2)}, u32[]{:S(2)}) collective-permute-start(f32[2,2,256,512]{3,2,1,0:T(8,128)} %get-tuple-element.48), channel_id=1, source_target_pairs={{0,32},{16,48},{32,64},{48,80},{64,96},{80,112},{96,0},{112,16},{1... | collective-permute-start | bytes 6291464 | tf_op jit(solution)/shard_map/ppermute | solution.py:519
  9.9 48.7 %collective-permute-start.13 = (f32[2,2,256,512]{3,2,1,0:T(8,128)}, f32[2,2,256,512]{3,2,1,0:T(8,128)}, u32[]{:S(2)}, u32[]{:S(2)}) collective-permute-start(f32[2,2,256,512]{3,2,1,0:T(8,128)} %get-tuple-element.49), channel_id=1, source_target_pairs={{0,96},{16,112},{32,0},{48,16},{64,32},{80,48},{96,64},{112,80},{1... | collective-permute-start | bytes 6291464 | tf_op jit(solution)/shard_map/ppermute | solution.py:519
  20.8 4.6 %collective-permute-start.1 = (f32[384,256]{1,0:T(8,128)S(1)}, f32[384,256]{1,0:T(8,128)S(1)}, u32[]{:S(2)}, u32[]{:S(2)}) collective-permute-start(f32[384,256]{1,0:T(8,128)S(1)} %dynamic-slice_bitcast_fusion), channel_id=1, source_target_pairs={{0,16},{16,0},{32,48},{48,32},{64,80},{80,64},{96,112},{112,96},{1... | collective-permute-start | bytes 1179656 | tf_op jit(solution)/shard_map/ppermute | solution.py:260
  26.4 9.6 %collective-permute-start.2 = (f32[96,256]{1,0:T(8,128)S(1)}, f32[96,256]{1,0:T(8,128)S(1)}, u32[]{:S(2)}, u32[]{:S(2)}) collective-permute-start(f32[96,256]{1,0:T(8,128)S(1)} %get-tuple-element.66), channel_id=1, source_target_pairs={{0,1},{1,2},{2,3},{3,0},{4,5},{5,6},{6,7},{7,4},{8,9},{9,10},{10,1... | collective-permute-start | bytes 294920 | tf_op jit(solution)/shard_map/ppermute | solution.py:260
  27.5 11.4 %collective-permute-start.3 = (f32[96,256]{1,0:T(8,128)S(1)}, f32[96,256]{1,0:T(8,128)S(1)}, u32[]{:S(2)}, u32[]{:S(2)}) collective-permute-start(f32[96,256]{1,0:T(8,128)S(1)} %get-tuple-element.68), channel_id=1, source_target_pairs={{0,2},{1,3},{2,0},{3,1},{4,6},{5,7},{6,4},{7,5},{8,10},{9,11},{10,... | collective-permute-start | bytes 294920 | tf_op jit(solution)/shard_map/ppermute | solution.py:260
  34.0 4.9 %collective-permute-start.4 = (f32[96,256]{1,0:T(8,128)S(1)}, f32[96,256]{1,0:T(8,128)S(1)}, u32[]{:S(2)}, u32[]{:S(2)}) collective-permute-start(f32[96,256]{1,0:T(8,128)S(1)} %get-tuple-element.67), channel_id=1, source_target_pairs={{0,3},{1,0},{2,1},{3,2},{4,7},{5,4},{6,5},{7,6},{8,11},{9,8},{10,9... | collective-permute-start | bytes 294920 | tf_op jit(solution)/shard_map/ppermute | solution.py:260
  39.0 6.9 %collective-permute-start.5 = (f32[24,256]{1,0:T(8,128)S(1)}, f32[24,256]{1,0:T(8,128)S(1)}, u32[]{:S(2)}, u32[]{:S(2)}) collective-permute-start(f32[24,256]{1,0:T(8,128)S(1)} %get-tuple-element.73), channel_id=1, source_target_pairs={{0,4},{1,5},{2,6},{3,7},{4,8},{5,9},{6,10},{7,11},{8,12},{9,13},{1... | collective-permute-start | bytes 73736 | tf_op jit(solution)/shard_map/ppermute | solution.py:260
  40.7 6.9 %collective-permute-start.6 = (f32[24,256]{1,0:T(8,128)S(1)}, f32[24,256]{1,0:T(8,128)S(1)}, u32[]{:S(2)}, u32[]{:S(2)}) collective-permute-start(f32[24,256]{1,0:T(8,128)S(1)} %get-tuple-element.75), channel_id=1, source_target_pairs={{0,8},{1,9},{2,10},{3,11},{4,12},{5,13},{6,14},{7,15},{8,0},{9,1},... | collective-permute-start | bytes 73736 | tf_op jit(solution)/shard_map/ppermute | solution.py:260
  44.4 3.1 %collective-permute-start.7 = (f32[24,256]{1,0:T(8,128)S(1)}, f32[24,256]{1,0:T(8,128)S(1)}, u32[]{:S(2)}, u32[]{:S(2)}) collective-permute-start(f32[24,256]{1,0:T(8,128)S(1)} %get-tuple-element.74), channel_id=1, source_target_pairs={{0,12},{1,13},{2,14},{3,15},{4,0},{5,1},{6,2},{7,3},{8,4},{9,5},{1... | collective-permute-start | bytes 73736 | tf_op jit(solution)/shard_map/ppermute | solution.py:260
  45.9 2.5 %collective-permute-start.8 = (f32[8,128]{1,0:T(8,128)S(1)}, f32[8,128]{1,0:T(8,128)S(1)}, u32[]{:S(2)}, u32[]{:S(2)}) collective-permute-start(f32[8,128]{1,0:T(8,128)S(1)} %scatter.4), channel_id=1, source_target_pairs={{0,16},{16,0},{32,48},{48,32},{64,80},{80,64},{96,112},{112,96},{1... | collective-permute-start | bytes 12296 | tf_op jit(solution)/shard_map/ppermute | solution.py:522
  48.3 11.5 %collective-permute-start.10 = (f32[32,256]{1,0:T(8,128)S(1)}, f32[32,256]{1,0:T(8,128)S(1)}, u32[]{:S(2)}, u32[]{:S(2)}) collective-permute-start(f32[32,256]{1,0:T(8,128)S(1)} %maximum_maximum_fusion), channel_id=1, source_target_pairs={{0,64},{16,80},{32,96},{48,112},{64,0},{80,16},{96,32},{112,48},{1... | collective-permute-start | bytes 98312 | tf_op jit(solution)/shard_map/ppermute | solution.py:274
  50.1 9.8 %collective-permute-start.11 = (f32[32,256]{1,0:T(8,128)S(1)}, f32[32,256]{1,0:T(8,128)S(1)}, u32[]{:S(2)}, u32[]{:S(2)}) collective-permute-start(f32[32,256]{1,0:T(8,128)S(1)} %maximum_maximum_fusion), channel_id=1, source_target_pairs={{0,32},{16,48},{32,64},{48,80},{64,96},{80,112},{96,0},{112,16},{1... | collective-permute-start | bytes 98312 | tf_op jit(solution)/shard_map/ppermute | solution.py:274
  50.7 9.3 %collective-permute-start.9 = (f32[32,256]{1,0:T(8,128)S(1)}, f32[32,256]{1,0:T(8,128)S(1)}, u32[]{:S(2)}, u32[]{:S(2)}) collective-permute-start(f32[32,256]{1,0:T(8,128)S(1)} %maximum_maximum_fusion), channel_id=1, source_target_pairs={{0,96},{16,112},{32,0},{48,16},{64,32},{80,48},{96,64},{112,80},{1... | collective-permute-start | bytes 98312 | tf_op jit(solution)/shard_map/ppermute | solution.py:274
  59.9 57.4 %collective-permute-start.24 = (f32[1032,512]{1,0:T(8,128)}, f32[1032,512]{1,0:T(8,128)S(1)}, u32[]{:S(2)}, u32[]{:S(2)}) collective-permute-start(f32[1032,512]{1,0:T(8,128)} %constant_dynamic-update-slice_fusion), channel_id=1, source_target_pairs={{0,64},{16,80},{32,96},{48,112},{64,0},{80,16},{96,32},{112,48},{1... | collective-permute-start | bytes 6340616 | tf_op jit(solution)/shard_map/ppermute | solution.py:519
  65.2 45.4 %collective-permute-start.25 = (f32[2,2,256,512]{3,2,1,0:T(8,128)}, f32[2,2,256,512]{3,2,1,0:T(8,128)}, u32[]{:S(2)}, u32[]{:S(2)}) collective-permute-start(f32[2,2,256,512]{3,2,1,0:T(8,128)} %second_pairs.1), channel_id=1, source_target_pairs={{0,16},{16,0},{32,48},{48,32},{64,80},{80,64},{96,112},{112,96},{1... | collective-permute-start | bytes 6291464 | tf_op jit(solution)/shard_map/ppermute | solution.py:522
  67.0 4.5 %collective-permute-start.14 = (f32[24,256]{1,0:T(8,128)S(1)}, f32[24,256]{1,0:T(8,128)S(1)}, u32[]{:S(2)}, u32[]{:S(2)}) collective-permute-start(f32[24,256]{1,0:T(8,128)S(1)} %select_add_fusion), channel_id=1, source_target_pairs={{0,4},{1,5},{2,6},{3,7},{4,8},{5,9},{6,10},{7,11},{8,12},{9,13},{1... | collective-permute-start | bytes 73736 | tf_op jit(solution)/shard_map/ppermute | solution.py:274
  68.9 4.5 %collective-permute-start.15 = (f32[24,256]{1,0:T(8,128)S(1)}, f32[24,256]{1,0:T(8,128)S(1)}, u32[]{:S(2)}, u32[]{:S(2)}) collective-permute-start(f32[24,256]{1,0:T(8,128)S(1)} %select_add_fusion), channel_id=1, source_target_pairs={{0,8},{1,9},{2,10},{3,11},{4,12},{5,13},{6,14},{7,15},{8,0},{9,1},... | collective-permute-start | bytes 73736 | tf_op jit(solution)/shard_map/ppermute | solution.py:274
  69.5 3.9 %collective-permute-start.16 = (f32[24,256]{1,0:T(8,128)S(1)}, f32[24,256]{1,0:T(8,128)S(1)}, u32[]{:S(2)}, u32[]{:S(2)}) collective-permute-start(f32[24,256]{1,0:T(8,128)S(1)} %select_add_fusion), channel_id=1, source_target_pairs={{0,12},{1,13},{2,14},{3,15},{4,0},{5,1},{6,2},{7,3},{8,4},{9,5},{1... | collective-permute-start | bytes 73736 | tf_op jit(solution)/shard_map/ppermute | solution.py:274
  73.4 6.3 %collective-permute-start.17 = (f32[96,256]{1,0:T(8,128)S(1)}, f32[96,256]{1,0:T(8,128)S(1)}, u32[]{:S(2)}, u32[]{:S(2)}) collective-permute-start(f32[96,256]{1,0:T(8,128)S(1)} %pad_maximum_fusion.refs_0_), channel_id=1, source_target_pairs={{0,3},{1,0},{2,1},{3,2},{4,7},{5,4},{6,5},{7,6},{8,11},{9,8},{10,9... | collective-permute-start | bytes 294920 | tf_op jit(solution)/shard_map/ppermute | solution.py:274
  77.1 5.3 %collective-permute-start.18 = (f32[96,256]{1,0:T(8,128)S(1)}, f32[96,256]{1,0:T(8,128)S(1)}, u32[]{:S(2)}, u32[]{:S(2)}) collective-permute-start(f32[96,256]{1,0:T(8,128)S(1)} %pad_maximum_fusion.refs_0_), channel_id=1, source_target_pairs={{0,2},{1,3},{2,0},{3,1},{4,6},{5,7},{6,4},{7,5},{8,10},{9,11},{10,... | collective-permute-start | bytes 294920 | tf_op jit(solution)/shard_map/ppermute | solution.py:274
  77.1 8.1 %collective-permute-start.19 = (f32[96,256]{1,0:T(8,128)S(1)}, f32[96,256]{1,0:T(8,128)S(1)}, u32[]{:S(2)}, u32[]{:S(2)}) collective-permute-start(f32[96,256]{1,0:T(8,128)S(1)} %pad_maximum_fusion.refs_0_), channel_id=1, source_target_pairs={{0,1},{1,2},{2,3},{3,0},{4,5},{5,6},{6,7},{7,4},{8,9},{9,10},{10,1... | collective-permute-start | bytes 294920 | tf_op jit(solution)/shard_map/ppermute | solution.py:274
  79.7 6.1 %collective-permute-start.20 = (f32[96,256]{1,0:T(8,128)S(1)}, f32[96,256]{1,0:T(8,128)S(1)}, u32[]{:S(2)}, u32[]{:S(2)}) collective-permute-start(f32[96,256]{1,0:T(8,128)S(1)} %pad_maximum_fusion.refs_0_), channel_id=1, source_target_pairs={{0,16},{16,0},{32,48},{48,32},{64,80},{80,64},{96,112},{112,96},{1... | collective-permute-start | bytes 294920 | tf_op jit(solution)/shard_map/ppermute | solution.py:522
  82.4 3.7 %collective-permute-start.21 = (f32[96,256]{1,0:T(8,128)S(1)}, f32[96,256]{1,0:T(8,128)S(1)}, u32[]{:S(2)}, u32[]{:S(2)}) collective-permute-start(f32[96,256]{1,0:T(8,128)S(1)} %collective-permute-done.17.refs_1_), channel_id=1, source_target_pairs={{0,16},{16,0},{32,48},{48,32},{64,80},{80,64},{96,112},{112,96},{1... | collective-permute-start | bytes 294920 | tf_op jit(solution)/shard_map/ppermute | solution.py:522
  (7 other events, 94.2 us)

commit v9 on v8

--- a/solution.py
+++ b/solution.py
@@ -370,24 +370,24 @@
     work[HALF:, HALF:] = gram_ref[2 * HALF :, :] / row_count
     work[HALF:, :HALF] = jnp.zeros((HALF, HALF), jnp.float32)
 
-    @pl.loop(0, size // BLOCK)
-    def _(k):
-        offset = pl.multiple_of(k * BLOCK, BLOCK)
-        here = pl.ds(offset, BLOCK)
-        upper, inverse = sweep(work[here, here])
+    steps = size // BLOCK
+    block = work[:BLOCK, :BLOCK]
+    for k in range(steps):
+        offset, end = k * BLOCK, (k + 1) * BLOCK
+        here, below = pl.ds(offset, BLOCK), pl.ds(end, size - end)
+        upper, inverse = sweep(block)
+        if k < steps - 1:
+            ahead = dot32(inverse, work[here, end : end + BLOCK])
+            block = work[end : end + BLOCK, end : end + BLOCK] - dot32(ahead, ahead, 0, 0)
         right = dot32(inverse, work[here, :])
-        lane = lax.broadcasted_iota(jnp.int32, (BLOCK, size), 1)
-        beyond = jnp.where(lane >= offset + BLOCK, right, 0.0)
-        factor_ref[here, :] = beyond
+        factor_ref[here, :] = jnp.zeros((BLOCK, size), jnp.float32)
         factor_ref[here, here] = upper
         work[here, :] = right
         work[here, here] = inverse
-
-        @pl.when(k < size // BLOCK - 1)
-        def _():
-            row = lax.broadcasted_iota(jnp.int32, (size, BLOCK), 0)
-            work[:, here] = jnp.where(row >= offset + BLOCK, 0.0, work[:, here])
-            work[...] = work[...] - dot32(beyond, work[here, :], 0, 0)
+        if k < steps - 1:
+            factor_ref[here, end:] = right[:, end:]
+            work[below, here] = jnp.zeros((size - end, BLOCK), jnp.float32)
+            work[below, :] = work[below, :] - dot32(right[:, end:], work[here, :], 0, 0)
 
     row = lax.broadcasted_iota(jnp.int32, work.shape, 0)
     lane = lax.broadcasted_iota(jnp.int32, work.shape, 1)
@@ -484,15 +484,29 @@
     )(*operands)
 
 
-def second_pairs_kernel(first_ref, second_ref, out_ref, sems):
-    copies = [
-        pltpu.make_async_copy(ref.at[1], out_ref.at[i], sems.at[i])
-        for i, ref in enumerate((first_ref, second_ref))
+def second_pairs_kernel(first_ref, second_ref, out_ref, staged, sems):
+    rows = staged.shape[2] // 2
+    pieces = [
+        (i, rank, part) for i in range(2) for rank in range(PAIR) for part in range(0, 2 * rows, rows)
     ]
-    for copy in copies:
-        copy.start()
-    for copy in copies:
-        copy.wait()
+
+    def load(n):
+        i, rank, part = pieces[n]
+        source = (first_ref, second_ref)[i].at[1, rank, pl.ds(part, rows)]
+        return pltpu.make_async_copy(source, staged.at[i, rank, pl.ds(part, rows)], sems.at[n])
+
+    def store(n):
+        i, rank, part = pieces[n]
+        source = staged.at[i, rank, pl.ds(part, rows)]
+        return pltpu.make_async_copy(source, out_ref.at[i, rank, pl.ds(part, rows)], sems.at[n])
+
+    for n in range(len(pieces)):
+        load(n).start()
+    for n in range(len(pieces)):
+        load(n).wait()
+        store(n).start()
+    for n in range(len(pieces)):
+        store(n).wait()
 
 
 def second_pairs(first, second):
@@ -501,8 +515,11 @@
         second_pairs_kernel,
         out_shape=jax.ShapeDtypeStruct(first.shape, first.dtype),
         in_specs=[hbm, hbm],
-        out_specs=pl.BlockSpec(memory_space=pltpu.VMEM),
-        scratch_shapes=[pltpu.SemaphoreType.DMA((2,))],
+        out_specs=hbm,
+        scratch_shapes=[
+            pltpu.VMEM(first.shape, first.dtype),
+            pltpu.SemaphoreType.DMA((4 * PAIR,)),
+        ],
         cost_estimate=pl.CostEstimate(
             flops=1_000_000, bytes_accessed=1 << 16, transcendentals=0
         ),

time: 119 us -> 118 us (level)
  starting transfers between devices: 51.3 us -> 44.5 us
  Pallas kernels: 44.5 us -> 49.8 us
    ppermute x7, starting transfers between devices: 18.3 us -> 10.8 us  [scatter_sum(): lax.ppermute(sent, axis, ring_pairs(size, span, stride, shift))]
    pallas_call x1, Pallas kernels: 6.9 us -> 12 us  [gram(): pl.pallas_call(gram_kernel, out_shape=(jax.ShapeDtypeStruct((3 * HALF, HA...]
    ppermute x3, starting transfers between devices: 8.6 us -> 4.62 us  [along_z(): return lax.ppermute(value, 'scene', ring_pairs(scenes, chips, 2, up))]
    ppermute x9, starting transfers between devices: 13.1 us -> 16 us  [from_ahead(): lax.ppermute(value, axis, ring_pairs(size, span, stride, span - ahead))]
    pallas_call x1, Pallas kernels: 3.21 us -> 5.42 us  [pack(): pl.pallas_call(pack_kernel, out_shape=(two_pairs, two_pairs, two_pairs, t...]
    ppermute x7, waiting for transfers between devices: 4.26 us -> 6.25 us  [scatter_sum(): lax.ppermute(sent, axis, ring_pairs(size, span, stride, shift))]
    ppermute x9, waiting for transfers between devices: 5.21 us -> 3.42 us  [from_ahead(): lax.ppermute(value, axis, ring_pairs(size, span, stride, span - ahead))]
    ppermute x7, starting transfers between devices: 11.3 us -> 13 us  [other_core(): return lax.ppermute(value, 'scene', ring_pairs(scenes, 2, 1, 1))]
  transfers between devices with their start and end apart: 26 -> 26, of which waited for: 11 -> 12; matrix products, arithmetic and copies ran while one was open for 4% -> 4% of each run, Pallas kernels for 32% -> 36%
where the time goes in v9:
time: 118 us
  Pallas kernels  49.8 us (42%)
  starting transfers between devices  44.5 us (38%)
  waiting for transfers between devices  15.6 us (13%)
  local copies, waits for them, and re-layouts  5.05 us (4%)
  between operations  1.76 us (1%)
    pallas_call x1, Pallas kernels, factor(): pl.pallas_call(functools.partial(factor_kernel, row_count), out_shape=(ja...  22.5 us
    ppermute x9, starting transfers between devices, from_ahead(): lax.ppermute(value, axis, ring_pairs(size, span, stride, span - ahead))  16 us
    ppermute x7, starting transfers between devices, other_core(): return lax.ppermute(value, 'scene', ring_pairs(scenes, 2, 1, 1))  13 us
    pallas_call x1, Pallas kernels, gram(): pl.pallas_call(gram_kernel, out_shape=(jax.ShapeDtypeStruct((3 * HALF, HA...  12 us
    ppermute x7, starting transfers between devices, scatter_sum(): lax.ppermute(sent, axis, ring_pairs(size, span, stride, shift))  10.8 us
    pallas_call x2, Pallas kernels, finish(): pl.pallas_call(functools.partial(finish_kernel, pairs), out_shape=jax.Sha...  7.49 us
    ppermute x7, waiting for transfers between devices, scatter_sum(): lax.ppermute(sent, axis, ring_pairs(size, span, stride, shift))  6.25 us
    pallas_call x1, Pallas kernels, pack(): pl.pallas_call(pack_kernel, out_shape=(two_pairs, two_pairs, two_pairs, t...  5.42 us
  transfers between devices with their start and end apart: 26, of which 12 were waited for; matrix products, arithmetic and copies ran while one was open for 4% of the time, Pallas kernels for 36%

profile of v9, /device:TPU:1, one launch (start us, length us, event | category | flops | bytes accessed | tf_op | source)
XLA Modules:
  0.0 117.9 jit_solution(10806797416526549474)
XLA Ops:
  1.3 5.4 %pack.1 = (f32[2,2,256,512]{3,2,1,0:T(8,128)}, f32[2,2,256,512]{3,2,1,0:T(8,128)}, f32[2,2,256,512]{3,2,1,0:T(8,128)}, s32[16]{0:T(128)}, s32[16]{0:T(128)}) custom-call(s32[1]{0:T(128)S(6)} %copy.10.count_ref, s32[16]{0:T(128)} %owner_ref.1, s32[16]{0:T(128)} %slot_ref.1, f32[16,256,512]{2,1,0:T(8,128)} %tile_ref), custom_call_target="tpu_custom_call" | custom-call | bytes 8388608 | tf_op jit(solution)/shard_map/pack/pallas_call | solution.py:124
  6.7 2.8 %collective-permute-start = (f32[2,2,256,512]{3,2,1,0:T(8,128)}, f32[2,2,256,512]{3,2,1,0:T(8,128)}, u32[]{:S(2)}, u32[]{:S(2)}) collective-permute-start(f32[2,2,256,512]{3,2,1,0:T(8,128)} %get-tuple-element.43), channel_id=1, source_target_pairs={{0,16},{16,0},{32,48},{48,32},{64,80},{80,64},{96,112},{112,96},{1... | collective-permute-start | bytes 6291464 | tf_op jit(solution)/shard_map/ppermute | solution.py:539
  12.2 12.0 %gram.1 = (f32[768,256]{1,0:T(8,128)}, f32[512,512]{1,0:T(8,128)}, f32[1032,512]{1,0:T(8,128)}) custom-call(s32[1]{0:T(128)S(6)} %copy.10.count_ref, s32[16]{0:T(128)} %get-tuple-element.40.seat_ref, f32[16,256,512]{2,1,0:T(8,128)} %tile_ref, f32[512,512]{1,0:T(8,128)} %inverse_ref.3), custom_call_target="tpu_custom_call" | custom-call | flops 1000000 | bytes 65536 | tf_op jit(solution)/shard_map/gram/pallas_call | solution.py:207
  25.2 3.2 %collective-permute-start.1 = (f32[384,256]{1,0:T(8,128)S(1)}, f32[384,256]{1,0:T(8,128)S(1)}, u32[]{:S(2)}, u32[]{:S(2)}) collective-permute-start(f32[384,256]{1,0:T(8,128)S(1)} %dynamic-slice_bitcast_fusion), channel_id=1, source_target_pairs={{0,16},{16,0},{32,48},{48,32},{64,80},{80,64},{96,112},{112,96},{1... | collective-permute-start | bytes 1179656 | tf_op jit(solution)/shard_map/ppermute | solution.py:260
  30.9 2.2 %collective-permute-start.2 = (f32[96,256]{1,0:T(8,128)S(1)}, f32[96,256]{1,0:T(8,128)S(1)}, u32[]{:S(2)}, u32[]{:S(2)}) collective-permute-start(f32[96,256]{1,0:T(8,128)S(1)} %get-tuple-element.66), channel_id=1, source_target_pairs={{0,1},{1,2},{2,3},{3,0},{4,5},{5,6},{6,7},{7,4},{8,9},{9,10},{10,1... | collective-permute-start | bytes 294920 | tf_op jit(solution)/shard_map/ppermute | solution.py:260
  33.1 2.5 %collective-permute-start.3 = (f32[96,256]{1,0:T(8,128)S(1)}, f32[96,256]{1,0:T(8,128)S(1)}, u32[]{:S(2)}, u32[]{:S(2)}) collective-permute-start(f32[96,256]{1,0:T(8,128)S(1)} %get-tuple-element.68), channel_id=1, source_target_pairs={{0,2},{1,3},{2,0},{3,1},{4,6},{5,7},{6,4},{7,5},{8,10},{9,11},{10,... | collective-permute-start | bytes 294920 | tf_op jit(solution)/shard_map/ppermute | solution.py:260
  35.6 1.9 %collective-permute-done.2 = f32[96,256]{1,0:T(8,128)S(1)} collective-permute-done((f32[96,256]{1,0:T(8,128)S(1)}, f32[96,256]{1,0:T(8,128)S(1)}, u32[]{:S(2)}, u32[]{:S(2)}) %collective-permute-start.2) | collective-permute-done | bytes 98336 | tf_op jit(solution)/shard_map/ppermute | solution.py:260
  37.4 3.0 %collective-permute-done.3 = f32[96,256]{1,0:T(8,128)S(1)} collective-permute-done((f32[96,256]{1,0:T(8,128)S(1)}, f32[96,256]{1,0:T(8,128)S(1)}, u32[]{:S(2)}, u32[]{:S(2)}) %collective-permute-start.3) | collective-permute-done | bytes 98336 | tf_op jit(solution)/shard_map/ppermute | solution.py:260
  40.6 2.8 %collective-permute-start.6 = (f32[24,256]{1,0:T(8,128)S(1)}, f32[24,256]{1,0:T(8,128)S(1)}, u32[]{:S(2)}, u32[]{:S(2)}) collective-permute-start(f32[24,256]{1,0:T(8,128)S(1)} %get-tuple-element.75), channel_id=1, source_target_pairs={{0,8},{1,9},{2,10},{3,11},{4,12},{5,13},{6,14},{7,15},{8,0},{9,1},... | collective-permute-start | bytes 73736 | tf_op jit(solution)/shard_map/ppermute | solution.py:260
  44.9 1.8 %collective-permute-start.8 = (f32[8,128]{1,0:T(8,128)S(1)}, f32[8,128]{1,0:T(8,128)S(1)}, u32[]{:S(2)}, u32[]{:S(2)}) collective-permute-start(f32[8,128]{1,0:T(8,128)S(1)} %scatter.4), channel_id=1, source_target_pairs={{0,16},{16,0},{32,48},{48,32},{64,80},{80,64},{96,112},{112,96},{1... | collective-permute-start | bytes 12296 | tf_op jit(solution)/shard_map/ppermute | solution.py:539
  47.5 2.9 %collective-permute-start.10 = (f32[32,256]{1,0:T(8,128)S(1)}, f32[32,256]{1,0:T(8,128)S(1)}, u32[]{:S(2)}, u32[]{:S(2)}) collective-permute-start(f32[32,256]{1,0:T(8,128)S(1)} %maximum_maximum_fusion), channel_id=1, source_target_pairs={{0,64},{16,80},{32,96},{48,112},{64,0},{80,16},{96,32},{112,48},{1... | collective-permute-start | bytes 98312 | tf_op jit(solution)/shard_map/ppermute | solution.py:274
  51.5 1.6 %collective-permute-start.9 = (f32[32,256]{1,0:T(8,128)S(1)}, f32[32,256]{1,0:T(8,128)S(1)}, u32[]{:S(2)}, u32[]{:S(2)}) collective-permute-start(f32[32,256]{1,0:T(8,128)S(1)} %maximum_maximum_fusion), channel_id=1, source_target_pairs={{0,96},{16,112},{32,0},{48,16},{64,32},{80,48},{96,64},{112,80},{1... | collective-permute-start | bytes 98312 | tf_op jit(solution)/shard_map/ppermute | solution.py:274
  54.2 3.9 %collective-permute-done.12.first_ref.refs_2_ = f32[2,2,256,512]{3,2,1,0:T(8,128)S(1)} collective-permute-done((f32[2,2,256,512]{3,2,1,0:T(8,128)}, f32[2,2,256,512]{3,2,1,0:T(8,128)S(1)}, u32[]{:S(2)}, u32[]{:S(2)}) %collective-permute-start.12) | collective-permute-done | bytes 2097184 | tf_op jit(solution)/shard_map/ppermute | solution.py:536
  59.5 1.9 %collective-permute-start.24 = (f32[1032,512]{1,0:T(8,128)}, f32[1032,512]{1,0:T(8,128)S(1)}, u32[]{:S(2)}, u32[]{:S(2)}) collective-permute-start(f32[1032,512]{1,0:T(8,128)} %constant_dynamic-update-slice_fusion), channel_id=1, source_target_pairs={{0,64},{16,80},{32,96},{48,112},{64,0},{80,16},{96,32},{112,48},{1... | collective-permute-start | bytes 6340616 | tf_op jit(solution)/shard_map/ppermute | solution.py:536
  61.5 2.5 %second_pairs.1 = f32[2,2,256,512]{3,2,1,0:T(8,128)} custom-call(f32[2,2,256,512]{3,2,1,0:T(8,128)} %copy-done, f32[2,2,256,512]{3,2,1,0:T(8,128)} %collective-permute-done.13.second_ref.refs_3_), custom_call_target="tpu_custom_call" | custom-call | flops 1000000 | bytes 65536 | tf_op jit(solution)/shard_map/second_pairs/pallas_call | solution.py:514
  64.0 2.0 %collective-permute-start.25 = (f32[2,2,256,512]{3,2,1,0:T(8,128)}, f32[2,2,256,512]{3,2,1,0:T(8,128)}, u32[]{:S(2)}, u32[]{:S(2)}) collective-permute-start(f32[2,2,256,512]{3,2,1,0:T(8,128)} %second_pairs.1), channel_id=1, source_target_pairs={{0,16},{16,0},{32,48},{48,32},{64,80},{80,64},{96,112},{112,96},{1... | collective-permute-start | bytes 6291464 | tf_op jit(solution)/shard_map/ppermute | solution.py:539
  66.7 3.4 %collective-permute-start.15 = (f32[24,256]{1,0:T(8,128)S(1)}, f32[24,256]{1,0:T(8,128)S(1)}, u32[]{:S(2)}, u32[]{:S(2)}) collective-permute-start(f32[24,256]{1,0:T(8,128)S(1)} %select_add_fusion), channel_id=1, source_target_pairs={{0,8},{1,9},{2,10},{3,11},{4,12},{5,13},{6,14},{7,15},{8,0},{9,1},... | collective-permute-start | bytes 73736 | tf_op jit(solution)/shard_map/ppermute | solution.py:274
  70.1 2.1 %collective-permute-start.16 = (f32[24,256]{1,0:T(8,128)S(1)}, f32[24,256]{1,0:T(8,128)S(1)}, u32[]{:S(2)}, u32[]{:S(2)}) collective-permute-start(f32[24,256]{1,0:T(8,128)S(1)} %select_add_fusion), channel_id=1, source_target_pairs={{0,12},{1,13},{2,14},{3,15},{4,0},{5,1},{6,2},{7,3},{8,4},{9,5},{1... | collective-permute-start | bytes 73736 | tf_op jit(solution)/shard_map/ppermute | solution.py:274
  73.1 3.1 %collective-permute-start.17 = (f32[96,256]{1,0:T(8,128)S(1)}, f32[96,256]{1,0:T(8,128)S(1)}, u32[]{:S(2)}, u32[]{:S(2)}) collective-permute-start(f32[96,256]{1,0:T(8,128)S(1)} %pad_maximum_fusion.refs_0_), channel_id=1, source_target_pairs={{0,3},{1,0},{2,1},{3,2},{4,7},{5,4},{6,5},{7,6},{8,11},{9,8},{10,9... | collective-permute-start | bytes 294920 | tf_op jit(solution)/shard_map/ppermute | solution.py:274
  77.8 2.7 %collective-permute-start.20 = (f32[96,256]{1,0:T(8,128)S(1)}, f32[96,256]{1,0:T(8,128)S(1)}, u32[]{:S(2)}, u32[]{:S(2)}) collective-permute-start(f32[96,256]{1,0:T(8,128)S(1)} %pad_maximum_fusion.refs_0_), channel_id=1, source_target_pairs={{0,16},{16,0},{32,48},{48,32},{64,80},{80,64},{96,112},{112,96},{1... | collective-permute-start | bytes 294920 | tf_op jit(solution)/shard_map/ppermute | solution.py:539
  81.5 2.8 %collective-permute-start.21 = (f32[96,256]{1,0:T(8,128)S(1)}, f32[96,256]{1,0:T(8,128)S(1)}, u32[]{:S(2)}, u32[]{:S(2)}) collective-permute-start(f32[96,256]{1,0:T(8,128)S(1)} %collective-permute-done.17.refs_1_), channel_id=1, source_target_pairs={{0,16},{16,0},{32,48},{48,32},{64,80},{80,64},{96,112},{112,96},{1... | collective-permute-start | bytes 294920 | tf_op jit(solution)/shard_map/ppermute | solution.py:539
  86.5 22.5 %factor.1 = (f32[512,512]{1,0:T(8,128)}, bf16[512,512]{1,0:T(8,128)(2,1)S(1)}, bf16[512,512]{1,0:T(8,128)(2,1)S(1)}) custom-call(f32[512,512]{1,0:T(8,128)S(1)} %copy-done.2, f32[96,256]{1,0:T(8,128)S(1)} %pad_maximum_fusion.refs_0_, f32[96,256]{1,0:T(8,128)S(1)} %collective-permute-done.17.refs_1_, f32[96,256]{1,0:T(8,128)S(1)} %collective-permute-done.18.refs_2_, ...), custom_call_target="tpu_custom_call" | custom-call | flops 1000000 | bytes 65536 | tf_op jit(solution)/shard_map/factor/pallas_call | solution.py:401
  110.2 5.0 %finish_near.1.refs_2_ = f32[8,256,512]{2,1,0:T(8,128)} custom-call(s32[12]{0:T(128)S(1)} %bitcast.51, bf16[512,512]{1,0:T(8,128)(2,1)S(1)} %get-tuple-element.59.head_ref, bf16[512,512]{1,0:T(8,128)(2,1)S(1)} %get-tuple-element.60.tail_ref, f32[512,512]{1,0:T(8,128)S(1)} %copy-done.3, f32[2,2,256,512]{3,2,1,0:T(8,128)} %collective-permute-done.refs_1_, ...), custom_call_target="tpu_custom_call" | custom-call | flops 1000000 | bytes 65536 | tf_op jit(solution)/shard_map/finish_near/pallas_call | solution.py:466
  115.3 2.5 %finish_far.1 = f32[8,256,512]{2,1,0:T(8,128)} custom-call(s32[4]{0:T(128)S(1)} %slice.74.slot_ref, bf16[512,512]{1,0:T(8,128)(2,1)S(1)} %get-tuple-element.59.head_ref, bf16[512,512]{1,0:T(8,128)(2,1)S(1)} %get-tuple-element.60.tail_ref, f32[1032,512]{1,0:T(8,128)S(1)} %collective-permute-done.24.refs_0_.refs_1_, ...), custom_call_target="tpu_custom_call", output_to_operand_aliasing={{}: (5, {})} | custom-call | flops 1000000 | bytes 65536 | tf_op jit(solution)/shard_map/finish_far/pallas_call | solution.py:466
  (63 shorter events, 19.8 us)
Async XLA Ops:
  6.7 17.5 %collective-permute-start = (f32[2,2,256,512]{3,2,1,0:T(8,128)}, f32[2,2,256,512]{3,2,1,0:T(8,128)}, u32[]{:S(2)}, u32[]{:S(2)}) collective-permute-start(f32[2,2,256,512]{3,2,1,0:T(8,128)} %get-tuple-element.43), channel_id=1, source_target_pairs={{0,16},{16,0},{32,48},{48,32},{64,80},{80,64},{96,112},{112,96},{1... | collective-permute-start | bytes 6291464 | tf_op jit(solution)/shard_map/ppermute | solution.py:539
  9.5 48.6 %collective-permute-start.12 = (f32[2,2,256,512]{3,2,1,0:T(8,128)}, f32[2,2,256,512]{3,2,1,0:T(8,128)S(1)}, u32[]{:S(2)}, u32[]{:S(2)}) collective-permute-start(f32[2,2,256,512]{3,2,1,0:T(8,128)} %get-tuple-element.48), channel_id=1, source_target_pairs={{0,32},{16,48},{32,64},{48,80},{64,96},{80,112},{96,0},{112,16},{1... | collective-permute-start | bytes 6291464 | tf_op jit(solution)/shard_map/ppermute | solution.py:536
  10.9 47.2 %collective-permute-start.13 = (f32[2,2,256,512]{3,2,1,0:T(8,128)}, f32[2,2,256,512]{3,2,1,0:T(8,128)}, u32[]{:S(2)}, u32[]{:S(2)}) collective-permute-start(f32[2,2,256,512]{3,2,1,0:T(8,128)} %get-tuple-element.49), channel_id=1, source_target_pairs={{0,96},{16,112},{32,0},{48,16},{64,32},{80,48},{96,64},{112,80},{1... | collective-permute-start | bytes 6291464 | tf_op jit(solution)/shard_map/ppermute | solution.py:536
  25.2 4.6 %collective-permute-start.1 = (f32[384,256]{1,0:T(8,128)S(1)}, f32[384,256]{1,0:T(8,128)S(1)}, u32[]{:S(2)}, u32[]{:S(2)}) collective-permute-start(f32[384,256]{1,0:T(8,128)S(1)} %dynamic-slice_bitcast_fusion), channel_id=1, source_target_pairs={{0,16},{16,0},{32,48},{48,32},{64,80},{80,64},{96,112},{112,96},{1... | collective-permute-start | bytes 1179656 | tf_op jit(solution)/shard_map/ppermute | solution.py:260
  30.9 6.5 %collective-permute-start.2 = (f32[96,256]{1,0:T(8,128)S(1)}, f32[96,256]{1,0:T(8,128)S(1)}, u32[]{:S(2)}, u32[]{:S(2)}) collective-permute-start(f32[96,256]{1,0:T(8,128)S(1)} %get-tuple-element.66), channel_id=1, source_target_pairs={{0,1},{1,2},{2,3},{3,0},{4,5},{5,6},{6,7},{7,4},{8,9},{9,10},{10,1... | collective-permute-start | bytes 294920 | tf_op jit(solution)/shard_map/ppermute | solution.py:260
  33.1 7.4 %collective-permute-start.3 = (f32[96,256]{1,0:T(8,128)S(1)}, f32[96,256]{1,0:T(8,128)S(1)}, u32[]{:S(2)}, u32[]{:S(2)}) collective-permute-start(f32[96,256]{1,0:T(8,128)S(1)} %get-tuple-element.68), channel_id=1, source_target_pairs={{0,2},{1,3},{2,0},{3,1},{4,6},{5,7},{6,4},{7,5},{8,10},{9,11},{10,... | collective-permute-start | bytes 294920 | tf_op jit(solution)/shard_map/ppermute | solution.py:260
  35.5 4.9 %collective-permute-start.4 = (f32[96,256]{1,0:T(8,128)S(1)}, f32[96,256]{1,0:T(8,128)S(1)}, u32[]{:S(2)}, u32[]{:S(2)}) collective-permute-start(f32[96,256]{1,0:T(8,128)S(1)} %get-tuple-element.67), channel_id=1, source_target_pairs={{0,3},{1,0},{2,1},{3,2},{4,7},{5,4},{6,5},{7,6},{8,11},{9,8},{10,9... | collective-permute-start | bytes 294920 | tf_op jit(solution)/shard_map/ppermute | solution.py:260
  40.5 4.4 %collective-permute-start.5 = (f32[24,256]{1,0:T(8,128)S(1)}, f32[24,256]{1,0:T(8,128)S(1)}, u32[]{:S(2)}, u32[]{:S(2)}) collective-permute-start(f32[24,256]{1,0:T(8,128)S(1)} %get-tuple-element.73), channel_id=1, source_target_pairs={{0,4},{1,5},{2,6},{3,7},{4,8},{5,9},{6,10},{7,11},{8,12},{9,13},{1... | collective-permute-start | bytes 73736 | tf_op jit(solution)/shard_map/ppermute | solution.py:260
  40.6 6.1 %collective-permute-start.6 = (f32[24,256]{1,0:T(8,128)S(1)}, f32[24,256]{1,0:T(8,128)S(1)}, u32[]{:S(2)}, u32[]{:S(2)}) collective-permute-start(f32[24,256]{1,0:T(8,128)S(1)} %get-tuple-element.75), channel_id=1, source_target_pairs={{0,8},{1,9},{2,10},{3,11},{4,12},{5,13},{6,14},{7,15},{8,0},{9,1},... | collective-permute-start | bytes 73736 | tf_op jit(solution)/shard_map/ppermute | solution.py:260
  43.4 3.3 %collective-permute-start.7 = (f32[24,256]{1,0:T(8,128)S(1)}, f32[24,256]{1,0:T(8,128)S(1)}, u32[]{:S(2)}, u32[]{:S(2)}) collective-permute-start(f32[24,256]{1,0:T(8,128)S(1)} %get-tuple-element.74), channel_id=1, source_target_pairs={{0,12},{1,13},{2,14},{3,15},{4,0},{5,1},{6,2},{7,3},{8,4},{9,5},{1... | collective-permute-start | bytes 73736 | tf_op jit(solution)/shard_map/ppermute | solution.py:260
  44.9 2.7 %collective-permute-start.8 = (f32[8,128]{1,0:T(8,128)S(1)}, f32[8,128]{1,0:T(8,128)S(1)}, u32[]{:S(2)}, u32[]{:S(2)}) collective-permute-start(f32[8,128]{1,0:T(8,128)S(1)} %scatter.4), channel_id=1, source_target_pairs={{0,16},{16,0},{32,48},{48,32},{64,80},{80,64},{96,112},{112,96},{1... | collective-permute-start | bytes 12296 | tf_op jit(solution)/shard_map/ppermute | solution.py:539
  47.5 11.8 %collective-permute-start.10 = (f32[32,256]{1,0:T(8,128)S(1)}, f32[32,256]{1,0:T(8,128)S(1)}, u32[]{:S(2)}, u32[]{:S(2)}) collective-permute-start(f32[32,256]{1,0:T(8,128)S(1)} %maximum_maximum_fusion), channel_id=1, source_target_pairs={{0,64},{16,80},{32,96},{48,112},{64,0},{80,16},{96,32},{112,48},{1... | collective-permute-start | bytes 98312 | tf_op jit(solution)/shard_map/ppermute | solution.py:274
  50.4 8.9 %collective-permute-start.11 = (f32[32,256]{1,0:T(8,128)S(1)}, f32[32,256]{1,0:T(8,128)S(1)}, u32[]{:S(2)}, u32[]{:S(2)}) collective-permute-start(f32[32,256]{1,0:T(8,128)S(1)} %maximum_maximum_fusion), channel_id=1, source_target_pairs={{0,32},{16,48},{32,64},{48,80},{64,96},{80,112},{96,0},{112,16},{1... | collective-permute-start | bytes 98312 | tf_op jit(solution)/shard_map/ppermute | solution.py:274
  51.5 8.0 %collective-permute-start.9 = (f32[32,256]{1,0:T(8,128)S(1)}, f32[32,256]{1,0:T(8,128)S(1)}, u32[]{:S(2)}, u32[]{:S(2)}) collective-permute-start(f32[32,256]{1,0:T(8,128)S(1)} %maximum_maximum_fusion), channel_id=1, source_target_pairs={{0,96},{16,112},{32,0},{48,16},{64,32},{80,48},{96,64},{112,80},{1... | collective-permute-start | bytes 98312 | tf_op jit(solution)/shard_map/ppermute | solution.py:274
  59.5 55.8 %collective-permute-start.24 = (f32[1032,512]{1,0:T(8,128)}, f32[1032,512]{1,0:T(8,128)S(1)}, u32[]{:S(2)}, u32[]{:S(2)}) collective-permute-start(f32[1032,512]{1,0:T(8,128)} %constant_dynamic-update-slice_fusion), channel_id=1, source_target_pairs={{0,64},{16,80},{32,96},{48,112},{64,0},{80,16},{96,32},{112,48},{1... | collective-permute-start | bytes 6340616 | tf_op jit(solution)/shard_map/ppermute | solution.py:536
  64.0 45.0 %collective-permute-start.25 = (f32[2,2,256,512]{3,2,1,0:T(8,128)}, f32[2,2,256,512]{3,2,1,0:T(8,128)}, u32[]{:S(2)}, u32[]{:S(2)}) collective-permute-start(f32[2,2,256,512]{3,2,1,0:T(8,128)} %second_pairs.1), channel_id=1, source_target_pairs={{0,16},{16,0},{32,48},{48,32},{64,80},{80,64},{96,112},{112,96},{1... | collective-permute-start | bytes 6291464 | tf_op jit(solution)/shard_map/ppermute | solution.py:539
  65.9 6.4 %collective-permute-start.14 = (f32[24,256]{1,0:T(8,128)S(1)}, f32[24,256]{1,0:T(8,128)S(1)}, u32[]{:S(2)}, u32[]{:S(2)}) collective-permute-start(f32[24,256]{1,0:T(8,128)S(1)} %select_add_fusion), channel_id=1, source_target_pairs={{0,4},{1,5},{2,6},{3,7},{4,8},{5,9},{6,10},{7,11},{8,12},{9,13},{1... | collective-permute-start | bytes 73736 | tf_op jit(solution)/shard_map/ppermute | solution.py:274
  66.7 5.7 %collective-permute-start.15 = (f32[24,256]{1,0:T(8,128)S(1)}, f32[24,256]{1,0:T(8,128)S(1)}, u32[]{:S(2)}, u32[]{:S(2)}) collective-permute-start(f32[24,256]{1,0:T(8,128)S(1)} %select_add_fusion), channel_id=1, source_target_pairs={{0,8},{1,9},{2,10},{3,11},{4,12},{5,13},{6,14},{7,15},{8,0},{9,1},... | collective-permute-start | bytes 73736 | tf_op jit(solution)/shard_map/ppermute | solution.py:274
  70.1 3.0 %collective-permute-start.16 = (f32[24,256]{1,0:T(8,128)S(1)}, f32[24,256]{1,0:T(8,128)S(1)}, u32[]{:S(2)}, u32[]{:S(2)}) collective-permute-start(f32[24,256]{1,0:T(8,128)S(1)} %select_add_fusion), channel_id=1, source_target_pairs={{0,12},{1,13},{2,14},{3,15},{4,0},{5,1},{6,2},{7,3},{8,4},{9,5},{1... | collective-permute-start | bytes 73736 | tf_op jit(solution)/shard_map/ppermute | solution.py:274
  73.1 4.7 %collective-permute-start.17 = (f32[96,256]{1,0:T(8,128)S(1)}, f32[96,256]{1,0:T(8,128)S(1)}, u32[]{:S(2)}, u32[]{:S(2)}) collective-permute-start(f32[96,256]{1,0:T(8,128)S(1)} %pad_maximum_fusion.refs_0_), channel_id=1, source_target_pairs={{0,3},{1,0},{2,1},{3,2},{4,7},{5,4},{6,5},{7,6},{8,11},{9,8},{10,9... | collective-permute-start | bytes 294920 | tf_op jit(solution)/shard_map/ppermute | solution.py:274
  76.2 5.3 %collective-permute-start.18 = (f32[96,256]{1,0:T(8,128)S(1)}, f32[96,256]{1,0:T(8,128)S(1)}, u32[]{:S(2)}, u32[]{:S(2)}) collective-permute-start(f32[96,256]{1,0:T(8,128)S(1)} %pad_maximum_fusion.refs_0_), channel_id=1, source_target_pairs={{0,2},{1,3},{2,0},{3,1},{4,6},{5,7},{6,4},{7,5},{8,10},{9,11},{10,... | collective-permute-start | bytes 294920 | tf_op jit(solution)/shard_map/ppermute | solution.py:274
  76.6 7.6 %collective-permute-start.19 = (f32[96,256]{1,0:T(8,128)S(1)}, f32[96,256]{1,0:T(8,128)S(1)}, u32[]{:S(2)}, u32[]{:S(2)}) collective-permute-start(f32[96,256]{1,0:T(8,128)S(1)} %pad_maximum_fusion.refs_0_), channel_id=1, source_target_pairs={{0,1},{1,2},{2,3},{3,0},{4,5},{5,6},{6,7},{7,4},{8,9},{9,10},{10,1... | collective-permute-start | bytes 294920 | tf_op jit(solution)/shard_map/ppermute | solution.py:274
  77.8 7.4 %collective-permute-start.20 = (f32[96,256]{1,0:T(8,128)S(1)}, f32[96,256]{1,0:T(8,128)S(1)}, u32[]{:S(2)}, u32[]{:S(2)}) collective-permute-start(f32[96,256]{1,0:T(8,128)S(1)} %pad_maximum_fusion.refs_0_), channel_id=1, source_target_pairs={{0,16},{16,0},{32,48},{48,32},{64,80},{80,64},{96,112},{112,96},{1... | collective-permute-start | bytes 294920 | tf_op jit(solution)/shard_map/ppermute | solution.py:539
  81.5 3.8 %collective-permute-start.21 = (f32[96,256]{1,0:T(8,128)S(1)}, f32[96,256]{1,0:T(8,128)S(1)}, u32[]{:S(2)}, u32[]{:S(2)}) collective-permute-start(f32[96,256]{1,0:T(8,128)S(1)} %collective-permute-done.17.refs_1_), channel_id=1, source_target_pairs={{0,16},{16,0},{32,48},{48,32},{64,80},{80,64},{96,112},{112,96},{1... | collective-permute-start | bytes 294920 | tf_op jit(solution)/shard_map/ppermute | solution.py:539
  (7 other events, 86.8 us)

commit v10 on v9

--- a/solution.py
+++ b/solution.py
@@ -13,6 +13,7 @@
 HALF = 256
 PAIR = 2
 SPARE = 8
+ROOM = 24 << 10
 GROUP = 4
 
 
@@ -202,7 +203,7 @@
 
 def gram(tiles, inverse_factor, tile_count, seats):
     capacity, rows, columns = tiles.shape
-    pair = jax.ShapeDtypeStruct((PAIR * rows, columns), jnp.float32)
+    pair = jax.ShapeDtypeStruct((ROOM, columns), jnp.float32)
     hbm = pl.BlockSpec(memory_space=pl.ANY)
     return pl.pallas_call(
         gram_kernel,

time: 118 us -> 117 us (level)
  starting transfers between devices: 44.5 us -> 53.5 us
  Pallas kernels: 49.8 us -> 43 us
  waiting for transfers between devices: 15.6 us -> 13.8 us
    ppermute x7, starting transfers between devices: 10.8 us -> 18.8 us  [scatter_sum(): lax.ppermute(sent, axis, ring_pairs(size, span, stride, shift))]
    pallas_call x1, Pallas kernels: 12 us -> 6.89 us  [gram(): pl.pallas_call(gram_kernel, out_shape=(jax.ShapeDtypeStruct((3 * HALF, HA...]
    pallas_call x1, Pallas kernels: 5.42 us -> 3.23 us  [pack(): pl.pallas_call(pack_kernel, out_shape=(two_pairs, two_pairs, two_pairs, t...]
    ppermute x7, starting transfers between devices: 13 us -> 15 us  [other_core(): return lax.ppermute(value, 'scene', ring_pairs(scenes, 2, 1, 1))]
    ppermute x7, waiting for transfers between devices: 6.25 us -> 4.3 us  [scatter_sum(): lax.ppermute(sent, axis, ring_pairs(size, span, stride, shift))]
  transfers between devices with their start and end apart: 26 -> 26, of which waited for: 12 -> 13; matrix products, arithmetic and copies ran while one was open for 4% -> 4% of each run, Pallas kernels for 36% -> 31%
where the time goes in v10:
time: 117 us
  starting transfers between devices  53.5 us (46%)
  Pallas kernels  43 us (37%)
  waiting for transfers between devices  13.8 us (12%)
  local copies, waits for them, and re-layouts  4 us (3%)
  between operations  1.64 us (1%)
    pallas_call x1, Pallas kernels, factor(): pl.pallas_call(functools.partial(factor_kernel, row_count), out_shape=(ja...  22.5 us
    ppermute x7, starting transfers between devices, scatter_sum(): lax.ppermute(sent, axis, ring_pairs(size, span, stride, shift))  18.8 us
    ppermute x9, starting transfers between devices, from_ahead(): lax.ppermute(value, axis, ring_pairs(size, span, stride, span - ahead))  15 us
    ppermute x7, starting transfers between devices, other_core(): return lax.ppermute(value, 'scene', ring_pairs(scenes, 2, 1, 1))  15 us
    pallas_call x2, Pallas kernels, finish(): pl.pallas_call(functools.partial(finish_kernel, pairs), out_shape=jax.Sha...  7.96 us
    pallas_call x1, Pallas kernels, gram(): pl.pallas_call(gram_kernel, out_shape=(jax.ShapeDtypeStruct((3 * HALF, HA...  6.89 us
    ppermute x3, starting transfers between devices, along_z(): return lax.ppermute(value, 'scene', ring_pairs(scenes, chips, 2, up))  4.67 us
    ppermute x7, waiting for transfers between devices, scatter_sum(): lax.ppermute(sent, axis, ring_pairs(size, span, stride, shift))  4.3 us
  transfers between devices with their start and end apart: 26, of which 13 were waited for; matrix products, arithmetic and copies ran while one was open for 4% of the time, Pallas kernels for 31%

profile of v10, /device:TPU:1, one launch (start us, length us, event | category | flops | bytes accessed | tf_op | source)
XLA Modules:
  0.0 117.2 jit_solution(13312199097078336367)
XLA Ops:
  1.3 3.2 %pack.1 = (f32[2,2,256,512]{3,2,1,0:T(8,128)}, f32[2,2,256,512]{3,2,1,0:T(8,128)}, f32[2,2,256,512]{3,2,1,0:T(8,128)}, s32[16]{0:T(128)}, s32[16]{0:T(128)}) custom-call(s32[1]{0:T(128)S(6)} %copy.10.count_ref, s32[16]{0:T(128)} %owner_ref.1, s32[16]{0:T(128)} %slot_ref.1, f32[16,256,512]{2,1,0:T(8,128)} %tile_ref), custom_call_target="tpu_custom_call" | custom-call | bytes 8388608 | tf_op jit(solution)/shard_map/pack/pallas_call | solution.py:125
  4.5 5.0 %collective-permute-start = (f32[2,2,256,512]{3,2,1,0:T(8,128)}, f32[2,2,256,512]{3,2,1,0:T(8,128)}, u32[]{:S(2)}, u32[]{:S(2)}) collective-permute-start(f32[2,2,256,512]{3,2,1,0:T(8,128)} %get-tuple-element.43), channel_id=1, source_target_pairs={{0,16},{16,0},{32,48},{48,32},{64,80},{80,64},{96,112},{112,96},{1... | collective-permute-start | bytes 6291464 | tf_op jit(solution)/shard_map/ppermute | solution.py:540
  9.5 2.7 %collective-permute-start.13 = (f32[2,2,256,512]{3,2,1,0:T(8,128)}, f32[2,2,256,512]{3,2,1,0:T(8,128)}, u32[]{:S(2)}, u32[]{:S(2)}) collective-permute-start(f32[2,2,256,512]{3,2,1,0:T(8,128)} %get-tuple-element.49), channel_id=1, source_target_pairs={{0,96},{16,112},{32,0},{48,16},{64,32},{80,48},{96,64},{112,80},{1... | collective-permute-start | bytes 6291464 | tf_op jit(solution)/shard_map/ppermute | solution.py:537
  12.2 6.9 %gram.1 = (f32[768,256]{1,0:T(8,128)}, f32[24576,512]{1,0:T(8,128)}, f32[1032,512]{1,0:T(8,128)}) custom-call(s32[1]{0:T(128)S(6)} %copy.10.count_ref, s32[16]{0:T(128)} %get-tuple-element.40.seat_ref, f32[16,256,512]{2,1,0:T(8,128)} %tile_ref, f32[512,512]{1,0:T(8,128)} %inverse_ref.3), custom_call_target="tpu_custom_call" | custom-call | flops 1000000 | bytes 65536 | tf_op jit(solution)/shard_map/gram/pallas_call | solution.py:208
  20.2 8.3 %collective-permute-start.1 = (f32[384,256]{1,0:T(8,128)S(1)}, f32[384,256]{1,0:T(8,128)S(1)}, u32[]{:S(2)}, u32[]{:S(2)}) collective-permute-start(f32[384,256]{1,0:T(8,128)S(1)} %dynamic-slice_bitcast_fusion), channel_id=1, source_target_pairs={{0,16},{16,0},{32,48},{48,32},{64,80},{80,64},{96,112},{112,96},{1... | collective-permute-start | bytes 1179656 | tf_op jit(solution)/shard_map/ppermute | solution.py:261
  30.9 2.9 %collective-permute-start.3 = (f32[96,256]{1,0:T(8,128)S(1)}, f32[96,256]{1,0:T(8,128)S(1)}, u32[]{:S(2)}, u32[]{:S(2)}) collective-permute-start(f32[96,256]{1,0:T(8,128)S(1)} %get-tuple-element.68), channel_id=1, source_target_pairs={{0,2},{1,3},{2,0},{3,1},{4,6},{5,7},{6,4},{7,5},{8,10},{9,11},{10,... | collective-permute-start | bytes 294920 | tf_op jit(solution)/shard_map/ppermute | solution.py:261
  33.9 2.0 %collective-permute-start.4 = (f32[96,256]{1,0:T(8,128)S(1)}, f32[96,256]{1,0:T(8,128)S(1)}, u32[]{:S(2)}, u32[]{:S(2)}) collective-permute-start(f32[96,256]{1,0:T(8,128)S(1)} %get-tuple-element.67), channel_id=1, source_target_pairs={{0,3},{1,0},{2,1},{3,2},{4,7},{5,4},{6,5},{7,6},{8,11},{9,8},{10,9... | collective-permute-start | bytes 294920 | tf_op jit(solution)/shard_map/ppermute | solution.py:261
  36.1 2.6 %collective-permute-done.3 = f32[96,256]{1,0:T(8,128)S(1)} collective-permute-done((f32[96,256]{1,0:T(8,128)S(1)}, f32[96,256]{1,0:T(8,128)S(1)}, u32[]{:S(2)}, u32[]{:S(2)}) %collective-permute-start.3) | collective-permute-done | bytes 98336 | tf_op jit(solution)/shard_map/ppermute | solution.py:261
  40.1 3.5 %collective-permute-start.6 = (f32[24,256]{1,0:T(8,128)S(1)}, f32[24,256]{1,0:T(8,128)S(1)}, u32[]{:S(2)}, u32[]{:S(2)}) collective-permute-start(f32[24,256]{1,0:T(8,128)S(1)} %get-tuple-element.75), channel_id=1, source_target_pairs={{0,8},{1,9},{2,10},{3,11},{4,12},{5,13},{6,14},{7,15},{8,0},{9,1},... | collective-permute-start | bytes 73736 | tf_op jit(solution)/shard_map/ppermute | solution.py:261
  45.8 1.8 %collective-permute-start.8 = (f32[8,128]{1,0:T(8,128)S(1)}, f32[8,128]{1,0:T(8,128)S(1)}, u32[]{:S(2)}, u32[]{:S(2)}) collective-permute-start(f32[8,128]{1,0:T(8,128)S(1)} %scatter.4), channel_id=1, source_target_pairs={{0,16},{16,0},{32,48},{48,32},{64,80},{80,64},{96,112},{112,96},{1... | collective-permute-start | bytes 12296 | tf_op jit(solution)/shard_map/ppermute | solution.py:540
  48.4 2.3 %collective-permute-start.10 = (f32[32,256]{1,0:T(8,128)S(1)}, f32[32,256]{1,0:T(8,128)S(1)}, u32[]{:S(2)}, u32[]{:S(2)}) collective-permute-start(f32[32,256]{1,0:T(8,128)S(1)} %maximum_maximum_fusion), channel_id=1, source_target_pairs={{0,64},{16,80},{32,96},{48,112},{64,0},{80,16},{96,32},{112,48},{1... | collective-permute-start | bytes 98312 | tf_op jit(solution)/shard_map/ppermute | solution.py:275
  51.9 1.5 %collective-permute-start.9 = (f32[32,256]{1,0:T(8,128)S(1)}, f32[32,256]{1,0:T(8,128)S(1)}, u32[]{:S(2)}, u32[]{:S(2)}) collective-permute-start(f32[32,256]{1,0:T(8,128)S(1)} %maximum_maximum_fusion), channel_id=1, source_target_pairs={{0,96},{16,112},{32,0},{48,16},{64,32},{80,48},{96,64},{112,80},{1... | collective-permute-start | bytes 98312 | tf_op jit(solution)/shard_map/ppermute | solution.py:275
  54.4 3.7 %collective-permute-done.12.first_ref.refs_2_ = f32[2,2,256,512]{3,2,1,0:T(8,128)S(1)} collective-permute-done((f32[2,2,256,512]{3,2,1,0:T(8,128)}, f32[2,2,256,512]{3,2,1,0:T(8,128)S(1)}, u32[]{:S(2)}, u32[]{:S(2)}) %collective-permute-start.12) | collective-permute-done | bytes 2097184 | tf_op jit(solution)/shard_map/ppermute | solution.py:537
  59.5 2.0 %collective-permute-start.24 = (f32[1032,512]{1,0:T(8,128)}, f32[1032,512]{1,0:T(8,128)S(1)}, u32[]{:S(2)}, u32[]{:S(2)}) collective-permute-start(f32[1032,512]{1,0:T(8,128)} %constant_dynamic-update-slice_fusion), channel_id=1, source_target_pairs={{0,64},{16,80},{32,96},{48,112},{64,0},{80,16},{96,32},{112,48},{1... | collective-permute-start | bytes 6340616 | tf_op jit(solution)/shard_map/ppermute | solution.py:537
  61.5 2.5 %second_pairs.1 = f32[2,2,256,512]{3,2,1,0:T(8,128)} custom-call(f32[2,2,256,512]{3,2,1,0:T(8,128)} %copy-done, f32[2,2,256,512]{3,2,1,0:T(8,128)} %collective-permute-done.13.second_ref.refs_3_), custom_call_target="tpu_custom_call" | custom-call | flops 1000000 | bytes 65536 | tf_op jit(solution)/shard_map/second_pairs/pallas_call | solution.py:515
  64.0 1.5 %collective-permute-start.25 = (f32[2,2,256,512]{3,2,1,0:T(8,128)}, f32[2,2,256,512]{3,2,1,0:T(8,128)}, u32[]{:S(2)}, u32[]{:S(2)}) collective-permute-start(f32[2,2,256,512]{3,2,1,0:T(8,128)} %second_pairs.1), channel_id=1, source_target_pairs={{0,16},{16,0},{32,48},{48,32},{64,80},{80,64},{96,112},{112,96},{1... | collective-permute-start | bytes 6291464 | tf_op jit(solution)/shard_map/ppermute | solution.py:540
  65.4 1.7 %collective-permute-start.14 = (f32[24,256]{1,0:T(8,128)S(1)}, f32[24,256]{1,0:T(8,128)S(1)}, u32[]{:S(2)}, u32[]{:S(2)}) collective-permute-start(f32[24,256]{1,0:T(8,128)S(1)} %select_add_fusion), channel_id=1, source_target_pairs={{0,4},{1,5},{2,6},{3,7},{4,8},{5,9},{6,10},{7,11},{8,12},{9,13},{1... | collective-permute-start | bytes 73736 | tf_op jit(solution)/shard_map/ppermute | solution.py:275
  67.1 3.5 %collective-permute-start.15 = (f32[24,256]{1,0:T(8,128)S(1)}, f32[24,256]{1,0:T(8,128)S(1)}, u32[]{:S(2)}, u32[]{:S(2)}) collective-permute-start(f32[24,256]{1,0:T(8,128)S(1)} %select_add_fusion), channel_id=1, source_target_pairs={{0,8},{1,9},{2,10},{3,11},{4,12},{5,13},{6,14},{7,15},{8,0},{9,1},... | collective-permute-start | bytes 73736 | tf_op jit(solution)/shard_map/ppermute | solution.py:275
  73.6 2.5 %collective-permute-start.17 = (f32[96,256]{1,0:T(8,128)S(1)}, f32[96,256]{1,0:T(8,128)S(1)}, u32[]{:S(2)}, u32[]{:S(2)}) collective-permute-start(f32[96,256]{1,0:T(8,128)S(1)} %pad_maximum_fusion.refs_0_), channel_id=1, source_target_pairs={{0,3},{1,0},{2,1},{3,2},{4,7},{5,4},{6,5},{7,6},{8,11},{9,8},{10,9... | collective-permute-start | bytes 294920 | tf_op jit(solution)/shard_map/ppermute | solution.py:275
  77.8 3.0 %collective-permute-start.20 = (f32[96,256]{1,0:T(8,128)S(1)}, f32[96,256]{1,0:T(8,128)S(1)}, u32[]{:S(2)}, u32[]{:S(2)}) collective-permute-start(f32[96,256]{1,0:T(8,128)S(1)} %pad_maximum_fusion.refs_0_), channel_id=1, source_target_pairs={{0,16},{16,0},{32,48},{48,32},{64,80},{80,64},{96,112},{112,96},{1... | collective-permute-start | bytes 294920 | tf_op jit(solution)/shard_map/ppermute | solution.py:540
  81.5 2.8 %collective-permute-start.21 = (f32[96,256]{1,0:T(8,128)S(1)}, f32[96,256]{1,0:T(8,128)S(1)}, u32[]{:S(2)}, u32[]{:S(2)}) collective-permute-start(f32[96,256]{1,0:T(8,128)S(1)} %collective-permute-done.17.refs_1_), channel_id=1, source_target_pairs={{0,16},{16,0},{32,48},{48,32},{64,80},{80,64},{96,112},{112,96},{1... | collective-permute-start | bytes 294920 | tf_op jit(solution)/shard_map/ppermute | solution.py:540
  86.5 22.5 %factor.1 = (f32[512,512]{1,0:T(8,128)}, bf16[512,512]{1,0:T(8,128)(2,1)S(1)}, bf16[512,512]{1,0:T(8,128)(2,1)S(1)}) custom-call(f32[512,512]{1,0:T(8,128)S(1)} %copy-done.2, f32[96,256]{1,0:T(8,128)S(1)} %pad_maximum_fusion.refs_0_, f32[96,256]{1,0:T(8,128)S(1)} %collective-permute-done.17.refs_1_, f32[96,256]{1,0:T(8,128)S(1)} %collective-permute-done.18.refs_2_, ...), custom_call_target="tpu_custom_call" | custom-call | flops 1000000 | bytes 65536 | tf_op jit(solution)/shard_map/factor/pallas_call | solution.py:402
  109.0 5.0 %finish_near.1.refs_2_ = f32[8,256,512]{2,1,0:T(8,128)} custom-call(s32[12]{0:T(128)S(1)} %bitcast.51, bf16[512,512]{1,0:T(8,128)(2,1)S(1)} %get-tuple-element.59.head_ref, bf16[512,512]{1,0:T(8,128)(2,1)S(1)} %get-tuple-element.60.tail_ref, f32[24576,512]{1,0:T(8,128)} %get-tuple-element.62.refs_0_, f32[2,2,256,512]{3,2,1,0:T(8,128)} %collective-permute-done.refs_1_, ...), custom_call_target="tpu_custom_call" | custom-call | flops 1000000 | bytes 65536 | tf_op jit(solution)/shard_map/finish_near/pallas_call | solution.py:467
  114.0 3.0 %finish_far.1 = f32[8,256,512]{2,1,0:T(8,128)} custom-call(s32[4]{0:T(128)S(1)} %slice.74.slot_ref, bf16[512,512]{1,0:T(8,128)(2,1)S(1)} %get-tuple-element.59.head_ref, bf16[512,512]{1,0:T(8,128)(2,1)S(1)} %get-tuple-element.60.tail_ref, f32[1032,512]{1,0:T(8,128)S(1)} %collective-permute-done.24.refs_0_.refs_1_, ...), custom_call_target="tpu_custom_call", output_to_operand_aliasing={{}: (5, {})} | custom-call | flops 1000000 | bytes 65536 | tf_op jit(solution)/shard_map/finish_far/pallas_call | solution.py:467
  (61 shorter events, 19.3 us)
Async XLA Ops:
  4.5 14.6 %collective-permute-start = (f32[2,2,256,512]{3,2,1,0:T(8,128)}, f32[2,2,256,512]{3,2,1,0:T(8,128)}, u32[]{:S(2)}, u32[]{:S(2)}) collective-permute-start(f32[2,2,256,512]{3,2,1,0:T(8,128)} %get-tuple-element.43), channel_id=1, source_target_pairs={{0,16},{16,0},{32,48},{48,32},{64,80},{80,64},{96,112},{112,96},{1... | collective-permute-start | bytes 6291464 | tf_op jit(solution)/shard_map/ppermute | solution.py:540
  9.5 48.6 %collective-permute-start.12 = (f32[2,2,256,512]{3,2,1,0:T(8,128)}, f32[2,2,256,512]{3,2,1,0:T(8,128)S(1)}, u32[]{:S(2)}, u32[]{:S(2)}) collective-permute-start(f32[2,2,256,512]{3,2,1,0:T(8,128)} %get-tuple-element.48), channel_id=1, source_target_pairs={{0,32},{16,48},{32,64},{48,80},{64,96},{80,112},{96,0},{112,16},{1... | collective-permute-start | bytes 6291464 | tf_op jit(solution)/shard_map/ppermute | solution.py:537
  9.5 48.6 %collective-permute-start.13 = (f32[2,2,256,512]{3,2,1,0:T(8,128)}, f32[2,2,256,512]{3,2,1,0:T(8,128)}, u32[]{:S(2)}, u32[]{:S(2)}) collective-permute-start(f32[2,2,256,512]{3,2,1,0:T(8,128)} %get-tuple-element.49), channel_id=1, source_target_pairs={{0,96},{16,112},{32,0},{48,16},{64,32},{80,48},{96,64},{112,80},{1... | collective-permute-start | bytes 6291464 | tf_op jit(solution)/shard_map/ppermute | solution.py:537
  20.2 9.6 %collective-permute-start.1 = (f32[384,256]{1,0:T(8,128)S(1)}, f32[384,256]{1,0:T(8,128)S(1)}, u32[]{:S(2)}, u32[]{:S(2)}) collective-permute-start(f32[384,256]{1,0:T(8,128)S(1)} %dynamic-slice_bitcast_fusion), channel_id=1, source_target_pairs={{0,16},{16,0},{32,48},{48,32},{64,80},{80,64},{96,112},{112,96},{1... | collective-permute-start | bytes 1179656 | tf_op jit(solution)/shard_map/ppermute | solution.py:261
  30.9 5.3 %collective-permute-start.2 = (f32[96,256]{1,0:T(8,128)S(1)}, f32[96,256]{1,0:T(8,128)S(1)}, u32[]{:S(2)}, u32[]{:S(2)}) collective-permute-start(f32[96,256]{1,0:T(8,128)S(1)} %get-tuple-element.66), channel_id=1, source_target_pairs={{0,1},{1,2},{2,3},{3,0},{4,5},{5,6},{6,7},{7,4},{8,9},{9,10},{10,1... | collective-permute-start | bytes 294920 | tf_op jit(solution)/shard_map/ppermute | solution.py:261
  30.9 7.8 %collective-permute-start.3 = (f32[96,256]{1,0:T(8,128)S(1)}, f32[96,256]{1,0:T(8,128)S(1)}, u32[]{:S(2)}, u32[]{:S(2)}) collective-permute-start(f32[96,256]{1,0:T(8,128)S(1)} %get-tuple-element.68), channel_id=1, source_target_pairs={{0,2},{1,3},{2,0},{3,1},{4,6},{5,7},{6,4},{7,5},{8,10},{9,11},{10,... | collective-permute-start | bytes 294920 | tf_op jit(solution)/shard_map/ppermute | solution.py:261
  33.9 4.9 %collective-permute-start.4 = (f32[96,256]{1,0:T(8,128)S(1)}, f32[96,256]{1,0:T(8,128)S(1)}, u32[]{:S(2)}, u32[]{:S(2)}) collective-permute-start(f32[96,256]{1,0:T(8,128)S(1)} %get-tuple-element.67), channel_id=1, source_target_pairs={{0,3},{1,0},{2,1},{3,2},{4,7},{5,4},{6,5},{7,6},{8,11},{9,8},{10,9... | collective-permute-start | bytes 294920 | tf_op jit(solution)/shard_map/ppermute | solution.py:261
  38.8 6.9 %collective-permute-start.5 = (f32[24,256]{1,0:T(8,128)S(1)}, f32[24,256]{1,0:T(8,128)S(1)}, u32[]{:S(2)}, u32[]{:S(2)}) collective-permute-start(f32[24,256]{1,0:T(8,128)S(1)} %get-tuple-element.73), channel_id=1, source_target_pairs={{0,4},{1,5},{2,6},{3,7},{4,8},{5,9},{6,10},{7,11},{8,12},{9,13},{1... | collective-permute-start | bytes 73736 | tf_op jit(solution)/shard_map/ppermute | solution.py:261
  40.1 7.5 %collective-permute-start.6 = (f32[24,256]{1,0:T(8,128)S(1)}, f32[24,256]{1,0:T(8,128)S(1)}, u32[]{:S(2)}, u32[]{:S(2)}) collective-permute-start(f32[24,256]{1,0:T(8,128)S(1)} %get-tuple-element.75), channel_id=1, source_target_pairs={{0,8},{1,9},{2,10},{3,11},{4,12},{5,13},{6,14},{7,15},{8,0},{9,1},... | collective-permute-start | bytes 73736 | tf_op jit(solution)/shard_map/ppermute | solution.py:261
  43.7 3.9 %collective-permute-start.7 = (f32[24,256]{1,0:T(8,128)S(1)}, f32[24,256]{1,0:T(8,128)S(1)}, u32[]{:S(2)}, u32[]{:S(2)}) collective-permute-start(f32[24,256]{1,0:T(8,128)S(1)} %get-tuple-element.74), channel_id=1, source_target_pairs={{0,12},{1,13},{2,14},{3,15},{4,0},{5,1},{6,2},{7,3},{8,4},{9,5},{1... | collective-permute-start | bytes 73736 | tf_op jit(solution)/shard_map/ppermute | solution.py:261
  45.8 2.6 %collective-permute-start.8 = (f32[8,128]{1,0:T(8,128)S(1)}, f32[8,128]{1,0:T(8,128)S(1)}, u32[]{:S(2)}, u32[]{:S(2)}) collective-permute-start(f32[8,128]{1,0:T(8,128)S(1)} %scatter.4), channel_id=1, source_target_pairs={{0,16},{16,0},{32,48},{48,32},{64,80},{80,64},{96,112},{112,96},{1... | collective-permute-start | bytes 12296 | tf_op jit(solution)/shard_map/ppermute | solution.py:540
  48.4 10.2 %collective-permute-start.10 = (f32[32,256]{1,0:T(8,128)S(1)}, f32[32,256]{1,0:T(8,128)S(1)}, u32[]{:S(2)}, u32[]{:S(2)}) collective-permute-start(f32[32,256]{1,0:T(8,128)S(1)} %maximum_maximum_fusion), channel_id=1, source_target_pairs={{0,64},{16,80},{32,96},{48,112},{64,0},{80,16},{96,32},{112,48},{1... | collective-permute-start | bytes 98312 | tf_op jit(solution)/shard_map/ppermute | solution.py:275
  50.7 8.5 %collective-permute-start.11 = (f32[32,256]{1,0:T(8,128)S(1)}, f32[32,256]{1,0:T(8,128)S(1)}, u32[]{:S(2)}, u32[]{:S(2)}) collective-permute-start(f32[32,256]{1,0:T(8,128)S(1)} %maximum_maximum_fusion), channel_id=1, source_target_pairs={{0,32},{16,48},{32,64},{48,80},{64,96},{80,112},{96,0},{112,16},{1... | collective-permute-start | bytes 98312 | tf_op jit(solution)/shard_map/ppermute | solution.py:275
  51.9 7.6 %collective-permute-start.9 = (f32[32,256]{1,0:T(8,128)S(1)}, f32[32,256]{1,0:T(8,128)S(1)}, u32[]{:S(2)}, u32[]{:S(2)}) collective-permute-start(f32[32,256]{1,0:T(8,128)S(1)} %maximum_maximum_fusion), channel_id=1, source_target_pairs={{0,96},{16,112},{32,0},{48,16},{64,32},{80,48},{96,64},{112,80},{1... | collective-permute-start | bytes 98312 | tf_op jit(solution)/shard_map/ppermute | solution.py:275
  59.5 54.5 %collective-permute-start.24 = (f32[1032,512]{1,0:T(8,128)}, f32[1032,512]{1,0:T(8,128)S(1)}, u32[]{:S(2)}, u32[]{:S(2)}) collective-permute-start(f32[1032,512]{1,0:T(8,128)} %constant_dynamic-update-slice_fusion), channel_id=1, source_target_pairs={{0,64},{16,80},{32,96},{48,112},{64,0},{80,16},{96,32},{112,48},{1... | collective-permute-start | bytes 6340616 | tf_op jit(solution)/shard_map/ppermute | solution.py:537
  64.0 45.0 %collective-permute-start.25 = (f32[2,2,256,512]{3,2,1,0:T(8,128)}, f32[2,2,256,512]{3,2,1,0:T(8,128)}, u32[]{:S(2)}, u32[]{:S(2)}) collective-permute-start(f32[2,2,256,512]{3,2,1,0:T(8,128)} %second_pairs.1), channel_id=1, source_target_pairs={{0,16},{16,0},{32,48},{48,32},{64,80},{80,64},{96,112},{112,96},{1... | collective-permute-start | bytes 6291464 | tf_op jit(solution)/shard_map/ppermute | solution.py:540
  65.4 6.3 %collective-permute-start.14 = (f32[24,256]{1,0:T(8,128)S(1)}, f32[24,256]{1,0:T(8,128)S(1)}, u32[]{:S(2)}, u32[]{:S(2)}) collective-permute-start(f32[24,256]{1,0:T(8,128)S(1)} %select_add_fusion), channel_id=1, source_target_pairs={{0,4},{1,5},{2,6},{3,7},{4,8},{5,9},{6,10},{7,11},{8,12},{9,13},{1... | collective-permute-start | bytes 73736 | tf_op jit(solution)/shard_map/ppermute | solution.py:275
  67.1 5.3 %collective-permute-start.15 = (f32[24,256]{1,0:T(8,128)S(1)}, f32[24,256]{1,0:T(8,128)S(1)}, u32[]{:S(2)}, u32[]{:S(2)}) collective-permute-start(f32[24,256]{1,0:T(8,128)S(1)} %select_add_fusion), channel_id=1, source_target_pairs={{0,8},{1,9},{2,10},{3,11},{4,12},{5,13},{6,14},{7,15},{8,0},{9,1},... | collective-permute-start | bytes 73736 | tf_op jit(solution)/shard_map/ppermute | solution.py:275
  70.6 3.0 %collective-permute-start.16 = (f32[24,256]{1,0:T(8,128)S(1)}, f32[24,256]{1,0:T(8,128)S(1)}, u32[]{:S(2)}, u32[]{:S(2)}) collective-permute-start(f32[24,256]{1,0:T(8,128)S(1)} %select_add_fusion), channel_id=1, source_target_pairs={{0,12},{1,13},{2,14},{3,15},{4,0},{5,1},{6,2},{7,3},{8,4},{9,5},{1... | collective-permute-start | bytes 73736 | tf_op jit(solution)/shard_map/ppermute | solution.py:275
  73.6 4.2 %collective-permute-start.17 = (f32[96,256]{1,0:T(8,128)S(1)}, f32[96,256]{1,0:T(8,128)S(1)}, u32[]{:S(2)}, u32[]{:S(2)}) collective-permute-start(f32[96,256]{1,0:T(8,128)S(1)} %pad_maximum_fusion.refs_0_), channel_id=1, source_target_pairs={{0,3},{1,0},{2,1},{3,2},{4,7},{5,4},{6,5},{7,6},{8,11},{9,8},{10,9... | collective-permute-start | bytes 294920 | tf_op jit(solution)/shard_map/ppermute | solution.py:275
  76.2 5.3 %collective-permute-start.18 = (f32[96,256]{1,0:T(8,128)S(1)}, f32[96,256]{1,0:T(8,128)S(1)}, u32[]{:S(2)}, u32[]{:S(2)}) collective-permute-start(f32[96,256]{1,0:T(8,128)S(1)} %pad_maximum_fusion.refs_0_), channel_id=1, source_target_pairs={{0,2},{1,3},{2,0},{3,1},{4,6},{5,7},{6,4},{7,5},{8,10},{9,11},{10,... | collective-permute-start | bytes 294920 | tf_op jit(solution)/shard_map/ppermute | solution.py:275
  76.9 7.3 %collective-permute-start.19 = (f32[96,256]{1,0:T(8,128)S(1)}, f32[96,256]{1,0:T(8,128)S(1)}, u32[]{:S(2)}, u32[]{:S(2)}) collective-permute-start(f32[96,256]{1,0:T(8,128)S(1)} %pad_maximum_fusion.refs_0_), channel_id=1, source_target_pairs={{0,1},{1,2},{2,3},{3,0},{4,5},{5,6},{6,7},{7,4},{8,9},{9,10},{10,1... | collective-permute-start | bytes 294920 | tf_op jit(solution)/shard_map/ppermute | solution.py:275
  77.8 7.4 %collective-permute-start.20 = (f32[96,256]{1,0:T(8,128)S(1)}, f32[96,256]{1,0:T(8,128)S(1)}, u32[]{:S(2)}, u32[]{:S(2)}) collective-permute-start(f32[96,256]{1,0:T(8,128)S(1)} %pad_maximum_fusion.refs_0_), channel_id=1, source_target_pairs={{0,16},{16,0},{32,48},{48,32},{64,80},{80,64},{96,112},{112,96},{1... | collective-permute-start | bytes 294920 | tf_op jit(solution)/shard_map/ppermute | solution.py:540
  81.5 3.8 %collective-permute-start.21 = (f32[96,256]{1,0:T(8,128)S(1)}, f32[96,256]{1,0:T(8,128)S(1)}, u32[]{:S(2)}, u32[]{:S(2)}) collective-permute-start(f32[96,256]{1,0:T(8,128)S(1)} %collective-permute-done.17.refs_1_), channel_id=1, source_target_pairs={{0,16},{16,0},{32,48},{48,32},{64,80},{80,64},{96,112},{112,96},{1... | collective-permute-start | bytes 294920 | tf_op jit(solution)/shard_map/ppermute | solution.py:540
  (6 other events, 92.3 us)
